TPU v7x, 128 devices: a whole 4x4x4 slice. The times are simulated.
128 devices in a mesh: dp: 4 (over x), grid: 32 (over z, y, core).
Axes of the slice: x: 4, y: 4, z: 4, core: 2. Of those that a mesh axis runs over, the one named last changes fastest.
Arguments:
- intensities: bfloat16 [8192, 32, 128], P(('dp', 'grid')), may hold values from -6 to 6
- gridding: bfloat16 [8192, 32, 512], P(('dp', 'grid')), may hold values from -0.0625 to 0.0625
- dest_slab: int32 [8192, 1], P(('dp', 'grid')), may hold values from 0 to 31; in each aligned block of 64 rows (0 to 63, 64 to 127, ...) at most 4 rows name the same one
- spectral_weights: float32 [4, 128, 128, 128], P('dp', None, 'grid'), may hold values from 0.05 to 2
Outputs:
- solution_field: float32 [128, 128, 128], P('grid')
- residual: float32 [128, 128, 128], P('grid')
Inputs may be any that keep to these rules, and one draw needn't show every extreme that they name: `dest_slab`: at most 4 of one device's 64 snapshots name the same slab, and in every draw some device has exactly 4 that name one slab.
All inputs are finite; a program needn't handle non-finite values.
Results may differ from a plain program's by a relative error of at most 0.0003.
Values may be sent and summed in bfloat16 or wider, within the bound.
No kernel may reach another device: no remote copies, remote signals or barrier semaphores. Data moves between devices by JAX's collectives and lax.ppermute only.
A program may use at most 128 MiB of HBM per device.

v0:
```python
import functools

import jax
import jax.numpy as jnp
import numpy as np
from jax import lax
from jax.experimental import pallas as pl
from jax.experimental.pallas import tpu as pltpu
from jax.sharding import PartitionSpec as P


ITERS = 8
MOMENTS = 2 * ITERS + 1
LOW_LANE = 64
ALL = ("dp", "grid")
HIGHEST = lax.Precision.HIGHEST


def two_sum(a, b):
    s = a + b
    v = s - a
    return s, (a - (s - v)) + (b - v)


def quick_sum(a, b):
    s = a + b
    return s, b - (s - a)


def halves(a):
    c = a * 4097.0
    high = c - (c - a)
    return high, a - high


def two_prod(a, b, a_parts=None, b_parts=None):
    p = a * b
    ah, al = a_parts or halves(a)
    bh, bl = b_parts or halves(b)
    return p, ((ah * bh - p) + ah * bl + al * bh) + al * bl


def dd_add(a, b):
    s, e = two_sum(a[0], b[0])
    t, f = two_sum(a[1], b[1])
    s, e = quick_sum(s, e + t)
    return quick_sum(s, e + f)


def dd_mul(a, b):
    p, e = two_prod(a[0], b[0])
    return quick_sum(p, e + (a[0] * b[1] + a[1] * b[0]))


def dd_times(a, b):
    p, e = two_prod(a[0], b)
    return quick_sum(p, e + a[1] * b)


def dd_scale(a, factor):
    return a[0] * factor, a[1] * factor


def dd_neg(a):
    return -a[0], -a[1]


def dd_div(a, b):
    inverse = 1.0 / b[0]
    first = a[0] * inverse
    rest = dd_add(a, dd_neg(dd_times(b, first)))
    second = rest[0] * inverse
    rest = dd_add(rest, dd_neg(dd_times(b, second)))
    high, low = quick_sum(first, second)
    return quick_sum(high, low + rest[0] * inverse)


def dot(a, b):
    return jax.lax.dot_general(
        a, b, (((1,), (0,)), ((), ())), precision=HIGHEST, preferred_element_type=jnp.float32
    )


SIDE = 4
CORES = 2
ORDERS = ((0, 1, 2), (1, 2, 0))


def place_of(device):
    chip = device // CORES
    return chip // SIDE**2, chip % SIDE, (chip // SIDE) % SIDE, device % CORES


def chip_at(x, y, z):
    return (x * SIDE + z) * SIDE + y


def shift_pairs(axes, hop):
    pairs = []
    for device in range(SIDE**3 * CORES):
        place = list(place_of(device))
        axis = axes[place[3]]
        place[axis] = (place[axis] + hop) % (CORES if axis == 3 else SIDE)
        pairs.append((device, chip_at(*place[:3]) * CORES + place[3]))
    return pairs


def held_rows(size):
    chip, core = np.arange(size) // CORES, np.arange(size) % CORES
    return np.where(chip == 0, core * size // 2, np.where(core == 0, chip, size - chip))


def weight_rows(size, ndp):
    d = np.arange(size)
    return ndp * (d % (size // ndp)) + d // (size // ndp)


def dft_tables(size, ndp):
    index = np.arange(size)
    angle = 2.0 * np.pi * ((index[:, None] * index[None, :]) % size) / size
    cos, sin = np.cos(angle), np.sin(angle)
    held, order = held_rows(size), weight_rows(size, ndp)
    as_f32 = lambda a: np.ascontiguousarray(a, dtype=np.float32)
    half = size // 2
    packed = np.concatenate([cos[:, :half], cos[:, half : half + 1], -sin[:, 1:half]], 1)
    high = packed.astype(jnp.bfloat16)
    low = (packed - high.astype(np.float64)).astype(jnp.bfloat16)
    return dict(
        packed=np.stack([np.concatenate([p[:, :half], q[:, :half]], 1) for p, q in ((high, low), (high[:, half:], low[:, half:]))]),
        lanes=as_f32(np.concatenate([cos, sin], 1)),
        ky_rows=as_f32(np.concatenate([cos[order], sin[order]], 0)),
        ky_lanes=as_f32(np.concatenate([cos[order], sin[order]], 1)),
        back=as_f32(
            np.concatenate(
                [np.concatenate([cos[held], sin[held]], 1), np.concatenate([-sin[held], cos[held]], 1)], 0
            )
        ),
        held=as_f32(held[:, None] == index[None, :]),
        mirror=as_f32(((index[:, None] + index[None, :]) % size) == 0),
        ky_mirror=as_f32(((order[:, None] + order[None, :]) % size) == 0),
    )


def dot_as(a, b, left, right):
    return lax.dot_general(
        a, b, (((left,), (right,)), ((), ())), precision=HIGHEST, preferred_element_type=jnp.float32
    )


STEPS = 2
HALVES = 2


def sublane_turn(tiles):
    row = lax.broadcasted_iota(jnp.int32, tiles[0].shape, 0)
    for bit in (4, 2, 1):
        low = (row & bit) == 0
        turned = list(tiles)
        for i in range(8):
            if i & bit == 0:
                a, b = tiles[i], tiles[i + bit]
                turned[i] = jnp.where(low, a, pltpu.roll(b, bit, 0))
                turned[i + bit] = jnp.where(low, pltpu.roll(a, 8 - bit, 0), b)
        tiles = turned
    return tiles


def grid_kernel(*refs, kind, part, capacity):
    first, kept = kind == "first", kind == "kept"
    if first:
        dest_ref, place_ref, values_ref, matrix_ref, packed_ref, weights_ref = refs[:6]
        out_ref, wave_ref, count_ref, list_ref = refs[6:10]
    else:
        count_ref, list_ref, place_ref, wave_ref, matrix_ref = refs[:5]
        other_ref, outs, out_ref = (refs[5], refs[6:], None) if kept else (None, None, refs[5])
    nent, rows, width = matrix_ref.shape
    size = width // SIDE
    half = size // 2
    nslab = count_ref.shape[0]
    core = place_ref[3] if kept else 1 - place_ref[3]
    step = pl.program_id(0)

    def clear(s, _):
        count_ref[s] = 0
        return 0

    def enter(e, _):
        slab = dest_ref[e]
        taken = count_ref[slab]
        list_ref[slab * capacity + taken] = e
        count_ref[slab] = taken + 1
        return 0

    def prepare():
        lax.fori_loop(0, nslab, clear, 0)
        lax.fori_loop(0, nent, enter, 0)
        for r, slice_ref in enumerate(refs[10:]):
            slice_ref[...] = weights_ref[0, :, (place_ref[0] + r) % SIDE, :]
        chip = lax.broadcasted_iota(jnp.int32, (half, half), 0)
        slot = lax.broadcasted_iota(jnp.int32, (half, half), 1)
        digits = (slot // SIDE**2, (slot // SIDE) % SIDE, slot % SIDE)
        pieces = []
        for owner in range(CORES):
            at = [place_ref[0], place_ref[1], place_ref[2]]
            for digit, axis in zip(digits, ORDERS[owner]):
                at[axis] = (at[axis] + digit) % SIDE
            pick = (chip == chip_at(*at)).astype(jnp.float32).astype(jnp.bfloat16)
            for start in (0, half):
                piece = packed_ref[owner, :, start : start + half]
                pieces.append(jnp.dot(piece, pick, preferred_element_type=jnp.float32).astype(jnp.bfloat16))
        both = jnp.dot(
            values_ref[...].reshape(nent * rows, size),
            jnp.concatenate(pieces, 1),
            preferred_element_type=jnp.float32,
        )
        for owner in range(CORES):
            wave = both[:, owner * size : owner * size + half] + both[:, owner * size + half : (owner + 1) * size]
            high = wave.astype(jnp.bfloat16)
            low = (wave - high.astype(jnp.float32)).astype(jnp.bfloat16)
            wave_ref[owner] = jnp.concatenate([high, low], 1).reshape(nent, rows, size)

    if first:
        pl.when(step == 0)(prepare)

    pairs = nslab // (2 * STEPS * HALVES)
    for pair in range(pairs):
        products = []
        for near in range(2):
            slab = part * (nslab // HALVES) + (step * pairs + pair) * 2 + near
            taken = count_ref[slab]
            waves, matrices = [], []
            for m in range(capacity):
                entry = jnp.where(m < taken, list_ref[slab * capacity + m], 0)
                wave = wave_ref[core, entry]
                waves.append(jnp.where(m < taken, wave, jnp.zeros_like(wave)))
                matrices.append(matrix_ref[entry])
            product = lax.dot_general(
                jnp.concatenate(waves, 0),
                jnp.concatenate(matrices, 0),
                (((0,), (0,)), ((), ())),
                preferred_element_type=jnp.float32,
            )
            products.append(product[:half] + product[half:])
        place = slice(pair * 8, pair * 8 + 8)
        for start in range(0, half, 8):
            tiles = [
                product[start : start + 8, p * size : (p + 1) * size] for product in products for p in range(SIDE)
            ]
            for index, block in enumerate(sublane_turn(tiles), start):
                if kept:
                    outs[index // SIDE**2][index % SIDE**2, place, :] = block + other_ref[index, place, :]
                else:
                    out_ref[index, place, :] = block


def grid_call(kind, part, nslab, capacity, *args):
    scalars = pl.BlockSpec(memory_space=pltpu.SMEM)
    fixed = lambda shape: pl.BlockSpec(shape, lambda i: (0,) * len(shape))
    matrix = args[3] if kind == "first" else args[4]
    nent, rows, width = matrix.shape
    size, blocks = width // SIDE, SIDE**3
    moving = lambda count: pl.BlockSpec((count, size // (STEPS * HALVES), size), lambda i: (0, i, 0))
    f32 = lambda *shape: jax.ShapeDtypeStruct(shape, jnp.float32)
    if kind == "kept":
        out_shape, out_specs = [f32(SIDE**2, size // HALVES, size)] * SIDE, [moving(SIDE**2)] * SIDE
    else:
        out_shape, out_specs = [f32(blocks, size // HALVES, size)], [moving(blocks)]
    if kind == "first":
        wave = (CORES, nent, rows, size)
        out_shape += [
            jax.ShapeDtypeStruct(wave, jnp.bfloat16),
            jax.ShapeDtypeStruct((nslab,), jnp.int32),
            jax.ShapeDtypeStruct((nslab * capacity,), jnp.int32),
        ] + [f32(size, size)] * SIDE
        out_specs += [fixed(wave), scalars, scalars] + [fixed((size, size))] * SIDE
    in_specs = [scalars if a.dtype == jnp.int32 else fixed(a.shape) for a in args]
    if kind == "kept":
        in_specs[-1] = moving(blocks)
    return pl.pallas_call(
        functools.partial(grid_kernel, kind=kind, part=part, capacity=capacity),
        grid=(STEPS,),
        out_shape=out_shape,
        in_specs=in_specs,
        out_specs=out_specs,
    )(*args)


def weight_kernel(w0_ref, w1_ref, w2_ref, w3_ref, held_ref, out_ref):
    size = w0_ref.shape[0]
    own = ((w0_ref[...] + w1_ref[...]) + w2_ref[...]) + w3_ref[...]
    low = jnp.min(jnp.min(own, axis=0, keepdims=True), axis=1, keepdims=True)
    high = jnp.max(jnp.max(own, axis=0, keepdims=True), axis=1, keepdims=True)
    lane = lax.broadcasted_iota(jnp.int32, (size, size), 1)
    out_ref[:, 0, :] = dot_as(held_ref[...], own, 1, 1)
    out_ref[:, 1, :] = jnp.where(lane < size // 2, low, high)


def symmetry_kernel(given_ref, other_ref, place_ref, ky_mirror_ref, mirror_ref, scaled_ref, range_ref):
    size = scaled_ref.shape[0]
    ends = given_ref[:, 1, :]
    low = jnp.min(jnp.min(ends, axis=0, keepdims=True), axis=1, keepdims=True)
    high = jnp.max(jnp.max(ends, axis=0, keepdims=True), axis=1, keepdims=True)
    half = jnp.maximum((high - low) * 0.5, high * 1e-4)
    half = jnp.broadcast_to(half, (1, size))
    range_ref[0:1, :] = half
    range_ref[1:2, :] = jnp.broadcast_to((high + low) * 0.5, (1, size)) / half
    range_ref[2:8, :] = jnp.zeros((6, size), jnp.float32)
    own = given_ref[:, 0, :]
    partner = jnp.where(place_ref[4] == 1, own, other_ref[:, 0, :])
    mirrored = dot(ky_mirror_ref[...], dot(partner, mirror_ref[...]))
    scaled_ref[...] = (own + mirrored) * 0.5 / half


def sublane_total(a):
    for shift in (4, 2, 1):
        a = dd_add(a, (pltpu.roll(a[0], shift, 0), pltpu.roll(a[1], shift, 0)))
    return a


def lane_total(a):
    for shift in (64, 32, 16, 8, 4, 2, 1):
        a = dd_add(a, (pltpu.roll(a[0], shift, 1), pltpu.roll(a[1], shift, 1)))
    return a


def moment_kernel(own_ref, other_ref, place_ref, scaled_ref, range_ref, lanes_ref, rows_ref, real_ref, imag_ref, send_ref):
    size = own_ref.shape[0]
    centre = range_ref[1:2, :]
    mine, theirs = own_ref[...], other_ref[...]
    second, alone = place_ref[3] == 1, place_ref[4] == 1
    re = jnp.where(jnp.logical_and(second, jnp.logical_not(alone)), theirs, mine)
    im = jnp.where(alone, jnp.zeros_like(mine), jnp.where(second, -mine, theirs))
    ends = dot_as(jnp.concatenate([re, im], 1), lanes_ref[...], 0, 0)
    mid_real = ends[:size, :size] + ends[size:, size:]
    mid_imag = ends[size:, :size] - ends[:size, size:]
    both = dot(rows_ref[...], jnp.concatenate([mid_real, mid_imag], 1))
    real = both[:size, :size] + both[size:, size:]
    imag = both[:size, size:] - both[size:, :size]
    real_ref[...] = real
    imag_ref[...] = imag
    scaled = scaled_ref[...]
    power = real * real + imag * imag
    chunk = 24
    totals = [None] * MOMENTS
    for start in (0, size // 4, size // 4 + chunk):
        row = lax.broadcasted_iota(jnp.int32, (chunk, size), 0) + start
        if start == 0:
            share = jnp.where(row % (size // 8) == 0, 1.0, jnp.where(row < size // 8, 2.0, 0.0))
        else:
            share = 2.0
        t = scaled[start : start + chunk] - centre
        p = power[start : start + chunk] * share
        p_parts = halves(p)
        t2 = t * 2.0
        t2_parts = halves(t2)
        zero = jnp.zeros_like(t)
        before, here = (jnp.ones_like(t), zero), (t, zero)
        for order in range(MOMENTS):
            value = before
            v_parts = halves(value[0])
            term, low_term = two_prod(value[0], p, v_parts, p_parts)
            term = (term, low_term + value[1] * p)
            rows = [(term[0][i : i + 8], term[1][i : i + 8]) for i in range(0, chunk, 8)]
            rows = [dd_add(dd_add(rows[0], rows[1]), rows[2])]
            totals[order] = rows[0] if totals[order] is None else dd_add(totals[order], rows[0])
            if order + 1 < MOMENTS:
                up, low_up = two_prod(here[0], t2, None, t2_parts)
                up, low_up = quick_sum(up, low_up + here[1] * t2)
                following = dd_add((up, low_up), dd_neg(before))
                before, here = here, following
    row = lax.broadcasted_iota(jnp.int32, (8, size), 0)
    lane = lax.broadcasted_iota(jnp.int32, (8, size), 1)
    out = jnp.zeros((8, size), jnp.float32)
    for base in range(0, MOMENTS, 8):
        high_rows = jnp.zeros((8, size), jnp.float32)
        low_rows = jnp.zeros((8, size), jnp.float32)
        for order in range(base, min(base + 8, MOMENTS)):
            total = sublane_total(totals[order])
            high_rows = jnp.where(row == order - base, total[0], high_rows)
            low_rows = jnp.where(row == order - base, total[1], low_rows)
        high_rows, low_rows = lane_total((high_rows, low_rows))
        out = jnp.where(lane == row + base, high_rows, out)
        out = jnp.where(lane == row + (base + LOW_LANE), low_rows, out)
    line = jnp.sum(out, axis=0, keepdims=True)
    send_ref[...] = jnp.broadcast_to(line, (size, size))


def lane_of(a, lane):
    pick = lambda v: jnp.broadcast_to(v[:, lane : lane + 1], v.shape)
    return pick(a[0]), pick(a[1])


def solve_kernel(
    sums_ref, range_ref, scaled_ref, real_ref, imag_ref, lanes_ref, ky_lanes_ref, out_ref, gain_ref, *, scale
):
    size = scaled_ref.shape[0]
    given = sums_ref[...]
    low = pltpu.roll(given, size - LOW_LANE, 1)
    rows = [(given[i : i + 8], low[i : i + 8]) for i in range(0, given.shape[0], 8)]
    while len(rows) > 1:
        rows = [dd_add(rows[i], rows[i + 1]) for i in range(0, len(rows), 2)]
    moments = sublane_total(rows[0])
    half = range_ref[0:1, :]
    centre = jnp.broadcast_to(range_ref[1:2, :], moments[0].shape)
    centre = (centre, jnp.zeros_like(centre))
    lane = lax.broadcasted_iota(jnp.int32, moments[0].shape, 1)
    resid, direct = moments, moments
    held = lane_of(resid, 0)
    steps, turns = [], []
    decay = jnp.ones((1, size), jnp.float32)
    for k in range(ITERS):
        after = tuple(pltpu.roll(v, size - 1, 1) for v in direct)
        prior = tuple(pltpu.roll(v, 1, 1) for v in direct)
        prior = tuple(jnp.where(lane == 0, a, p) for a, p in zip(after, prior))
        image = dd_add(dd_mul(direct, centre), dd_scale(dd_add(after, prior), 0.5))
        alpha = dd_div(held, lane_of(image, k))
        fresh = dd_add(resid, dd_neg(dd_mul(alpha, image)))
        reached = lane_of(fresh, k + 1)
        beta = dd_mul(alpha, dd_div(reached, held))
        held = reached
        beta = dd_scale(beta, -1.0 if k == 0 else -0.5)
        direct = dd_add(fresh, dd_mul(beta, direct))
        resid = fresh
        steps.append(alpha[0][0:1])
        turns.append(beta[0][0:1])
        decay = decay * beta[0][0:1]
    gain = lax.rsqrt(jnp.maximum(jnp.abs(decay), 1e-30)) / centre[0][0:1]
    gain_ref[...] = jnp.broadcast_to(gain, gain_ref.shape)
    scaled = scaled_ref[...]
    field = steps[0]
    solved = jnp.broadcast_to(field, scaled.shape)
    left = 1.0 - field * scaled
    toward = left + turns[0]
    for k in range(1, ITERS):
        solved = solved + steps[k] * toward
        left = left - steps[k] * (scaled * toward)
        if k + 1 < ITERS:
            toward = left + turns[k] * toward
    solved = solved * (scale / half)
    left = left * (gain * scale)
    real, imag = real_ref[...], imag_ref[...]
    back_real = solved * real - left * imag
    back_imag = solved * imag + left * real
    ends = dot(jnp.concatenate([back_real, back_imag], 0), lanes_ref[...])
    mid_real = ends[:size, :size] - ends[size:, size:]
    mid_imag = ends[size:, :size] + ends[:size, size:]
    ends = dot_as(jnp.concatenate([mid_real, mid_imag], 1), ky_lanes_ref[...], 0, 0)
    real = ends[:size, :size] - ends[size:, size:]
    imag = ends[size:, :size] + ends[:size, size:]
    for copy in range(out_ref.shape[0] // (2 * size)):
        out_ref[pl.ds(copy * 2 * size, size, stride=2), :] = real
        out_ref[pl.ds(copy * 2 * size + 1, size, stride=2), :] = imag


def output_kernel(given_ref, gain_ref, back_ref, field_ref, resid_ref):
    planes, size = field_ref.shape[0], field_ref.shape[1]
    step = 2 * planes
    shrink = 1.0 / gain_ref[0:1, :]
    for j in range(planes):
        pieces = [given_ref[pl.ds(2 * j + part, size, stride=step), :] for part in range(2)]
        both = dot_as(jnp.concatenate(pieces, 0), back_ref[...], 0, 0)
        field_ref[j] = both[:, :size]
        resid_ref[j] = both[:, size:] * shrink


def call(kernel, shapes, *args):
    whole = pl.BlockSpec(memory_space=pltpu.VMEM)
    scalars = pl.BlockSpec(memory_space=pltpu.SMEM)
    return pl.pallas_call(
        kernel,
        out_shape=[jax.ShapeDtypeStruct(s, jnp.float32) for s in shapes],
        in_specs=[scalars if a.dtype == jnp.int32 else whole for a in args],
        out_specs=[whole] * len(shapes),
    )(*args)


def exchange(parts, axes):
    return [parts[0]] + [lax.ppermute(parts[r], ALL, shift_pairs(axes, r)) for r in range(1, SIDE)]


def summed(parts):
    return ((parts[0] + parts[1]) + parts[2]) + parts[3]


def body(intensities, gridding, dest_slab, spectral_weights):
    ngrid = lax.axis_size("grid")
    ndp = lax.axis_size("dp")
    nent, _, size = intensities.shape
    planes = gridding.shape[2] // size
    count = ngrid * ndp
    capacity = max(2, 2 * nent // ngrid)
    table = dft_tables(size, ndp)
    square = (size, size)
    swap = lambda a: lax.ppermute(a, ALL, shift_pairs((3, 3), 1))

    chip = lax.axis_index("dp") * (ngrid // CORES) + lax.axis_index("grid") // CORES
    core = lax.axis_index("grid") % CORES
    step = jnp.arange(5, dtype=jnp.int32)
    x, y, z = place_of(chip * CORES)[:3]
    place = jnp.where(
        step == 0, x, jnp.where(step == 1, y, jnp.where(step == 2, z, jnp.where(step == 3, core, chip == 0)))
    ).astype(jnp.int32)

    together = lax.optimization_barrier
    away, wave, counts, lists, *pieces = grid_call(
        "first", 0, ngrid, capacity, dest_slab[:, 0], place, intensities, gridding, table["packed"], spectral_weights
    )
    members = (counts, lists, place, wave, gridding)
    arrived = [swap(away)]
    weights = exchange(pieces, (0, 0))
    (away,) = grid_call("away", 1, ngrid, capacity, *members)
    arrived.append(swap(away))
    (turned,) = call(weight_kernel, [(size, 2, size)], *weights, table["held"])
    arrived[0], turned = together((arrived[0], turned))
    pieces = []
    for part in range(HALVES):
        kept = grid_call("kept", part, ngrid, capacity, *members, arrived[part])
        if part == 1:
            kept, turned = together((kept, turned))
        pieces.append(exchange(kept, [order[0] for order in ORDERS]))
    given = lax.all_to_all(turned, ALL, 0, 0, tiled=True)
    pieces, given = together((pieces, given))
    scaled, ends = call(
        symmetry_kernel, [square, (8, size)],
        given, swap(given), place, table["ky_mirror"], table["mirror"],
    )
    total = jnp.concatenate([summed(parts) for parts in pieces], 1)
    quarter = lambda a: [p.reshape(p.shape[1:]) for p in jnp.split(a.reshape((SIDE, -1) + a.shape[1:]), SIDE)]
    parts = exchange(quarter(total), [order[1] for order in ORDERS])
    parts, scaled, ends = together((parts, scaled, ends))
    parts = exchange(quarter(summed(parts)), [order[2] for order in ORDERS])
    own = summed(parts).reshape(square)
    real, imag, send = call(
        moment_kernel, [square, square, square],
        own, swap(own), place, scaled, ends, table["lanes"], table["ky_rows"],
    )
    sums = lax.all_to_all(send.reshape(count, 1, size), ALL, 0, 0, tiled=True).reshape(count, size)
    back, gain = call(
        functools.partial(solve_kernel, scale=1.0 / size**3), [(ndp * 2 * size, size), (8, size)],
        sums, ends, scaled, real, imag, table["lanes"], table["ky_lanes"],
    )
    landed = lax.all_to_all(back.reshape(count, 2 * planes, size), ALL, 0, 0, tiled=True)
    return tuple(
        call(
            output_kernel, [(planes, size, size)] * 2,
            landed.reshape(count * 2 * planes, size), gain, table["back"],
        )
    )


def solution(mesh):
    return jax.shard_map(
        body,
        mesh=mesh,
        in_specs=(
            P(("dp", "grid"), None, None),
            P(("dp", "grid"), None, None),
            P(("dp", "grid"), None),
            P("dp", None, "grid", None),
        ),
        out_specs=(P("grid", None, None), P("grid", None, None)),
        check_vma=False,
    )
```

profile of v0, /device:TPU:1, one launch (start us, length us, event | category | flops | bytes accessed | tf_op | source)
XLA Modules:
  0.0 141.6 jit_solution(236806467121847525)
XLA Ops:
  1.2 6.7 %shard_map.131 = (f32[64,64,128]{2,1,0:T(8,128)}, bf16[2,64,32,128]{3,2,1,0:T(8,128)(2,1)}, s32[32]{0:T(128)}, s32[128]{0:T(128)}, f32[128,128]{1,0:T(8,128)}, /...) custom-call(s32[64]{0:T(128)} %bitcast.13, s32[5]{0:T(128)} %compare_select_fusion.3.refs_1_.refs_2_.place_ref, ...), custom_call_target="tpu_custom_call" | custom-call | tf_op jit(solution)/shard_map/pallas_call | solution.py:279
  7.9 1.5 %collective-permute-start = (f32[64,64,128]{2,1,0:T(8,128)}, f32[64,64,128]{2,1,0:T(8,128)S(1)}, u32[]{:S(2)}, u32[]{:S(2)}) collective-permute-start(f32[64,64,128]{2,1,0:T(8,128)} %get-tuple-element.50), channel_id=1, source_target_pairs={{0,1},{1,0},{2,3},{3,2},{4,5},{5,4},{6,7},{7,6},{8,9},{9,8},{10,11... | collective-permute-start | bytes 6291464 | tf_op jit(solution)/shard_map/ppermute | solution.py:494
  9.4 4.1 %shard_map.134 = f32[64,64,128]{2,1,0:T(8,128)} custom-call(s32[32]{0:T(128)} %get-tuple-element.47.refs_0_, s32[128]{0:T(128)} %get-tuple-element.48.refs_1_, s32[5]{0:T(128)} %compare_select_fusion.3.refs_1_.refs_2_.place_ref, bf16[2,64,32,128]{3,2,1,0:T(8,128)(2,1)} %get-tuple-element.49.refs_3_, bf16[64,32,512]{2,1,0:T(8,128)(2,1)} %refs_4_.6), custom_call_target="tpu_custom_call" | custom-call | tf_op jit(solution)/shard_map/pallas_call | solution.py:279
  13.5 1.4 collective-permute-start.1
  14.8 2.5 %collective-permute-start.2 = (f32[128,128]{1,0:T(8,128)S(1)}, f32[128,128]{1,0:T(8,128)S(1)}, u32[]{:S(2)}, u32[]{:S(2)}) collective-permute-start(f32[128,128]{1,0:T(8,128)S(1)} %copy-done.13), channel_id=1, source_target_pairs={{0,64},{1,65},{2,66},{3,67},{4,68},{5,69},{6,70},{7,71},{8,72},{9,... | collective-permute-start | bytes 196616 | tf_op jit(solution)/shard_map/ppermute | solution.py:478
  18.5 1.7 %collective-permute-done.2.w2_ref = f32[128,128]{1,0:T(8,128)S(1)} collective-permute-done((f32[128,128]{1,0:T(8,128)S(1)}, f32[128,128]{1,0:T(8,128)S(1)}, u32[]{:S(2)}, u32[]{:S(2)}) %collective-permute-start.2) | collective-permute-done | bytes 65568 | tf_op jit(solution)/shard_map/ppermute | solution.py:478
  21.3 1.9 %shard_map.132 = f32[128,2,128]{2,1,0:T(2,128)} custom-call(f32[128,128]{1,0:T(8,128)} %get-tuple-element.51.w0_ref, f32[128,128]{1,0:T(8,128)} %copy-done.6, f32[128,128]{1,0:T(8,128)} %copy-done.7, f32[128,128]{1,0:T(8,128)} %copy-done.8, f32[128,128]{1,0:T(8,128)} %constant.95.clone.held_ref), custom_call_target="tpu_custom_call" | custom-call | tf_op jit(solution)/shard_map/pallas_call | solution.py:469
  23.2 5.2 %shard_map.135 = (f32[16,64,128]{2,1,0:T(8,128)}, f32[16,64,128]{2,1,0:T(8,128)}, f32[16,64,128]{2,1,0:T(8,128)}, f32[16,64,128]{2,1,0:T(8,128)}) custom-call(s32[32]{0:T(128)} %get-tuple-element.47.refs_0_, s32[128]{0:T(128)} %get-tuple-element.48.refs_1_, s32[5]{0:T(128)} %compare_select_fusion.3.refs_1_.refs_2_.place_ref, ...), custom_call_target="tpu_custom_call" | custom-call | tf_op jit(solution)/shard_map/pallas_call | solution.py:279
  28.5 1.4 collective-permute-start.8
  29.9 4.5 %shard_map.133 = (f32[16,64,128]{2,1,0:T(8,128)}, f32[16,64,128]{2,1,0:T(8,128)}, f32[16,64,128]{2,1,0:T(8,128)}, f32[16,64,128]{2,1,0:T(8,128)}) custom-call(s32[32]{0:T(128)} %get-tuple-element.47.refs_0_, s32[128]{0:T(128)} %get-tuple-element.48.refs_1_, s32[5]{0:T(128)} %compare_select_fusion.3.refs_1_.refs_2_.place_ref, ...), custom_call_target="tpu_custom_call" | custom-call | tf_op jit(solution)/shard_map/pallas_call | solution.py:279
  34.4 2.7 %collective-permute-start.9 = (f32[16,64,128]{2,1,0:T(8,128)S(1)}, f32[16,64,128]{2,1,0:T(8,128)S(1)}, u32[]{:S(2)}, u32[]{:S(2)}) collective-permute-start(f32[16,64,128]{2,1,0:T(8,128)S(1)} %copy-done.11), channel_id=1, source_target_pairs={{0,64},{1,5},{2,66},{3,7},{4,68},{5,1},{6,70},{7,3},{8,72},{9,13},... | collective-permute-start | bytes 1572872 | tf_op jit(solution)/shard_map/ppermute | solution.py:478
  39.4 1.6 %collective-permute-start.6 = (f32[16,64,128]{2,1,0:T(8,128)}, f32[16,64,128]{2,1,0:T(8,128)S(1)}, u32[]{:S(2)}, u32[]{:S(2)}) collective-permute-start(f32[16,64,128]{2,1,0:T(8,128)} %get-tuple-element.59), channel_id=1, source_target_pairs={{0,96},{1,7},{2,98},{3,1},{4,100},{5,3},{6,102},{7,5},{8,104},{9,1... | collective-permute-start | bytes 1572872 | tf_op jit(solution)/shard_map/ppermute | solution.py:478
  41.0 29.1 %all_to_all.15.given_ref = f32[128,2,128]{2,1,0:T(2,128)S(1)} all-to-all(f32[128,2,128]{2,1,0:T(2,128)S(1)} %copy-done.2), channel_id=1, replica_groups=mesh['dp'=4,'grid'=32] {'dp','grid'}, dimensions={0} | all-to-all | bytes 262144 | tf_op jit(solution)/shard_map/all_to_all | solution.py:521
  70.1 1.5 %add_add_fusion = (f32[16,64,128]{2,1,0:T(8,128)S(1)}, f32[16,64,128]{2,1,0:T(8,128)S(1)}) fusion(f32[16,64,128]{2,1,0:T(8,128)S(1)} %collective-permute-done.10, f32[16,64,128]{2,1,0:T(8,128)S(1)} %collective-permute-done.9, f32[16,64,128]{2,1,0:T(8,128)S(1)} %copy-done.1, f32[16,64,128]{2,1,0:T(8,128)S(1)} %collective-permute-done.8, ...), kind=kLoop, calls=%fused_computation.6 | loop fusion | flops 786432 | bytes 5242880 | tf_op jit(solution)/shard_map/add | solution.py:482
  77.1 2.1 %shard_map.136 = (f32[128,128]{1,0:T(8,128)}, f32[8,128]{1,0:T(8,128)}) custom-call(f32[128,2,128]{2,1,0:T(2,128)} %copy-done.3, f32[128,2,128]{2,1,0:T(2,128)} %copy-done.5, s32[5]{0:T(128)} %compare_select_fusion.3.refs_1_.refs_2_.place_ref, f32[128,128]{1,0:T(8,128)} %constant.96.clone.ky_mirror_ref, f32[128,128]{1,0:T(8,128)} %constant.97.clone.mirror_ref), custom_call_target="tpu_custom_call" | custom-call | tf_op jit(solution)/shard_map/pallas_call | solution.py:469
  79.2 2.3 %collective-permute-done.11 = f32[4,128,128]{2,1,0:T(8,128)S(1)} collective-permute-done((f32[4,128,128]{2,1,0:T(8,128)S(1)}, f32[4,128,128]{2,1,0:T(8,128)S(1)}, u32[]{:S(2)}, u32[]{:S(2)}) %collective-permute-start.11) | collective-permute-done | bytes 262176 | tf_op jit(solution)/shard_map/ppermute | solution.py:478
  82.6 1.7 %collective-permute-start.17 = (f32[1,128,128]{2,1,0:T(8,128)S(1)}, f32[1,128,128]{2,1,0:T(8,128)S(1)}, u32[]{:S(2)}, u32[]{:S(2)}) collective-permute-start(f32[1,128,128]{2,1,0:T(8,128)S(1)} %get-tuple-element.97), channel_id=1, source_target_pairs={{0,24},{1,97},{2,26},{3,99},{4,28},{5,101},{6,30},{7,103},{8,0},{9... | collective-permute-start | bytes 196616 | tf_op jit(solution)/shard_map/ppermute | solution.py:478
  86.0 3.0 %collective-permute-done.16 = f32[1,128,128]{2,1,0:T(8,128)S(1)} collective-permute-done((f32[1,128,128]{2,1,0:T(8,128)S(1)}, f32[1,128,128]{2,1,0:T(8,128)S(1)}, u32[]{:S(2)}, u32[]{:S(2)}) %collective-permute-start.16) | collective-permute-done | bytes 65568 | tf_op jit(solution)/shard_map/ppermute | solution.py:478
  89.0 4.0 %collective-permute-start.18 = (f32[128,128]{1,0:T(8,128)S(1)}, f32[128,128]{1,0:T(8,128)S(1)}, u32[]{:S(2)}, u32[]{:S(2)}) collective-permute-start(f32[128,128]{1,0:T(8,128)S(1)} %fusion.5.own_ref), channel_id=1, source_target_pairs={{0,1},{1,0},{2,3},{3,2},{4,5},{5,4},{6,7},{7,6},{8,9},{9,8},{10,11... | collective-permute-start | bytes 196616 | tf_op jit(solution)/shard_map/ppermute | solution.py:494
  94.6 4.6 %shard_map.137 = (f32[128,128]{1,0:T(8,128)}, f32[128,128]{1,0:T(8,128)}, f32[128,128]{1,0:T(8,128)}) custom-call(f32[128,128]{1,0:T(8,128)} %copy-done.4, f32[128,128]{1,0:T(8,128)} %copy-done.9, s32[5]{0:T(128)} %compare_select_fusion.3.refs_1_.refs_2_.place_ref, f32[128,128]{1,0:T(8,128)} %get-tuple-element.85.scaled_ref, ...), custom_call_target="tpu_custom_call" | custom-call | tf_op jit(solution)/shard_map/pallas_call | solution.py:469
  99.2 14.3 %all_to_all.16 = f32[128,1,128]{2,1,0:T(1,128)} all-to-all(f32[128,1,128]{2,1,0:T(1,128)} %bitcast.12), channel_id=1, replica_groups=mesh['dp'=4,'grid'=32] {'dp','grid'}, dimensions={0} | all-to-all | bytes 131072 | tf_op jit(solution)/shard_map/all_to_all | solution.py:537
  113.5 6.3 %shard_map.138 = (f32[1024,128]{1,0:T(8,128)}, f32[8,128]{1,0:T(8,128)}) custom-call(f32[128,128]{1,0:T(8,128)} %bitcast.11, f32[8,128]{1,0:T(8,128)} %get-tuple-element.86.range_ref, f32[128,128]{1,0:T(8,128)} %get-tuple-element.85.scaled_ref, f32[128,128]{1,0:T(8,128)} %get-tuple-element.88.real_ref, f32[128,128]{1,0:T(8,128)} %get-tuple-element.89.imag_ref, ...), custom_call_target="tpu_custom_call" | custom-call | tf_op jit(solution)/shard_map/pallas_call | solution.py:469
  119.8 19.2 %all_to_all.17 = f32[128,8,128]{2,1,0:T(8,128)} all-to-all(f32[128,8,128]{2,1,0:T(8,128)} %bitcast.10), channel_id=1, replica_groups=mesh['dp'=4,'grid'=32] {'dp','grid'}, dimensions={0} | all-to-all | bytes 1048576 | tf_op jit(solution)/shard_map/all_to_all | solution.py:542
  139.0 2.6 %shard_map.139 = (f32[4,128,128]{2,1,0:T(8,128)}, f32[4,128,128]{2,1,0:T(8,128)}) custom-call(f32[1024,128]{1,0:T(8,128)} %bitcast.9, f32[8,128]{1,0:T(8,128)} %get-tuple-element.91.gain_ref, f32[256,256]{1,0:T(8,128)} %constant.101.clone.back_ref), custom_call_target="tpu_custom_call" | custom-call | tf_op jit(solution)/shard_map/pallas_call | solution.py:469
  (62 shorter events, 14.9 us)
Async XLA Ops:
  7.9 15.4 %collective-permute-start = (f32[64,64,128]{2,1,0:T(8,128)}, f32[64,64,128]{2,1,0:T(8,128)S(1)}, u32[]{:S(2)}, u32[]{:S(2)}) collective-permute-start(f32[64,64,128]{2,1,0:T(8,128)} %get-tuple-element.50), channel_id=1, source_target_pairs={{0,1},{1,0},{2,3},{3,2},{4,5},{5,4},{6,7},{7,6},{8,9},{9,8},{10,11... | collective-permute-start | bytes 6291464 | tf_op jit(solution)/shard_map/ppermute | solution.py:494
  9.3 8.0 %copy-start.12 = (f32[128,128]{1,0:T(8,128)S(1)}, f32[128,128]{1,0:T(8,128)}, u32[]{:S(2)}) copy-start(f32[128,128]{1,0:T(8,128)} %get-tuple-element.54) | copy-start | bytes 196612
  13.4 9.8 %collective-permute-start.7 = (f32[64,64,128]{2,1,0:T(8,128)}, f32[64,64,128]{2,1,0:T(8,128)}, u32[]{:S(2)}, u32[]{:S(2)}) collective-permute-start(f32[64,64,128]{2,1,0:T(8,128)} %shard_map.134), channel_id=1, source_target_pairs={{0,1},{1,0},{2,3},{3,2},{4,5},{5,4},{6,7},{7,6},{8,9},{9,8},{10,11... | collective-permute-start | bytes 6291464 | tf_op jit(solution)/shard_map/ppermute | solution.py:494
  13.5 5.0 %collective-permute-start.1 = (f32[128,128]{1,0:T(8,128)S(1)}, f32[128,128]{1,0:T(8,128)S(1)}, u32[]{:S(2)}, u32[]{:S(2)}) collective-permute-start(f32[128,128]{1,0:T(8,128)S(1)} %copy-done.14), channel_id=1, source_target_pairs={{0,32},{1,33},{2,34},{3,35},{4,36},{5,37},{6,38},{7,39},{8,40},{9,... | collective-permute-start | bytes 196616 | tf_op jit(solution)/shard_map/ppermute | solution.py:478
  14.8 5.3 %collective-permute-start.2 = (f32[128,128]{1,0:T(8,128)S(1)}, f32[128,128]{1,0:T(8,128)S(1)}, u32[]{:S(2)}, u32[]{:S(2)}) collective-permute-start(f32[128,128]{1,0:T(8,128)S(1)} %copy-done.13), channel_id=1, source_target_pairs={{0,64},{1,65},{2,66},{3,67},{4,68},{5,69},{6,70},{7,71},{8,72},{9,... | collective-permute-start | bytes 196616 | tf_op jit(solution)/shard_map/ppermute | solution.py:478
  17.3 3.4 %collective-permute-start.3 = (f32[128,128]{1,0:T(8,128)S(1)}, f32[128,128]{1,0:T(8,128)S(1)}, u32[]{:S(2)}, u32[]{:S(2)}) collective-permute-start(f32[128,128]{1,0:T(8,128)S(1)} %copy-done.12), channel_id=1, source_target_pairs={{0,96},{1,97},{2,98},{3,99},{4,100},{5,101},{6,102},{7,103},{8,104... | collective-permute-start | bytes 196616 | tf_op jit(solution)/shard_map/ppermute | solution.py:478
  28.5 5.9 %copy-start.11 = (f32[16,64,128]{2,1,0:T(8,128)S(1)}, f32[16,64,128]{2,1,0:T(8,128)}, u32[]{:S(2)}) copy-start(f32[16,64,128]{2,1,0:T(8,128)} %get-tuple-element.67) | copy-start | bytes 1572868
  28.5 8.6 %copy-start.10 = (f32[16,64,128]{2,1,0:T(8,128)S(1)}, f32[16,64,128]{2,1,0:T(8,128)}, u32[]{:S(2)}) copy-start(f32[16,64,128]{2,1,0:T(8,128)} %get-tuple-element.68) | copy-start | bytes 1572868
  28.5 12.5 %copy-start.2 = (f32[128,2,128]{2,1,0:T(2,128)S(1)}, f32[128,2,128]{2,1,0:T(2,128)}, u32[]{:S(2)}) copy-start(f32[128,2,128]{2,1,0:T(2,128)} %shard_map.132) | copy-start | bytes 393220
  28.5 41.6 %copy-start.1 = (f32[16,64,128]{2,1,0:T(8,128)S(1)}, f32[16,64,128]{2,1,0:T(8,128)}, u32[]{:S(2)}) copy-start(f32[16,64,128]{2,1,0:T(8,128)} %get-tuple-element.74) | copy-start | bytes 1572868
  28.5 10.8 %collective-permute-start.8 = (f32[16,64,128]{2,1,0:T(8,128)}, f32[16,64,128]{2,1,0:T(8,128)S(1)}, u32[]{:S(2)}, u32[]{:S(2)}) collective-permute-start(f32[16,64,128]{2,1,0:T(8,128)} %get-tuple-element.66), channel_id=1, source_target_pairs={{0,32},{1,3},{2,34},{3,5},{4,36},{5,7},{6,38},{7,1},{8,40},{9,11},... | collective-permute-start | bytes 1572872 | tf_op jit(solution)/shard_map/ppermute | solution.py:478
  34.4 35.7 %collective-permute-start.9 = (f32[16,64,128]{2,1,0:T(8,128)S(1)}, f32[16,64,128]{2,1,0:T(8,128)S(1)}, u32[]{:S(2)}, u32[]{:S(2)}) collective-permute-start(f32[16,64,128]{2,1,0:T(8,128)S(1)} %copy-done.11), channel_id=1, source_target_pairs={{0,64},{1,5},{2,66},{3,7},{4,68},{5,1},{6,70},{7,3},{8,72},{9,13},... | collective-permute-start | bytes 1572872 | tf_op jit(solution)/shard_map/ppermute | solution.py:478
  37.1 33.0 %collective-permute-start.10 = (f32[16,64,128]{2,1,0:T(8,128)S(1)}, f32[16,64,128]{2,1,0:T(8,128)S(1)}, u32[]{:S(2)}, u32[]{:S(2)}) collective-permute-start(f32[16,64,128]{2,1,0:T(8,128)S(1)} %copy-done.10), channel_id=1, source_target_pairs={{0,96},{1,7},{2,98},{3,1},{4,100},{5,3},{6,102},{7,5},{8,104},{9,1... | collective-permute-start | bytes 1572872 | tf_op jit(solution)/shard_map/ppermute | solution.py:478
  38.2 31.9 %collective-permute-start.4 = (f32[16,64,128]{2,1,0:T(8,128)}, f32[16,64,128]{2,1,0:T(8,128)S(1)}, u32[]{:S(2)}, u32[]{:S(2)}) collective-permute-start(f32[16,64,128]{2,1,0:T(8,128)} %get-tuple-element.57), channel_id=1, source_target_pairs={{0,32},{1,3},{2,34},{3,5},{4,36},{5,7},{6,38},{7,1},{8,40},{9,11},... | collective-permute-start | bytes 1572872 | tf_op jit(solution)/shard_map/ppermute | solution.py:478
  38.6 31.5 %collective-permute-start.5 = (f32[16,64,128]{2,1,0:T(8,128)}, f32[16,64,128]{2,1,0:T(8,128)S(1)}, u32[]{:S(2)}, u32[]{:S(2)}) collective-permute-start(f32[16,64,128]{2,1,0:T(8,128)} %get-tuple-element.58), channel_id=1, source_target_pairs={{0,64},{1,5},{2,66},{3,7},{4,68},{5,1},{6,70},{7,3},{8,72},{9,13},... | collective-permute-start | bytes 1572872 | tf_op jit(solution)/shard_map/ppermute | solution.py:478
  39.4 30.8 %collective-permute-start.6 = (f32[16,64,128]{2,1,0:T(8,128)}, f32[16,64,128]{2,1,0:T(8,128)S(1)}, u32[]{:S(2)}, u32[]{:S(2)}) collective-permute-start(f32[16,64,128]{2,1,0:T(8,128)} %get-tuple-element.59), channel_id=1, source_target_pairs={{0,96},{1,7},{2,98},{3,1},{4,100},{5,3},{6,102},{7,5},{8,104},{9,1... | collective-permute-start | bytes 1572872 | tf_op jit(solution)/shard_map/ppermute | solution.py:478
  71.7 7.5 %collective-permute-start.13 = (f32[4,128,128]{2,1,0:T(8,128)S(1)}, f32[4,128,128]{2,1,0:T(8,128)S(1)}, u32[]{:S(2)}, u32[]{:S(2)}) collective-permute-start(f32[4,128,128]{2,1,0:T(8,128)S(1)} %get-tuple-element.92), channel_id=1, source_target_pairs={{0,6},{1,25},{2,0},{3,27},{4,2},{5,29},{6,4},{7,31},{8,14},{9,1},{... | collective-permute-start | bytes 786440 | tf_op jit(solution)/shard_map/ppermute | solution.py:478
  72.0 9.5 %collective-permute-start.11 = (f32[4,128,128]{2,1,0:T(8,128)S(1)}, f32[4,128,128]{2,1,0:T(8,128)S(1)}, u32[]{:S(2)}, u32[]{:S(2)}) collective-permute-start(f32[4,128,128]{2,1,0:T(8,128)S(1)} %get-tuple-element.94), channel_id=1, source_target_pairs={{0,2},{1,9},{2,4},{3,11},{4,6},{5,13},{6,0},{7,15},{8,10},{9,17},{... | collective-permute-start | bytes 786440 | tf_op jit(solution)/shard_map/ppermute | solution.py:478
  73.2 8.3 %collective-permute-start.12 = (f32[4,128,128]{2,1,0:T(8,128)S(1)}, f32[4,128,128]{2,1,0:T(8,128)S(1)}, u32[]{:S(2)}, u32[]{:S(2)}) collective-permute-start(f32[4,128,128]{2,1,0:T(8,128)S(1)} %get-tuple-element.95), channel_id=1, source_target_pairs={{0,4},{1,17},{2,6},{3,19},{4,0},{5,21},{6,2},{7,23},{8,12},{9,25},... | collective-permute-start | bytes 786440 | tf_op jit(solution)/shard_map/ppermute | solution.py:478
  74.2 2.3 %collective-permute-start.14 = (f32[128,2,128]{2,1,0:T(2,128)S(1)}, f32[128,2,128]{2,1,0:T(2,128)S(1)}, u32[]{:S(2)}, u32[]{:S(2)}) collective-permute-start(f32[128,2,128]{2,1,0:T(2,128)S(1)} %all_to_all.15.given_ref), channel_id=1, source_target_pairs={{0,1},{1,0},{2,3},{3,2},{4,5},{5,4},{6,7},{7,6},{8,9},{9,8},{10,11... | collective-permute-start | bytes 393224 | tf_op jit(solution)/shard_map/ppermute | solution.py:494
  81.6 4.4 %collective-permute-start.15 = (f32[1,128,128]{2,1,0:T(8,128)S(1)}, f32[1,128,128]{2,1,0:T(8,128)S(1)}, u32[]{:S(2)}, u32[]{:S(2)}) collective-permute-start(f32[1,128,128]{2,1,0:T(8,128)S(1)} %get-tuple-element.96), channel_id=1, source_target_pairs={{0,8},{1,33},{2,10},{3,35},{4,12},{5,37},{6,14},{7,39},{8,16},{9,4... | collective-permute-start | bytes 196616 | tf_op jit(solution)/shard_map/ppermute | solution.py:478
  82.6 3.4 %collective-permute-start.17 = (f32[1,128,128]{2,1,0:T(8,128)S(1)}, f32[1,128,128]{2,1,0:T(8,128)S(1)}, u32[]{:S(2)}, u32[]{:S(2)}) collective-permute-start(f32[1,128,128]{2,1,0:T(8,128)S(1)} %get-tuple-element.97), channel_id=1, source_target_pairs={{0,24},{1,97},{2,26},{3,99},{4,28},{5,101},{6,30},{7,103},{8,0},{9... | collective-permute-start | bytes 196616 | tf_op jit(solution)/shard_map/ppermute | solution.py:478
  84.4 4.6 %collective-permute-start.16 = (f32[1,128,128]{2,1,0:T(8,128)S(1)}, f32[1,128,128]{2,1,0:T(8,128)S(1)}, u32[]{:S(2)}, u32[]{:S(2)}) collective-permute-start(f32[1,128,128]{2,1,0:T(8,128)S(1)} %get-tuple-element.98), channel_id=1, source_target_pairs={{0,16},{1,65},{2,18},{3,67},{4,20},{5,69},{6,22},{7,71},{8,24},{9,... | collective-permute-start | bytes 196616 | tf_op jit(solution)/shard_map/ppermute | solution.py:478
  89.0 4.9 %collective-permute-start.18 = (f32[128,128]{1,0:T(8,128)S(1)}, f32[128,128]{1,0:T(8,128)S(1)}, u32[]{:S(2)}, u32[]{:S(2)}) collective-permute-start(f32[128,128]{1,0:T(8,128)S(1)} %fusion.5.own_ref), channel_id=1, source_target_pairs={{0,1},{1,0},{2,3},{3,2},{4,5},{5,4},{6,7},{7,6},{8,9},{9,8},{10,11... | collective-permute-start | bytes 196616 | tf_op jit(solution)/shard_map/ppermute | solution.py:494
  (10 other events, 28.7 us)
where the time goes:
time: 142 us
  blocking collectives  62.7 us (44%)
  Pallas kernels  38 us (27%)
  starting transfers between devices  25.9 us (18%)
  waiting for transfers between devices  10.2 us (7%)
  other arithmetic  2.09 us (1%)
  local copies, waits for them, and re-layouts  1.96 us (1%)
    all_to_all x1, blocking collectives, body(): given = lax.all_to_all(turned, ALL, 0, 0, tiled=True)  29.1 us
    pallas_call x4, Pallas kernels, grid_call(): pl.pallas_call(functools.partial(grid_kernel, kind=kind, part=part, capac...  20.5 us
    all_to_all x1, blocking collectives, body(): lax.all_to_all(back.reshape(count, 2 * planes, size), ALL, 0, 0, tiled=True)  19.2 us
    ppermute x15, starting transfers between devices, exchange(): lax.ppermute(parts[r], ALL, shift_pairs(axes, r))  19.1 us
    pallas_call x5, Pallas kernels, call(): pl.pallas_call(kernel, out_shape=[jax.ShapeDtypeStruct(s, jnp.float32) fo...  17.5 us
    all_to_all x1, blocking collectives, body(): lax.all_to_all(send.reshape(count, 1, size), ALL, 0, 0, tiled=True)  14.3 us
    ppermute x15, waiting for transfers between devices, exchange(): lax.ppermute(parts[r], ALL, shift_pairs(axes, r))  8.27 us
    ppermute x4, starting transfers between devices, body(): swap = lambda a: lax.ppermute(a, ALL, shift_pairs((3, 3), 1))  6.81 us
  transfers between devices with their start and end apart: 19, of which 7 were waited for; matrix products, arithmetic and copies ran while one was open for 0% of the time, Pallas kernels for 9%

commit v1 on v0

--- a/solution.py
+++ b/solution.py
@@ -42,9 +42,7 @@
 
 def dd_add(a, b):
     s, e = two_sum(a[0], b[0])
-    t, f = two_sum(a[1], b[1])
-    s, e = quick_sum(s, e + t)
-    return quick_sum(s, e + f)
+    return quick_sum(s, e + (a[1] + b[1]))
 
 
 def dd_mul(a, b):
@@ -69,10 +67,7 @@
     inverse = 1.0 / b[0]
     first = a[0] * inverse
     rest = dd_add(a, dd_neg(dd_times(b, first)))
-    second = rest[0] * inverse
-    rest = dd_add(rest, dd_neg(dd_times(b, second)))
-    high, low = quick_sum(first, second)
-    return quick_sum(high, low + rest[0] * inverse)
+    return quick_sum(first, rest[0] * inverse)
 
 
 def dot(a, b):
@@ -147,8 +142,8 @@
     )
 
 
-STEPS = 2
 HALVES = 2
+STEPS = 4
 
 
 def sublane_turn(tiles):
@@ -165,14 +160,13 @@
     return tiles
 
 
-def grid_kernel(*refs, kind, part, capacity):
-    first, kept = kind == "first", kind == "kept"
-    if first:
+def grid_kernel(*refs, kept, part, capacity):
+    if kept:
+        count_ref, list_ref, place_ref, wave_ref, matrix_ref, other_ref = refs[:6]
+        outs = refs[6:]
+    else:
         dest_ref, place_ref, values_ref, matrix_ref, packed_ref, weights_ref = refs[:6]
         out_ref, wave_ref, count_ref, list_ref = refs[6:10]
-    else:
-        count_ref, list_ref, place_ref, wave_ref, matrix_ref = refs[:5]
-        other_ref, outs, out_ref = (refs[5], refs[6:], None) if kept else (None, None, refs[5])
     nent, rows, width = matrix_ref.shape
     size = width // SIDE
     half = size // 2
@@ -219,14 +213,14 @@
             low = (wave - high.astype(jnp.float32)).astype(jnp.bfloat16)
             wave_ref[owner] = jnp.concatenate([high, low], 1).reshape(nent, rows, size)
 
-    if first:
+    if not kept:
         pl.when(step == 0)(prepare)
 
-    pairs = nslab // (2 * STEPS * HALVES)
+    pairs = nslab // (2 * STEPS)
     for pair in range(pairs):
         products = []
         for near in range(2):
-            slab = part * (nslab // HALVES) + (step * pairs + pair) * 2 + near
+            slab = ((part * (STEPS // HALVES) + step) * pairs + pair) * 2 + near
             taken = count_ref[slab]
             waves, matrices = [], []
             for m in range(capacity):
@@ -253,32 +247,31 @@
                     out_ref[index, place, :] = block
 
 
-def grid_call(kind, part, nslab, capacity, *args):
+def grid_call(kept, part, nslab, capacity, *args):
     scalars = pl.BlockSpec(memory_space=pltpu.SMEM)
     fixed = lambda shape: pl.BlockSpec(shape, lambda i: (0,) * len(shape))
-    matrix = args[3] if kind == "first" else args[4]
+    matrix = args[4] if kept else args[3]
     nent, rows, width = matrix.shape
     size, blocks = width // SIDE, SIDE**3
-    moving = lambda count: pl.BlockSpec((count, size // (STEPS * HALVES), size), lambda i: (0, i, 0))
+    steps = STEPS // HALVES if kept else STEPS
+    moving = lambda count, start=0: pl.BlockSpec((count, size // STEPS, size), lambda i: (0, start + i, 0))
     f32 = lambda *shape: jax.ShapeDtypeStruct(shape, jnp.float32)
-    if kind == "kept":
+    in_specs = [scalars if a.dtype == jnp.int32 else fixed(a.shape) for a in args]
+    if kept:
         out_shape, out_specs = [f32(SIDE**2, size // HALVES, size)] * SIDE, [moving(SIDE**2)] * SIDE
+        in_specs[-1] = moving(blocks, part * steps)
     else:
-        out_shape, out_specs = [f32(blocks, size // HALVES, size)], [moving(blocks)]
-    if kind == "first":
         wave = (CORES, nent, rows, size)
-        out_shape += [
+        out_shape = [
+            f32(blocks, size, size),
             jax.ShapeDtypeStruct(wave, jnp.bfloat16),
             jax.ShapeDtypeStruct((nslab,), jnp.int32),
             jax.ShapeDtypeStruct((nslab * capacity,), jnp.int32),
         ] + [f32(size, size)] * SIDE
-        out_specs += [fixed(wave), scalars, scalars] + [fixed((size, size))] * SIDE
-    in_specs = [scalars if a.dtype == jnp.int32 else fixed(a.shape) for a in args]
-    if kind == "kept":
-        in_specs[-1] = moving(blocks)
+        out_specs = [moving(blocks), fixed(wave), scalars, scalars] + [fixed((size, size))] * SIDE
     return pl.pallas_call(
-        functools.partial(grid_kernel, kind=kind, part=part, capacity=capacity),
-        grid=(STEPS,),
+        functools.partial(grid_kernel, kept=kept, part=part, capacity=capacity),
+        grid=(steps,),
         out_shape=out_shape,
         in_specs=in_specs,
         out_specs=out_specs,
@@ -360,14 +353,19 @@
             v_parts = halves(value[0])
             term, low_term = two_prod(value[0], p, v_parts, p_parts)
             term = (term, low_term + value[1] * p)
-            rows = [(term[0][i : i + 8], term[1][i : i + 8]) for i in range(0, chunk, 8)]
-            rows = [dd_add(dd_add(rows[0], rows[1]), rows[2])]
-            totals[order] = rows[0] if totals[order] is None else dd_add(totals[order], rows[0])
+            total, spill = totals[order] or (None, None)
+            for i in range(0, chunk, 8):
+                piece, rest = term[0][i : i + 8], term[1][i : i + 8]
+                if total is None:
+                    total, spill = piece, rest
+                else:
+                    total, lost = two_sum(total, piece)
+                    spill = spill + (lost + rest)
+            totals[order] = total, spill
             if order + 1 < MOMENTS:
                 up, low_up = two_prod(here[0], t2, None, t2_parts)
-                up, low_up = quick_sum(up, low_up + here[1] * t2)
-                following = dd_add((up, low_up), dd_neg(before))
-                before, here = here, following
+                following, lost = two_sum(up, -before[0])
+                before, here = here, (following, lost + ((low_up + here[1] * t2) - before[1]))
     row = lax.broadcasted_iota(jnp.int32, (8, size), 0)
     lane = lax.broadcasted_iota(jnp.int32, (8, size), 1)
     out = jnp.zeros((8, size), jnp.float32)
@@ -375,7 +373,7 @@
         high_rows = jnp.zeros((8, size), jnp.float32)
         low_rows = jnp.zeros((8, size), jnp.float32)
         for order in range(base, min(base + 8, MOMENTS)):
-            total = sublane_total(totals[order])
+            total = sublane_total(quick_sum(*totals[order]))
             high_rows = jnp.where(row == order - base, total[0], high_rows)
             low_rows = jnp.where(row == order - base, total[1], low_rows)
         high_rows, low_rows = lane_total((high_rows, low_rows))
@@ -503,18 +501,16 @@
 
     together = lax.optimization_barrier
     away, wave, counts, lists, *pieces = grid_call(
-        "first", 0, ngrid, capacity, dest_slab[:, 0], place, intensities, gridding, table["packed"], spectral_weights
+        False, 0, ngrid, capacity, dest_slab[:, 0], place, intensities, gridding, table["packed"], spectral_weights
     )
     members = (counts, lists, place, wave, gridding)
-    arrived = [swap(away)]
+    arrived = swap(away)
     weights = exchange(pieces, (0, 0))
-    (away,) = grid_call("away", 1, ngrid, capacity, *members)
-    arrived.append(swap(away))
     (turned,) = call(weight_kernel, [(size, 2, size)], *weights, table["held"])
-    arrived[0], turned = together((arrived[0], turned))
+    arrived, turned = together((arrived, turned))
     pieces = []
     for part in range(HALVES):
-        kept = grid_call("kept", part, ngrid, capacity, *members, arrived[part])
+        kept = grid_call(True, part, ngrid, capacity, *members, arrived)
         if part == 1:
             kept, turned = together((kept, turned))
         pieces.append(exchange(kept, [order[0] for order in ORDERS]))

time: 142 us -> 138 us (0.972)
  Pallas kernels: 38 us -> 33.9 us
    pallas_call x4 -> x3, Pallas kernels: 20.5 us -> 17.4 us  [grid_call(): pl.pallas_call(functools.partial(grid_kernel, kept=kept, part=part, capac...]
    ppermute x4 -> x3, starting transfers between devices: 6.81 us -> 6.77 us  [body(): swap = lambda a: lax.ppermute(a, ALL, shift_pairs((3, 3), 1))]
  transfers between devices with their start and end apart: 19 -> 18, of which waited for: 7 -> 8; matrix products, arithmetic and copies ran while one was open for 0% -> 0% of each run, Pallas kernels for 9% -> 6%
where the time goes in v1:
time: 138 us; the launch traced here: 137 us
  blocking collectives  62.1 us (45%)
  Pallas kernels  33.9 us (25%)
  starting transfers between devices  25.8 us (19%)
  waiting for transfers between devices  10.5 us (8%)
  other arithmetic  2.13 us (2%)
  local copies, waits for them, and re-layouts  1.97 us (1%)
    all_to_all x1, blocking collectives, body(): given = lax.all_to_all(turned, ALL, 0, 0, tiled=True)  28.6 us
    ppermute x15, starting transfers between devices, exchange(): lax.ppermute(parts[r], ALL, shift_pairs(axes, r))  19 us
    all_to_all x1, blocking collectives, body(): lax.all_to_all(back.reshape(count, 2 * planes, size), ALL, 0, 0, tiled=True)  18.9 us
    pallas_call x3, Pallas kernels, grid_call(): pl.pallas_call(functools.partial(grid_kernel, kept=kept, part=part, capac...  17.4 us
    pallas_call x5, Pallas kernels, call(): pl.pallas_call(kernel, out_shape=[jax.ShapeDtypeStruct(s, jnp.float32) fo...  16.5 us
    all_to_all x1, blocking collectives, body(): lax.all_to_all(send.reshape(count, 1, size), ALL, 0, 0, tiled=True)  14.6 us
    ppermute x15, waiting for transfers between devices, exchange(): lax.ppermute(parts[r], ALL, shift_pairs(axes, r))  8.58 us
    ppermute x3, starting transfers between devices, body(): swap = lambda a: lax.ppermute(a, ALL, shift_pairs((3, 3), 1))  6.77 us
  transfers between devices with their start and end apart: 18, of which 8 were waited for; matrix products, arithmetic and copies ran while one was open for 0% of the time, Pallas kernels for 6%

profile of v1, /device:TPU:1, one launch (start us, length us, event | category | flops | bytes accessed | tf_op | source)
XLA Modules:
  0.0 137.2 jit_solution(16086298030032862100)
XLA Ops:
  1.3 8.3 %shard_map.131 = (f32[64,128,128]{2,1,0:T(8,128)}, bf16[2,64,32,128]{3,2,1,0:T(8,128)(2,1)}, s32[32]{0:T(128)}, s32[128]{0:T(128)}, f32[128,128]{1,0:T(8,128)}, ...) custom-call(s32[64]{0:T(128)} %bitcast.13, s32[5]{0:T(128)} %compare_select_fusion.3.refs_1_.refs_2_.place_ref, ...), custom_call_target="tpu_custom_call" | custom-call | tf_op jit(solution)/shard_map/pallas_call | solution.py:272
  9.6 1.5 %collective-permute-start = (f32[64,128,128]{2,1,0:T(8,128)}, f32[64,128,128]{2,1,0:T(8,128)}, u32[]{:S(2)}, u32[]{:S(2)}) collective-permute-start(f32[64,128,128]{2,1,0:T(8,128)} %get-tuple-element.50), channel_id=1, source_target_pairs={{0,1},{1,0},{2,3},{3,2},{4,5},{5,4},{6,7},{7,6},{8,9},{9,8},{10,11... | collective-permute-start | bytes 12582920 | tf_op jit(solution)/shard_map/ppermute | solution.py:492
  11.0 1.3 collective-permute-start.1
  12.4 2.4 %collective-permute-start.2 = (f32[128,128]{1,0:T(8,128)}, f32[128,128]{1,0:T(8,128)S(1)}, u32[]{:S(2)}, u32[]{:S(2)}) collective-permute-start(f32[128,128]{1,0:T(8,128)} %get-tuple-element.53), channel_id=1, source_target_pairs={{0,64},{1,65},{2,66},{3,67},{4,68},{5,69},{6,70},{7,71},{8,72},{9,... | collective-permute-start | bytes 196616 | tf_op jit(solution)/shard_map/ppermute | solution.py:476
  16.0 2.5 %collective-permute-done.2.w2_ref = f32[128,128]{1,0:T(8,128)S(1)} collective-permute-done((f32[128,128]{1,0:T(8,128)}, f32[128,128]{1,0:T(8,128)S(1)}, u32[]{:S(2)}, u32[]{:S(2)}) %collective-permute-start.2) | collective-permute-done | bytes 65568 | tf_op jit(solution)/shard_map/ppermute | solution.py:476
  19.2 1.9 %shard_map.132 = f32[128,2,128]{2,1,0:T(2,128)} custom-call(f32[128,128]{1,0:T(8,128)} %get-tuple-element.51.w0_ref, f32[128,128]{1,0:T(8,128)} %copy-done.5, f32[128,128]{1,0:T(8,128)} %copy-done.6, f32[128,128]{1,0:T(8,128)} %copy-done.7, f32[128,128]{1,0:T(8,128)} %constant.95.clone.held_ref), custom_call_target="tpu_custom_call" | custom-call | tf_op jit(solution)/shard_map/pallas_call | solution.py:467
  21.1 4.5 %shard_map.134 = (f32[16,64,128]{2,1,0:T(8,128)}, f32[16,64,128]{2,1,0:T(8,128)}, f32[16,64,128]{2,1,0:T(8,128)}, f32[16,64,128]{2,1,0:T(8,128)}) custom-call(s32[32]{0:T(128)} %get-tuple-element.47.refs_0_, s32[128]{0:T(128)} %get-tuple-element.48.refs_1_, s32[5]{0:T(128)} %compare_select_fusion.3.refs_1_.refs_2_.place_ref, ...), custom_call_target="tpu_custom_call" | custom-call | tf_op jit(solution)/shard_map/pallas_call | solution.py:272
  25.6 1.4 collective-permute-start.7
  27.0 4.5 %shard_map.133 = (f32[16,64,128]{2,1,0:T(8,128)}, f32[16,64,128]{2,1,0:T(8,128)}, f32[16,64,128]{2,1,0:T(8,128)}, f32[16,64,128]{2,1,0:T(8,128)}) custom-call(s32[32]{0:T(128)} %get-tuple-element.47.refs_0_, s32[128]{0:T(128)} %get-tuple-element.48.refs_1_, s32[5]{0:T(128)} %compare_select_fusion.3.refs_1_.refs_2_.place_ref, ...), custom_call_target="tpu_custom_call" | custom-call | tf_op jit(solution)/shard_map/pallas_call | solution.py:272
  31.5 2.7 %collective-permute-start.8 = (f32[16,64,128]{2,1,0:T(8,128)S(1)}, f32[16,64,128]{2,1,0:T(8,128)S(1)}, u32[]{:S(2)}, u32[]{:S(2)}) collective-permute-start(f32[16,64,128]{2,1,0:T(8,128)S(1)} %copy-done.10), channel_id=1, source_target_pairs={{0,64},{1,5},{2,66},{3,7},{4,68},{5,1},{6,70},{7,3},{8,72},{9,13},... | collective-permute-start | bytes 1572872 | tf_op jit(solution)/shard_map/ppermute | solution.py:476
  36.5 1.6 %collective-permute-start.6 = (f32[16,64,128]{2,1,0:T(8,128)}, f32[16,64,128]{2,1,0:T(8,128)S(1)}, u32[]{:S(2)}, u32[]{:S(2)}) collective-permute-start(f32[16,64,128]{2,1,0:T(8,128)} %get-tuple-element.59), channel_id=1, source_target_pairs={{0,96},{1,7},{2,98},{3,1},{4,100},{5,3},{6,102},{7,5},{8,104},{9,1... | collective-permute-start | bytes 1572872 | tf_op jit(solution)/shard_map/ppermute | solution.py:476
  38.1 28.6 %all_to_all.15.given_ref = f32[128,2,128]{2,1,0:T(2,128)S(1)} all-to-all(f32[128,2,128]{2,1,0:T(2,128)S(1)} %copy-done.1), channel_id=1, replica_groups=mesh['dp'=4,'grid'=32] {'dp','grid'}, dimensions={0} | all-to-all | bytes 262144 | tf_op jit(solution)/shard_map/all_to_all | solution.py:517
  66.8 1.5 %add_add_fusion = (f32[16,64,128]{2,1,0:T(8,128)S(1)}, f32[16,64,128]{2,1,0:T(8,128)S(1)}) fusion(f32[16,64,128]{2,1,0:T(8,128)S(1)} %collective-permute-done.9, f32[16,64,128]{2,1,0:T(8,128)S(1)} %collective-permute-done.8, f32[16,64,128]{2,1,0:T(8,128)S(1)} %copy-done, f32[16,64,128]{2,1,0:T(8,128)S(1)} %collective-permute-done.7, ...), kind=kLoop, calls=%fused_computation.6 | loop fusion | flops 786432 | bytes 5242880 | tf_op jit(solution)/shard_map/add | solution.py:480
  73.7 2.1 %shard_map.135 = (f32[128,128]{1,0:T(8,128)}, f32[8,128]{1,0:T(8,128)}) custom-call(f32[128,2,128]{2,1,0:T(2,128)} %copy-done.2, f32[128,2,128]{2,1,0:T(2,128)} %copy-done.4, s32[5]{0:T(128)} %compare_select_fusion.3.refs_1_.refs_2_.place_ref, f32[128,128]{1,0:T(8,128)} %constant.96.clone.ky_mirror_ref, f32[128,128]{1,0:T(8,128)} %constant.97.clone.mirror_ref), custom_call_target="tpu_custom_call" | custom-call | tf_op jit(solution)/shard_map/pallas_call | solution.py:467
  75.9 2.3 %collective-permute-done.10 = f32[4,128,128]{2,1,0:T(8,128)S(1)} collective-permute-done((f32[4,128,128]{2,1,0:T(8,128)S(1)}, f32[4,128,128]{2,1,0:T(8,128)S(1)}, u32[]{:S(2)}, u32[]{:S(2)}) %collective-permute-start.10) | collective-permute-done | bytes 262176 | tf_op jit(solution)/shard_map/ppermute | solution.py:476
  78.3 1.4 %collective-permute-start.14 = (f32[1,128,128]{2,1,0:T(8,128)S(1)}, f32[1,128,128]{2,1,0:T(8,128)S(1)}, u32[]{:S(2)}, u32[]{:S(2)}) collective-permute-start(f32[1,128,128]{2,1,0:T(8,128)S(1)} %get-tuple-element.96), channel_id=1, source_target_pairs={{0,8},{1,33},{2,10},{3,35},{4,12},{5,37},{6,14},{7,39},{8,16},{9,4... | collective-permute-start | bytes 196616 | tf_op jit(solution)/shard_map/ppermute | solution.py:476
  79.7 1.4 collective-permute-start.16
  82.8 2.9 %collective-permute-done.15 = f32[1,128,128]{2,1,0:T(8,128)S(1)} collective-permute-done((f32[1,128,128]{2,1,0:T(8,128)S(1)}, f32[1,128,128]{2,1,0:T(8,128)S(1)}, u32[]{:S(2)}, u32[]{:S(2)}) %collective-permute-start.15) | collective-permute-done | bytes 65568 | tf_op jit(solution)/shard_map/ppermute | solution.py:476
  85.7 4.0 %collective-permute-start.17 = (f32[128,128]{1,0:T(8,128)S(1)}, f32[128,128]{1,0:T(8,128)S(1)}, u32[]{:S(2)}, u32[]{:S(2)}) collective-permute-start(f32[128,128]{1,0:T(8,128)S(1)} %fusion.5.own_ref), channel_id=1, source_target_pairs={{0,1},{1,0},{2,3},{3,2},{4,5},{5,4},{6,7},{7,6},{8,9},{9,8},{10,11... | collective-permute-start | bytes 196616 | tf_op jit(solution)/shard_map/ppermute | solution.py:492
  91.3 4.2 %shard_map.136 = (f32[128,128]{1,0:T(8,128)}, f32[128,128]{1,0:T(8,128)}, f32[128,128]{1,0:T(8,128)}) custom-call(f32[128,128]{1,0:T(8,128)} %copy-done.3, f32[128,128]{1,0:T(8,128)} %copy-done.8, s32[5]{0:T(128)} %compare_select_fusion.3.refs_1_.refs_2_.place_ref, f32[128,128]{1,0:T(8,128)} %get-tuple-element.85.scaled_ref, ...), custom_call_target="tpu_custom_call" | custom-call | tf_op jit(solution)/shard_map/pallas_call | solution.py:467
  95.5 14.6 %all_to_all.16 = f32[128,1,128]{2,1,0:T(1,128)} all-to-all(f32[128,1,128]{2,1,0:T(1,128)} %bitcast.12), channel_id=1, replica_groups=mesh['dp'=4,'grid'=32] {'dp','grid'}, dimensions={0} | all-to-all | bytes 131072 | tf_op jit(solution)/shard_map/all_to_all | solution.py:533
  110.1 5.7 %shard_map.137 = (f32[1024,128]{1,0:T(8,128)}, f32[8,128]{1,0:T(8,128)}) custom-call(f32[128,128]{1,0:T(8,128)} %bitcast.11, f32[8,128]{1,0:T(8,128)} %get-tuple-element.86.range_ref, f32[128,128]{1,0:T(8,128)} %get-tuple-element.85.scaled_ref, f32[128,128]{1,0:T(8,128)} %get-tuple-element.88.real_ref, f32[128,128]{1,0:T(8,128)} %get-tuple-element.89.imag_ref, ...), custom_call_target="tpu_custom_call" | custom-call | tf_op jit(solution)/shard_map/pallas_call | solution.py:467
  115.7 18.9 %all_to_all.17 = f32[128,8,128]{2,1,0:T(8,128)} all-to-all(f32[128,8,128]{2,1,0:T(8,128)} %bitcast.10), channel_id=1, replica_groups=mesh['dp'=4,'grid'=32] {'dp','grid'}, dimensions={0} | all-to-all | bytes 1048576 | tf_op jit(solution)/shard_map/all_to_all | solution.py:538
  134.7 2.6 %shard_map.138 = (f32[4,128,128]{2,1,0:T(8,128)}, f32[4,128,128]{2,1,0:T(8,128)}) custom-call(f32[1024,128]{1,0:T(8,128)} %bitcast.9, f32[8,128]{1,0:T(8,128)} %get-tuple-element.91.gain_ref, f32[256,256]{1,0:T(8,128)} %constant.101.clone.back_ref), custom_call_target="tpu_custom_call" | custom-call | tf_op jit(solution)/shard_map/pallas_call | solution.py:467
  (51 shorter events, 13.5 us)
Async XLA Ops:
  9.6 11.5 %collective-permute-start = (f32[64,128,128]{2,1,0:T(8,128)}, f32[64,128,128]{2,1,0:T(8,128)}, u32[]{:S(2)}, u32[]{:S(2)}) collective-permute-start(f32[64,128,128]{2,1,0:T(8,128)} %get-tuple-element.50), channel_id=1, source_target_pairs={{0,1},{1,0},{2,3},{3,2},{4,5},{5,4},{6,7},{7,6},{8,9},{9,8},{10,11... | collective-permute-start | bytes 12582920 | tf_op jit(solution)/shard_map/ppermute | solution.py:492
  11.0 5.0 %collective-permute-start.1 = (f32[128,128]{1,0:T(8,128)}, f32[128,128]{1,0:T(8,128)S(1)}, u32[]{:S(2)}, u32[]{:S(2)}) collective-permute-start(f32[128,128]{1,0:T(8,128)} %get-tuple-element.52), channel_id=1, source_target_pairs={{0,32},{1,33},{2,34},{3,35},{4,36},{5,37},{6,38},{7,39},{8,40},{9,... | collective-permute-start | bytes 196616 | tf_op jit(solution)/shard_map/ppermute | solution.py:476
  12.4 6.1 %collective-permute-start.2 = (f32[128,128]{1,0:T(8,128)}, f32[128,128]{1,0:T(8,128)S(1)}, u32[]{:S(2)}, u32[]{:S(2)}) collective-permute-start(f32[128,128]{1,0:T(8,128)} %get-tuple-element.53), channel_id=1, source_target_pairs={{0,64},{1,65},{2,66},{3,67},{4,68},{5,69},{6,70},{7,71},{8,72},{9,... | collective-permute-start | bytes 196616 | tf_op jit(solution)/shard_map/ppermute | solution.py:476
  14.8 3.7 %collective-permute-start.3 = (f32[128,128]{1,0:T(8,128)}, f32[128,128]{1,0:T(8,128)S(1)}, u32[]{:S(2)}, u32[]{:S(2)}) collective-permute-start(f32[128,128]{1,0:T(8,128)} %get-tuple-element.54), channel_id=1, source_target_pairs={{0,96},{1,97},{2,98},{3,99},{4,100},{5,101},{6,102},{7,103},{8,104... | collective-permute-start | bytes 196616 | tf_op jit(solution)/shard_map/ppermute | solution.py:476
  25.6 5.9 %copy-start.10 = (f32[16,64,128]{2,1,0:T(8,128)S(1)}, f32[16,64,128]{2,1,0:T(8,128)}, u32[]{:S(2)}) copy-start(f32[16,64,128]{2,1,0:T(8,128)} %get-tuple-element.67) | copy-start | bytes 1572868
  25.6 8.6 %copy-start.9 = (f32[16,64,128]{2,1,0:T(8,128)S(1)}, f32[16,64,128]{2,1,0:T(8,128)}, u32[]{:S(2)}) copy-start(f32[16,64,128]{2,1,0:T(8,128)} %get-tuple-element.68) | copy-start | bytes 1572868
  25.6 12.5 %copy-start.1 = (f32[128,2,128]{2,1,0:T(2,128)S(1)}, f32[128,2,128]{2,1,0:T(2,128)}, u32[]{:S(2)}) copy-start(f32[128,2,128]{2,1,0:T(2,128)} %shard_map.132) | copy-start | bytes 393220
  25.6 41.2 %copy-start = (f32[16,64,128]{2,1,0:T(8,128)S(1)}, f32[16,64,128]{2,1,0:T(8,128)}, u32[]{:S(2)}) copy-start(f32[16,64,128]{2,1,0:T(8,128)} %get-tuple-element.74) | copy-start | bytes 1572868
  25.6 10.9 %collective-permute-start.7 = (f32[16,64,128]{2,1,0:T(8,128)}, f32[16,64,128]{2,1,0:T(8,128)S(1)}, u32[]{:S(2)}, u32[]{:S(2)}) collective-permute-start(f32[16,64,128]{2,1,0:T(8,128)} %get-tuple-element.66), channel_id=1, source_target_pairs={{0,32},{1,3},{2,34},{3,5},{4,36},{5,7},{6,38},{7,1},{8,40},{9,11},... | collective-permute-start | bytes 1572872 | tf_op jit(solution)/shard_map/ppermute | solution.py:476
  31.5 35.2 %collective-permute-start.8 = (f32[16,64,128]{2,1,0:T(8,128)S(1)}, f32[16,64,128]{2,1,0:T(8,128)S(1)}, u32[]{:S(2)}, u32[]{:S(2)}) collective-permute-start(f32[16,64,128]{2,1,0:T(8,128)S(1)} %copy-done.10), channel_id=1, source_target_pairs={{0,64},{1,5},{2,66},{3,7},{4,68},{5,1},{6,70},{7,3},{8,72},{9,13},... | collective-permute-start | bytes 1572872 | tf_op jit(solution)/shard_map/ppermute | solution.py:476
  34.2 32.5 %collective-permute-start.9 = (f32[16,64,128]{2,1,0:T(8,128)S(1)}, f32[16,64,128]{2,1,0:T(8,128)S(1)}, u32[]{:S(2)}, u32[]{:S(2)}) collective-permute-start(f32[16,64,128]{2,1,0:T(8,128)S(1)} %copy-done.9), channel_id=1, source_target_pairs={{0,96},{1,7},{2,98},{3,1},{4,100},{5,3},{6,102},{7,5},{8,104},{9,1... | collective-permute-start | bytes 1572872 | tf_op jit(solution)/shard_map/ppermute | solution.py:476
  35.3 31.4 %collective-permute-start.4 = (f32[16,64,128]{2,1,0:T(8,128)}, f32[16,64,128]{2,1,0:T(8,128)S(1)}, u32[]{:S(2)}, u32[]{:S(2)}) collective-permute-start(f32[16,64,128]{2,1,0:T(8,128)} %get-tuple-element.57), channel_id=1, source_target_pairs={{0,32},{1,3},{2,34},{3,5},{4,36},{5,7},{6,38},{7,1},{8,40},{9,11},... | collective-permute-start | bytes 1572872 | tf_op jit(solution)/shard_map/ppermute | solution.py:476
  35.7 31.1 %collective-permute-start.5 = (f32[16,64,128]{2,1,0:T(8,128)}, f32[16,64,128]{2,1,0:T(8,128)S(1)}, u32[]{:S(2)}, u32[]{:S(2)}) collective-permute-start(f32[16,64,128]{2,1,0:T(8,128)} %get-tuple-element.58), channel_id=1, source_target_pairs={{0,64},{1,5},{2,66},{3,7},{4,68},{5,1},{6,70},{7,3},{8,72},{9,13},... | collective-permute-start | bytes 1572872 | tf_op jit(solution)/shard_map/ppermute | solution.py:476
  36.5 30.3 %collective-permute-start.6 = (f32[16,64,128]{2,1,0:T(8,128)}, f32[16,64,128]{2,1,0:T(8,128)S(1)}, u32[]{:S(2)}, u32[]{:S(2)}) collective-permute-start(f32[16,64,128]{2,1,0:T(8,128)} %get-tuple-element.59), channel_id=1, source_target_pairs={{0,96},{1,7},{2,98},{3,1},{4,100},{5,3},{6,102},{7,5},{8,104},{9,1... | collective-permute-start | bytes 1572872 | tf_op jit(solution)/shard_map/ppermute | solution.py:476
  66.7 6.3 %copy-start.2 = (f32[128,2,128]{2,1,0:T(2,128)}, f32[128,2,128]{2,1,0:T(2,128)S(1)}, u32[]{:S(2)}) copy-start(f32[128,2,128]{2,1,0:T(2,128)S(1)} %all_to_all.15.given_ref) | copy-start | bytes 393220
  68.3 7.5 %collective-permute-start.12 = (f32[4,128,128]{2,1,0:T(8,128)S(1)}, f32[4,128,128]{2,1,0:T(8,128)S(1)}, u32[]{:S(2)}, u32[]{:S(2)}) collective-permute-start(f32[4,128,128]{2,1,0:T(8,128)S(1)} %get-tuple-element.92), channel_id=1, source_target_pairs={{0,6},{1,25},{2,0},{3,27},{4,2},{5,29},{6,4},{7,31},{8,14},{9,1},{... | collective-permute-start | bytes 786440 | tf_op jit(solution)/shard_map/ppermute | solution.py:476
  68.7 9.5 %collective-permute-start.10 = (f32[4,128,128]{2,1,0:T(8,128)S(1)}, f32[4,128,128]{2,1,0:T(8,128)S(1)}, u32[]{:S(2)}, u32[]{:S(2)}) collective-permute-start(f32[4,128,128]{2,1,0:T(8,128)S(1)} %get-tuple-element.94), channel_id=1, source_target_pairs={{0,2},{1,9},{2,4},{3,11},{4,6},{5,13},{6,0},{7,15},{8,10},{9,17},{... | collective-permute-start | bytes 786440 | tf_op jit(solution)/shard_map/ppermute | solution.py:476
  69.9 8.3 %collective-permute-start.11 = (f32[4,128,128]{2,1,0:T(8,128)S(1)}, f32[4,128,128]{2,1,0:T(8,128)S(1)}, u32[]{:S(2)}, u32[]{:S(2)}) collective-permute-start(f32[4,128,128]{2,1,0:T(8,128)S(1)} %get-tuple-element.95), channel_id=1, source_target_pairs={{0,4},{1,17},{2,6},{3,19},{4,0},{5,21},{6,2},{7,23},{8,12},{9,25},... | collective-permute-start | bytes 786440 | tf_op jit(solution)/shard_map/ppermute | solution.py:476
  70.8 2.3 %collective-permute-start.13 = (f32[128,2,128]{2,1,0:T(2,128)S(1)}, f32[128,2,128]{2,1,0:T(2,128)S(1)}, u32[]{:S(2)}, u32[]{:S(2)}) collective-permute-start(f32[128,2,128]{2,1,0:T(2,128)S(1)} %all_to_all.15.given_ref), channel_id=1, source_target_pairs={{0,1},{1,0},{2,3},{3,2},{4,5},{5,4},{6,7},{7,6},{8,9},{9,8},{10,11... | collective-permute-start | bytes 393224 | tf_op jit(solution)/shard_map/ppermute | solution.py:492
  78.3 4.4 %collective-permute-start.14 = (f32[1,128,128]{2,1,0:T(8,128)S(1)}, f32[1,128,128]{2,1,0:T(8,128)S(1)}, u32[]{:S(2)}, u32[]{:S(2)}) collective-permute-start(f32[1,128,128]{2,1,0:T(8,128)S(1)} %get-tuple-element.96), channel_id=1, source_target_pairs={{0,8},{1,33},{2,10},{3,35},{4,12},{5,37},{6,14},{7,39},{8,16},{9,4... | collective-permute-start | bytes 196616 | tf_op jit(solution)/shard_map/ppermute | solution.py:476
  79.7 3.1 %collective-permute-start.16 = (f32[1,128,128]{2,1,0:T(8,128)S(1)}, f32[1,128,128]{2,1,0:T(8,128)S(1)}, u32[]{:S(2)}, u32[]{:S(2)}) collective-permute-start(f32[1,128,128]{2,1,0:T(8,128)S(1)} %get-tuple-element.97), channel_id=1, source_target_pairs={{0,24},{1,97},{2,26},{3,99},{4,28},{5,101},{6,30},{7,103},{8,0},{9... | collective-permute-start | bytes 196616 | tf_op jit(solution)/shard_map/ppermute | solution.py:476
  81.0 4.6 %collective-permute-start.15 = (f32[1,128,128]{2,1,0:T(8,128)S(1)}, f32[1,128,128]{2,1,0:T(8,128)S(1)}, u32[]{:S(2)}, u32[]{:S(2)}) collective-permute-start(f32[1,128,128]{2,1,0:T(8,128)S(1)} %get-tuple-element.98), channel_id=1, source_target_pairs={{0,16},{1,65},{2,18},{3,67},{4,20},{5,69},{6,22},{7,71},{8,24},{9,... | collective-permute-start | bytes 196616 | tf_op jit(solution)/shard_map/ppermute | solution.py:476
  85.7 5.0 %copy-start.3 = (f32[128,128]{1,0:T(8,128)}, f32[128,128]{1,0:T(8,128)S(1)}, u32[]{:S(2)}) copy-start(f32[128,128]{1,0:T(8,128)S(1)} %fusion.5.own_ref) | copy-start | bytes 196612
  85.7 4.9 %collective-permute-start.17 = (f32[128,128]{1,0:T(8,128)S(1)}, f32[128,128]{1,0:T(8,128)S(1)}, u32[]{:S(2)}, u32[]{:S(2)}) collective-permute-start(f32[128,128]{1,0:T(8,128)S(1)} %fusion.5.own_ref), channel_id=1, source_target_pairs={{0,1},{1,0},{2,3},{3,2},{4,5},{5,4},{6,7},{7,6},{8,9},{9,8},{10,11... | collective-permute-start | bytes 196616 | tf_op jit(solution)/shard_map/ppermute | solution.py:492
  (5 other events, 5.1 us)

commit v2 on v1

--- a/solution.py
+++ b/solution.py
@@ -105,16 +105,11 @@
     return np.where(chip == 0, core * size // 2, np.where(core == 0, chip, size - chip))
 
 
-def weight_rows(size, ndp):
-    d = np.arange(size)
-    return ndp * (d % (size // ndp)) + d // (size // ndp)
-
-
-def dft_tables(size, ndp):
+def dft_tables(size):
     index = np.arange(size)
     angle = 2.0 * np.pi * ((index[:, None] * index[None, :]) % size) / size
     cos, sin = np.cos(angle), np.sin(angle)
-    held, order = held_rows(size), weight_rows(size, ndp)
+    held = held_rows(size)
     as_f32 = lambda a: np.ascontiguousarray(a, dtype=np.float32)
     half = size // 2
     packed = np.concatenate([cos[:, :half], cos[:, half : half + 1], -sin[:, 1:half]], 1)
@@ -123,16 +118,13 @@
     return dict(
         packed=np.stack([np.concatenate([p[:, :half], q[:, :half]], 1) for p, q in ((high, low), (high[:, half:], low[:, half:]))]),
         lanes=as_f32(np.concatenate([cos, sin], 1)),
-        ky_rows=as_f32(np.concatenate([cos[order], sin[order]], 0)),
-        ky_lanes=as_f32(np.concatenate([cos[order], sin[order]], 1)),
+        rows=as_f32(np.concatenate([cos, sin], 0)),
         back=as_f32(
             np.concatenate(
                 [np.concatenate([cos[held], sin[held]], 1), np.concatenate([-sin[held], cos[held]], 1)], 0
             )
         ),
-        held=as_f32(held[:, None] == index[None, :]),
         mirror=as_f32(((index[:, None] + index[None, :]) % size) == 0),
-        ky_mirror=as_f32(((order[:, None] + order[None, :]) % size) == 0),
     )
 
 
@@ -192,13 +184,10 @@
             slice_ref[...] = weights_ref[0, :, (place_ref[0] + r) % SIDE, :]
         chip = lax.broadcasted_iota(jnp.int32, (half, half), 0)
         slot = lax.broadcasted_iota(jnp.int32, (half, half), 1)
-        digits = (slot // SIDE**2, (slot // SIDE) % SIDE, slot % SIDE)
+        digits = digits_of(slot)
         pieces = []
         for owner in range(CORES):
-            at = [place_ref[0], place_ref[1], place_ref[2]]
-            for digit, axis in zip(digits, ORDERS[owner]):
-                at[axis] = (at[axis] + digit) % SIDE
-            pick = (chip == chip_at(*at)).astype(jnp.float32).astype(jnp.bfloat16)
+            pick = (chip == chip_at(*moved(place_ref, digits, owner, 1))).astype(jnp.float32).astype(jnp.bfloat16)
             for start in (0, half):
                 piece = packed_ref[owner, :, start : start + half]
                 pieces.append(jnp.dot(piece, pick, preferred_element_type=jnp.float32).astype(jnp.bfloat16))
@@ -278,30 +267,38 @@
     )(*args)
 
 
-def weight_kernel(w0_ref, w1_ref, w2_ref, w3_ref, held_ref, out_ref):
+def moved(place_ref, digits, owner, sign):
+    at = [place_ref[0], place_ref[1], place_ref[2]]
+    for digit, axis in zip(digits, ORDERS[owner]):
+        at[axis] = (at[axis] + sign * digit + SIDE) % SIDE
+    return at
+
+
+def digits_of(index):
+    return index // SIDE**2, (index // SIDE) % SIDE, index % SIDE
+
+
+def weight_kernel(w0_ref, w1_ref, w2_ref, w3_ref, place_ref, *outs):
     size = w0_ref.shape[0]
+    half = size // 2
     own = ((w0_ref[...] + w1_ref[...]) + w2_ref[...]) + w3_ref[...]
     low = jnp.min(jnp.min(own, axis=0, keepdims=True), axis=1, keepdims=True)
     high = jnp.max(jnp.max(own, axis=0, keepdims=True), axis=1, keepdims=True)
+    row = lax.broadcasted_iota(jnp.int32, (size, size), 0)
     lane = lax.broadcasted_iota(jnp.int32, (size, size), 1)
-    out_ref[:, 0, :] = dot_as(held_ref[...], own, 1, 1)
-    out_ref[:, 1, :] = jnp.where(lane < size // 2, low, high)
-
-
-def symmetry_kernel(given_ref, other_ref, place_ref, ky_mirror_ref, mirror_ref, scaled_ref, range_ref):
-    size = scaled_ref.shape[0]
-    ends = given_ref[:, 1, :]
-    low = jnp.min(jnp.min(ends, axis=0, keepdims=True), axis=1, keepdims=True)
-    high = jnp.max(jnp.max(ends, axis=0, keepdims=True), axis=1, keepdims=True)
-    half = jnp.maximum((high - low) * 0.5, high * 1e-4)
-    half = jnp.broadcast_to(half, (1, size))
-    range_ref[0:1, :] = half
-    range_ref[1:2, :] = jnp.broadcast_to((high + low) * 0.5, (1, size)) / half
-    range_ref[2:8, :] = jnp.zeros((6, size), jnp.float32)
-    own = given_ref[:, 0, :]
-    partner = jnp.where(place_ref[4] == 1, own, other_ref[:, 0, :])
-    mirrored = dot(ky_mirror_ref[...], dot(partner, mirror_ref[...]))
-    scaled_ref[...] = (own + mirrored) * 0.5 / half
+    chips = [chip_at(*moved(place_ref, digits_of(row % half), owner, 1)) for owner in range(CORES)]
+    chip = jnp.where(place_ref[3] == 0, chips[0], chips[1])
+    negative = jnp.where(chip == 0, half, size - chip)
+    pick = (lane == jnp.where(row < half, chip, negative)).astype(jnp.float32)
+    rows = dot_as(pick, own, 1, 1)
+    ends = jnp.where(lax.broadcasted_iota(jnp.int32, (8, size), 1) < half, low, -high)
+    count = half // SIDE
+    for r, out_ref in enumerate(outs):
+        out_ref[:, 0:8, :] = jnp.zeros((count, 8, size), jnp.float32)
+        out_ref[:, 8:16, :] = jnp.broadcast_to(ends[None], (count, 8, size))
+        for sign in range(2):
+            at = sign * half + r * count
+            out_ref[:, 2 * r + sign, :] = rows[at : at + count]
 
 
 def sublane_total(a):
@@ -316,14 +313,50 @@
     return a
 
 
-def moment_kernel(own_ref, other_ref, place_ref, scaled_ref, range_ref, lanes_ref, rows_ref, real_ref, imag_ref, send_ref):
-    size = own_ref.shape[0]
-    centre = range_ref[1:2, :]
-    mine, theirs = own_ref[...], other_ref[...]
+def moment_kernel(
+    own_ref, other_ref, place_ref, lanes_ref, rows_ref, mirror_ref, real_ref, imag_ref, scaled_ref, range_ref, send_ref
+):
+    size = scaled_ref.shape[0]
     second, alone = place_ref[3] == 1, place_ref[4] == 1
+    lane8 = lax.broadcasted_iota(jnp.int32, (8, size), 1)
+    ends = jnp.minimum(own_ref[2 * size :, :], other_ref[2 * size :, :])
+    least = lambda v: jnp.min(jnp.min(v, axis=0, keepdims=True), axis=1, keepdims=True)
+    low = least(jnp.where(lane8 < size // 2, ends, 1e30))
+    high = -least(jnp.where(lane8 < size // 2, 1e30, ends))
+    span = jnp.broadcast_to(jnp.maximum((high - low) * 0.5, high * 1e-4), (1, size))
+    centre = jnp.broadcast_to((high + low) * 0.5, (1, size)) / span
+    range_ref[0:1, :] = span
+    range_ref[1:2, :] = centre
+    range_ref[2:8, :] = jnp.zeros((6, size), jnp.float32)
+
+    ky = lax.broadcasted_iota(jnp.int32, (size, size), 0)
+    row = lax.broadcasted_iota(jnp.int32, (size, size), 1)
+    found = row // 2
+    back = (found % SIDE, (found // SIDE) % SIDE, found // SIDE**2)
+    sources = []
+    for owner in range(CORES):
+        x, y, z = moved(place_ref, back, owner, -1)
+        sources.append(SIDE * (z * (SIDE * CORES) + y * CORES + owner) + x)
+    from_own = jnp.where(second, sources[1], sources[0])
+    from_other = jnp.where(second, sources[0], sources[1])
+    given = jnp.concatenate([own_ref[size : 2 * size, :], other_ref[size : 2 * size, :]], 0)
+    picks = [
+        jnp.concatenate(
+            [jnp.where(row % 2 == sign, (ky == source).astype(jnp.float32), 0.0) for source in (from_own, from_other)], 1
+        )
+        for sign in range(2)
+    ]
+    signs = dot(jnp.concatenate(picks, 0), given)
+    plus, minus = signs[:size], signs[size:]
+    mine = jnp.where(second, minus, plus)
+    partner = jnp.where(alone, mine, jnp.where(second, plus, minus))
+    scaled = (mine + dot(dot(mirror_ref[...], partner), mirror_ref[...])) * 0.5 / span
+    scaled_ref[...] = scaled.T
+
+    mine, theirs = own_ref[:size, :], other_ref[:size, :]
     re = jnp.where(jnp.logical_and(second, jnp.logical_not(alone)), theirs, mine)
     im = jnp.where(alone, jnp.zeros_like(mine), jnp.where(second, -mine, theirs))
-    ends = dot_as(jnp.concatenate([re, im], 1), lanes_ref[...], 0, 0)
+    ends = dot(jnp.concatenate([re, im], 0), lanes_ref[...])
     mid_real = ends[:size, :size] + ends[size:, size:]
     mid_imag = ends[size:, :size] - ends[:size, size:]
     both = dot(rows_ref[...], jnp.concatenate([mid_real, mid_imag], 1))
@@ -335,12 +368,9 @@
     power = real * real + imag * imag
     chunk = 24
     totals = [None] * MOMENTS
-    for start in (0, size // 4, size // 4 + chunk):
+    for start in range(0, size // 2 + 8, chunk):
         row = lax.broadcasted_iota(jnp.int32, (chunk, size), 0) + start
-        if start == 0:
-            share = jnp.where(row % (size // 8) == 0, 1.0, jnp.where(row < size // 8, 2.0, 0.0))
-        else:
-            share = 2.0
+        share = jnp.where(row % (size // 2) == 0, 1.0, jnp.where(row < size // 2, 2.0, 0.0))
         t = scaled[start : start + chunk] - centre
         p = power[start : start + chunk] * share
         p_parts = halves(p)
@@ -389,7 +419,7 @@
 
 
 def solve_kernel(
-    sums_ref, range_ref, scaled_ref, real_ref, imag_ref, lanes_ref, ky_lanes_ref, out_ref, gain_ref, *, scale
+    sums_ref, range_ref, scaled_ref, real_ref, imag_ref, lanes_ref, rows_ref, out_ref, gain_ref, *, scale
 ):
     size = scaled_ref.shape[0]
     given = sums_ref[...]
@@ -442,9 +472,9 @@
     ends = dot(jnp.concatenate([back_real, back_imag], 0), lanes_ref[...])
     mid_real = ends[:size, :size] - ends[size:, size:]
     mid_imag = ends[size:, :size] + ends[:size, size:]
-    ends = dot_as(jnp.concatenate([mid_real, mid_imag], 1), ky_lanes_ref[...], 0, 0)
-    real = ends[:size, :size] - ends[size:, size:]
-    imag = ends[size:, :size] + ends[:size, size:]
+    both = dot(rows_ref[...], jnp.concatenate([mid_real, mid_imag], 1))
+    real = both[:size, :size] - both[size:, size:]
+    imag = both[:size, size:] + both[size:, :size]
     for copy in range(out_ref.shape[0] // (2 * size)):
         out_ref[pl.ds(copy * 2 * size, size, stride=2), :] = real
         out_ref[pl.ds(copy * 2 * size + 1, size, stride=2), :] = imag
@@ -483,11 +513,11 @@
 def body(intensities, gridding, dest_slab, spectral_weights):
     ngrid = lax.axis_size("grid")
     ndp = lax.axis_size("dp")
-    nent, _, size = intensities.shape
+    nent, rows, size = intensities.shape
     planes = gridding.shape[2] // size
     count = ngrid * ndp
     capacity = max(2, 2 * nent // ngrid)
-    table = dft_tables(size, ndp)
+    table = dft_tables(size)
     square = (size, size)
     swap = lambda a: lax.ppermute(a, ALL, shift_pairs((3, 3), 1))
 
@@ -506,34 +536,40 @@
     members = (counts, lists, place, wave, gridding)
     arrived = swap(away)
     weights = exchange(pieces, (0, 0))
-    (turned,) = call(weight_kernel, [(size, 2, size)], *weights, table["held"])
-    arrived, turned = together((arrived, turned))
-    pieces = []
+    axes = [[order[stage] for order in ORDERS] for stage in range(3)]
+    quarter = lambda a: [p.reshape(p.shape[1:]) for p in jnp.split(a.reshape((SIDE, -1) + a.shape[1:]), SIDE)]
+    least = lambda parts: functools.reduce(jnp.minimum, parts)
+    data = []
     for part in range(HALVES):
         kept = grid_call(True, part, ngrid, capacity, *members, arrived)
         if part == 1:
-            kept, turned = together((kept, turned))
-        pieces.append(exchange(kept, [order[0] for order in ORDERS]))
-    given = lax.all_to_all(turned, ALL, 0, 0, tiled=True)
-    pieces, given = together((pieces, given))
-    scaled, ends = call(
-        symmetry_kernel, [square, (8, size)],
-        given, swap(given), place, table["ky_mirror"], table["mirror"],
-    )
-    total = jnp.concatenate([summed(parts) for parts in pieces], 1)
-    quarter = lambda a: [p.reshape(p.shape[1:]) for p in jnp.split(a.reshape((SIDE, -1) + a.shape[1:]), SIDE)]
-    parts = exchange(quarter(total), [order[1] for order in ORDERS])
-    parts, scaled, ends = together((parts, scaled, ends))
-    parts = exchange(quarter(summed(parts)), [order[2] for order in ORDERS])
-    own = summed(parts).reshape(square)
-    real, imag, send = call(
-        moment_kernel, [square, square, square],
-        own, swap(own), place, scaled, ends, table["lanes"], table["ky_rows"],
+            kept, rows = together((kept, rows))
+        data.append(exchange(kept, axes[0]))
+        if part == 0:
+            kept, weights = together((kept, weights))
+            rows = call(weight_kernel, [(SIDE**2, 16, size)] * SIDE, *weights, place)
+            arrived, rows = together((arrived, rows))
+    rows = exchange(rows, axes[0])
+    held = summed([a[:, :8] for a in rows])
+    ends = least([a[:, 8:] for a in rows])
+    parts = quarter(jnp.concatenate([summed(data[0]), summed(data[1]), held, ends], 1))
+    for stage in (1, 2):
+        parts = exchange(parts, axes[stage])
+        parts = [
+            summed([a[:, :size] for a in parts]),
+            jnp.concatenate([a[:, size:-8] for a in parts], 1),
+            least([a[:, -8:] for a in parts]),
+        ]
+        parts = jnp.concatenate(parts, 1)
+        parts = quarter(parts) if stage == 1 else parts[0]
+    real, imag, scaled, ends, send = call(
+        moment_kernel, [square, square, square, (8, size), square],
+        parts, swap(parts), place, table["lanes"], table["rows"], table["mirror"],
     )
     sums = lax.all_to_all(send.reshape(count, 1, size), ALL, 0, 0, tiled=True).reshape(count, size)
     back, gain = call(
         functools.partial(solve_kernel, scale=1.0 / size**3), [(ndp * 2 * size, size), (8, size)],
-        sums, ends, scaled, real, imag, table["lanes"], table["ky_lanes"],
+        sums, ends, scaled, real, imag, table["lanes"], table["rows"],
     )
     landed = lax.all_to_all(back.reshape(count, 2 * planes, size), ALL, 0, 0, tiled=True)
     return tuple(

time: 138 us -> 149 us (1.080)
  waiting for transfers between devices: 10.5 us -> 38.1 us
  blocking collectives: 62.1 us -> 37.1 us
  starting transfers between devices: 25.8 us -> 36.2 us
    all_to_all x1 -> x0, blocking collectives: 28.6 us -> none  [body(): given = lax.all_to_all(turned, ALL, 0, 0, tiled=True)]
    ppermute x15 -> x18, waiting for transfers between devices: 8.58 us -> 30 us  [exchange(): lax.ppermute(parts[r], ALL, shift_pairs(axes, r))]
    ppermute x3 -> x2, waiting for transfers between devices: 1.89 us -> 8.12 us  [body(): swap = lambda a: lax.ppermute(a, ALL, shift_pairs((3, 3), 1))]
    ppermute x3 -> x2, starting transfers between devices: 6.77 us -> 12.6 us  [body(): swap = lambda a: lax.ppermute(a, ALL, shift_pairs((3, 3), 1))]
    ppermute x15 -> x18, starting transfers between devices: 19 us -> 23.6 us  [exchange(): lax.ppermute(parts[r], ALL, shift_pairs(axes, r))]
    all_to_all x1, blocking collectives: 14.6 us -> 17.9 us  [body(): lax.all_to_all(send.reshape(count, 1, size), ALL, 0, 0, tiled=True)]
    pallas_call x5 -> x4, Pallas kernels: 16.5 us -> 15.2 us  [call(): pl.pallas_call(kernel, out_shape=[jax.ShapeDtypeStruct(s, jnp.float32) fo...]
  transfers between devices with their start and end apart: 18 -> 20, of which waited for: 8 -> 11; matrix products, arithmetic and copies ran while one was open for 0% -> 0% of each run, Pallas kernels for 6% -> 5%
where the time goes in v2:
time: 149 us; the launch traced here: 148 us
  waiting for transfers between devices  38.1 us (26%)
  blocking collectives  37.1 us (25%)
  starting transfers between devices  36.2 us (24%)
  Pallas kernels  32.7 us (22%)
  other arithmetic  2.08 us (1%)
    ppermute x18, waiting for transfers between devices, exchange(): lax.ppermute(parts[r], ALL, shift_pairs(axes, r))  30 us
    ppermute x18, starting transfers between devices, exchange(): lax.ppermute(parts[r], ALL, shift_pairs(axes, r))  23.6 us
    all_to_all x1, blocking collectives, body(): lax.all_to_all(back.reshape(count, 2 * planes, size), ALL, 0, 0, tiled=True)  19.2 us
    all_to_all x1, blocking collectives, body(): lax.all_to_all(send.reshape(count, 1, size), ALL, 0, 0, tiled=True)  17.9 us
    pallas_call x3, Pallas kernels, grid_call(): pl.pallas_call(functools.partial(grid_kernel, kept=kept, part=part, capac...  17.5 us
    pallas_call x4, Pallas kernels, call(): pl.pallas_call(kernel, out_shape=[jax.ShapeDtypeStruct(s, jnp.float32) fo...  15.2 us
    ppermute x2, starting transfers between devices, body(): swap = lambda a: lax.ppermute(a, ALL, shift_pairs((3, 3), 1))  12.6 us
    ppermute x2, waiting for transfers between devices, body(): swap = lambda a: lax.ppermute(a, ALL, shift_pairs((3, 3), 1))  8.12 us
  transfers between devices with their start and end apart: 20, of which 11 were waited for; matrix products, arithmetic and copies ran while one was open for 0% of the time, Pallas kernels for 5%

profile of v2, /device:TPU:1, one launch (start us, length us, event | category | flops | bytes accessed | tf_op | source)
XLA Modules:
  0.0 148.5 jit_solution(17038792002368175201)
XLA Ops:
  1.3 8.3 %shard_map.104 = (f32[64,128,128]{2,1,0:T(8,128)}, bf16[2,64,32,128]{3,2,1,0:T(8,128)(2,1)}, s32[32]{0:T(128)}, s32[128]{0:T(128)}, f32[128,128]{1,0:T(8,128)}, ...) custom-call(s32[64]{0:T(128)} %bitcast.14, s32[5]{0:T(128)} %compare_select_fusion.3.refs_1_.refs_2_.place_ref, ...), custom_call_target="tpu_custom_call" | custom-call | tf_op jit(solution)/shard_map/pallas_call | solution.py:261
  11.1 7.1 %collective-permute-done.refs_5_ = f32[64,128,128]{2,1,0:T(8,128)} collective-permute-done((f32[64,128,128]{2,1,0:T(8,128)}, f32[64,128,128]{2,1,0:T(8,128)}, u32[]{:S(2)}, u32[]{:S(2)}) %collective-permute-start) | collective-permute-done | bytes 4194336 | tf_op jit(solution)/shard_map/ppermute | solution.py:522
  18.2 4.5 %shard_map.105 = (f32[16,64,128]{2,1,0:T(8,128)}, f32[16,64,128]{2,1,0:T(8,128)}, f32[16,64,128]{2,1,0:T(8,128)}, f32[16,64,128]{2,1,0:T(8,128)}) custom-call(s32[32]{0:T(128)} %get-tuple-element.46.refs_0_, s32[128]{0:T(128)} %get-tuple-element.47.refs_1_, s32[5]{0:T(128)} %compare_select_fusion.3.refs_1_.refs_2_.place_ref, ...), custom_call_target="tpu_custom_call" | custom-call | tf_op jit(solution)/shard_map/pallas_call | solution.py:261
  25.4 2.5 %collective-permute-start.5 = (f32[128,128]{1,0:T(8,128)S(1)}, f32[128,128]{1,0:T(8,128)S(1)}, u32[]{:S(2)}, u32[]{:S(2)}) collective-permute-start(f32[128,128]{1,0:T(8,128)S(1)} %copy-done.11), channel_id=1, source_target_pairs={{0,64},{1,65},{2,66},{3,67},{4,68},{5,69},{6,70},{7,71},{8,72},{9,... | collective-permute-start | bytes 196616 | tf_op jit(solution)/shard_map/ppermute | solution.py:506
  29.0 2.6 %collective-permute-start.2 = (f32[16,64,128]{2,1,0:T(8,128)}, f32[16,64,128]{2,1,0:T(8,128)S(1)}, u32[]{:S(2)}, u32[]{:S(2)}) collective-permute-start(f32[16,64,128]{2,1,0:T(8,128)} %get-tuple-element.52), channel_id=1, source_target_pairs={{0,64},{1,5},{2,66},{3,7},{4,68},{5,1},{6,70},{7,3},{8,72},{9,13},... | collective-permute-start | bytes 1572872 | tf_op jit(solution)/shard_map/ppermute | solution.py:506
  33.3 2.2 %shard_map.106 = (f32[16,16,128]{2,1,0:T(8,128)}, f32[16,16,128]{2,1,0:T(8,128)}, f32[16,16,128]{2,1,0:T(8,128)}, f32[16,16,128]{2,1,0:T(8,128)}) custom-call(f32[128,128]{1,0:T(8,128)} %get-tuple-element.58.w0_ref, f32[128,128]{1,0:T(8,128)} %copy-done.4, f32[128,128]{1,0:T(8,128)} %copy-done.5, f32[128,128]{1,0:T(8,128)} %copy-done.6, ...), custom_call_target="tpu_custom_call" | custom-call | tf_op jit(solution)/shard_map/pallas_call | solution.py:497
  35.5 4.7 %shard_map.107 = (f32[16,64,128]{2,1,0:T(8,128)}, f32[16,64,128]{2,1,0:T(8,128)}, f32[16,64,128]{2,1,0:T(8,128)}, f32[16,64,128]{2,1,0:T(8,128)}) custom-call(s32[32]{0:T(128)} %get-tuple-element.46.refs_0_, s32[128]{0:T(128)} %get-tuple-element.47.refs_1_, s32[5]{0:T(128)} %compare_select_fusion.3.refs_1_.refs_2_.place_ref, ...), custom_call_target="tpu_custom_call" | custom-call | tf_op jit(solution)/shard_map/pallas_call | solution.py:261
  42.2 4.5 %collective-permute-done.10 = f32[16,16,128]{2,1,0:T(8,128)S(1)} collective-permute-done((f32[16,16,128]{2,1,0:T(8,128)S(1)}, f32[16,16,128]{2,1,0:T(8,128)S(1)}, u32[]{:S(2)}, u32[]{:S(2)}) %collective-permute-start.10) | collective-permute-done | bytes 131104 | tf_op jit(solution)/shard_map/ppermute | solution.py:506
  48.2 2.6 %collective-permute-done.12 = f32[16,16,128]{2,1,0:T(8,128)S(1)} collective-permute-done((f32[16,16,128]{2,1,0:T(8,128)S(1)}, f32[16,16,128]{2,1,0:T(8,128)S(1)}, u32[]{:S(2)}, u32[]{:S(2)}) %collective-permute-start.12) | collective-permute-done | bytes 131104 | tf_op jit(solution)/shard_map/ppermute | solution.py:506
  50.8 1.7 %collective-permute-start.9 = (f32[16,64,128]{2,1,0:T(8,128)}, f32[16,64,128]{2,1,0:T(8,128)S(1)}, u32[]{:S(2)}, u32[]{:S(2)}) collective-permute-start(f32[16,64,128]{2,1,0:T(8,128)} %get-tuple-element.78), channel_id=1, source_target_pairs={{0,96},{1,7},{2,98},{3,1},{4,100},{5,3},{6,102},{7,5},{8,104},{9,1... | collective-permute-start | bytes 1572872 | tf_op jit(solution)/shard_map/ppermute | solution.py:506
  52.7 3.5 %collective-permute-done.7 = f32[16,64,128]{2,1,0:T(8,128)S(1)} collective-permute-done((f32[16,64,128]{2,1,0:T(8,128)}, f32[16,64,128]{2,1,0:T(8,128)S(1)}, u32[]{:S(2)}, u32[]{:S(2)}) %collective-permute-start.7) | collective-permute-done | bytes 524320 | tf_op jit(solution)/shard_map/ppermute | solution.py:506
  56.3 5.6 %collective-permute-done.8 = f32[16,64,128]{2,1,0:T(8,128)S(1)} collective-permute-done((f32[16,64,128]{2,1,0:T(8,128)}, f32[16,64,128]{2,1,0:T(8,128)S(1)}, u32[]{:S(2)}, u32[]{:S(2)}) %collective-permute-start.8) | collective-permute-done | bytes 524320 | tf_op jit(solution)/shard_map/ppermute | solution.py:506
  61.9 3.5 %collective-permute-done.9 = f32[16,64,128]{2,1,0:T(8,128)S(1)} collective-permute-done((f32[16,64,128]{2,1,0:T(8,128)}, f32[16,64,128]{2,1,0:T(8,128)S(1)}, u32[]{:S(2)}, u32[]{:S(2)}) %collective-permute-start.9) | collective-permute-done | bytes 524320 | tf_op jit(solution)/shard_map/ppermute | solution.py:506
  66.6 1.7 %collective-permute-start.13 = (f32[4,144,128]{2,1,0:T(8,128)S(1)}, f32[4,144,128]{2,1,0:T(8,128)S(1)}, u32[]{:S(2)}, u32[]{:S(2)}) collective-permute-start(f32[4,144,128]{2,1,0:T(8,128)S(1)} %get-tuple-element.94), channel_id=1, source_target_pairs={{0,2},{1,9},{2,4},{3,11},{4,6},{5,13},{6,0},{7,15},{8,10},{9,17},{... | collective-permute-start | bytes 884744 | tf_op jit(solution)/shard_map/ppermute | solution.py:506
  68.3 3.3 %collective-permute-start.14 = (f32[4,144,128]{2,1,0:T(8,128)S(1)}, f32[4,144,128]{2,1,0:T(8,128)S(1)}, u32[]{:S(2)}, u32[]{:S(2)}) collective-permute-start(f32[4,144,128]{2,1,0:T(8,128)S(1)} %get-tuple-element.95), channel_id=1, source_target_pairs={{0,4},{1,17},{2,6},{3,19},{4,0},{5,21},{6,2},{7,23},{8,12},{9,25},... | collective-permute-start | bytes 884744 | tf_op jit(solution)/shard_map/ppermute | solution.py:506
  72.3 2.2 %collective-permute-done.13 = f32[4,144,128]{2,1,0:T(8,128)S(1)} collective-permute-done((f32[4,144,128]{2,1,0:T(8,128)S(1)}, f32[4,144,128]{2,1,0:T(8,128)S(1)}, u32[]{:S(2)}, u32[]{:S(2)}) %collective-permute-start.13) | collective-permute-done | bytes 294944 | tf_op jit(solution)/shard_map/ppermute | solution.py:506
  74.6 4.3 %collective-permute-done.14 = f32[4,144,128]{2,1,0:T(8,128)S(1)} collective-permute-done((f32[4,144,128]{2,1,0:T(8,128)S(1)}, f32[4,144,128]{2,1,0:T(8,128)S(1)}, u32[]{:S(2)}, u32[]{:S(2)}) %collective-permute-start.14) | collective-permute-done | bytes 294944 | tf_op jit(solution)/shard_map/ppermute | solution.py:506
  81.8 3.1 %collective-permute-done.16 = f32[1,168,128]{2,1,0:T(8,128)S(1)} collective-permute-done((f32[1,168,128]{2,1,0:T(8,128)S(1)}, f32[1,168,128]{2,1,0:T(8,128)S(1)}, u32[]{:S(2)}, u32[]{:S(2)}) %collective-permute-start.16) | collective-permute-done | bytes 86048 | tf_op jit(solution)/shard_map/ppermute | solution.py:506
  85.6 11.2 %collective-permute-start.19 = (f32[264,128]{1,0:T(8,128)S(1)}, f32[264,128]{1,0:T(8,128)S(1)}, u32[]{:S(2)}, u32[]{:S(2)}) collective-permute-start(f32[264,128]{1,0:T(8,128)S(1)} %bitcast.10), channel_id=1, source_target_pairs={{0,1},{1,0},{2,3},{3,2},{4,5},{5,4},{6,7},{7,6},{8,9},{9,8},{10,11... | collective-permute-start | bytes 405512 | tf_op jit(solution)/shard_map/ppermute | solution.py:522
  98.4 4.8 %shard_map.108 = (f32[128,128]{1,0:T(8,128)}, f32[128,128]{1,0:T(8,128)}, f32[128,128]{1,0:T(8,128)}, f32[8,128]{1,0:T(8,128)}, f32[128,128]{1,0:T(8,128)}) custom-call(f32[264,128]{1,0:T(8,128)} %bitcast.11, f32[264,128]{1,0:T(8,128)} %copy-done.2, s32[5]{0:T(128)} %compare_select_fusion.3.refs_1_.refs_2_.place_ref, f32[128,256]{1,0:T(8,128)} %constant.89.clone.lanes_ref, ...), custom_call_target="tpu_custom_call" | custom-call | tf_op jit(solution)/shard_map/pallas_call | solution.py:497
  103.2 17.9 %all_to_all.10 = f32[128,1,128]{2,1,0:T(1,128)} all-to-all(f32[128,1,128]{2,1,0:T(1,128)} %bitcast.13), channel_id=1, replica_groups=mesh['dp'=4,'grid'=32] {'dp','grid'}, dimensions={0} | all-to-all | bytes 131072 | tf_op jit(solution)/shard_map/all_to_all | solution.py:569
  121.1 5.6 %shard_map.109 = (f32[1024,128]{1,0:T(8,128)}, f32[8,128]{1,0:T(8,128)}) custom-call(f32[128,128]{1,0:T(8,128)} %bitcast.12, f32[8,128]{1,0:T(8,128)} %get-tuple-element.84.range_ref, f32[128,128]{1,0:T(8,128)} %get-tuple-element.85.scaled_ref, f32[128,128]{1,0:T(8,128)} %get-tuple-element.86.real_ref, f32[128,128]{1,0:T(8,128)} %get-tuple-element.87.imag_ref, ...), custom_call_target="tpu_custom_call" | custom-call | tf_op jit(solution)/shard_map/pallas_call | solution.py:497
  126.7 19.2 %all_to_all.11 = f32[128,8,128]{2,1,0:T(8,128)} all-to-all(f32[128,8,128]{2,1,0:T(8,128)} %bitcast.9), channel_id=1, replica_groups=mesh['dp'=4,'grid'=32] {'dp','grid'}, dimensions={0} | all-to-all | bytes 1048576 | tf_op jit(solution)/shard_map/all_to_all | solution.py:574
  145.9 2.6 %shard_map.110 = (f32[4,128,128]{2,1,0:T(8,128)}, f32[4,128,128]{2,1,0:T(8,128)}) custom-call(f32[1024,128]{1,0:T(8,128)} %bitcast.8, f32[8,128]{1,0:T(8,128)} %get-tuple-element.89.gain_ref, f32[256,256]{1,0:T(8,128)} %constant.92.clone.back_ref), custom_call_target="tpu_custom_call" | custom-call | tf_op jit(solution)/shard_map/pallas_call | solution.py:497
  (69 shorter events, 18.3 us)
Async XLA Ops:
  9.6 15.8 %copy-start.11 = (f32[128,128]{1,0:T(8,128)S(1)}, f32[128,128]{1,0:T(8,128)}, u32[]{:S(2)}) copy-start(f32[128,128]{1,0:T(8,128)} %get-tuple-element.56) | copy-start | bytes 196612
  9.6 18.3 %copy-start.10 = (f32[128,128]{1,0:T(8,128)S(1)}, f32[128,128]{1,0:T(8,128)}, u32[]{:S(2)}) copy-start(f32[128,128]{1,0:T(8,128)} %get-tuple-element.57) | copy-start | bytes 196612
  9.6 8.6 %collective-permute-start = (f32[64,128,128]{2,1,0:T(8,128)}, f32[64,128,128]{2,1,0:T(8,128)}, u32[]{:S(2)}, u32[]{:S(2)}) collective-permute-start(f32[64,128,128]{2,1,0:T(8,128)} %get-tuple-element.49), channel_id=1, source_target_pairs={{0,1},{1,0},{2,3},{3,2},{4,5},{5,4},{6,7},{7,6},{8,9},{9,8},{10,11... | collective-permute-start | bytes 12582920 | tf_op jit(solution)/shard_map/ppermute | solution.py:522
  22.7 29.9 %copy-start = (f32[16,64,128]{2,1,0:T(8,128)S(1)}, f32[16,64,128]{2,1,0:T(8,128)}, u32[]{:S(2)}) copy-start(f32[16,64,128]{2,1,0:T(8,128)} %get-tuple-element.50) | copy-start | bytes 1572868
  22.7 28.1 %collective-permute-start.1 = (f32[16,64,128]{2,1,0:T(8,128)}, f32[16,64,128]{2,1,0:T(8,128)S(1)}, u32[]{:S(2)}, u32[]{:S(2)}) collective-permute-start(f32[16,64,128]{2,1,0:T(8,128)} %get-tuple-element.51), channel_id=1, source_target_pairs={{0,32},{1,3},{2,34},{3,5},{4,36},{5,7},{6,38},{7,1},{8,40},{9,11},... | collective-permute-start | bytes 1572872 | tf_op jit(solution)/shard_map/ppermute | solution.py:506
  24.2 7.4 %collective-permute-start.4 = (f32[128,128]{1,0:T(8,128)S(1)}, f32[128,128]{1,0:T(8,128)S(1)}, u32[]{:S(2)}, u32[]{:S(2)}) collective-permute-start(f32[128,128]{1,0:T(8,128)S(1)} %copy-done.12), channel_id=1, source_target_pairs={{0,32},{1,33},{2,34},{3,35},{4,36},{5,37},{6,38},{7,39},{8,40},{9,... | collective-permute-start | bytes 196616 | tf_op jit(solution)/shard_map/ppermute | solution.py:506
  25.4 7.3 %collective-permute-start.5 = (f32[128,128]{1,0:T(8,128)S(1)}, f32[128,128]{1,0:T(8,128)S(1)}, u32[]{:S(2)}, u32[]{:S(2)}) collective-permute-start(f32[128,128]{1,0:T(8,128)S(1)} %copy-done.11), channel_id=1, source_target_pairs={{0,64},{1,65},{2,66},{3,67},{4,68},{5,69},{6,70},{7,71},{8,72},{9,... | collective-permute-start | bytes 196616 | tf_op jit(solution)/shard_map/ppermute | solution.py:506
  27.8 4.8 %collective-permute-start.6 = (f32[128,128]{1,0:T(8,128)S(1)}, f32[128,128]{1,0:T(8,128)S(1)}, u32[]{:S(2)}, u32[]{:S(2)}) collective-permute-start(f32[128,128]{1,0:T(8,128)S(1)} %copy-done.10), channel_id=1, source_target_pairs={{0,96},{1,97},{2,98},{3,99},{4,100},{5,101},{6,102},{7,103},{8,104... | collective-permute-start | bytes 196616 | tf_op jit(solution)/shard_map/ppermute | solution.py:506
  29.0 23.6 %collective-permute-start.2 = (f32[16,64,128]{2,1,0:T(8,128)}, f32[16,64,128]{2,1,0:T(8,128)S(1)}, u32[]{:S(2)}, u32[]{:S(2)}) collective-permute-start(f32[16,64,128]{2,1,0:T(8,128)} %get-tuple-element.52), channel_id=1, source_target_pairs={{0,64},{1,5},{2,66},{3,7},{4,68},{5,1},{6,70},{7,3},{8,72},{9,13},... | collective-permute-start | bytes 1572872 | tf_op jit(solution)/shard_map/ppermute | solution.py:506
  31.6 21.0 %collective-permute-start.3 = (f32[16,64,128]{2,1,0:T(8,128)}, f32[16,64,128]{2,1,0:T(8,128)S(1)}, u32[]{:S(2)}, u32[]{:S(2)}) collective-permute-start(f32[16,64,128]{2,1,0:T(8,128)} %get-tuple-element.53), channel_id=1, source_target_pairs={{0,96},{1,7},{2,98},{3,1},{4,100},{5,3},{6,102},{7,5},{8,104},{9,1... | collective-permute-start | bytes 1572872 | tf_op jit(solution)/shard_map/ppermute | solution.py:506
  35.5 17.0 %copy-start.3 = (f32[16,16,128]{2,1,0:T(8,128)S(1)}, f32[16,16,128]{2,1,0:T(8,128)}, u32[]{:S(2)}) copy-start(f32[16,16,128]{2,1,0:T(8,128)} %get-tuple-element.79) | copy-start | bytes 393220
  40.2 6.5 %collective-permute-start.10 = (f32[16,16,128]{2,1,0:T(8,128)S(1)}, f32[16,16,128]{2,1,0:T(8,128)S(1)}, u32[]{:S(2)}, u32[]{:S(2)}) collective-permute-start(f32[16,16,128]{2,1,0:T(8,128)S(1)} %copy-done.9), channel_id=1, source_target_pairs={{0,32},{1,3},{2,34},{3,5},{4,36},{5,7},{6,38},{7,1},{8,40},{9,11},... | collective-permute-start | bytes 393224 | tf_op jit(solution)/shard_map/ppermute | solution.py:506
  40.7 6.0 %collective-permute-start.11 = (f32[16,16,128]{2,1,0:T(8,128)S(1)}, f32[16,16,128]{2,1,0:T(8,128)S(1)}, u32[]{:S(2)}, u32[]{:S(2)}) collective-permute-start(f32[16,16,128]{2,1,0:T(8,128)S(1)} %copy-done.8), channel_id=1, source_target_pairs={{0,64},{1,5},{2,66},{3,7},{4,68},{5,1},{6,70},{7,3},{8,72},{9,13},... | collective-permute-start | bytes 393224 | tf_op jit(solution)/shard_map/ppermute | solution.py:506
  46.7 4.1 %collective-permute-start.12 = (f32[16,16,128]{2,1,0:T(8,128)S(1)}, f32[16,16,128]{2,1,0:T(8,128)S(1)}, u32[]{:S(2)}, u32[]{:S(2)}) collective-permute-start(f32[16,16,128]{2,1,0:T(8,128)S(1)} %copy-done.7), channel_id=1, source_target_pairs={{0,96},{1,7},{2,98},{3,1},{4,100},{5,3},{6,102},{7,5},{8,104},{9,1... | collective-permute-start | bytes 393224 | tf_op jit(solution)/shard_map/ppermute | solution.py:506
  46.7 9.5 %collective-permute-start.7 = (f32[16,64,128]{2,1,0:T(8,128)}, f32[16,64,128]{2,1,0:T(8,128)S(1)}, u32[]{:S(2)}, u32[]{:S(2)}) collective-permute-start(f32[16,64,128]{2,1,0:T(8,128)} %get-tuple-element.76), channel_id=1, source_target_pairs={{0,32},{1,3},{2,34},{3,5},{4,36},{5,7},{6,38},{7,1},{8,40},{9,11},... | collective-permute-start | bytes 1572872 | tf_op jit(solution)/shard_map/ppermute | solution.py:506
  50.8 11.0 %collective-permute-start.8 = (f32[16,64,128]{2,1,0:T(8,128)}, f32[16,64,128]{2,1,0:T(8,128)S(1)}, u32[]{:S(2)}, u32[]{:S(2)}) collective-permute-start(f32[16,64,128]{2,1,0:T(8,128)} %get-tuple-element.77), channel_id=1, source_target_pairs={{0,64},{1,5},{2,66},{3,7},{4,68},{5,1},{6,70},{7,3},{8,72},{9,13},... | collective-permute-start | bytes 1572872 | tf_op jit(solution)/shard_map/ppermute | solution.py:506
  50.8 14.5 %collective-permute-start.9 = (f32[16,64,128]{2,1,0:T(8,128)}, f32[16,64,128]{2,1,0:T(8,128)S(1)}, u32[]{:S(2)}, u32[]{:S(2)}) collective-permute-start(f32[16,64,128]{2,1,0:T(8,128)} %get-tuple-element.78), channel_id=1, source_target_pairs={{0,96},{1,7},{2,98},{3,1},{4,100},{5,3},{6,102},{7,5},{8,104},{9,1... | collective-permute-start | bytes 1572872 | tf_op jit(solution)/shard_map/ppermute | solution.py:506
  66.6 7.9 %collective-permute-start.13 = (f32[4,144,128]{2,1,0:T(8,128)S(1)}, f32[4,144,128]{2,1,0:T(8,128)S(1)}, u32[]{:S(2)}, u32[]{:S(2)}) collective-permute-start(f32[4,144,128]{2,1,0:T(8,128)S(1)} %get-tuple-element.94), channel_id=1, source_target_pairs={{0,2},{1,9},{2,4},{3,11},{4,6},{5,13},{6,0},{7,15},{8,10},{9,17},{... | collective-permute-start | bytes 884744 | tf_op jit(solution)/shard_map/ppermute | solution.py:506
  68.3 10.6 %collective-permute-start.14 = (f32[4,144,128]{2,1,0:T(8,128)S(1)}, f32[4,144,128]{2,1,0:T(8,128)S(1)}, u32[]{:S(2)}, u32[]{:S(2)}) collective-permute-start(f32[4,144,128]{2,1,0:T(8,128)S(1)} %get-tuple-element.95), channel_id=1, source_target_pairs={{0,4},{1,17},{2,6},{3,19},{4,0},{5,21},{6,2},{7,23},{8,12},{9,25},... | collective-permute-start | bytes 884744 | tf_op jit(solution)/shard_map/ppermute | solution.py:506
  71.6 7.3 %collective-permute-start.15 = (f32[4,144,128]{2,1,0:T(8,128)S(1)}, f32[4,144,128]{2,1,0:T(8,128)S(1)}, u32[]{:S(2)}, u32[]{:S(2)}) collective-permute-start(f32[4,144,128]{2,1,0:T(8,128)S(1)} %get-tuple-element.96), channel_id=1, source_target_pairs={{0,6},{1,25},{2,0},{3,27},{4,2},{5,29},{6,4},{7,31},{8,14},{9,1},{... | collective-permute-start | bytes 884744 | tf_op jit(solution)/shard_map/ppermute | solution.py:506
  79.1 5.8 %collective-permute-start.16 = (f32[1,168,128]{2,1,0:T(8,128)S(1)}, f32[1,168,128]{2,1,0:T(8,128)S(1)}, u32[]{:S(2)}, u32[]{:S(2)}) collective-permute-start(f32[1,168,128]{2,1,0:T(8,128)S(1)} %get-tuple-element.99), channel_id=1, source_target_pairs={{0,8},{1,33},{2,10},{3,35},{4,12},{5,37},{6,14},{7,39},{8,16},{9,4... | collective-permute-start | bytes 258056 | tf_op jit(solution)/shard_map/ppermute | solution.py:506
  79.1 5.7 %collective-permute-start.17 = (f32[1,168,128]{2,1,0:T(8,128)S(1)}, f32[1,168,128]{2,1,0:T(8,128)S(1)}, u32[]{:S(2)}, u32[]{:S(2)}) collective-permute-start(f32[1,168,128]{2,1,0:T(8,128)S(1)} %get-tuple-element.101), channel_id=1, source_target_pairs={{0,16},{1,65},{2,18},{3,67},{4,20},{5,69},{6,22},{7,71},{8,24},{9,... | collective-permute-start | bytes 258056 | tf_op jit(solution)/shard_map/ppermute | solution.py:506
  80.2 5.3 %collective-permute-start.18 = (f32[1,168,128]{2,1,0:T(8,128)S(1)}, f32[1,168,128]{2,1,0:T(8,128)S(1)}, u32[]{:S(2)}, u32[]{:S(2)}) collective-permute-start(f32[1,168,128]{2,1,0:T(8,128)S(1)} %get-tuple-element.100), channel_id=1, source_target_pairs={{0,24},{1,97},{2,26},{3,99},{4,28},{5,101},{6,30},{7,103},{8,0},{9... | collective-permute-start | bytes 258056 | tf_op jit(solution)/shard_map/ppermute | solution.py:506
  85.6 12.2 %collective-permute-start.19 = (f32[264,128]{1,0:T(8,128)S(1)}, f32[264,128]{1,0:T(8,128)S(1)}, u32[]{:S(2)}, u32[]{:S(2)}) collective-permute-start(f32[264,128]{1,0:T(8,128)S(1)} %bitcast.10), channel_id=1, source_target_pairs={{0,1},{1,0},{2,3},{3,2},{4,5},{5,4},{6,7},{7,6},{8,9},{9,8},{10,11... | collective-permute-start | bytes 405512 | tf_op jit(solution)/shard_map/ppermute | solution.py:522
  (9 other events, 50.8 us)

commit v3 on v2

--- a/solution.py
+++ b/solution.py
@@ -158,12 +158,11 @@
         outs = refs[6:]
     else:
         dest_ref, place_ref, values_ref, matrix_ref, packed_ref, weights_ref = refs[:6]
-        out_ref, wave_ref, count_ref, list_ref = refs[6:10]
+        out_refs, (kept_wave_ref, count_ref, list_ref), wave_ref = refs[6:8], refs[8:11], refs[-1]
     nent, rows, width = matrix_ref.shape
     size = width // SIDE
     half = size // 2
     nslab = count_ref.shape[0]
-    core = place_ref[3] if kept else 1 - place_ref[3]
     step = pl.program_id(0)
 
     def clear(s, _):
@@ -180,14 +179,15 @@
     def prepare():
         lax.fori_loop(0, nslab, clear, 0)
         lax.fori_loop(0, nent, enter, 0)
-        for r, slice_ref in enumerate(refs[10:]):
+        for r, slice_ref in enumerate(refs[11:-1]):
             slice_ref[...] = weights_ref[0, :, (place_ref[0] + r) % SIDE, :]
         chip = lax.broadcasted_iota(jnp.int32, (half, half), 0)
         slot = lax.broadcasted_iota(jnp.int32, (half, half), 1)
         digits = digits_of(slot)
         pieces = []
-        for owner in range(CORES):
-            pick = (chip == chip_at(*moved(place_ref, digits, owner, 1))).astype(jnp.float32).astype(jnp.bfloat16)
+        chips = [chip_at(*moved(place_ref, digits, owner, 1)) for owner in range(CORES)]
+        for owner in (1 - place_ref[3], place_ref[3]):
+            pick = (chip == jnp.where(owner == 0, chips[0], chips[1])).astype(jnp.float32).astype(jnp.bfloat16)
             for start in (0, half):
                 piece = packed_ref[owner, :, start : start + half]
                 pieces.append(jnp.dot(piece, pick, preferred_element_type=jnp.float32).astype(jnp.bfloat16))
@@ -196,44 +196,60 @@
             jnp.concatenate(pieces, 1),
             preferred_element_type=jnp.float32,
         )
-        for owner in range(CORES):
-            wave = both[:, owner * size : owner * size + half] + both[:, owner * size + half : (owner + 1) * size]
+        for at, target_ref in ((0, wave_ref), (size, kept_wave_ref)):
+            wave = both[:, at : at + half] + both[:, at + half : at + size]
             high = wave.astype(jnp.bfloat16)
             low = (wave - high.astype(jnp.float32)).astype(jnp.bfloat16)
-            wave_ref[owner] = jnp.concatenate([high, low], 1).reshape(nent, rows, size)
+            target_ref[...] = jnp.concatenate([high, low], 1).reshape(nent, rows, size)
 
     if not kept:
         pl.when(step == 0)(prepare)
 
     pairs = nslab // (2 * STEPS)
-    for pair in range(pairs):
-        products = []
-        for near in range(2):
-            slab = ((part * (STEPS // HALVES) + step) * pairs + pair) * 2 + near
-            taken = count_ref[slab]
-            waves, matrices = [], []
-            for m in range(capacity):
-                entry = jnp.where(m < taken, list_ref[slab * capacity + m], 0)
-                wave = wave_ref[core, entry]
-                waves.append(jnp.where(m < taken, wave, jnp.zeros_like(wave)))
-                matrices.append(matrix_ref[entry])
-            product = lax.dot_general(
-                jnp.concatenate(waves, 0),
-                jnp.concatenate(matrices, 0),
-                (((0,), (0,)), ((), ())),
-                preferred_element_type=jnp.float32,
-            )
-            products.append(product[:half] + product[half:])
-        place = slice(pair * 8, pair * 8 + 8)
-        for start in range(0, half, 8):
-            tiles = [
-                product[start : start + 8, p * size : (p + 1) * size] for product in products for p in range(SIDE)
-            ]
-            for index, block in enumerate(sublane_turn(tiles), start):
-                if kept:
-                    outs[index // SIDE**2][index % SIDE**2, place, :] = block + other_ref[index, place, :]
-                else:
-                    out_ref[index, place, :] = block
+
+    def products(out):
+        for pair in range(pairs):
+            halves_of_tile = []
+            for near in range(2):
+                slab = ((part * (STEPS // HALVES) + step) * pairs + pair) * 2 + near
+                taken = count_ref[slab]
+                waves, matrices = [], []
+                for m in range(capacity):
+                    entry = jnp.where(m < taken, list_ref[slab * capacity + m], 0)
+                    wave = wave_ref[entry]
+                    waves.append(jnp.where(m < taken, wave, jnp.zeros_like(wave)))
+                    matrices.append(matrix_ref[entry])
+                product = lax.dot_general(
+                    jnp.concatenate(waves, 0),
+                    jnp.concatenate(matrices, 0),
+                    (((0,), (0,)), ((), ())),
+                    preferred_element_type=jnp.float32,
+                )
+                halves_of_tile.append(product[:half] + product[half:])
+            place = slice(pair * 8, pair * 8 + 8)
+            for start in range(0, half, 8):
+                tiles = [
+                    product[start : start + 8, p * size : (p + 1) * size]
+                    for product in halves_of_tile
+                    for p in range(SIDE)
+                ]
+                for index, block in enumerate(sublane_turn(tiles), start):
+                    out(index, place, block)
+
+    def keep(index, place, block):
+        outs[index // SIDE**2][index % SIDE**2, place, :] = block + other_ref[index, place, :]
+
+    def send(out_ref):
+        def write(index, place, block):
+            out_ref[index, place, :] = block
+
+        return write
+
+    if kept:
+        products(keep)
+    else:
+        pl.when(step < STEPS // HALVES)(lambda: products(send(out_refs[0])))
+        pl.when(step >= STEPS // HALVES)(lambda: products(send(out_refs[1])))
 
 
 def grid_call(kept, part, nslab, capacity, *args):
@@ -243,27 +259,33 @@
     nent, rows, width = matrix.shape
     size, blocks = width // SIDE, SIDE**3
     steps = STEPS // HALVES if kept else STEPS
-    moving = lambda count, start=0: pl.BlockSpec((count, size // STEPS, size), lambda i: (0, start + i, 0))
+    moving = lambda count: pl.BlockSpec((count, size // STEPS, size), lambda i: (0, i, 0))
     f32 = lambda *shape: jax.ShapeDtypeStruct(shape, jnp.float32)
     in_specs = [scalars if a.dtype == jnp.int32 else fixed(a.shape) for a in args]
     if kept:
         out_shape, out_specs = [f32(SIDE**2, size // HALVES, size)] * SIDE, [moving(SIDE**2)] * SIDE
-        in_specs[-1] = moving(blocks, part * steps)
+        in_specs[-1] = moving(blocks)
+        scratch = []
     else:
-        wave = (CORES, nent, rows, size)
-        out_shape = [
-            f32(blocks, size, size),
+        wave = (nent, rows, size)
+        out_shape = [f32(blocks, size // HALVES, size)] * HALVES + [
             jax.ShapeDtypeStruct(wave, jnp.bfloat16),
             jax.ShapeDtypeStruct((nslab,), jnp.int32),
             jax.ShapeDtypeStruct((nslab * capacity,), jnp.int32),
         ] + [f32(size, size)] * SIDE
-        out_specs = [moving(blocks), fixed(wave), scalars, scalars] + [fixed((size, size))] * SIDE
+        block = (blocks, size // STEPS, size)
+        out_specs = [
+            pl.BlockSpec(block, lambda i: (0, jnp.minimum(i, STEPS // HALVES - 1), 0)),
+            pl.BlockSpec(block, lambda i: (0, jnp.maximum(i - STEPS // HALVES, 0), 0)),
+        ] + [fixed(wave), scalars, scalars] + [fixed((size, size))] * SIDE
+        scratch = [pltpu.VMEM(wave, jnp.bfloat16)]
     return pl.pallas_call(
         functools.partial(grid_kernel, kept=kept, part=part, capacity=capacity),
         grid=(steps,),
         out_shape=out_shape,
         in_specs=in_specs,
         out_specs=out_specs,
+        scratch_shapes=scratch,
     )(*args)
 
 
@@ -530,25 +552,21 @@
     ).astype(jnp.int32)
 
     together = lax.optimization_barrier
-    away, wave, counts, lists, *pieces = grid_call(
+    *away, wave, counts, lists, p0, p1, p2, p3 = grid_call(
         False, 0, ngrid, capacity, dest_slab[:, 0], place, intensities, gridding, table["packed"], spectral_weights
     )
     members = (counts, lists, place, wave, gridding)
-    arrived = swap(away)
-    weights = exchange(pieces, (0, 0))
+    arrived = [swap(a) for a in away]
+    weights = exchange([p0, p1, p2, p3], (0, 0))
     axes = [[order[stage] for order in ORDERS] for stage in range(3)]
     quarter = lambda a: [p.reshape(p.shape[1:]) for p in jnp.split(a.reshape((SIDE, -1) + a.shape[1:]), SIDE)]
     least = lambda parts: functools.reduce(jnp.minimum, parts)
     data = []
     for part in range(HALVES):
-        kept = grid_call(True, part, ngrid, capacity, *members, arrived)
-        if part == 1:
-            kept, rows = together((kept, rows))
+        kept = grid_call(True, part, ngrid, capacity, *members, arrived[part])
         data.append(exchange(kept, axes[0]))
-        if part == 0:
-            kept, weights = together((kept, weights))
-            rows = call(weight_kernel, [(SIDE**2, 16, size)] * SIDE, *weights, place)
-            arrived, rows = together((arrived, rows))
+    kept, weights = together((kept, weights))
+    rows = call(weight_kernel, [(SIDE**2, 16, size)] * SIDE, *weights, place)
     rows = exchange(rows, axes[0])
     held = summed([a[:, :8] for a in rows])
     ends = least([a[:, 8:] for a in rows])

time: 149 us -> 143 us (0.960)
  waiting for transfers between devices: 38.1 us -> 30.9 us
    ppermute x18, waiting for transfers between devices: 30 us -> 25.9 us  [exchange(): lax.ppermute(parts[r], ALL, shift_pairs(axes, r))]
    ppermute x2 -> x3, waiting for transfers between devices: 8.12 us -> 5.03 us  [body(): swap = lambda a: lax.ppermute(a, ALL, shift_pairs((3, 3), 1))]
    ppermute x18, starting transfers between devices: 23.6 us -> 25.2 us  [exchange(): lax.ppermute(parts[r], ALL, shift_pairs(axes, r))]
    ppermute x2 -> x3, starting transfers between devices: 12.6 us -> 11.4 us  [body(): swap = lambda a: lax.ppermute(a, ALL, shift_pairs((3, 3), 1))]
  transfers between devices with their start and end apart: 20 -> 21, of which waited for: 11 -> 11; matrix products, arithmetic and copies ran while one was open for 0% -> 2% of each run, Pallas kernels for 5% -> 8%
where the time goes in v3:
time: 143 us; the launch traced here: 142 us
  blocking collectives  36.8 us (26%)
  starting transfers between devices  36.6 us (26%)
  Pallas kernels  32.5 us (23%)
  waiting for transfers between devices  30.9 us (22%)
  other arithmetic  3.16 us (2%)
    ppermute x18, waiting for transfers between devices, exchange(): lax.ppermute(parts[r], ALL, shift_pairs(axes, r))  25.9 us
    ppermute x18, starting transfers between devices, exchange(): lax.ppermute(parts[r], ALL, shift_pairs(axes, r))  25.2 us
    all_to_all x1, blocking collectives, body(): lax.all_to_all(back.reshape(count, 2 * planes, size), ALL, 0, 0, tiled=True)  19.2 us
    all_to_all x1, blocking collectives, body(): lax.all_to_all(send.reshape(count, 1, size), ALL, 0, 0, tiled=True)  17.6 us
    pallas_call x3, Pallas kernels, grid_call(): pl.pallas_call(functools.partial(grid_kernel, kept=kept, part=part, capac...  17.3 us
    pallas_call x4, Pallas kernels, call(): pl.pallas_call(kernel, out_shape=[jax.ShapeDtypeStruct(s, jnp.float32) fo...  15.2 us
    ppermute x3, starting transfers between devices, body(): swap = lambda a: lax.ppermute(a, ALL, shift_pairs((3, 3), 1))  11.4 us
    ppermute x3, waiting for transfers between devices, body(): swap = lambda a: lax.ppermute(a, ALL, shift_pairs((3, 3), 1))  5.03 us
  transfers between devices with their start and end apart: 21, of which 11 were waited for; matrix products, arithmetic and copies ran while one was open for 2% of the time, Pallas kernels for 8%

profile of v3, /device:TPU:1, one launch (start us, length us, event | category | flops | bytes accessed | tf_op | source)
XLA Modules:
  0.0 142.2 jit_solution(13915375117367604746)
XLA Ops:
  1.3 8.4 %shard_map.104 = (f32[64,64,128]{2,1,0:T(8,128)}, f32[64,64,128]{2,1,0:T(8,128)}, bf16[64,32,128]{2,1,0:T(8,128)(2,1)}, s32[32]{0:T(128)}, s32[128]{0:T(128)}, /...) custom-call(s32[64]{0:T(128)} %bitcast.14, ...), custom_call_target="tpu_custom_call" | custom-call | tf_op jit(solution)/shard_map/pallas_call | solution.py:282
  11.3 4.0 %collective-permute-done.4.refs_5_ = f32[64,64,128]{2,1,0:T(8,128)} collective-permute-done((f32[64,64,128]{2,1,0:T(8,128)}, f32[64,64,128]{2,1,0:T(8,128)}, u32[]{:S(2)}, u32[]{:S(2)}) %collective-permute-start.4) | collective-permute-done | bytes 2097184 | tf_op jit(solution)/shard_map/ppermute | solution.py:544
  15.3 4.4 %shard_map.106 = (f32[16,64,128]{2,1,0:T(8,128)}, f32[16,64,128]{2,1,0:T(8,128)}, f32[16,64,128]{2,1,0:T(8,128)}, f32[16,64,128]{2,1,0:T(8,128)}) custom-call(s32[32]{0:T(128)} %get-tuple-element.34.refs_0_, s32[128]{0:T(128)} %get-tuple-element.35.refs_1_, s32[5]{0:T(128)} %compare_select_fusion.3.refs_1_.refs_2_.place_ref, ...), custom_call_target="tpu_custom_call" | custom-call | tf_op jit(solution)/shard_map/pallas_call | solution.py:282
  22.4 2.4 %collective-permute-start.9 = (f32[128,128]{1,0:T(8,128)S(1)}, f32[128,128]{1,0:T(8,128)S(1)}, u32[]{:S(2)}, u32[]{:S(2)}) collective-permute-start(f32[128,128]{1,0:T(8,128)S(1)} %copy-done.10), channel_id=1, source_target_pairs={{0,64},{1,65},{2,66},{3,67},{4,68},{5,69},{6,70},{7,71},{8,72},{9,... | collective-permute-start | bytes 196616 | tf_op jit(solution)/shard_map/ppermute | solution.py:528
  26.5 2.6 %collective-permute-start.6 = (f32[16,64,128]{2,1,0:T(8,128)}, f32[16,64,128]{2,1,0:T(8,128)}, u32[]{:S(2)}, u32[]{:S(2)}) collective-permute-start(f32[16,64,128]{2,1,0:T(8,128)} %get-tuple-element.45), channel_id=1, source_target_pairs={{0,64},{1,5},{2,66},{3,7},{4,68},{5,1},{6,70},{7,3},{8,72},{9,13},... | collective-permute-start | bytes 1572872 | tf_op jit(solution)/shard_map/ppermute | solution.py:528
  30.8 2.2 %shard_map.107 = (f32[16,16,128]{2,1,0:T(8,128)}, f32[16,16,128]{2,1,0:T(8,128)}, f32[16,16,128]{2,1,0:T(8,128)}, f32[16,16,128]{2,1,0:T(8,128)}) custom-call(f32[128,128]{1,0:T(8,128)} %get-tuple-element.51.w0_ref, f32[128,128]{1,0:T(8,128)} %copy-done.6, f32[128,128]{1,0:T(8,128)} %copy-done.7, f32[128,128]{1,0:T(8,128)} %copy-done.8, ...), custom_call_target="tpu_custom_call" | custom-call | tf_op jit(solution)/shard_map/pallas_call | solution.py:519
  33.3 2.1 %collective-permute-start.12 = (f32[16,16,128]{2,1,0:T(8,128)}, f32[16,16,128]{2,1,0:T(8,128)S(1)}, u32[]{:S(2)}, u32[]{:S(2)}) collective-permute-start(f32[16,16,128]{2,1,0:T(8,128)} %get-tuple-element.57), channel_id=1, source_target_pairs={{0,64},{1,5},{2,66},{3,7},{4,68},{5,1},{6,70},{7,3},{8,72},{9,13},... | collective-permute-start | bytes 393224 | tf_op jit(solution)/shard_map/ppermute | solution.py:528
  35.5 4.6 %collective-permute-done.11 = f32[16,16,128]{2,1,0:T(8,128)S(1)} collective-permute-done((f32[16,16,128]{2,1,0:T(8,128)}, f32[16,16,128]{2,1,0:T(8,128)S(1)}, u32[]{:S(2)}, u32[]{:S(2)}) %collective-permute-start.11) | collective-permute-done | bytes 131104 | tf_op jit(solution)/shard_map/ppermute | solution.py:528
  40.0 4.5 %shard_map.105 = (f32[16,64,128]{2,1,0:T(8,128)}, f32[16,64,128]{2,1,0:T(8,128)}, f32[16,64,128]{2,1,0:T(8,128)}, f32[16,64,128]{2,1,0:T(8,128)}) custom-call(s32[32]{0:T(128)} %get-tuple-element.34.refs_0_, s32[128]{0:T(128)} %get-tuple-element.35.refs_1_, s32[5]{0:T(128)} %compare_select_fusion.3.refs_1_.refs_2_.place_ref, ...), custom_call_target="tpu_custom_call" | custom-call | tf_op jit(solution)/shard_map/pallas_call | solution.py:282
  47.1 1.7 %collective-permute-start.3 = (f32[16,64,128]{2,1,0:T(8,128)}, f32[16,64,128]{2,1,0:T(8,128)S(1)}, u32[]{:S(2)}, u32[]{:S(2)}) collective-permute-start(f32[16,64,128]{2,1,0:T(8,128)} %get-tuple-element.41), channel_id=1, source_target_pairs={{0,96},{1,7},{2,98},{3,1},{4,100},{5,3},{6,102},{7,5},{8,104},{9,1... | collective-permute-start | bytes 1572872 | tf_op jit(solution)/shard_map/ppermute | solution.py:528
  51.0 8.9 %collective-permute-done.1 = f32[16,64,128]{2,1,0:T(8,128)S(1)} collective-permute-done((f32[16,64,128]{2,1,0:T(8,128)}, f32[16,64,128]{2,1,0:T(8,128)S(1)}, u32[]{:S(2)}, u32[]{:S(2)}) %collective-permute-start.1) | collective-permute-done | bytes 524320 | tf_op jit(solution)/shard_map/ppermute | solution.py:528
  60.7 1.8 %collective-permute-start.14 = (f32[4,144,128]{2,1,0:T(8,128)S(1)}, f32[4,144,128]{2,1,0:T(8,128)S(1)}, u32[]{:S(2)}, u32[]{:S(2)}) collective-permute-start(f32[4,144,128]{2,1,0:T(8,128)S(1)} %get-tuple-element.70), channel_id=1, source_target_pairs={{0,2},{1,9},{2,4},{3,11},{4,6},{5,13},{6,0},{7,15},{8,10},{9,17},{... | collective-permute-start | bytes 884744 | tf_op jit(solution)/shard_map/ppermute | solution.py:528
  62.5 3.3 %collective-permute-start.15 = (f32[4,144,128]{2,1,0:T(8,128)S(1)}, f32[4,144,128]{2,1,0:T(8,128)S(1)}, u32[]{:S(2)}, u32[]{:S(2)}) collective-permute-start(f32[4,144,128]{2,1,0:T(8,128)S(1)} %get-tuple-element.71), channel_id=1, source_target_pairs={{0,4},{1,17},{2,6},{3,19},{4,0},{5,21},{6,2},{7,23},{8,12},{9,25},... | collective-permute-start | bytes 884744 | tf_op jit(solution)/shard_map/ppermute | solution.py:528
  66.5 2.2 %collective-permute-done.14 = f32[4,144,128]{2,1,0:T(8,128)S(1)} collective-permute-done((f32[4,144,128]{2,1,0:T(8,128)S(1)}, f32[4,144,128]{2,1,0:T(8,128)S(1)}, u32[]{:S(2)}, u32[]{:S(2)}) %collective-permute-start.14) | collective-permute-done | bytes 294944 | tf_op jit(solution)/shard_map/ppermute | solution.py:528
  68.7 4.3 %collective-permute-done.15 = f32[4,144,128]{2,1,0:T(8,128)S(1)} collective-permute-done((f32[4,144,128]{2,1,0:T(8,128)S(1)}, f32[4,144,128]{2,1,0:T(8,128)S(1)}, u32[]{:S(2)}, u32[]{:S(2)}) %collective-permute-start.15) | collective-permute-done | bytes 294944 | tf_op jit(solution)/shard_map/ppermute | solution.py:528
  73.3 2.7 %collective-permute-start.19 = (f32[1,168,128]{2,1,0:T(8,128)S(1)}, f32[1,168,128]{2,1,0:T(8,128)S(1)}, u32[]{:S(2)}, u32[]{:S(2)}) collective-permute-start(f32[1,168,128]{2,1,0:T(8,128)S(1)} %get-tuple-element.76), channel_id=1, source_target_pairs={{0,24},{1,97},{2,26},{3,99},{4,28},{5,101},{6,30},{7,103},{8,0},{9... | collective-permute-start | bytes 258056 | tf_op jit(solution)/shard_map/ppermute | solution.py:528
  76.0 2.2 %collective-permute-done.17 = f32[1,168,128]{2,1,0:T(8,128)S(1)} collective-permute-done((f32[1,168,128]{2,1,0:T(8,128)S(1)}, f32[1,168,128]{2,1,0:T(8,128)S(1)}, u32[]{:S(2)}, u32[]{:S(2)}) %collective-permute-start.17) | collective-permute-done | bytes 86048 | tf_op jit(solution)/shard_map/ppermute | solution.py:528
  78.3 2.5 %collective-permute-done.18 = f32[1,168,128]{2,1,0:T(8,128)S(1)} collective-permute-done((f32[1,168,128]{2,1,0:T(8,128)S(1)}, f32[1,168,128]{2,1,0:T(8,128)S(1)}, u32[]{:S(2)}, u32[]{:S(2)}) %collective-permute-start.18) | collective-permute-done | bytes 86048 | tf_op jit(solution)/shard_map/ppermute | solution.py:528
  80.9 9.9 %collective-permute-start.20 = (f32[264,128]{1,0:T(8,128)S(1)}, f32[264,128]{1,0:T(8,128)S(1)}, u32[]{:S(2)}, u32[]{:S(2)}) collective-permute-start(f32[264,128]{1,0:T(8,128)S(1)} %bitcast.10), channel_id=1, source_target_pairs={{0,1},{1,0},{2,3},{3,2},{4,5},{5,4},{6,7},{7,6},{8,9},{9,8},{10,11... | collective-permute-start | bytes 405512 | tf_op jit(solution)/shard_map/ppermute | solution.py:544
  92.4 4.8 %shard_map.108 = (f32[128,128]{1,0:T(8,128)}, f32[128,128]{1,0:T(8,128)}, f32[128,128]{1,0:T(8,128)}, f32[8,128]{1,0:T(8,128)}, f32[128,128]{1,0:T(8,128)}) custom-call(f32[264,128]{1,0:T(8,128)} %bitcast.11, f32[264,128]{1,0:T(8,128)} %copy-done.4, s32[5]{0:T(128)} %compare_select_fusion.3.refs_1_.refs_2_.place_ref, f32[128,256]{1,0:T(8,128)} %constant.89.clone.lanes_ref, ...), custom_call_target="tpu_custom_call" | custom-call | tf_op jit(solution)/shard_map/pallas_call | solution.py:519
  97.2 17.6 %all_to_all.10 = f32[128,1,128]{2,1,0:T(1,128)} all-to-all(f32[128,1,128]{2,1,0:T(1,128)} %bitcast.13), channel_id=1, replica_groups=mesh['dp'=4,'grid'=32] {'dp','grid'}, dimensions={0} | all-to-all | bytes 131072 | tf_op jit(solution)/shard_map/all_to_all | solution.py:587
  114.8 5.6 %shard_map.109 = (f32[1024,128]{1,0:T(8,128)}, f32[8,128]{1,0:T(8,128)}) custom-call(f32[128,128]{1,0:T(8,128)} %bitcast.12, f32[8,128]{1,0:T(8,128)} %get-tuple-element.60.range_ref, f32[128,128]{1,0:T(8,128)} %get-tuple-element.61.scaled_ref, f32[128,128]{1,0:T(8,128)} %get-tuple-element.62.real_ref, f32[128,128]{1,0:T(8,128)} %get-tuple-element.63.imag_ref, ...), custom_call_target="tpu_custom_call" | custom-call | tf_op jit(solution)/shard_map/pallas_call | solution.py:519
  120.5 19.2 %all_to_all.11 = f32[128,8,128]{2,1,0:T(8,128)} all-to-all(f32[128,8,128]{2,1,0:T(8,128)} %bitcast.9), channel_id=1, replica_groups=mesh['dp'=4,'grid'=32] {'dp','grid'}, dimensions={0} | all-to-all | bytes 1048576 | tf_op jit(solution)/shard_map/all_to_all | solution.py:592
  139.6 2.6 %shard_map.110 = (f32[4,128,128]{2,1,0:T(8,128)}, f32[4,128,128]{2,1,0:T(8,128)}) custom-call(f32[1024,128]{1,0:T(8,128)} %bitcast.8, f32[8,128]{1,0:T(8,128)} %get-tuple-element.65.gain_ref, f32[256,256]{1,0:T(8,128)} %constant.92.clone.back_ref), custom_call_target="tpu_custom_call" | custom-call | tf_op jit(solution)/shard_map/pallas_call | solution.py:519
  (69 shorter events, 16.8 us)
Async XLA Ops:
  9.7 5.6 %collective-permute-start.4 = (f32[64,64,128]{2,1,0:T(8,128)}, f32[64,64,128]{2,1,0:T(8,128)}, u32[]{:S(2)}, u32[]{:S(2)}) collective-permute-start(f32[64,64,128]{2,1,0:T(8,128)} %get-tuple-element.42), channel_id=1, source_target_pairs={{0,1},{1,0},{2,3},{3,2},{4,5},{5,4},{6,7},{7,6},{8,9},{9,8},{10,11... | collective-permute-start | bytes 6291464 | tf_op jit(solution)/shard_map/ppermute | solution.py:544
  11.2 22.1 %collective-permute-start = (f32[64,64,128]{2,1,0:T(8,128)}, f32[64,64,128]{2,1,0:T(8,128)S(1)}, u32[]{:S(2)}, u32[]{:S(2)}) collective-permute-start(f32[64,64,128]{2,1,0:T(8,128)} %get-tuple-element.37), channel_id=1, source_target_pairs={{0,1},{1,0},{2,3},{3,2},{4,5},{5,4},{6,7},{7,6},{8,9},{9,8},{10,11... | collective-permute-start | bytes 6291464 | tf_op jit(solution)/shard_map/ppermute | solution.py:544
  19.8 27.3 %collective-permute-start.5 = (f32[16,64,128]{2,1,0:T(8,128)}, f32[16,64,128]{2,1,0:T(8,128)S(1)}, u32[]{:S(2)}, u32[]{:S(2)}) collective-permute-start(f32[16,64,128]{2,1,0:T(8,128)} %get-tuple-element.44), channel_id=1, source_target_pairs={{0,32},{1,3},{2,34},{3,5},{4,36},{5,7},{6,38},{7,1},{8,40},{9,11},... | collective-permute-start | bytes 1572872 | tf_op jit(solution)/shard_map/ppermute | solution.py:528
  21.2 5.3 %collective-permute-start.8 = (f32[128,128]{1,0:T(8,128)S(1)}, f32[128,128]{1,0:T(8,128)S(1)}, u32[]{:S(2)}, u32[]{:S(2)}) collective-permute-start(f32[128,128]{1,0:T(8,128)S(1)} %copy-done.11), channel_id=1, source_target_pairs={{0,32},{1,33},{2,34},{3,35},{4,36},{5,37},{6,38},{7,39},{8,40},{9,... | collective-permute-start | bytes 196616 | tf_op jit(solution)/shard_map/ppermute | solution.py:528
  22.4 6.6 %collective-permute-start.9 = (f32[128,128]{1,0:T(8,128)S(1)}, f32[128,128]{1,0:T(8,128)S(1)}, u32[]{:S(2)}, u32[]{:S(2)}) collective-permute-start(f32[128,128]{1,0:T(8,128)S(1)} %copy-done.10), channel_id=1, source_target_pairs={{0,64},{1,65},{2,66},{3,67},{4,68},{5,69},{6,70},{7,71},{8,72},{9,... | collective-permute-start | bytes 196616 | tf_op jit(solution)/shard_map/ppermute | solution.py:528
  24.8 5.4 %collective-permute-start.10 = (f32[128,128]{1,0:T(8,128)S(1)}, f32[128,128]{1,0:T(8,128)S(1)}, u32[]{:S(2)}, u32[]{:S(2)}) collective-permute-start(f32[128,128]{1,0:T(8,128)S(1)} %copy-done.9), channel_id=1, source_target_pairs={{0,96},{1,97},{2,98},{3,99},{4,100},{5,101},{6,102},{7,103},{8,104... | collective-permute-start | bytes 196616 | tf_op jit(solution)/shard_map/ppermute | solution.py:528
  26.5 23.2 %collective-permute-start.6 = (f32[16,64,128]{2,1,0:T(8,128)}, f32[16,64,128]{2,1,0:T(8,128)}, u32[]{:S(2)}, u32[]{:S(2)}) collective-permute-start(f32[16,64,128]{2,1,0:T(8,128)} %get-tuple-element.45), channel_id=1, source_target_pairs={{0,64},{1,5},{2,66},{3,7},{4,68},{5,1},{6,70},{7,3},{8,72},{9,13},... | collective-permute-start | bytes 1572872 | tf_op jit(solution)/shard_map/ppermute | solution.py:528
  29.1 20.6 %collective-permute-start.7 = (f32[16,64,128]{2,1,0:T(8,128)}, f32[16,64,128]{2,1,0:T(8,128)}, u32[]{:S(2)}, u32[]{:S(2)}) collective-permute-start(f32[16,64,128]{2,1,0:T(8,128)} %get-tuple-element.46), channel_id=1, source_target_pairs={{0,96},{1,7},{2,98},{3,1},{4,100},{5,3},{6,102},{7,5},{8,104},{9,1... | collective-permute-start | bytes 1572872 | tf_op jit(solution)/shard_map/ppermute | solution.py:528
  33.0 7.0 %collective-permute-start.11 = (f32[16,16,128]{2,1,0:T(8,128)}, f32[16,16,128]{2,1,0:T(8,128)S(1)}, u32[]{:S(2)}, u32[]{:S(2)}) collective-permute-start(f32[16,16,128]{2,1,0:T(8,128)} %get-tuple-element.56), channel_id=1, source_target_pairs={{0,32},{1,3},{2,34},{3,5},{4,36},{5,7},{6,38},{7,1},{8,40},{9,11},... | collective-permute-start | bytes 393224 | tf_op jit(solution)/shard_map/ppermute | solution.py:528
  33.3 11.2 %collective-permute-start.12 = (f32[16,16,128]{2,1,0:T(8,128)}, f32[16,16,128]{2,1,0:T(8,128)S(1)}, u32[]{:S(2)}, u32[]{:S(2)}) collective-permute-start(f32[16,16,128]{2,1,0:T(8,128)} %get-tuple-element.57), channel_id=1, source_target_pairs={{0,64},{1,5},{2,66},{3,7},{4,68},{5,1},{6,70},{7,3},{8,72},{9,13},... | collective-permute-start | bytes 393224 | tf_op jit(solution)/shard_map/ppermute | solution.py:528
  40.0 9.7 %copy-start.1 = (f32[16,64,128]{2,1,0:T(8,128)S(1)}, f32[16,64,128]{2,1,0:T(8,128)}, u32[]{:S(2)}) copy-start(f32[16,64,128]{2,1,0:T(8,128)} %get-tuple-element.43) | copy-start | bytes 1572868
  40.0 5.9 %collective-permute-start.13 = (f32[16,16,128]{2,1,0:T(8,128)}, f32[16,16,128]{2,1,0:T(8,128)}, u32[]{:S(2)}, u32[]{:S(2)}) collective-permute-start(f32[16,16,128]{2,1,0:T(8,128)} %get-tuple-element.58), channel_id=1, source_target_pairs={{0,96},{1,7},{2,98},{3,1},{4,100},{5,3},{6,102},{7,5},{8,104},{9,1... | collective-permute-start | bytes 393224 | tf_op jit(solution)/shard_map/ppermute | solution.py:528
  44.5 15.9 %copy-start.2 = (f32[16,64,128]{2,1,0:T(8,128)S(1)}, f32[16,64,128]{2,1,0:T(8,128)}, u32[]{:S(2)}) copy-start(f32[16,64,128]{2,1,0:T(8,128)} %get-tuple-element.38) | copy-start | bytes 1572868
  44.5 15.4 %collective-permute-start.1 = (f32[16,64,128]{2,1,0:T(8,128)}, f32[16,64,128]{2,1,0:T(8,128)S(1)}, u32[]{:S(2)}, u32[]{:S(2)}) collective-permute-start(f32[16,64,128]{2,1,0:T(8,128)} %get-tuple-element.39), channel_id=1, source_target_pairs={{0,32},{1,3},{2,34},{3,5},{4,36},{5,7},{6,38},{7,1},{8,40},{9,11},... | collective-permute-start | bytes 1572872 | tf_op jit(solution)/shard_map/ppermute | solution.py:528
  46.0 14.0 %collective-permute-start.2 = (f32[16,64,128]{2,1,0:T(8,128)}, f32[16,64,128]{2,1,0:T(8,128)S(1)}, u32[]{:S(2)}, u32[]{:S(2)}) collective-permute-start(f32[16,64,128]{2,1,0:T(8,128)} %get-tuple-element.40), channel_id=1, source_target_pairs={{0,64},{1,5},{2,66},{3,7},{4,68},{5,1},{6,70},{7,3},{8,72},{9,13},... | collective-permute-start | bytes 1572872 | tf_op jit(solution)/shard_map/ppermute | solution.py:528
  47.1 13.4 %collective-permute-start.3 = (f32[16,64,128]{2,1,0:T(8,128)}, f32[16,64,128]{2,1,0:T(8,128)S(1)}, u32[]{:S(2)}, u32[]{:S(2)}) collective-permute-start(f32[16,64,128]{2,1,0:T(8,128)} %get-tuple-element.41), channel_id=1, source_target_pairs={{0,96},{1,7},{2,98},{3,1},{4,100},{5,3},{6,102},{7,5},{8,104},{9,1... | collective-permute-start | bytes 1572872 | tf_op jit(solution)/shard_map/ppermute | solution.py:528
  60.7 8.1 %collective-permute-start.14 = (f32[4,144,128]{2,1,0:T(8,128)S(1)}, f32[4,144,128]{2,1,0:T(8,128)S(1)}, u32[]{:S(2)}, u32[]{:S(2)}) collective-permute-start(f32[4,144,128]{2,1,0:T(8,128)S(1)} %get-tuple-element.70), channel_id=1, source_target_pairs={{0,2},{1,9},{2,4},{3,11},{4,6},{5,13},{6,0},{7,15},{8,10},{9,17},{... | collective-permute-start | bytes 884744 | tf_op jit(solution)/shard_map/ppermute | solution.py:528
  62.5 10.6 %collective-permute-start.15 = (f32[4,144,128]{2,1,0:T(8,128)S(1)}, f32[4,144,128]{2,1,0:T(8,128)S(1)}, u32[]{:S(2)}, u32[]{:S(2)}) collective-permute-start(f32[4,144,128]{2,1,0:T(8,128)S(1)} %get-tuple-element.71), channel_id=1, source_target_pairs={{0,4},{1,17},{2,6},{3,19},{4,0},{5,21},{6,2},{7,23},{8,12},{9,25},... | collective-permute-start | bytes 884744 | tf_op jit(solution)/shard_map/ppermute | solution.py:528
  65.8 7.3 %collective-permute-start.16 = (f32[4,144,128]{2,1,0:T(8,128)S(1)}, f32[4,144,128]{2,1,0:T(8,128)S(1)}, u32[]{:S(2)}, u32[]{:S(2)}) collective-permute-start(f32[4,144,128]{2,1,0:T(8,128)S(1)} %get-tuple-element.72), channel_id=1, source_target_pairs={{0,6},{1,25},{2,0},{3,27},{4,2},{5,29},{6,4},{7,31},{8,14},{9,1},{... | collective-permute-start | bytes 884744 | tf_op jit(solution)/shard_map/ppermute | solution.py:528
  73.2 4.9 %collective-permute-start.17 = (f32[1,168,128]{2,1,0:T(8,128)S(1)}, f32[1,168,128]{2,1,0:T(8,128)S(1)}, u32[]{:S(2)}, u32[]{:S(2)}) collective-permute-start(f32[1,168,128]{2,1,0:T(8,128)S(1)} %get-tuple-element.75), channel_id=1, source_target_pairs={{0,8},{1,33},{2,10},{3,35},{4,12},{5,37},{6,14},{7,39},{8,16},{9,4... | collective-permute-start | bytes 258056 | tf_op jit(solution)/shard_map/ppermute | solution.py:528
  73.3 5.0 %collective-permute-start.19 = (f32[1,168,128]{2,1,0:T(8,128)S(1)}, f32[1,168,128]{2,1,0:T(8,128)S(1)}, u32[]{:S(2)}, u32[]{:S(2)}) collective-permute-start(f32[1,168,128]{2,1,0:T(8,128)S(1)} %get-tuple-element.76), channel_id=1, source_target_pairs={{0,24},{1,97},{2,26},{3,99},{4,28},{5,101},{6,30},{7,103},{8,0},{9... | collective-permute-start | bytes 258056 | tf_op jit(solution)/shard_map/ppermute | solution.py:528
  76.0 4.8 %collective-permute-start.18 = (f32[1,168,128]{2,1,0:T(8,128)S(1)}, f32[1,168,128]{2,1,0:T(8,128)S(1)}, u32[]{:S(2)}, u32[]{:S(2)}) collective-permute-start(f32[1,168,128]{2,1,0:T(8,128)S(1)} %get-tuple-element.77), channel_id=1, source_target_pairs={{0,16},{1,65},{2,18},{3,67},{4,20},{5,69},{6,22},{7,71},{8,24},{9,... | collective-permute-start | bytes 258056 | tf_op jit(solution)/shard_map/ppermute | solution.py:528
  80.9 10.9 %copy-start.3 = (f32[1,264,128]{2,1,0:T(8,128)}, f32[1,264,128]{2,1,0:T(8,128)S(1)}, u32[]{:S(2)}) copy-start(f32[1,264,128]{2,1,0:T(8,128)S(1)} %constant_dynamic-update-slice_fusion.6) | copy-start | bytes 405508
  80.9 10.9 %collective-permute-start.20 = (f32[264,128]{1,0:T(8,128)S(1)}, f32[264,128]{1,0:T(8,128)S(1)}, u32[]{:S(2)}, u32[]{:S(2)}) collective-permute-start(f32[264,128]{1,0:T(8,128)S(1)} %bitcast.10), channel_id=1, source_target_pairs={{0,1},{1,0},{2,3},{3,2},{4,5},{5,4},{6,7},{7,6},{8,9},{9,8},{10,11... | collective-permute-start | bytes 405512 | tf_op jit(solution)/shard_map/ppermute | solution.py:544
  (9 other events, 44.0 us)

commit v4 on v3

--- a/solution.py
+++ b/solution.py
@@ -78,7 +78,7 @@
 
 SIDE = 4
 CORES = 2
-ORDERS = ((0, 1, 2), (1, 2, 0))
+ORDERS = ((0, 2, 1), (1, 2, 0))
 
 
 def place_of(device):
@@ -115,16 +115,24 @@
     packed = np.concatenate([cos[:, :half], cos[:, half : half + 1], -sin[:, 1:half]], 1)
     high = packed.astype(jnp.bfloat16)
     low = (packed - high.astype(np.float64)).astype(jnp.bfloat16)
+    lanes, rows = np.concatenate([cos, sin], 1), np.concatenate([cos, sin], 0)
+    back = np.concatenate(
+        [np.concatenate([cos[held], sin[held]], 1), np.concatenate([-sin[held], cos[held]], 1)], 0
+    )
+
+    def thrice(table, axis):
+        above = table.astype(jnp.bfloat16)
+        below = (table - above.astype(np.float64)).astype(jnp.bfloat16)
+        return np.concatenate([above, above, below], axis)
+
     return dict(
         packed=np.stack([np.concatenate([p[:, :half], q[:, :half]], 1) for p, q in ((high, low), (high[:, half:], low[:, half:]))]),
-        lanes=as_f32(np.concatenate([cos, sin], 1)),
-        rows=as_f32(np.concatenate([cos, sin], 0)),
-        back=as_f32(
-            np.concatenate(
-                [np.concatenate([cos[held], sin[held]], 1), np.concatenate([-sin[held], cos[held]], 1)], 0
-            )
-        ),
-        mirror=as_f32(((index[:, None] + index[None, :]) % size) == 0),
+        lanes=as_f32(lanes),
+        rows=as_f32(rows),
+        lanes_pieces=thrice(lanes, 0),
+        rows_pieces=thrice(rows, 1),
+        back_pieces=thrice(back, 0),
+        mirror=(((index[:, None] + index[None, :]) % size) == 0).astype(jnp.bfloat16),
     )
 
 
@@ -132,6 +140,36 @@
     return lax.dot_general(
         a, b, (((left,), (right,)), ((), ())), precision=HIGHEST, preferred_element_type=jnp.float32
     )
+
+
+def pieces_of(a, count):
+    found = []
+    for _ in range(count):
+        piece = a.astype(jnp.bfloat16)
+        found.append(piece)
+        a = a - piece.astype(jnp.float32)
+    return found
+
+
+def dot_pieces(a, b, left, right):
+    return lax.dot_general(a, b, (((left,), (right,)), ((), ())), preferred_element_type=jnp.float32)
+
+
+def stacked(a, axis):
+    high, low = pieces_of(a, 2)
+    return jnp.concatenate([high, low, high], axis)
+
+
+def select_rows(one_hot, a):
+    width = a.shape[1]
+    found = dot_pieces(one_hot, jnp.concatenate(pieces_of(a, 3), 1), 1, 0)
+    return (found[:, :width] + found[:, width : 2 * width]) + found[:, 2 * width :]
+
+
+def select_lanes(a, one_hot):
+    height = a.shape[0]
+    found = dot_pieces(jnp.concatenate(pieces_of(a, 3), 0), one_hot, 1, 0)
+    return (found[:height] + found[height : 2 * height]) + found[2 * height :]
 
 
 HALVES = 2
@@ -316,11 +354,11 @@
     ends = jnp.where(lax.broadcasted_iota(jnp.int32, (8, size), 1) < half, low, -high)
     count = half // SIDE
     for r, out_ref in enumerate(outs):
-        out_ref[:, 0:8, :] = jnp.zeros((count, 8, size), jnp.float32)
-        out_ref[:, 8:16, :] = jnp.broadcast_to(ends[None], (count, 8, size))
+        out_ref[...] = jnp.zeros(out_ref.shape, jnp.float32)
+        out_ref[8 * count :, :] = ends
         for sign in range(2):
             at = sign * half + r * count
-            out_ref[:, 2 * r + sign, :] = rows[at : at + count]
+            out_ref[pl.ds(2 * r + sign, count, stride=8), :] = rows[at : at + count]
 
 
 def sublane_total(a):
@@ -364,15 +402,19 @@
     given = jnp.concatenate([own_ref[size : 2 * size, :], other_ref[size : 2 * size, :]], 0)
     picks = [
         jnp.concatenate(
-            [jnp.where(row % 2 == sign, (ky == source).astype(jnp.float32), 0.0) for source in (from_own, from_other)], 1
+            [
+                jnp.where(row % 2 == sign, (ky == source).astype(jnp.float32), 0.0).astype(jnp.bfloat16)
+                for source in (from_own, from_other)
+            ],
+            1,
         )
         for sign in range(2)
     ]
-    signs = dot(jnp.concatenate(picks, 0), given)
+    signs = select_rows(jnp.concatenate(picks, 0), given)
     plus, minus = signs[:size], signs[size:]
     mine = jnp.where(second, minus, plus)
     partner = jnp.where(alone, mine, jnp.where(second, plus, minus))
-    scaled = (mine + dot(dot(mirror_ref[...], partner), mirror_ref[...])) * 0.5 / span
+    scaled = (mine + select_lanes(select_rows(mirror_ref[...], partner), mirror_ref[...])) * 0.5 / span
     scaled_ref[...] = scaled.T
 
     mine, theirs = own_ref[:size, :], other_ref[:size, :]
@@ -491,10 +533,10 @@
     real, imag = real_ref[...], imag_ref[...]
     back_real = solved * real - left * imag
     back_imag = solved * imag + left * real
-    ends = dot(jnp.concatenate([back_real, back_imag], 0), lanes_ref[...])
+    ends = dot_pieces(stacked(jnp.concatenate([back_real, back_imag], 0), 1), lanes_ref[...], 1, 0)
     mid_real = ends[:size, :size] - ends[size:, size:]
     mid_imag = ends[size:, :size] + ends[:size, size:]
-    both = dot(rows_ref[...], jnp.concatenate([mid_real, mid_imag], 1))
+    both = dot_pieces(rows_ref[...], stacked(jnp.concatenate([mid_real, mid_imag], 1), 0), 1, 0)
     real = both[:size, :size] - both[size:, size:]
     imag = both[:size, size:] + both[size:, :size]
     for copy in range(out_ref.shape[0] // (2 * size)):
@@ -508,7 +550,7 @@
     shrink = 1.0 / gain_ref[0:1, :]
     for j in range(planes):
         pieces = [given_ref[pl.ds(2 * j + part, size, stride=step), :] for part in range(2)]
-        both = dot_as(jnp.concatenate(pieces, 0), back_ref[...], 0, 0)
+        both = dot_pieces(stacked(jnp.concatenate(pieces, 0), 0), back_ref[...], 0, 0)
         field_ref[j] = both[:, :size]
         resid_ref[j] = both[:, size:] * shrink
 
@@ -566,20 +608,27 @@
         kept = grid_call(True, part, ngrid, capacity, *members, arrived[part])
         data.append(exchange(kept, axes[0]))
     kept, weights = together((kept, weights))
-    rows = call(weight_kernel, [(SIDE**2, 16, size)] * SIDE, *weights, place)
+    rows = call(weight_kernel, [(SIDE**2 * 8 + 8, size)] * SIDE, *weights, place)
     rows = exchange(rows, axes[0])
-    held = summed([a[:, :8] for a in rows])
-    ends = least([a[:, 8:] for a in rows])
-    parts = quarter(jnp.concatenate([summed(data[0]), summed(data[1]), held, ends], 1))
+    parts = quarter(summed(data[0]))
+    early = exchange(parts, axes[1])
+    held = summed([a[: SIDE**2 * 8] for a in rows]).reshape(SIDE**2, 8, size)
+    ends = jnp.broadcast_to(least([a[SIDE**2 * 8 :] for a in rows])[None], (SIDE**2, 8, size))
+    parts = exchange(quarter(jnp.concatenate([summed(data[1]), held, ends], 1)), axes[1])
+    late = size // HALVES
     for stage in (1, 2):
-        parts = exchange(parts, axes[stage])
-        parts = [
-            summed([a[:, :size] for a in parts]),
-            jnp.concatenate([a[:, size:-8] for a in parts], 1),
+        if stage == 2:
+            parts = exchange(quarter(parts), axes[2])
+            late = size
+        found = [
+            summed([a[:, :late] for a in parts]),
+            jnp.concatenate([a[:, late:-8] for a in parts], 1),
             least([a[:, -8:] for a in parts]),
         ]
-        parts = jnp.concatenate(parts, 1)
-        parts = quarter(parts) if stage == 1 else parts[0]
+        if stage == 1:
+            found = [summed(early)] + found
+        parts = jnp.concatenate(found, 1)
+    parts = parts[0]
     real, imag, scaled, ends, send = call(
         moment_kernel, [square, square, square, (8, size), square],
         parts, swap(parts), place, table["lanes"], table["rows"], table["mirror"],
@@ -587,13 +636,13 @@
     sums = lax.all_to_all(send.reshape(count, 1, size), ALL, 0, 0, tiled=True).reshape(count, size)
     back, gain = call(
         functools.partial(solve_kernel, scale=1.0 / size**3), [(ndp * 2 * size, size), (8, size)],
-        sums, ends, scaled, real, imag, table["lanes"], table["rows"],
+        sums, ends, scaled, real, imag, table["lanes_pieces"], table["rows_pieces"],
     )
     landed = lax.all_to_all(back.reshape(count, 2 * planes, size), ALL, 0, 0, tiled=True)
     return tuple(
         call(
             output_kernel, [(planes, size, size)] * 2,
-            landed.reshape(count * 2 * planes, size), gain, table["back"],
+            landed.reshape(count * 2 * planes, size), gain, table["back_pieces"],
         )
     )
 

time: 143 us -> 134 us (0.937)
  waiting for transfers between devices: 30.9 us -> 27.6 us
  blocking collectives: 36.8 us -> 34.1 us
    ppermute x3, starting transfers between devices: 11.4 us -> 5.08 us  [body(): swap = lambda a: lax.ppermute(a, ALL, shift_pairs((3, 3), 1))]
    ppermute x18 -> x21, starting transfers between devices: 25.2 us -> 30.3 us  [exchange(): lax.ppermute(parts[r], ALL, shift_pairs(axes, r))]
    ppermute x3, waiting for transfers between devices: 5.03 us -> 1 us  [body(): swap = lambda a: lax.ppermute(a, ALL, shift_pairs((3, 3), 1))]
    all_to_all x1, blocking collectives: 17.6 us -> 15.2 us  [body(): lax.all_to_all(send.reshape(count, 1, size), ALL, 0, 0, tiled=True)]
    ppermute x18 -> x21, waiting for transfers between devices: 25.9 us -> 26.6 us  [exchange(): lax.ppermute(parts[r], ALL, shift_pairs(axes, r))]
  transfers between devices with their start and end apart: 21 -> 24, of which waited for: 11 -> 9; matrix products, arithmetic and copies ran while one was open for 2% -> 1% of each run, Pallas kernels for 8% -> 8%
where the time goes in v4:
time: 134 us
  starting transfers between devices  35.3 us (26%)
  blocking collectives  34.1 us (25%)
  Pallas kernels  31.2 us (23%)
  waiting for transfers between devices  27.6 us (21%)
  local copies, waits for them, and re-layouts  2.75 us (2%)
  other arithmetic  2.08 us (2%)
    ppermute x21, starting transfers between devices, exchange(): lax.ppermute(parts[r], ALL, shift_pairs(axes, r))  30.3 us
    ppermute x21, waiting for transfers between devices, exchange(): lax.ppermute(parts[r], ALL, shift_pairs(axes, r))  26.6 us
    all_to_all x1, blocking collectives, body(): lax.all_to_all(back.reshape(count, 2 * planes, size), ALL, 0, 0, tiled=True)  18.9 us
    pallas_call x3, Pallas kernels, grid_call(): pl.pallas_call(functools.partial(grid_kernel, kept=kept, part=part, capac...  17.1 us
    all_to_all x1, blocking collectives, body(): lax.all_to_all(send.reshape(count, 1, size), ALL, 0, 0, tiled=True)  15.2 us
    pallas_call x4, Pallas kernels, call(): pl.pallas_call(kernel, out_shape=[jax.ShapeDtypeStruct(s, jnp.float32) fo...  14.1 us
    ppermute x3, starting transfers between devices, body(): swap = lambda a: lax.ppermute(a, ALL, shift_pairs((3, 3), 1))  5.08 us
  transfers between devices with their start and end apart: 24, of which 9 were waited for; matrix products, arithmetic and copies ran while one was open for 1% of the time, Pallas kernels for 8%

profile of v4, /device:TPU:1, one launch (start us, length us, event | category | flops | bytes accessed | tf_op | source)
XLA Modules:
  0.0 134.0 jit_solution(17626746749631356225)
XLA Ops:
  1.3 8.4 %shard_map.122 = (f32[64,64,128]{2,1,0:T(8,128)}, f32[64,64,128]{2,1,0:T(8,128)}, bf16[64,32,128]{2,1,0:T(8,128)(2,1)}, s32[32]{0:T(128)}, s32[128]{0:T(128)}, /...) custom-call(s32[64]{0:T(128)} %bitcast.20, ...), custom_call_target="tpu_custom_call" | custom-call | tf_op jit(solution)/shard_map/pallas_call | solution.py:320
  12.6 2.4 %collective-permute-start.12 = (f32[128,128]{1,0:T(8,128)}, f32[128,128]{1,0:T(8,128)S(1)}, u32[]{:S(2)}, u32[]{:S(2)}) collective-permute-start(f32[128,128]{1,0:T(8,128)} %get-tuple-element.49), channel_id=1, source_target_pairs={{0,64},{1,65},{2,66},{3,67},{4,68},{5,69},{6,70},{7,71},{8,72},{9,... | collective-permute-start | bytes 196616 | tf_op jit(solution)/shard_map/ppermute | solution.py:570
  16.2 4.4 %shard_map.124 = (f32[16,64,128]{2,1,0:T(8,128)}, f32[16,64,128]{2,1,0:T(8,128)}, f32[16,64,128]{2,1,0:T(8,128)}, f32[16,64,128]{2,1,0:T(8,128)}) custom-call(s32[32]{0:T(128)} %get-tuple-element.34.refs_0_, s32[128]{0:T(128)} %get-tuple-element.35.refs_1_, s32[5]{0:T(128)} %compare_select_fusion.3.refs_1_.refs_2_.place_ref, ...), custom_call_target="tpu_custom_call" | custom-call | tf_op jit(solution)/shard_map/pallas_call | solution.py:320
  21.2 2.0 %shard_map.125 = (f32[136,128]{1,0:T(8,128)}, f32[136,128]{1,0:T(8,128)}, f32[136,128]{1,0:T(8,128)}, f32[136,128]{1,0:T(8,128)}) custom-call(f32[128,128]{1,0:T(8,128)} %get-tuple-element.51.w0_ref, f32[128,128]{1,0:T(8,128)} %copy-done.5, f32[128,128]{1,0:T(8,128)} %copy-done.6, f32[128,128]{1,0:T(8,128)} %copy-done.7, ...), custom_call_target="tpu_custom_call" | custom-call | tf_op jit(solution)/shard_map/pallas_call | solution.py:561
  24.5 2.7 %collective-permute-start.15 = (f32[136,128]{1,0:T(8,128)}, f32[136,128]{1,0:T(8,128)S(1)}, u32[]{:S(2)}, u32[]{:S(2)}) collective-permute-start(f32[136,128]{1,0:T(8,128)} %get-tuple-element.57), channel_id=1, source_target_pairs={{0,64},{1,5},{2,66},{3,7},{4,68},{5,1},{6,70},{7,3},{8,72},{9,13},... | collective-permute-start | bytes 208904 | tf_op jit(solution)/shard_map/ppermute | solution.py:570
  29.6 4.3 %shard_map.123 = (f32[16,64,128]{2,1,0:T(8,128)}, f32[16,64,128]{2,1,0:T(8,128)}, f32[16,64,128]{2,1,0:T(8,128)}, f32[16,64,128]{2,1,0:T(8,128)}) custom-call(s32[32]{0:T(128)} %get-tuple-element.34.refs_0_, s32[128]{0:T(128)} %get-tuple-element.35.refs_1_, s32[5]{0:T(128)} %compare_select_fusion.3.refs_1_.refs_2_.place_ref, ...), custom_call_target="tpu_custom_call" | custom-call | tf_op jit(solution)/shard_map/pallas_call | solution.py:320
  35.2 1.7 %collective-permute-start.3 = (f32[16,64,128]{2,1,0:T(8,128)}, f32[16,64,128]{2,1,0:T(8,128)S(1)}, u32[]{:S(2)}, u32[]{:S(2)}) collective-permute-start(f32[16,64,128]{2,1,0:T(8,128)} %get-tuple-element.41), channel_id=1, source_target_pairs={{0,96},{1,7},{2,98},{3,1},{4,100},{5,3},{6,102},{7,5},{8,104},{9,1... | collective-permute-start | bytes 1572872 | tf_op jit(solution)/shard_map/ppermute | solution.py:570
  37.4 1.8 %collective-permute-start.9 = (f32[16,64,128]{2,1,0:T(8,128)S(1)}, f32[16,64,128]{2,1,0:T(8,128)S(1)}, u32[]{:S(2)}, u32[]{:S(2)}) collective-permute-start(f32[16,64,128]{2,1,0:T(8,128)S(1)} %copy-done.9), channel_id=1, source_target_pairs={{0,64},{1,5},{2,66},{3,7},{4,68},{5,1},{6,70},{7,3},{8,72},{9,13},... | collective-permute-start | bytes 1572872 | tf_op jit(solution)/shard_map/ppermute | solution.py:570
  39.2 10.2 %collective-permute-done.1 = f32[16,64,128]{2,1,0:T(8,128)S(1)} collective-permute-done((f32[16,64,128]{2,1,0:T(8,128)}, f32[16,64,128]{2,1,0:T(8,128)S(1)}, u32[]{:S(2)}, u32[]{:S(2)}) %collective-permute-start.1) | collective-permute-done | bytes 524320 | tf_op jit(solution)/shard_map/ppermute | solution.py:570
  51.3 1.7 %collective-permute-start.4 = (f32[4,64,128]{2,1,0:T(8,128)S(1)}, f32[4,64,128]{2,1,0:T(8,128)S(1)}, u32[]{:S(2)}, u32[]{:S(2)}) collective-permute-start(f32[4,64,128]{2,1,0:T(8,128)S(1)} %get-tuple-element.75), channel_id=1, source_target_pairs={{0,8},{1,9},{2,10},{3,11},{4,12},{5,13},{6,14},{7,15},{8,16},{9,17... | collective-permute-start | bytes 393224 | tf_op jit(solution)/shard_map/ppermute | solution.py:570
  53.0 2.2 %collective-permute-start.6 = (f32[4,64,128]{2,1,0:T(8,128)S(1)}, f32[4,64,128]{2,1,0:T(8,128)S(1)}, u32[]{:S(2)}, u32[]{:S(2)}) collective-permute-start(f32[4,64,128]{2,1,0:T(8,128)S(1)} %get-tuple-element.76), channel_id=1, source_target_pairs={{0,24},{1,25},{2,26},{3,27},{4,28},{5,29},{6,30},{7,31},{8,0},{9,1... | collective-permute-start | bytes 393224 | tf_op jit(solution)/shard_map/ppermute | solution.py:570
  55.2 5.5 %collective-permute-done.8 = f32[16,64,128]{2,1,0:T(8,128)S(1)} collective-permute-done((f32[16,64,128]{2,1,0:T(8,128)}, f32[16,64,128]{2,1,0:T(8,128)S(1)}, u32[]{:S(2)}, u32[]{:S(2)}) %collective-permute-start.8) | collective-permute-done | bytes 524320 | tf_op jit(solution)/shard_map/ppermute | solution.py:570
  60.6 3.6 %collective-permute-start.5 = (f32[4,64,128]{2,1,0:T(8,128)S(1)}, f32[4,64,128]{2,1,0:T(8,128)S(1)}, u32[]{:S(2)}, u32[]{:S(2)}) collective-permute-start(f32[4,64,128]{2,1,0:T(8,128)S(1)} %get-tuple-element.77), channel_id=1, source_target_pairs={{0,16},{1,17},{2,18},{3,19},{4,20},{5,21},{6,22},{7,23},{8,24},{9,... | collective-permute-start | bytes 393224 | tf_op jit(solution)/shard_map/ppermute | solution.py:570
  67.8 2.8 %collective-permute-done.17 = f32[4,80,128]{2,1,0:T(8,128)S(1)} collective-permute-done((f32[4,80,128]{2,1,0:T(8,128)S(1)}, f32[4,80,128]{2,1,0:T(8,128)S(1)}, u32[]{:S(2)}, u32[]{:S(2)}) %collective-permute-start.17) | collective-permute-done | bytes 163872 | tf_op jit(solution)/shard_map/ppermute | solution.py:570
  70.6 3.4 %collective-permute-done.18 = f32[4,80,128]{2,1,0:T(8,128)S(1)} collective-permute-done((f32[4,80,128]{2,1,0:T(8,128)S(1)}, f32[4,80,128]{2,1,0:T(8,128)S(1)}, u32[]{:S(2)}, u32[]{:S(2)}) %collective-permute-start.18) | collective-permute-done | bytes 163872 | tf_op jit(solution)/shard_map/ppermute | solution.py:570
  75.5 2.2 %collective-permute-start.22 = (f32[1,168,128]{2,1,0:T(8,128)S(1)}, f32[1,168,128]{2,1,0:T(8,128)S(1)}, u32[]{:S(2)}, u32[]{:S(2)}) collective-permute-start(f32[1,168,128]{2,1,0:T(8,128)S(1)} %get-tuple-element.79), channel_id=1, source_target_pairs={{0,6},{1,97},{2,0},{3,99},{4,2},{5,101},{6,4},{7,103},{8,14},{9,10... | collective-permute-start | bytes 258056 | tf_op jit(solution)/shard_map/ppermute | solution.py:570
  77.7 1.6 %collective-permute-start.21 = (f32[1,168,128]{2,1,0:T(8,128)S(1)}, f32[1,168,128]{2,1,0:T(8,128)S(1)}, u32[]{:S(2)}, u32[]{:S(2)}) collective-permute-start(f32[1,168,128]{2,1,0:T(8,128)S(1)} %get-tuple-element.80), channel_id=1, source_target_pairs={{0,4},{1,65},{2,6},{3,67},{4,0},{5,69},{6,2},{7,71},{8,12},{9,73},... | collective-permute-start | bytes 258056 | tf_op jit(solution)/shard_map/ppermute | solution.py:570
  79.6 3.0 %collective-permute-done.21 = f32[1,168,128]{2,1,0:T(8,128)S(1)} collective-permute-done((f32[1,168,128]{2,1,0:T(8,128)S(1)}, f32[1,168,128]{2,1,0:T(8,128)S(1)}, u32[]{:S(2)}, u32[]{:S(2)}) %collective-permute-start.21) | collective-permute-done | bytes 86048 | tf_op jit(solution)/shard_map/ppermute | solution.py:570
  82.7 3.6 %collective-permute-start.23 = (f32[264,128]{1,0:T(8,128)S(1)}, f32[264,128]{1,0:T(8,128)S(1)}, u32[]{:S(2)}, u32[]{:S(2)}) collective-permute-start(f32[264,128]{1,0:T(8,128)S(1)} %bitcast.16), channel_id=1, source_target_pairs={{0,1},{1,0},{2,3},{3,2},{4,5},{5,4},{6,7},{7,6},{8,9},{9,8},{10,11... | collective-permute-start | bytes 405512 | tf_op jit(solution)/shard_map/ppermute | solution.py:586
  87.9 4.5 %shard_map.126 = (f32[128,128]{1,0:T(8,128)}, f32[128,128]{1,0:T(8,128)}, f32[128,128]{1,0:T(8,128)}, f32[8,128]{1,0:T(8,128)}, f32[128,128]{1,0:T(8,128)}) custom-call(f32[264,128]{1,0:T(8,128)} %bitcast.17, f32[264,128]{1,0:T(8,128)} %copy-done.3, s32[5]{0:T(128)} %compare_select_fusion.3.refs_1_.refs_2_.place_ref, f32[128,256]{1,0:T(8,128)} %constant.93.clone.lanes_ref, ...), custom_call_target="tpu_custom_call" | custom-call | tf_op jit(solution)/shard_map/pallas_call | solution.py:561
  92.4 15.2 %all_to_all.10 = f32[128,1,128]{2,1,0:T(1,128)} all-to-all(f32[128,1,128]{2,1,0:T(1,128)} %bitcast.19), channel_id=1, replica_groups=mesh['dp'=4,'grid'=32] {'dp','grid'}, dimensions={0} | all-to-all | bytes 131072 | tf_op jit(solution)/shard_map/all_to_all | solution.py:636
  107.5 5.2 %shard_map.127 = (f32[1024,128]{1,0:T(8,128)}, f32[8,128]{1,0:T(8,128)}) custom-call(f32[128,128]{1,0:T(8,128)} %bitcast.18, f32[8,128]{1,0:T(8,128)} %get-tuple-element.60.range_ref, f32[128,128]{1,0:T(8,128)} %get-tuple-element.61.scaled_ref, f32[128,128]{1,0:T(8,128)} %get-tuple-element.62.real_ref, f32[128,128]{1,0:T(8,128)} %get-tuple-element.63.imag_ref, ...), custom_call_target="tpu_custom_call" | custom-call | tf_op jit(solution)/shard_map/pallas_call | solution.py:561
  112.7 18.9 %all_to_all.11 = f32[128,8,128]{2,1,0:T(8,128)} all-to-all(f32[128,8,128]{2,1,0:T(8,128)} %bitcast.14), channel_id=1, replica_groups=mesh['dp'=4,'grid'=32] {'dp','grid'}, dimensions={0} | all-to-all | bytes 1048576 | tf_op jit(solution)/shard_map/all_to_all | solution.py:641
  131.6 2.4 %shard_map.128 = (f32[4,128,128]{2,1,0:T(8,128)}, f32[4,128,128]{2,1,0:T(8,128)}) custom-call(f32[1024,128]{1,0:T(8,128)} %bitcast.13, f32[8,128]{1,0:T(8,128)} %get-tuple-element.65.gain_ref, bf16[768,256]{1,0:T(8,128)(2,1)} %constant.98.clone.back_ref), custom_call_target="tpu_custom_call" | custom-call | tf_op jit(solution)/shard_map/pallas_call | solution.py:561
  (76 shorter events, 19.4 us)
Async XLA Ops:
  9.7 6.5 %collective-permute-start.7 = (f32[64,64,128]{2,1,0:T(8,128)}, f32[64,64,128]{2,1,0:T(8,128)}, u32[]{:S(2)}, u32[]{:S(2)}) collective-permute-start(f32[64,64,128]{2,1,0:T(8,128)} %get-tuple-element.42), channel_id=1, source_target_pairs={{0,1},{1,0},{2,3},{3,2},{4,5},{5,4},{6,7},{7,6},{8,9},{9,8},{10,11... | collective-permute-start | bytes 6291464 | tf_op jit(solution)/shard_map/ppermute | solution.py:586
  11.1 17.2 %collective-permute-start = (f32[64,64,128]{2,1,0:T(8,128)}, f32[64,64,128]{2,1,0:T(8,128)S(1)}, u32[]{:S(2)}, u32[]{:S(2)}) collective-permute-start(f32[64,64,128]{2,1,0:T(8,128)} %get-tuple-element.37), channel_id=1, source_target_pairs={{0,1},{1,0},{2,3},{3,2},{4,5},{5,4},{6,7},{7,6},{8,9},{9,8},{10,11... | collective-permute-start | bytes 6291464 | tf_op jit(solution)/shard_map/ppermute | solution.py:586
  11.2 9.3 %collective-permute-start.11 = (f32[128,128]{1,0:T(8,128)}, f32[128,128]{1,0:T(8,128)S(1)}, u32[]{:S(2)}, u32[]{:S(2)}) collective-permute-start(f32[128,128]{1,0:T(8,128)} %get-tuple-element.48), channel_id=1, source_target_pairs={{0,32},{1,33},{2,34},{3,35},{4,36},{5,37},{6,38},{7,39},{8,40},{9,... | collective-permute-start | bytes 196616 | tf_op jit(solution)/shard_map/ppermute | solution.py:570
  12.6 8.0 %collective-permute-start.12 = (f32[128,128]{1,0:T(8,128)}, f32[128,128]{1,0:T(8,128)S(1)}, u32[]{:S(2)}, u32[]{:S(2)}) collective-permute-start(f32[128,128]{1,0:T(8,128)} %get-tuple-element.49), channel_id=1, source_target_pairs={{0,64},{1,65},{2,66},{3,67},{4,68},{5,69},{6,70},{7,71},{8,72},{9,... | collective-permute-start | bytes 196616 | tf_op jit(solution)/shard_map/ppermute | solution.py:570
  15.0 5.5 %collective-permute-start.13 = (f32[128,128]{1,0:T(8,128)}, f32[128,128]{1,0:T(8,128)S(1)}, u32[]{:S(2)}, u32[]{:S(2)}) collective-permute-start(f32[128,128]{1,0:T(8,128)} %get-tuple-element.50), channel_id=1, source_target_pairs={{0,96},{1,97},{2,98},{3,99},{4,100},{5,101},{6,102},{7,103},{8,104... | collective-permute-start | bytes 196616 | tf_op jit(solution)/shard_map/ppermute | solution.py:570
  23.3 12.0 %collective-permute-start.14 = (f32[136,128]{1,0:T(8,128)}, f32[136,128]{1,0:T(8,128)S(1)}, u32[]{:S(2)}, u32[]{:S(2)}) collective-permute-start(f32[136,128]{1,0:T(8,128)} %get-tuple-element.56), channel_id=1, source_target_pairs={{0,32},{1,3},{2,34},{3,5},{4,36},{5,7},{6,38},{7,1},{8,40},{9,11},... | collective-permute-start | bytes 208904 | tf_op jit(solution)/shard_map/ppermute | solution.py:570
  24.5 12.4 %collective-permute-start.15 = (f32[136,128]{1,0:T(8,128)}, f32[136,128]{1,0:T(8,128)S(1)}, u32[]{:S(2)}, u32[]{:S(2)}) collective-permute-start(f32[136,128]{1,0:T(8,128)} %get-tuple-element.57), channel_id=1, source_target_pairs={{0,64},{1,5},{2,66},{3,7},{4,68},{5,1},{6,70},{7,3},{8,72},{9,13},... | collective-permute-start | bytes 208904 | tf_op jit(solution)/shard_map/ppermute | solution.py:570
  27.2 10.2 %collective-permute-start.16 = (f32[136,128]{1,0:T(8,128)}, f32[136,128]{1,0:T(8,128)S(1)}, u32[]{:S(2)}, u32[]{:S(2)}) collective-permute-start(f32[136,128]{1,0:T(8,128)} %get-tuple-element.58), channel_id=1, source_target_pairs={{0,96},{1,7},{2,98},{3,1},{4,100},{5,3},{6,102},{7,5},{8,104},{9,1... | collective-permute-start | bytes 208904 | tf_op jit(solution)/shard_map/ppermute | solution.py:570
  34.0 15.4 %collective-permute-start.1 = (f32[16,64,128]{2,1,0:T(8,128)}, f32[16,64,128]{2,1,0:T(8,128)S(1)}, u32[]{:S(2)}, u32[]{:S(2)}) collective-permute-start(f32[16,64,128]{2,1,0:T(8,128)} %get-tuple-element.39), channel_id=1, source_target_pairs={{0,32},{1,3},{2,34},{3,5},{4,36},{5,7},{6,38},{7,1},{8,40},{9,11},... | collective-permute-start | bytes 1572872 | tf_op jit(solution)/shard_map/ppermute | solution.py:570
  34.4 15.0 %collective-permute-start.2 = (f32[16,64,128]{2,1,0:T(8,128)}, f32[16,64,128]{2,1,0:T(8,128)S(1)}, u32[]{:S(2)}, u32[]{:S(2)}) collective-permute-start(f32[16,64,128]{2,1,0:T(8,128)} %get-tuple-element.40), channel_id=1, source_target_pairs={{0,64},{1,5},{2,66},{3,7},{4,68},{5,1},{6,70},{7,3},{8,72},{9,13},... | collective-permute-start | bytes 1572872 | tf_op jit(solution)/shard_map/ppermute | solution.py:570
  35.2 14.8 %collective-permute-start.3 = (f32[16,64,128]{2,1,0:T(8,128)}, f32[16,64,128]{2,1,0:T(8,128)S(1)}, u32[]{:S(2)}, u32[]{:S(2)}) collective-permute-start(f32[16,64,128]{2,1,0:T(8,128)} %get-tuple-element.41), channel_id=1, source_target_pairs={{0,96},{1,7},{2,98},{3,1},{4,100},{5,3},{6,102},{7,5},{8,104},{9,1... | collective-permute-start | bytes 1572872 | tf_op jit(solution)/shard_map/ppermute | solution.py:570
  36.9 23.7 %collective-permute-start.8 = (f32[16,64,128]{2,1,0:T(8,128)}, f32[16,64,128]{2,1,0:T(8,128)S(1)}, u32[]{:S(2)}, u32[]{:S(2)}) collective-permute-start(f32[16,64,128]{2,1,0:T(8,128)} %get-tuple-element.44), channel_id=1, source_target_pairs={{0,32},{1,3},{2,34},{3,5},{4,36},{5,7},{6,38},{7,1},{8,40},{9,11},... | collective-permute-start | bytes 1572872 | tf_op jit(solution)/shard_map/ppermute | solution.py:570
  37.4 26.8 %collective-permute-start.9 = (f32[16,64,128]{2,1,0:T(8,128)S(1)}, f32[16,64,128]{2,1,0:T(8,128)S(1)}, u32[]{:S(2)}, u32[]{:S(2)}) collective-permute-start(f32[16,64,128]{2,1,0:T(8,128)S(1)} %copy-done.9), channel_id=1, source_target_pairs={{0,64},{1,5},{2,66},{3,7},{4,68},{5,1},{6,70},{7,3},{8,72},{9,13},... | collective-permute-start | bytes 1572872 | tf_op jit(solution)/shard_map/ppermute | solution.py:570
  49.4 14.8 %collective-permute-start.10 = (f32[16,64,128]{2,1,0:T(8,128)S(1)}, f32[16,64,128]{2,1,0:T(8,128)S(1)}, u32[]{:S(2)}, u32[]{:S(2)}) collective-permute-start(f32[16,64,128]{2,1,0:T(8,128)S(1)} %copy-done.8), channel_id=1, source_target_pairs={{0,96},{1,7},{2,98},{3,1},{4,100},{5,3},{6,102},{7,5},{8,104},{9,1... | collective-permute-start | bytes 1572872 | tf_op jit(solution)/shard_map/ppermute | solution.py:570
  51.3 15.2 %collective-permute-start.4 = (f32[4,64,128]{2,1,0:T(8,128)S(1)}, f32[4,64,128]{2,1,0:T(8,128)S(1)}, u32[]{:S(2)}, u32[]{:S(2)}) collective-permute-start(f32[4,64,128]{2,1,0:T(8,128)S(1)} %get-tuple-element.75), channel_id=1, source_target_pairs={{0,8},{1,9},{2,10},{3,11},{4,12},{5,13},{6,14},{7,15},{8,16},{9,17... | collective-permute-start | bytes 393224 | tf_op jit(solution)/shard_map/ppermute | solution.py:570
  53.0 14.8 %collective-permute-start.6 = (f32[4,64,128]{2,1,0:T(8,128)S(1)}, f32[4,64,128]{2,1,0:T(8,128)S(1)}, u32[]{:S(2)}, u32[]{:S(2)}) collective-permute-start(f32[4,64,128]{2,1,0:T(8,128)S(1)} %get-tuple-element.76), channel_id=1, source_target_pairs={{0,24},{1,25},{2,26},{3,27},{4,28},{5,29},{6,30},{7,31},{8,0},{9,1... | collective-permute-start | bytes 393224 | tf_op jit(solution)/shard_map/ppermute | solution.py:570
  60.6 7.1 %collective-permute-start.5 = (f32[4,64,128]{2,1,0:T(8,128)S(1)}, f32[4,64,128]{2,1,0:T(8,128)S(1)}, u32[]{:S(2)}, u32[]{:S(2)}) collective-permute-start(f32[4,64,128]{2,1,0:T(8,128)S(1)} %get-tuple-element.77), channel_id=1, source_target_pairs={{0,16},{1,17},{2,18},{3,19},{4,20},{5,21},{6,22},{7,23},{8,24},{9,... | collective-permute-start | bytes 393224 | tf_op jit(solution)/shard_map/ppermute | solution.py:570
  64.5 6.1 %collective-permute-start.17 = (f32[4,80,128]{2,1,0:T(8,128)S(1)}, f32[4,80,128]{2,1,0:T(8,128)S(1)}, u32[]{:S(2)}, u32[]{:S(2)}) collective-permute-start(f32[4,80,128]{2,1,0:T(8,128)S(1)} %get-tuple-element.72), channel_id=1, source_target_pairs={{0,8},{1,9},{2,10},{3,11},{4,12},{5,13},{6,14},{7,15},{8,16},{9,17... | collective-permute-start | bytes 491528 | tf_op jit(solution)/shard_map/ppermute | solution.py:570
  65.3 8.7 %collective-permute-start.18 = (f32[4,80,128]{2,1,0:T(8,128)S(1)}, f32[4,80,128]{2,1,0:T(8,128)S(1)}, u32[]{:S(2)}, u32[]{:S(2)}) collective-permute-start(f32[4,80,128]{2,1,0:T(8,128)S(1)} %get-tuple-element.73), channel_id=1, source_target_pairs={{0,16},{1,17},{2,18},{3,19},{4,20},{5,21},{6,22},{7,23},{8,24},{9,... | collective-permute-start | bytes 491528 | tf_op jit(solution)/shard_map/ppermute | solution.py:570
  66.5 8.3 %collective-permute-start.19 = (f32[4,80,128]{2,1,0:T(8,128)S(1)}, f32[4,80,128]{2,1,0:T(8,128)S(1)}, u32[]{:S(2)}, u32[]{:S(2)}) collective-permute-start(f32[4,80,128]{2,1,0:T(8,128)S(1)} %get-tuple-element.74), channel_id=1, source_target_pairs={{0,24},{1,25},{2,26},{3,27},{4,28},{5,29},{6,30},{7,31},{8,0},{9,1... | collective-permute-start | bytes 491528 | tf_op jit(solution)/shard_map/ppermute | solution.py:570
  75.0 4.6 %collective-permute-start.20 = (f32[1,168,128]{2,1,0:T(8,128)S(1)}, f32[1,168,128]{2,1,0:T(8,128)S(1)}, u32[]{:S(2)}, u32[]{:S(2)}) collective-permute-start(f32[1,168,128]{2,1,0:T(8,128)S(1)} %get-tuple-element.78), channel_id=1, source_target_pairs={{0,2},{1,33},{2,4},{3,35},{4,6},{5,37},{6,0},{7,39},{8,10},{9,41},... | collective-permute-start | bytes 258056 | tf_op jit(solution)/shard_map/ppermute | solution.py:570
  75.5 4.1 %collective-permute-start.22 = (f32[1,168,128]{2,1,0:T(8,128)S(1)}, f32[1,168,128]{2,1,0:T(8,128)S(1)}, u32[]{:S(2)}, u32[]{:S(2)}) collective-permute-start(f32[1,168,128]{2,1,0:T(8,128)S(1)} %get-tuple-element.79), channel_id=1, source_target_pairs={{0,6},{1,97},{2,0},{3,99},{4,2},{5,101},{6,4},{7,103},{8,14},{9,10... | collective-permute-start | bytes 258056 | tf_op jit(solution)/shard_map/ppermute | solution.py:570
  77.7 4.8 %collective-permute-start.21 = (f32[1,168,128]{2,1,0:T(8,128)S(1)}, f32[1,168,128]{2,1,0:T(8,128)S(1)}, u32[]{:S(2)}, u32[]{:S(2)}) collective-permute-start(f32[1,168,128]{2,1,0:T(8,128)S(1)} %get-tuple-element.80), channel_id=1, source_target_pairs={{0,4},{1,65},{2,6},{3,67},{4,0},{5,69},{6,2},{7,71},{8,12},{9,73},... | collective-permute-start | bytes 258056 | tf_op jit(solution)/shard_map/ppermute | solution.py:570
  82.7 4.5 %collective-permute-start.23 = (f32[264,128]{1,0:T(8,128)S(1)}, f32[264,128]{1,0:T(8,128)S(1)}, u32[]{:S(2)}, u32[]{:S(2)}) collective-permute-start(f32[264,128]{1,0:T(8,128)S(1)} %bitcast.16), channel_id=1, source_target_pairs={{0,1},{1,0},{2,3},{3,2},{4,5},{5,4},{6,7},{7,6},{8,9},{9,8},{10,11... | collective-permute-start | bytes 405512 | tf_op jit(solution)/shard_map/ppermute | solution.py:586
  (10 other events, 83.1 us)

commit v5 on v4

--- a/solution.py
+++ b/solution.py
@@ -79,6 +79,7 @@
 SIDE = 4
 CORES = 2
 ORDERS = ((0, 2, 1), (1, 2, 0))
+LATE_ORDERS = ((2, 0, 1), (2, 1, 0))
 
 
 def place_of(device):
@@ -172,8 +173,8 @@
     return (found[:height] + found[height : 2 * height]) + found[2 * height :]
 
 
-HALVES = 2
 STEPS = 4
+SHARES = (3, 1)
 
 
 def sublane_turn(tiles):
@@ -193,10 +194,10 @@
 def grid_kernel(*refs, kept, part, capacity):
     if kept:
         count_ref, list_ref, place_ref, wave_ref, matrix_ref, other_ref = refs[:6]
-        outs = refs[6:]
+        outs, weight_refs = refs[-SIDE:], refs[6:-SIDE]
     else:
         dest_ref, place_ref, values_ref, matrix_ref, packed_ref, weights_ref = refs[:6]
-        out_refs, (kept_wave_ref, count_ref, list_ref), wave_ref = refs[6:8], refs[8:11], refs[-1]
+        out_ref, kept_wave_ref, count_ref, list_ref, wave_ref = *refs[6:10], refs[-1]
     nent, rows, width = matrix_ref.shape
     size = width // SIDE
     half = size // 2
@@ -217,13 +218,13 @@
     def prepare():
         lax.fori_loop(0, nslab, clear, 0)
         lax.fori_loop(0, nent, enter, 0)
-        for r, slice_ref in enumerate(refs[11:-1]):
+        for r, slice_ref in enumerate(refs[10:-1]):
             slice_ref[...] = weights_ref[0, :, (place_ref[0] + r) % SIDE, :]
         chip = lax.broadcasted_iota(jnp.int32, (half, half), 0)
         slot = lax.broadcasted_iota(jnp.int32, (half, half), 1)
         digits = digits_of(slot)
         pieces = []
-        chips = [chip_at(*moved(place_ref, digits, owner, 1)) for owner in range(CORES)]
+        chips = [chip_at(*moved(place_ref, digits, order, 1)) for order in ORDERS]
         for owner in (1 - place_ref[3], place_ref[3]):
             pick = (chip == jnp.where(owner == 0, chips[0], chips[1])).astype(jnp.float32).astype(jnp.bfloat16)
             for start in (0, half):
@@ -249,7 +250,7 @@
         for pair in range(pairs):
             halves_of_tile = []
             for near in range(2):
-                slab = ((part * (STEPS // HALVES) + step) * pairs + pair) * 2 + near
+                slab = ((sum(SHARES[:part]) + step) * pairs + pair) * 2 + near
                 taken = count_ref[slab]
                 waves, matrices = [], []
                 for m in range(capacity):
@@ -275,19 +276,19 @@
                     out(index, place, block)
 
     def keep(index, place, block):
-        outs[index // SIDE**2][index % SIDE**2, place, :] = block + other_ref[index, place, :]
-
-    def send(out_ref):
-        def write(index, place, block):
-            out_ref[index, place, :] = block
-
-        return write
+        digits = digits_of(index)
+        first, second, third = digits if part == 0 else (digits[1], digits[0], digits[2])
+        outs[first][second * SIDE + third, place, :] = block + other_ref[index, place, :]
+
+    def send(index, place, block):
+        out_ref[index, place, :] = block
 
     if kept:
         products(keep)
+        if weight_refs:
+            write_rows(weight_refs, place_ref, outs, pairs * 8)
     else:
-        pl.when(step < STEPS // HALVES)(lambda: products(send(out_refs[0])))
-        pl.when(step >= STEPS // HALVES)(lambda: products(send(out_refs[1])))
+        products(send)
 
 
 def grid_call(kept, part, nslab, capacity, *args):
@@ -296,26 +297,28 @@
     matrix = args[4] if kept else args[3]
     nent, rows, width = matrix.shape
     size, blocks = width // SIDE, SIDE**3
-    steps = STEPS // HALVES if kept else STEPS
-    moving = lambda count: pl.BlockSpec((count, size // STEPS, size), lambda i: (0, i, 0))
+    steps = SHARES[part] if kept else STEPS
+    deep = [share * size // STEPS for share in SHARES]
+    moving = lambda count, start=0: pl.BlockSpec((count, size // STEPS, size), lambda i: (0, start + i, 0))
     f32 = lambda *shape: jax.ShapeDtypeStruct(shape, jnp.float32)
     in_specs = [scalars if a.dtype == jnp.int32 else fixed(a.shape) for a in args]
     if kept:
-        out_shape, out_specs = [f32(SIDE**2, size // HALVES, size)] * SIDE, [moving(SIDE**2)] * SIDE
-        in_specs[-1] = moving(blocks)
+        in_specs[5] = moving(blocks, sum(SHARES[:part]))
+        if part == 0:
+            out_shape, out_specs = [f32(SIDE**2, deep[0], size)] * SIDE, [moving(SIDE**2)] * SIDE
+        else:
+            shape = (SIDE**2, deep[1] + 16, size)
+            out_shape, out_specs = [f32(*shape)] * SIDE, [fixed(shape)] * SIDE
         scratch = []
     else:
         wave = (nent, rows, size)
-        out_shape = [f32(blocks, size // HALVES, size)] * HALVES + [
+        out_shape = [
+            f32(blocks, size, size),
             jax.ShapeDtypeStruct(wave, jnp.bfloat16),
             jax.ShapeDtypeStruct((nslab,), jnp.int32),
             jax.ShapeDtypeStruct((nslab * capacity,), jnp.int32),
         ] + [f32(size, size)] * SIDE
-        block = (blocks, size // STEPS, size)
-        out_specs = [
-            pl.BlockSpec(block, lambda i: (0, jnp.minimum(i, STEPS // HALVES - 1), 0)),
-            pl.BlockSpec(block, lambda i: (0, jnp.maximum(i - STEPS // HALVES, 0), 0)),
-        ] + [fixed(wave), scalars, scalars] + [fixed((size, size))] * SIDE
+        out_specs = [moving(blocks), fixed(wave), scalars, scalars] + [fixed((size, size))] * SIDE
         scratch = [pltpu.VMEM(wave, jnp.bfloat16)]
     return pl.pallas_call(
         functools.partial(grid_kernel, kept=kept, part=part, capacity=capacity),
@@ -327,9 +330,9 @@
     )(*args)
 
 
-def moved(place_ref, digits, owner, sign):
+def moved(place_ref, digits, order, sign):
     at = [place_ref[0], place_ref[1], place_ref[2]]
-    for digit, axis in zip(digits, ORDERS[owner]):
+    for digit, axis in zip(digits, order):
         at[axis] = (at[axis] + sign * digit + SIDE) % SIDE
     return at
 
@@ -338,15 +341,15 @@
     return index // SIDE**2, (index // SIDE) % SIDE, index % SIDE
 
 
-def weight_kernel(w0_ref, w1_ref, w2_ref, w3_ref, place_ref, *outs):
-    size = w0_ref.shape[0]
+def write_rows(weight_refs, place_ref, outs, base):
+    size = weight_refs[0].shape[0]
     half = size // 2
-    own = ((w0_ref[...] + w1_ref[...]) + w2_ref[...]) + w3_ref[...]
+    own = summed([ref[...] for ref in weight_refs])
     low = jnp.min(jnp.min(own, axis=0, keepdims=True), axis=1, keepdims=True)
     high = jnp.max(jnp.max(own, axis=0, keepdims=True), axis=1, keepdims=True)
     row = lax.broadcasted_iota(jnp.int32, (size, size), 0)
     lane = lax.broadcasted_iota(jnp.int32, (size, size), 1)
-    chips = [chip_at(*moved(place_ref, digits_of(row % half), owner, 1)) for owner in range(CORES)]
+    chips = [chip_at(*moved(place_ref, digits_of(row % half), order, 1)) for order in LATE_ORDERS]
     chip = jnp.where(place_ref[3] == 0, chips[0], chips[1])
     negative = jnp.where(chip == 0, half, size - chip)
     pick = (lane == jnp.where(row < half, chip, negative)).astype(jnp.float32)
@@ -354,11 +357,11 @@
     ends = jnp.where(lax.broadcasted_iota(jnp.int32, (8, size), 1) < half, low, -high)
     count = half // SIDE
     for r, out_ref in enumerate(outs):
-        out_ref[...] = jnp.zeros(out_ref.shape, jnp.float32)
-        out_ref[8 * count :, :] = ends
+        out_ref[:, base : base + 8, :] = jnp.zeros((count, 8, size), jnp.float32)
+        out_ref[:, base + 8 : base + 16, :] = jnp.broadcast_to(ends[None], (count, 8, size))
         for sign in range(2):
             at = sign * half + r * count
-            out_ref[pl.ds(2 * r + sign, count, stride=8), :] = rows[at : at + count]
+            out_ref[:, base + 2 * r + sign, :] = rows[at : at + count]
 
 
 def sublane_total(a):
@@ -394,8 +397,8 @@
     found = row // 2
     back = (found % SIDE, (found // SIDE) % SIDE, found // SIDE**2)
     sources = []
-    for owner in range(CORES):
-        x, y, z = moved(place_ref, back, owner, -1)
+    for owner, order in enumerate(LATE_ORDERS):
+        x, y, z = moved(place_ref, back, order, -1)
         sources.append(SIDE * (z * (SIDE * CORES) + y * CORES + owner) + x)
     from_own = jnp.where(second, sources[1], sources[0])
     from_other = jnp.where(second, sources[0], sources[1])
@@ -577,7 +580,7 @@
 def body(intensities, gridding, dest_slab, spectral_weights):
     ngrid = lax.axis_size("grid")
     ndp = lax.axis_size("dp")
-    nent, rows, size = intensities.shape
+    nent, _, size = intensities.shape
     planes = gridding.shape[2] // size
     count = ngrid * ndp
     capacity = max(2, 2 * nent // ngrid)
@@ -593,32 +596,28 @@
         step == 0, x, jnp.where(step == 1, y, jnp.where(step == 2, z, jnp.where(step == 3, core, chip == 0)))
     ).astype(jnp.int32)
 
-    together = lax.optimization_barrier
-    *away, wave, counts, lists, p0, p1, p2, p3 = grid_call(
+    away, wave, counts, lists, *pieces = grid_call(
         False, 0, ngrid, capacity, dest_slab[:, 0], place, intensities, gridding, table["packed"], spectral_weights
     )
     members = (counts, lists, place, wave, gridding)
-    arrived = [swap(a) for a in away]
-    weights = exchange([p0, p1, p2, p3], (0, 0))
-    axes = [[order[stage] for order in ORDERS] for stage in range(3)]
+    arrived = swap(away)
+    weights = exchange(pieces, (0, 0))
+    axes = [[[order[stage] for order in orders] for stage in range(3)] for orders in (ORDERS, LATE_ORDERS)]
     quarter = lambda a: [p.reshape(p.shape[1:]) for p in jnp.split(a.reshape((SIDE, -1) + a.shape[1:]), SIDE)]
     least = lambda parts: functools.reduce(jnp.minimum, parts)
     data = []
-    for part in range(HALVES):
-        kept = grid_call(True, part, ngrid, capacity, *members, arrived[part])
-        data.append(exchange(kept, axes[0]))
-    kept, weights = together((kept, weights))
-    rows = call(weight_kernel, [(SIDE**2 * 8 + 8, size)] * SIDE, *weights, place)
-    rows = exchange(rows, axes[0])
+    for part in range(2):
+        kept = grid_call(True, part, ngrid, capacity, *members, arrived, *(weights if part else ()))
+        data.append(exchange(kept, axes[part][0]))
     parts = quarter(summed(data[0]))
-    early = exchange(parts, axes[1])
-    held = summed([a[: SIDE**2 * 8] for a in rows]).reshape(SIDE**2, 8, size)
-    ends = jnp.broadcast_to(least([a[SIDE**2 * 8 :] for a in rows])[None], (SIDE**2, 8, size))
-    parts = exchange(quarter(jnp.concatenate([summed(data[1]), held, ends], 1)), axes[1])
-    late = size // HALVES
+    early = exchange(parts, axes[0][1])
+    late = SHARES[1] * size // STEPS
+    parts = [summed([a[:, :-8] for a in data[1]]), least([a[:, -8:] for a in data[1]])]
+    parts = quarter(jnp.concatenate(parts, 1))
+    parts = exchange(parts, axes[1][1])
     for stage in (1, 2):
         if stage == 2:
-            parts = exchange(quarter(parts), axes[2])
+            parts = exchange(quarter(parts), axes[0][2])
             late = size
         found = [
             summed([a[:, :late] for a in parts]),

time: 134 us -> 132 us (0.985)
  starting transfers between devices: 35.3 us -> 31.1 us
  blocking collectives: 34.1 us -> 37.2 us
  waiting for transfers between devices: 27.6 us -> 29.1 us
  local copies, waits for them, and re-layouts: 2.75 us -> 1.39 us
    ppermute x21 -> x18, starting transfers between devices: 30.3 us -> 25.8 us  [exchange(): lax.ppermute(parts[r], ALL, shift_pairs(axes, r))]
    all_to_all x1, blocking collectives: 15.2 us -> 18 us  [body(): lax.all_to_all(send.reshape(count, 1, size), ALL, 0, 0, tiled=True)]
    pallas_call x4 -> x3, Pallas kernels: 14.1 us -> 12 us  [call(): pl.pallas_call(kernel, out_shape=[jax.ShapeDtypeStruct(s, jnp.float32) fo...]
    ppermute x21 -> x18, waiting for transfers between devices: 26.6 us -> 28.1 us  [exchange(): lax.ppermute(parts[r], ALL, shift_pairs(axes, r))]
    unnamed x24 -> x19, local copies, waits for them, and re-layouts: 2.68 us -> 1.31 us
    ppermute x3 -> x2, starting transfers between devices: 5.08 us -> 5.29 us  [body(): swap = lambda a: lax.ppermute(a, ALL, shift_pairs((3, 3), 1))]
  transfers between devices with their start and end apart: 24 -> 20, of which waited for: 9 -> 9; matrix products, arithmetic and copies ran while one was open for 1% -> 0% of each run, Pallas kernels for 8% -> 5%
where the time goes in v5:
time: 132 us
  blocking collectives  37.2 us (28%)
  starting transfers between devices  31.1 us (24%)
  Pallas kernels  30.2 us (23%)
  waiting for transfers between devices  29.1 us (22%)
  other arithmetic  2.16 us (2%)
  local copies, waits for them, and re-layouts  1.39 us (1%)
    ppermute x18, waiting for transfers between devices, exchange(): lax.ppermute(parts[r], ALL, shift_pairs(axes, r))  28.1 us
    ppermute x18, starting transfers between devices, exchange(): lax.ppermute(parts[r], ALL, shift_pairs(axes, r))  25.8 us
    all_to_all x1, blocking collectives, body(): lax.all_to_all(back.reshape(count, 2 * planes, size), ALL, 0, 0, tiled=True)  19.2 us
    pallas_call x3, Pallas kernels, grid_call(): pl.pallas_call(functools.partial(grid_kernel, kept=kept, part=part, capac...  18.1 us
    all_to_all x1, blocking collectives, body(): lax.all_to_all(send.reshape(count, 1, size), ALL, 0, 0, tiled=True)  18 us
    pallas_call x3, Pallas kernels, call(): pl.pallas_call(kernel, out_shape=[jax.ShapeDtypeStruct(s, jnp.float32) fo...  12 us
    ppermute x2, starting transfers between devices, body(): swap = lambda a: lax.ppermute(a, ALL, shift_pairs((3, 3), 1))  5.29 us
  transfers between devices with their start and end apart: 20, of which 9 were waited for; matrix products, arithmetic and copies ran while one was open for 0% of the time, Pallas kernels for 5%

profile of v5, /device:TPU:1, one launch (start us, length us, event | category | flops | bytes accessed | tf_op | source)
XLA Modules:
  0.0 132.0 jit_solution(10139842905153937709)
XLA Ops:
  1.2 8.1 %shard_map.122 = (f32[64,128,128]{2,1,0:T(8,128)}, bf16[64,32,128]{2,1,0:T(8,128)(2,1)}, s32[32]{0:T(128)}, s32[128]{0:T(128)}, f32[128,128]{1,0:T(8,128)}, /*in...) custom-call(s32[64]{0:T(128)} %bitcast.14, s32[5]{0:T(128)} %compare_select_fusion.3.refs_1_.refs_2_.place_ref, ...), custom_call_target="tpu_custom_call" | custom-call | tf_op jit(solution)/shard_map/pallas_call | solution.py:323
  9.3 1.5 %collective-permute-start = (f32[64,128,128]{2,1,0:T(8,128)}, f32[64,128,128]{2,1,0:T(8,128)}, u32[]{:S(2)}, u32[]{:S(2)}) collective-permute-start(f32[64,128,128]{2,1,0:T(8,128)} %get-tuple-element.28), channel_id=1, source_target_pairs={{0,1},{1,0},{2,3},{3,2},{4,5},{5,4},{6,7},{7,6},{8,9},{9,8},{10,11... | collective-permute-start | bytes 12582920 | tf_op jit(solution)/shard_map/ppermute | solution.py:589
  10.8 1.3 collective-permute-start.7
  12.1 2.5 %collective-permute-start.8 = (f32[128,128]{1,0:T(8,128)}, f32[128,128]{1,0:T(8,128)S(1)}, u32[]{:S(2)}, u32[]{:S(2)}) collective-permute-start(f32[128,128]{1,0:T(8,128)} %get-tuple-element.35), channel_id=1, source_target_pairs={{0,64},{1,65},{2,66},{3,67},{4,68},{5,69},{6,70},{7,71},{8,72},{9,... | collective-permute-start | bytes 196616 | tf_op jit(solution)/shard_map/ppermute | solution.py:573
  15.8 2.5 %collective-permute-done.8.refs_8_ = f32[128,128]{1,0:T(8,128)S(1)} collective-permute-done((f32[128,128]{1,0:T(8,128)}, f32[128,128]{1,0:T(8,128)S(1)}, u32[]{:S(2)}, u32[]{:S(2)}) %collective-permute-start.8) | collective-permute-done | bytes 65568 | tf_op jit(solution)/shard_map/ppermute | solution.py:573
  18.9 4.0 %shard_map.124 = (f32[16,48,128]{2,1,0:T(8,128)}, f32[16,48,128]{2,1,0:T(8,128)}, f32[16,48,128]{2,1,0:T(8,128)}, f32[16,48,128]{2,1,0:T(8,128)}) custom-call(s32[32]{0:T(128)} %get-tuple-element.25.refs_0_, s32[128]{0:T(128)} %get-tuple-element.26.refs_1_, s32[5]{0:T(128)} %compare_select_fusion.3.refs_1_.refs_2_.place_ref, ...), custom_call_target="tpu_custom_call" | custom-call | tf_op jit(solution)/shard_map/pallas_call | solution.py:323
  23.0 1.7 %collective-permute-start.10 = (f32[16,48,128]{2,1,0:T(8,128)}, f32[16,48,128]{2,1,0:T(8,128)S(1)}, u32[]{:S(2)}, u32[]{:S(2)}) collective-permute-start(f32[16,48,128]{2,1,0:T(8,128)} %get-tuple-element.38), channel_id=1, source_target_pairs={{0,8},{1,9},{2,10},{3,11},{4,12},{5,13},{6,14},{7,15},{8,16},{9,17... | collective-permute-start | bytes 1179656 | tf_op jit(solution)/shard_map/ppermute | solution.py:573
  24.6 6.0 %shard_map.123 = (f32[16,96,128]{2,1,0:T(8,128)}, f32[16,96,128]{2,1,0:T(8,128)}, f32[16,96,128]{2,1,0:T(8,128)}, f32[16,96,128]{2,1,0:T(8,128)}) custom-call(s32[32]{0:T(128)} %get-tuple-element.25.refs_0_, s32[128]{0:T(128)} %get-tuple-element.26.refs_1_, s32[5]{0:T(128)} %compare_select_fusion.3.refs_1_.refs_2_.place_ref, ...), custom_call_target="tpu_custom_call" | custom-call | tf_op jit(solution)/shard_map/pallas_call | solution.py:323
  32.0 2.6 %collective-permute-start.2 = (f32[16,96,128]{2,1,0:T(8,128)}, f32[16,96,128]{2,1,0:T(8,128)S(1)}, u32[]{:S(2)}, u32[]{:S(2)}) collective-permute-start(f32[16,96,128]{2,1,0:T(8,128)} %get-tuple-element.31), channel_id=1, source_target_pairs={{0,64},{1,5},{2,66},{3,7},{4,68},{5,1},{6,70},{7,3},{8,72},{9,13},... | collective-permute-start | bytes 2359304 | tf_op jit(solution)/shard_map/ppermute | solution.py:573
  35.7 3.3 %collective-permute-start.11 = (f32[16,48,128]{2,1,0:T(8,128)S(1)}, f32[16,48,128]{2,1,0:T(8,128)S(1)}, u32[]{:S(2)}, u32[]{:S(2)}) collective-permute-start(f32[16,48,128]{2,1,0:T(8,128)S(1)} %copy-done.7), channel_id=1, source_target_pairs={{0,16},{1,17},{2,18},{3,19},{4,20},{5,21},{6,22},{7,23},{8,24},{9,... | collective-permute-start | bytes 1179656 | tf_op jit(solution)/shard_map/ppermute | solution.py:573
  39.7 7.3 %collective-permute-done.11 = f32[16,48,128]{2,1,0:T(8,128)S(1)} collective-permute-done((f32[16,48,128]{2,1,0:T(8,128)S(1)}, f32[16,48,128]{2,1,0:T(8,128)S(1)}, u32[]{:S(2)}, u32[]{:S(2)}) %collective-permute-start.11) | collective-permute-done | bytes 393248 | tf_op jit(solution)/shard_map/ppermute | solution.py:573
  47.0 8.4 %collective-permute-done.12 = f32[16,48,128]{2,1,0:T(8,128)S(1)} collective-permute-done((f32[16,48,128]{2,1,0:T(8,128)S(1)}, f32[16,48,128]{2,1,0:T(8,128)S(1)}, u32[]{:S(2)}, u32[]{:S(2)}) %collective-permute-start.12) | collective-permute-done | bytes 393248 | tf_op jit(solution)/shard_map/ppermute | solution.py:573
  55.6 1.4 %add_add_fusion = f32[16,96,128]{2,1,0:T(8,128)S(1)} fusion(f32[16,96,128]{2,1,0:T(8,128)S(1)} %collective-permute-done.3, f32[16,96,128]{2,1,0:T(8,128)S(1)} %collective-permute-done.2, f32[16,96,128]{2,1,0:T(8,128)} %get-tuple-element.29, f32[16,96,128]{2,1,0:T(8,128)S(1)} %collective-permute-done.1), kind=kLoop, calls=%fused_computation | loop fusion | flops 589824 | bytes 3932160 | tf_op jit(solution)/shard_map/add | solution.py:577
  57.0 2.2 %collective-permute-start.4 = (f32[4,96,128]{2,1,0:T(8,128)S(1)}, f32[4,96,128]{2,1,0:T(8,128)S(1)}, u32[]{:S(2)}, u32[]{:S(2)}) collective-permute-start(f32[4,96,128]{2,1,0:T(8,128)S(1)} %get-tuple-element.54), channel_id=1, source_target_pairs={{0,8},{1,9},{2,10},{3,11},{4,12},{5,13},{6,14},{7,15},{8,16},{9,17... | collective-permute-start | bytes 589832 | tf_op jit(solution)/shard_map/ppermute | solution.py:573
  59.2 2.5 %collective-permute-start.5 = (f32[4,96,128]{2,1,0:T(8,128)S(1)}, f32[4,96,128]{2,1,0:T(8,128)S(1)}, u32[]{:S(2)}, u32[]{:S(2)}) collective-permute-start(f32[4,96,128]{2,1,0:T(8,128)S(1)} %get-tuple-element.56), channel_id=1, source_target_pairs={{0,16},{1,17},{2,18},{3,19},{4,20},{5,21},{6,22},{7,23},{8,24},{9,... | collective-permute-start | bytes 589832 | tf_op jit(solution)/shard_map/ppermute | solution.py:573
  63.0 1.7 %collective-permute-done.4 = f32[4,96,128]{2,1,0:T(8,128)S(1)} collective-permute-done((f32[4,96,128]{2,1,0:T(8,128)S(1)}, f32[4,96,128]{2,1,0:T(8,128)S(1)}, u32[]{:S(2)}, u32[]{:S(2)}) %collective-permute-start.4) | collective-permute-done | bytes 196640 | tf_op jit(solution)/shard_map/ppermute | solution.py:573
  64.7 5.7 %collective-permute-done.5 = f32[4,96,128]{2,1,0:T(8,128)S(1)} collective-permute-done((f32[4,96,128]{2,1,0:T(8,128)S(1)}, f32[4,96,128]{2,1,0:T(8,128)S(1)}, u32[]{:S(2)}, u32[]{:S(2)}) %collective-permute-start.5) | collective-permute-done | bytes 196640 | tf_op jit(solution)/shard_map/ppermute | solution.py:573
  71.0 2.6 %collective-permute-start.17 = (f32[1,168,128]{2,1,0:T(8,128)S(1)}, f32[1,168,128]{2,1,0:T(8,128)S(1)}, u32[]{:S(2)}, u32[]{:S(2)}) collective-permute-start(f32[1,168,128]{2,1,0:T(8,128)S(1)} %get-tuple-element.62), channel_id=1, source_target_pairs={{0,4},{1,65},{2,6},{3,67},{4,0},{5,69},{6,2},{7,71},{8,12},{9,73},... | collective-permute-start | bytes 258056 | tf_op jit(solution)/shard_map/ppermute | solution.py:573
  77.3 3.8 %collective-permute-start.19 = (f32[264,128]{1,0:T(8,128)S(1)}, f32[264,128]{1,0:T(8,128)S(1)}, u32[]{:S(2)}, u32[]{:S(2)}) collective-permute-start(f32[264,128]{1,0:T(8,128)S(1)} %bitcast.10), channel_id=1, source_target_pairs={{0,1},{1,0},{2,3},{3,2},{4,5},{5,4},{6,7},{7,6},{8,9},{9,8},{10,11... | collective-permute-start | bytes 405512 | tf_op jit(solution)/shard_map/ppermute | solution.py:589
  82.8 4.5 %shard_map.125 = (f32[128,128]{1,0:T(8,128)}, f32[128,128]{1,0:T(8,128)}, f32[128,128]{1,0:T(8,128)}, f32[8,128]{1,0:T(8,128)}, f32[128,128]{1,0:T(8,128)}) custom-call(f32[264,128]{1,0:T(8,128)} %bitcast.11, f32[264,128]{1,0:T(8,128)} %copy-done.2, s32[5]{0:T(128)} %compare_select_fusion.3.refs_1_.refs_2_.place_ref, f32[128,256]{1,0:T(8,128)} %constant.93.clone.lanes_ref, ...), custom_call_target="tpu_custom_call" | custom-call | tf_op jit(solution)/shard_map/pallas_call | solution.py:564
  87.3 18.0 %all_to_all.10 = f32[128,1,128]{2,1,0:T(1,128)} all-to-all(f32[128,1,128]{2,1,0:T(1,128)} %bitcast.13), channel_id=1, replica_groups=mesh['dp'=4,'grid'=32] {'dp','grid'}, dimensions={0} | all-to-all | bytes 131072 | tf_op jit(solution)/shard_map/all_to_all | solution.py:635
  105.3 5.2 %shard_map.126 = (f32[1024,128]{1,0:T(8,128)}, f32[8,128]{1,0:T(8,128)}) custom-call(f32[128,128]{1,0:T(8,128)} %bitcast.12, f32[8,128]{1,0:T(8,128)} %get-tuple-element.42.range_ref, f32[128,128]{1,0:T(8,128)} %get-tuple-element.43.scaled_ref, f32[128,128]{1,0:T(8,128)} %get-tuple-element.44.real_ref, f32[128,128]{1,0:T(8,128)} %get-tuple-element.45.imag_ref, ...), custom_call_target="tpu_custom_call" | custom-call | tf_op jit(solution)/shard_map/pallas_call | solution.py:564
  110.5 19.2 %all_to_all.11 = f32[128,8,128]{2,1,0:T(8,128)} all-to-all(f32[128,8,128]{2,1,0:T(8,128)} %bitcast.9), channel_id=1, replica_groups=mesh['dp'=4,'grid'=32] {'dp','grid'}, dimensions={0} | all-to-all | bytes 1048576 | tf_op jit(solution)/shard_map/all_to_all | solution.py:640
  129.6 2.4 %shard_map.127 = (f32[4,128,128]{2,1,0:T(8,128)}, f32[4,128,128]{2,1,0:T(8,128)}) custom-call(f32[1024,128]{1,0:T(8,128)} %bitcast.8, f32[8,128]{1,0:T(8,128)} %get-tuple-element.47.gain_ref, bf16[768,256]{1,0:T(8,128)(2,1)} %constant.98.clone.back_ref), custom_call_target="tpu_custom_call" | custom-call | tf_op jit(solution)/shard_map/pallas_call | solution.py:564
  (60 shorter events, 12.8 us)
Async XLA Ops:
  9.3 9.0 %collective-permute-start = (f32[64,128,128]{2,1,0:T(8,128)}, f32[64,128,128]{2,1,0:T(8,128)}, u32[]{:S(2)}, u32[]{:S(2)}) collective-permute-start(f32[64,128,128]{2,1,0:T(8,128)} %get-tuple-element.28), channel_id=1, source_target_pairs={{0,1},{1,0},{2,3},{3,2},{4,5},{5,4},{6,7},{7,6},{8,9},{9,8},{10,11... | collective-permute-start | bytes 12582920 | tf_op jit(solution)/shard_map/ppermute | solution.py:589
  10.8 5.0 %collective-permute-start.7 = (f32[128,128]{1,0:T(8,128)}, f32[128,128]{1,0:T(8,128)S(1)}, u32[]{:S(2)}, u32[]{:S(2)}) collective-permute-start(f32[128,128]{1,0:T(8,128)} %get-tuple-element.34), channel_id=1, source_target_pairs={{0,32},{1,33},{2,34},{3,35},{4,36},{5,37},{6,38},{7,39},{8,40},{9,... | collective-permute-start | bytes 196616 | tf_op jit(solution)/shard_map/ppermute | solution.py:573
  12.1 6.2 %collective-permute-start.8 = (f32[128,128]{1,0:T(8,128)}, f32[128,128]{1,0:T(8,128)S(1)}, u32[]{:S(2)}, u32[]{:S(2)}) collective-permute-start(f32[128,128]{1,0:T(8,128)} %get-tuple-element.35), channel_id=1, source_target_pairs={{0,64},{1,65},{2,66},{3,67},{4,68},{5,69},{6,70},{7,71},{8,72},{9,... | collective-permute-start | bytes 196616 | tf_op jit(solution)/shard_map/ppermute | solution.py:573
  14.6 3.7 %collective-permute-start.9 = (f32[128,128]{1,0:T(8,128)}, f32[128,128]{1,0:T(8,128)S(1)}, u32[]{:S(2)}, u32[]{:S(2)}) collective-permute-start(f32[128,128]{1,0:T(8,128)} %get-tuple-element.36), channel_id=1, source_target_pairs={{0,96},{1,97},{2,98},{3,99},{4,100},{5,101},{6,102},{7,103},{8,104... | collective-permute-start | bytes 196616 | tf_op jit(solution)/shard_map/ppermute | solution.py:573
  22.9 12.7 %copy-start.7 = (f32[16,48,128]{2,1,0:T(8,128)S(1)}, f32[16,48,128]{2,1,0:T(8,128)}, u32[]{:S(2)}) copy-start(f32[16,48,128]{2,1,0:T(8,128)} %get-tuple-element.39) | copy-start | bytes 1179652
  22.9 16.1 %copy-start.6 = (f32[16,48,128]{2,1,0:T(8,128)S(1)}, f32[16,48,128]{2,1,0:T(8,128)}, u32[]{:S(2)}) copy-start(f32[16,48,128]{2,1,0:T(8,128)} %get-tuple-element.40) | copy-start | bytes 1179652
  22.9 32.5 %copy-start = (f32[16,48,128]{2,1,0:T(8,128)S(1)}, f32[16,48,128]{2,1,0:T(8,128)}, u32[]{:S(2)}) copy-start(f32[16,48,128]{2,1,0:T(8,128)} %get-tuple-element.37) | copy-start | bytes 1179652
  23.0 16.0 %collective-permute-start.10 = (f32[16,48,128]{2,1,0:T(8,128)}, f32[16,48,128]{2,1,0:T(8,128)S(1)}, u32[]{:S(2)}, u32[]{:S(2)}) collective-permute-start(f32[16,48,128]{2,1,0:T(8,128)} %get-tuple-element.38), channel_id=1, source_target_pairs={{0,8},{1,9},{2,10},{3,11},{4,12},{5,13},{6,14},{7,15},{8,16},{9,17... | collective-permute-start | bytes 1179656 | tf_op jit(solution)/shard_map/ppermute | solution.py:573
  30.7 24.9 %collective-permute-start.1 = (f32[16,96,128]{2,1,0:T(8,128)}, f32[16,96,128]{2,1,0:T(8,128)S(1)}, u32[]{:S(2)}, u32[]{:S(2)}) collective-permute-start(f32[16,96,128]{2,1,0:T(8,128)} %get-tuple-element.30), channel_id=1, source_target_pairs={{0,32},{1,3},{2,34},{3,5},{4,36},{5,7},{6,38},{7,1},{8,40},{9,11},... | collective-permute-start | bytes 2359304 | tf_op jit(solution)/shard_map/ppermute | solution.py:573
  32.0 23.6 %collective-permute-start.2 = (f32[16,96,128]{2,1,0:T(8,128)}, f32[16,96,128]{2,1,0:T(8,128)S(1)}, u32[]{:S(2)}, u32[]{:S(2)}) collective-permute-start(f32[16,96,128]{2,1,0:T(8,128)} %get-tuple-element.31), channel_id=1, source_target_pairs={{0,64},{1,5},{2,66},{3,7},{4,68},{5,1},{6,70},{7,3},{8,72},{9,13},... | collective-permute-start | bytes 2359304 | tf_op jit(solution)/shard_map/ppermute | solution.py:573
  34.6 21.0 %collective-permute-start.3 = (f32[16,96,128]{2,1,0:T(8,128)}, f32[16,96,128]{2,1,0:T(8,128)S(1)}, u32[]{:S(2)}, u32[]{:S(2)}) collective-permute-start(f32[16,96,128]{2,1,0:T(8,128)} %get-tuple-element.32), channel_id=1, source_target_pairs={{0,96},{1,7},{2,98},{3,1},{4,100},{5,3},{6,102},{7,5},{8,104},{9,1... | collective-permute-start | bytes 2359304 | tf_op jit(solution)/shard_map/ppermute | solution.py:573
  35.7 11.4 %collective-permute-start.11 = (f32[16,48,128]{2,1,0:T(8,128)S(1)}, f32[16,48,128]{2,1,0:T(8,128)S(1)}, u32[]{:S(2)}, u32[]{:S(2)}) collective-permute-start(f32[16,48,128]{2,1,0:T(8,128)S(1)} %copy-done.7), channel_id=1, source_target_pairs={{0,16},{1,17},{2,18},{3,19},{4,20},{5,21},{6,22},{7,23},{8,24},{9,... | collective-permute-start | bytes 1179656 | tf_op jit(solution)/shard_map/ppermute | solution.py:573
  39.0 16.4 %collective-permute-start.12 = (f32[16,48,128]{2,1,0:T(8,128)S(1)}, f32[16,48,128]{2,1,0:T(8,128)S(1)}, u32[]{:S(2)}, u32[]{:S(2)}) collective-permute-start(f32[16,48,128]{2,1,0:T(8,128)S(1)} %copy-done.6), channel_id=1, source_target_pairs={{0,24},{1,25},{2,26},{3,27},{4,28},{5,29},{6,30},{7,31},{8,0},{9,1... | collective-permute-start | bytes 1179656 | tf_op jit(solution)/shard_map/ppermute | solution.py:573
  57.0 7.7 %collective-permute-start.4 = (f32[4,96,128]{2,1,0:T(8,128)S(1)}, f32[4,96,128]{2,1,0:T(8,128)S(1)}, u32[]{:S(2)}, u32[]{:S(2)}) collective-permute-start(f32[4,96,128]{2,1,0:T(8,128)S(1)} %get-tuple-element.54), channel_id=1, source_target_pairs={{0,8},{1,9},{2,10},{3,11},{4,12},{5,13},{6,14},{7,15},{8,16},{9,17... | collective-permute-start | bytes 589832 | tf_op jit(solution)/shard_map/ppermute | solution.py:573
  59.2 11.2 %collective-permute-start.5 = (f32[4,96,128]{2,1,0:T(8,128)S(1)}, f32[4,96,128]{2,1,0:T(8,128)S(1)}, u32[]{:S(2)}, u32[]{:S(2)}) collective-permute-start(f32[4,96,128]{2,1,0:T(8,128)S(1)} %get-tuple-element.56), channel_id=1, source_target_pairs={{0,16},{1,17},{2,18},{3,19},{4,20},{5,21},{6,22},{7,23},{8,24},{9,... | collective-permute-start | bytes 589832 | tf_op jit(solution)/shard_map/ppermute | solution.py:573
  61.7 8.7 %collective-permute-start.6 = (f32[4,96,128]{2,1,0:T(8,128)S(1)}, f32[4,96,128]{2,1,0:T(8,128)S(1)}, u32[]{:S(2)}, u32[]{:S(2)}) collective-permute-start(f32[4,96,128]{2,1,0:T(8,128)S(1)} %get-tuple-element.55), channel_id=1, source_target_pairs={{0,24},{1,25},{2,26},{3,27},{4,28},{5,29},{6,30},{7,31},{8,0},{9,1... | collective-permute-start | bytes 589832 | tf_op jit(solution)/shard_map/ppermute | solution.py:573
  61.7 8.7 %collective-permute-start.13 = (f32[4,48,128]{2,1,0:T(8,128)S(1)}, f32[4,48,128]{2,1,0:T(8,128)S(1)}, u32[]{:S(2)}, u32[]{:S(2)}) collective-permute-start(f32[4,48,128]{2,1,0:T(8,128)S(1)} %get-tuple-element.57), channel_id=1, source_target_pairs={{0,32},{1,3},{2,34},{3,5},{4,36},{5,7},{6,38},{7,1},{8,40},{9,11},... | collective-permute-start | bytes 294920 | tf_op jit(solution)/shard_map/ppermute | solution.py:573
  62.2 8.2 %collective-permute-start.14 = (f32[4,48,128]{2,1,0:T(8,128)S(1)}, f32[4,48,128]{2,1,0:T(8,128)S(1)}, u32[]{:S(2)}, u32[]{:S(2)}) collective-permute-start(f32[4,48,128]{2,1,0:T(8,128)S(1)} %get-tuple-element.58), channel_id=1, source_target_pairs={{0,64},{1,5},{2,66},{3,7},{4,68},{5,1},{6,70},{7,3},{8,72},{9,13},... | collective-permute-start | bytes 294920 | tf_op jit(solution)/shard_map/ppermute | solution.py:573
  64.7 5.8 %collective-permute-start.15 = (f32[4,48,128]{2,1,0:T(8,128)S(1)}, f32[4,48,128]{2,1,0:T(8,128)S(1)}, u32[]{:S(2)}, u32[]{:S(2)}) collective-permute-start(f32[4,48,128]{2,1,0:T(8,128)S(1)} %get-tuple-element.59), channel_id=1, source_target_pairs={{0,96},{1,7},{2,98},{3,1},{4,100},{5,3},{6,102},{7,5},{8,104},{9,1... | collective-permute-start | bytes 294920 | tf_op jit(solution)/shard_map/ppermute | solution.py:573
  70.6 4.6 %collective-permute-start.16 = (f32[1,168,128]{2,1,0:T(8,128)S(1)}, f32[1,168,128]{2,1,0:T(8,128)S(1)}, u32[]{:S(2)}, u32[]{:S(2)}) collective-permute-start(f32[1,168,128]{2,1,0:T(8,128)S(1)} %get-tuple-element.60), channel_id=1, source_target_pairs={{0,2},{1,33},{2,4},{3,35},{4,6},{5,37},{6,0},{7,39},{8,10},{9,41},... | collective-permute-start | bytes 258056 | tf_op jit(solution)/shard_map/ppermute | solution.py:573
  71.0 5.4 %collective-permute-start.17 = (f32[1,168,128]{2,1,0:T(8,128)S(1)}, f32[1,168,128]{2,1,0:T(8,128)S(1)}, u32[]{:S(2)}, u32[]{:S(2)}) collective-permute-start(f32[1,168,128]{2,1,0:T(8,128)S(1)} %get-tuple-element.62), channel_id=1, source_target_pairs={{0,4},{1,65},{2,6},{3,67},{4,0},{5,69},{6,2},{7,71},{8,12},{9,73},... | collective-permute-start | bytes 258056 | tf_op jit(solution)/shard_map/ppermute | solution.py:573
  73.6 3.6 %collective-permute-start.18 = (f32[1,168,128]{2,1,0:T(8,128)S(1)}, f32[1,168,128]{2,1,0:T(8,128)S(1)}, u32[]{:S(2)}, u32[]{:S(2)}) collective-permute-start(f32[1,168,128]{2,1,0:T(8,128)S(1)} %get-tuple-element.61), channel_id=1, source_target_pairs={{0,6},{1,97},{2,0},{3,99},{4,2},{5,101},{6,4},{7,103},{8,14},{9,10... | collective-permute-start | bytes 258056 | tf_op jit(solution)/shard_map/ppermute | solution.py:573
  77.3 4.8 %copy-start.1 = (f32[1,264,128]{2,1,0:T(8,128)}, f32[1,264,128]{2,1,0:T(8,128)S(1)}, u32[]{:S(2)}) copy-start(f32[1,264,128]{2,1,0:T(8,128)S(1)} %constant_dynamic-update-slice_fusion.7) | copy-start | bytes 405508
  77.3 4.8 %collective-permute-start.19 = (f32[264,128]{1,0:T(8,128)S(1)}, f32[264,128]{1,0:T(8,128)S(1)}, u32[]{:S(2)}, u32[]{:S(2)}) collective-permute-start(f32[264,128]{1,0:T(8,128)S(1)} %bitcast.10), channel_id=1, source_target_pairs={{0,1},{1,0},{2,3},{3,2},{4,5},{5,4},{6,7},{7,6},{8,9},{9,8},{10,11... | collective-permute-start | bytes 405512 | tf_op jit(solution)/shard_map/ppermute | solution.py:589
  (4 other events, 4.5 us)

commit v6 on v4

--- a/solution.py
+++ b/solution.py
@@ -172,8 +172,8 @@
     return (found[:height] + found[height : 2 * height]) + found[2 * height :]
 
 
-HALVES = 2
 STEPS = 4
+SHARES = (2, 2)
 
 
 def sublane_turn(tiles):
@@ -193,7 +193,7 @@
 def grid_kernel(*refs, kept, part, capacity):
     if kept:
         count_ref, list_ref, place_ref, wave_ref, matrix_ref, other_ref = refs[:6]
-        outs = refs[6:]
+        outs, weight_refs = refs[-SIDE:], refs[6:-SIDE]
     else:
         dest_ref, place_ref, values_ref, matrix_ref, packed_ref, weights_ref = refs[:6]
         out_refs, (kept_wave_ref, count_ref, list_ref), wave_ref = refs[6:8], refs[8:11], refs[-1]
@@ -223,7 +223,7 @@
         slot = lax.broadcasted_iota(jnp.int32, (half, half), 1)
         digits = digits_of(slot)
         pieces = []
-        chips = [chip_at(*moved(place_ref, digits, owner, 1)) for owner in range(CORES)]
+        chips = [chip_at(*moved(place_ref, digits, order, 1)) for order in ORDERS]
         for owner in (1 - place_ref[3], place_ref[3]):
             pick = (chip == jnp.where(owner == 0, chips[0], chips[1])).astype(jnp.float32).astype(jnp.bfloat16)
             for start in (0, half):
@@ -243,13 +243,13 @@
     if not kept:
         pl.when(step == 0)(prepare)
 
-    pairs = nslab // (2 * STEPS)
+    pairs = nslab // (2 * STEPS) // (1 + (part > 0))
 
     def products(out):
         for pair in range(pairs):
             halves_of_tile = []
             for near in range(2):
-                slab = ((part * (STEPS // HALVES) + step) * pairs + pair) * 2 + near
+                slab = sum(SHARES[:part]) * (nslab // STEPS) + (step * pairs + pair) * 2 + near
                 taken = count_ref[slab]
                 waves, matrices = [], []
                 for m in range(capacity):
@@ -283,11 +283,14 @@
 
         return write
 
-    if kept:
+    if not kept:
+        pl.when(step < SHARES[0])(lambda: products(send(out_refs[0])))
+        pl.when(step >= SHARES[0])(lambda: products(send(out_refs[1])))
+    elif part == 0:
         products(keep)
     else:
-        pl.when(step < STEPS // HALVES)(lambda: products(send(out_refs[0])))
-        pl.when(step >= STEPS // HALVES)(lambda: products(send(out_refs[1])))
+        pl.when(step < 2 * SHARES[1])(lambda: products(keep))
+        pl.when(step == 2 * SHARES[1])(lambda: write_rows(weight_refs, place_ref, outs))
 
 
 def grid_call(kept, part, nslab, capacity, *args):
@@ -296,25 +299,34 @@
     matrix = args[4] if kept else args[3]
     nent, rows, width = matrix.shape
     size, blocks = width // SIDE, SIDE**3
-    steps = STEPS // HALVES if kept else STEPS
+    steps = STEPS
+    if kept:
+        steps = SHARES[0] if part == 0 else 2 * SHARES[1] + 1
+    deep = [share * size // STEPS for share in SHARES]
     moving = lambda count: pl.BlockSpec((count, size // STEPS, size), lambda i: (0, i, 0))
     f32 = lambda *shape: jax.ShapeDtypeStruct(shape, jnp.float32)
     in_specs = [scalars if a.dtype == jnp.int32 else fixed(a.shape) for a in args]
     if kept:
-        out_shape, out_specs = [f32(SIDE**2, size // HALVES, size)] * SIDE, [moving(SIDE**2)] * SIDE
-        in_specs[-1] = moving(blocks)
+        if part == 0:
+            in_specs[5] = moving(blocks)
+            out_shape, out_specs = [f32(SIDE**2, deep[0], size)] * SIDE, [moving(SIDE**2)] * SIDE
+        else:
+            depth = size // (2 * STEPS)
+            in_specs[5] = pl.BlockSpec((blocks, depth, size), lambda i: (0, jnp.minimum(i, steps - 2), 0))
+            out_shape = [f32(SIDE**2, deep[1] + 16, size)] * SIDE
+            out_specs = [pl.BlockSpec((SIDE**2, depth, size), lambda i: (0, i, 0))] * SIDE
         scratch = []
     else:
         wave = (nent, rows, size)
-        out_shape = [f32(blocks, size // HALVES, size)] * HALVES + [
+        out_shape = [f32(blocks, depth, size) for depth in deep] + [
             jax.ShapeDtypeStruct(wave, jnp.bfloat16),
             jax.ShapeDtypeStruct((nslab,), jnp.int32),
             jax.ShapeDtypeStruct((nslab * capacity,), jnp.int32),
         ] + [f32(size, size)] * SIDE
         block = (blocks, size // STEPS, size)
         out_specs = [
-            pl.BlockSpec(block, lambda i: (0, jnp.minimum(i, STEPS // HALVES - 1), 0)),
-            pl.BlockSpec(block, lambda i: (0, jnp.maximum(i - STEPS // HALVES, 0), 0)),
+            pl.BlockSpec(block, lambda i: (0, jnp.minimum(i, SHARES[0] - 1), 0)),
+            pl.BlockSpec(block, lambda i: (0, jnp.maximum(i - SHARES[0], 0), 0)),
         ] + [fixed(wave), scalars, scalars] + [fixed((size, size))] * SIDE
         scratch = [pltpu.VMEM(wave, jnp.bfloat16)]
     return pl.pallas_call(
@@ -327,9 +339,9 @@
     )(*args)
 
 
-def moved(place_ref, digits, owner, sign):
+def moved(place_ref, digits, order, sign):
     at = [place_ref[0], place_ref[1], place_ref[2]]
-    for digit, axis in zip(digits, ORDERS[owner]):
+    for digit, axis in zip(digits, order):
         at[axis] = (at[axis] + sign * digit + SIDE) % SIDE
     return at
 
@@ -338,15 +350,15 @@
     return index // SIDE**2, (index // SIDE) % SIDE, index % SIDE
 
 
-def weight_kernel(w0_ref, w1_ref, w2_ref, w3_ref, place_ref, *outs):
-    size = w0_ref.shape[0]
+def write_rows(weight_refs, place_ref, outs):
+    size = weight_refs[0].shape[0]
     half = size // 2
-    own = ((w0_ref[...] + w1_ref[...]) + w2_ref[...]) + w3_ref[...]
+    own = summed([ref[...] for ref in weight_refs])
     low = jnp.min(jnp.min(own, axis=0, keepdims=True), axis=1, keepdims=True)
     high = jnp.max(jnp.max(own, axis=0, keepdims=True), axis=1, keepdims=True)
     row = lax.broadcasted_iota(jnp.int32, (size, size), 0)
     lane = lax.broadcasted_iota(jnp.int32, (size, size), 1)
-    chips = [chip_at(*moved(place_ref, digits_of(row % half), owner, 1)) for owner in range(CORES)]
+    chips = [chip_at(*moved(place_ref, digits_of(row % half), order, 1)) for order in ORDERS]
     chip = jnp.where(place_ref[3] == 0, chips[0], chips[1])
     negative = jnp.where(chip == 0, half, size - chip)
     pick = (lane == jnp.where(row < half, chip, negative)).astype(jnp.float32)
@@ -354,11 +366,11 @@
     ends = jnp.where(lax.broadcasted_iota(jnp.int32, (8, size), 1) < half, low, -high)
     count = half // SIDE
     for r, out_ref in enumerate(outs):
-        out_ref[...] = jnp.zeros(out_ref.shape, jnp.float32)
-        out_ref[8 * count :, :] = ends
+        out_ref[:, 0:8, :] = jnp.zeros((count, 8, size), jnp.float32)
+        out_ref[:, 8:16, :] = jnp.broadcast_to(ends[None], (count, 8, size))
         for sign in range(2):
             at = sign * half + r * count
-            out_ref[pl.ds(2 * r + sign, count, stride=8), :] = rows[at : at + count]
+            out_ref[:, 2 * r + sign, :] = rows[at : at + count]
 
 
 def sublane_total(a):
@@ -394,8 +406,8 @@
     found = row // 2
     back = (found % SIDE, (found // SIDE) % SIDE, found // SIDE**2)
     sources = []
-    for owner in range(CORES):
-        x, y, z = moved(place_ref, back, owner, -1)
+    for owner, order in enumerate(ORDERS):
+        x, y, z = moved(place_ref, back, order, -1)
         sources.append(SIDE * (z * (SIDE * CORES) + y * CORES + owner) + x)
     from_own = jnp.where(second, sources[1], sources[0])
     from_other = jnp.where(second, sources[0], sources[1])
@@ -577,7 +589,7 @@
 def body(intensities, gridding, dest_slab, spectral_weights):
     ngrid = lax.axis_size("grid")
     ndp = lax.axis_size("dp")
-    nent, rows, size = intensities.shape
+    nent, _, size = intensities.shape
     planes = gridding.shape[2] // size
     count = ngrid * ndp
     capacity = max(2, 2 * nent // ngrid)
@@ -593,7 +605,6 @@
         step == 0, x, jnp.where(step == 1, y, jnp.where(step == 2, z, jnp.where(step == 3, core, chip == 0)))
     ).astype(jnp.int32)
 
-    together = lax.optimization_barrier
     *away, wave, counts, lists, p0, p1, p2, p3 = grid_call(
         False, 0, ngrid, capacity, dest_slab[:, 0], place, intensities, gridding, table["packed"], spectral_weights
     )
@@ -604,18 +615,15 @@
     quarter = lambda a: [p.reshape(p.shape[1:]) for p in jnp.split(a.reshape((SIDE, -1) + a.shape[1:]), SIDE)]
     least = lambda parts: functools.reduce(jnp.minimum, parts)
     data = []
-    for part in range(HALVES):
-        kept = grid_call(True, part, ngrid, capacity, *members, arrived[part])
+    for part in range(2):
+        kept = grid_call(True, part, ngrid, capacity, *members, arrived[part], *(weights if part else ()))
         data.append(exchange(kept, axes[0]))
-    kept, weights = together((kept, weights))
-    rows = call(weight_kernel, [(SIDE**2 * 8 + 8, size)] * SIDE, *weights, place)
-    rows = exchange(rows, axes[0])
     parts = quarter(summed(data[0]))
     early = exchange(parts, axes[1])
-    held = summed([a[: SIDE**2 * 8] for a in rows]).reshape(SIDE**2, 8, size)
-    ends = jnp.broadcast_to(least([a[SIDE**2 * 8 :] for a in rows])[None], (SIDE**2, 8, size))
-    parts = exchange(quarter(jnp.concatenate([summed(data[1]), held, ends], 1)), axes[1])
-    late = size // HALVES
+    late = SHARES[1] * size // STEPS
+    parts = [summed([a[:, :-8] for a in data[1]]), least([a[:, -8:] for a in data[1]])]
+    parts = quarter(jnp.concatenate(parts, 1))
+    parts = exchange(parts, axes[1])
     for stage in (1, 2):
         if stage == 2:
             parts = exchange(quarter(parts), axes[2])

time: 134 us -> 146 us (1.090)
  waiting for transfers between devices: 27.6 us -> 35.8 us
  starting transfers between devices: 35.3 us -> 38.7 us
    ppermute x3, starting transfers between devices: 5.08 us -> 12.7 us  [body(): swap = lambda a: lax.ppermute(a, ALL, shift_pairs((3, 3), 1))]
    ppermute x21 -> x18, starting transfers between devices: 30.3 us -> 26 us  [exchange(): lax.ppermute(parts[r], ALL, shift_pairs(axes, r))]
    ppermute x21 -> x18, waiting for transfers between devices: 26.6 us -> 30.7 us  [exchange(): lax.ppermute(parts[r], ALL, shift_pairs(axes, r))]
    ppermute x3, waiting for transfers between devices: 1 us -> 5.03 us  [body(): swap = lambda a: lax.ppermute(a, ALL, shift_pairs((3, 3), 1))]
    pallas_call x4 -> x3, Pallas kernels: 14.1 us -> 12.1 us  [call(): pl.pallas_call(kernel, out_shape=[jax.ShapeDtypeStruct(s, jnp.float32) fo...]
    pallas_call x3, Pallas kernels: 17.1 us -> 19 us  [grid_call(): pl.pallas_call(functools.partial(grid_kernel, kept=kept, part=part, capac...]
  transfers between devices with their start and end apart: 24 -> 21, of which waited for: 9 -> 11; matrix products, arithmetic and copies ran while one was open for 1% -> 1% of each run, Pallas kernels for 8% -> 7%
where the time goes in v6:
time: 146 us
  starting transfers between devices  38.7 us (27%)
  waiting for transfers between devices  35.8 us (25%)
  blocking collectives  35.3 us (24%)
  Pallas kernels  31.1 us (21%)
  local copies, waits for them, and re-layouts  2.14 us (1%)
  other arithmetic  2.12 us (1%)
    ppermute x18, waiting for transfers between devices, exchange(): lax.ppermute(parts[r], ALL, shift_pairs(axes, r))  30.7 us
    ppermute x18, starting transfers between devices, exchange(): lax.ppermute(parts[r], ALL, shift_pairs(axes, r))  26 us
    pallas_call x3, Pallas kernels, grid_call(): pl.pallas_call(functools.partial(grid_kernel, kept=kept, part=part, capac...  19 us
    all_to_all x1, blocking collectives, body(): lax.all_to_all(back.reshape(count, 2 * planes, size), ALL, 0, 0, tiled=True)  18.9 us
    all_to_all x1, blocking collectives, body(): lax.all_to_all(send.reshape(count, 1, size), ALL, 0, 0, tiled=True)  16.3 us
    ppermute x3, starting transfers between devices, body(): swap = lambda a: lax.ppermute(a, ALL, shift_pairs((3, 3), 1))  12.7 us
    pallas_call x3, Pallas kernels, call(): pl.pallas_call(kernel, out_shape=[jax.ShapeDtypeStruct(s, jnp.float32) fo...  12.1 us
    ppermute x3, waiting for transfers between devices, body(): swap = lambda a: lax.ppermute(a, ALL, shift_pairs((3, 3), 1))  5.03 us
  transfers between devices with their start and end apart: 21, of which 11 were waited for; matrix products, arithmetic and copies ran while one was open for 1% of the time, Pallas kernels for 7%

profile of v6, /device:TPU:1, one launch (start us, length us, event | category | flops | bytes accessed | tf_op | source)
XLA Modules:
  0.0 146.0 jit_solution(14028866184874603281)
XLA Ops:
  1.2 8.4 %shard_map.122 = (f32[64,64,128]{2,1,0:T(8,128)}, f32[64,64,128]{2,1,0:T(8,128)}, bf16[64,32,128]{2,1,0:T(8,128)(2,1)}, s32[32]{0:T(128)}, s32[128]{0:T(128)}, /...) custom-call(s32[64]{0:T(128)} %bitcast.14, ...), custom_call_target="tpu_custom_call" | custom-call | tf_op jit(solution)/shard_map/pallas_call | solution.py:332
  11.2 4.0 %collective-permute-done.refs_5_ = f32[64,64,128]{2,1,0:T(8,128)} collective-permute-done((f32[64,64,128]{2,1,0:T(8,128)}, f32[64,64,128]{2,1,0:T(8,128)}, u32[]{:S(2)}, u32[]{:S(2)}) %collective-permute-start) | collective-permute-done | bytes 2097184 | tf_op jit(solution)/shard_map/ppermute | solution.py:598
  15.3 4.4 %shard_map.123 = (f32[16,64,128]{2,1,0:T(8,128)}, f32[16,64,128]{2,1,0:T(8,128)}, f32[16,64,128]{2,1,0:T(8,128)}, f32[16,64,128]{2,1,0:T(8,128)}) custom-call(s32[32]{0:T(128)} %get-tuple-element.26.refs_0_, s32[128]{0:T(128)} %get-tuple-element.27.refs_1_, s32[5]{0:T(128)} %compare_select_fusion.3.refs_1_.refs_2_.place_ref, ...), custom_call_target="tpu_custom_call" | custom-call | tf_op jit(solution)/shard_map/pallas_call | solution.py:332
  21.1 2.6 %collective-permute-start.2 = (f32[16,64,128]{2,1,0:T(8,128)}, f32[16,64,128]{2,1,0:T(8,128)}, u32[]{:S(2)}, u32[]{:S(2)}) collective-permute-start(f32[16,64,128]{2,1,0:T(8,128)} %get-tuple-element.32), channel_id=1, source_target_pairs={{0,64},{1,5},{2,66},{3,7},{4,68},{5,1},{6,70},{7,3},{8,72},{9,13},... | collective-permute-start | bytes 1572872 | tf_op jit(solution)/shard_map/ppermute | solution.py:582
  26.0 4.1 %collective-permute-done.8.refs_7_ = f32[128,128]{1,0:T(8,128)S(1)} collective-permute-done((f32[128,128]{1,0:T(8,128)S(1)}, f32[128,128]{1,0:T(8,128)S(1)}, u32[]{:S(2)}, u32[]{:S(2)}) %collective-permute-start.8) | collective-permute-done | bytes 65568 | tf_op jit(solution)/shard_map/ppermute | solution.py:582
  30.1 1.5 %collective-permute-start.9 = (f32[128,128]{1,0:T(8,128)S(1)}, f32[128,128]{1,0:T(8,128)S(1)}, u32[]{:S(2)}, u32[]{:S(2)}) collective-permute-start(f32[128,128]{1,0:T(8,128)S(1)} %copy-done.9), channel_id=1, source_target_pairs={{0,64},{1,65},{2,66},{3,67},{4,68},{5,69},{6,70},{7,71},{8,72},{9,... | collective-permute-start | bytes 196616 | tf_op jit(solution)/shard_map/ppermute | solution.py:582
  31.6 4.2 %collective-permute-done.9.refs_8_ = f32[128,128]{1,0:T(8,128)S(1)} collective-permute-done((f32[128,128]{1,0:T(8,128)S(1)}, f32[128,128]{1,0:T(8,128)S(1)}, u32[]{:S(2)}, u32[]{:S(2)}) %collective-permute-start.9) | collective-permute-done | bytes 65568 | tf_op jit(solution)/shard_map/ppermute | solution.py:582
  36.8 2.1 %collective-permute-done.10.refs_9_ = f32[128,128]{1,0:T(8,128)S(1)} collective-permute-done((f32[128,128]{1,0:T(8,128)S(1)}, f32[128,128]{1,0:T(8,128)S(1)}, u32[]{:S(2)}, u32[]{:S(2)}) %collective-permute-start.10) | collective-permute-done | bytes 65568 | tf_op jit(solution)/shard_map/ppermute | solution.py:582
  40.3 6.2 %shard_map.124 = (f32[16,80,128]{2,1,0:T(8,128)}, f32[16,80,128]{2,1,0:T(8,128)}, f32[16,80,128]{2,1,0:T(8,128)}, f32[16,80,128]{2,1,0:T(8,128)}) custom-call(s32[32]{0:T(128)} %get-tuple-element.26.refs_0_, s32[128]{0:T(128)} %get-tuple-element.27.refs_1_, s32[5]{0:T(128)} %compare_select_fusion.3.refs_1_.refs_2_.place_ref, ...), custom_call_target="tpu_custom_call" | custom-call | tf_op jit(solution)/shard_map/pallas_call | solution.py:332
  47.4 1.5 %collective-permute-start.12 = (f32[16,80,128]{2,1,0:T(8,128)}, f32[16,80,128]{2,1,0:T(8,128)S(1)}, u32[]{:S(2)}, u32[]{:S(2)}) collective-permute-start(f32[16,80,128]{2,1,0:T(8,128)} %get-tuple-element.41), channel_id=1, source_target_pairs={{0,64},{1,5},{2,66},{3,7},{4,68},{5,1},{6,70},{7,3},{8,72},{9,13},... | collective-permute-start | bytes 1966088 | tf_op jit(solution)/shard_map/ppermute | solution.py:582
  51.4 1.7 %collective-permute-start.4 = (f32[4,64,128]{2,1,0:T(8,128)S(1)}, f32[4,64,128]{2,1,0:T(8,128)S(1)}, u32[]{:S(2)}, u32[]{:S(2)}) collective-permute-start(f32[4,64,128]{2,1,0:T(8,128)S(1)} %get-tuple-element.61), channel_id=1, source_target_pairs={{0,8},{1,9},{2,10},{3,11},{4,12},{5,13},{6,14},{7,15},{8,16},{9,17... | collective-permute-start | bytes 393224 | tf_op jit(solution)/shard_map/ppermute | solution.py:582
  53.1 2.2 %collective-permute-start.6 = (f32[4,64,128]{2,1,0:T(8,128)S(1)}, f32[4,64,128]{2,1,0:T(8,128)S(1)}, u32[]{:S(2)}, u32[]{:S(2)}) collective-permute-start(f32[4,64,128]{2,1,0:T(8,128)S(1)} %get-tuple-element.62), channel_id=1, source_target_pairs={{0,24},{1,25},{2,26},{3,27},{4,28},{5,29},{6,30},{7,31},{8,0},{9,1... | collective-permute-start | bytes 393224 | tf_op jit(solution)/shard_map/ppermute | solution.py:582
  55.2 9.5 %collective-permute-done.11 = f32[16,80,128]{2,1,0:T(8,128)S(1)} collective-permute-done((f32[16,80,128]{2,1,0:T(8,128)}, f32[16,80,128]{2,1,0:T(8,128)S(1)}, u32[]{:S(2)}, u32[]{:S(2)}) %collective-permute-start.11) | collective-permute-done | bytes 655392 | tf_op jit(solution)/shard_map/ppermute | solution.py:582
  64.7 3.6 %collective-permute-start.5 = (f32[4,64,128]{2,1,0:T(8,128)S(1)}, f32[4,64,128]{2,1,0:T(8,128)S(1)}, u32[]{:S(2)}, u32[]{:S(2)}) collective-permute-start(f32[4,64,128]{2,1,0:T(8,128)S(1)} %get-tuple-element.63), channel_id=1, source_target_pairs={{0,16},{1,17},{2,18},{3,19},{4,20},{5,21},{6,22},{7,23},{8,24},{9,... | collective-permute-start | bytes 393224 | tf_op jit(solution)/shard_map/ppermute | solution.py:582
  71.9 5.3 %collective-permute-done.14 = f32[4,80,128]{2,1,0:T(8,128)S(1)} collective-permute-done((f32[4,80,128]{2,1,0:T(8,128)S(1)}, f32[4,80,128]{2,1,0:T(8,128)S(1)}, u32[]{:S(2)}, u32[]{:S(2)}) %collective-permute-start.14) | collective-permute-done | bytes 163872 | tf_op jit(solution)/shard_map/ppermute | solution.py:582
  78.0 2.7 %collective-permute-start.19 = (f32[1,168,128]{2,1,0:T(8,128)S(1)}, f32[1,168,128]{2,1,0:T(8,128)S(1)}, u32[]{:S(2)}, u32[]{:S(2)}) collective-permute-start(f32[1,168,128]{2,1,0:T(8,128)S(1)} %get-tuple-element.65), channel_id=1, source_target_pairs={{0,6},{1,97},{2,0},{3,99},{4,2},{5,101},{6,4},{7,103},{8,14},{9,10... | collective-permute-start | bytes 258056 | tf_op jit(solution)/shard_map/ppermute | solution.py:582
  80.9 1.9 %collective-permute-done.17 = f32[1,168,128]{2,1,0:T(8,128)S(1)} collective-permute-done((f32[1,168,128]{2,1,0:T(8,128)S(1)}, f32[1,168,128]{2,1,0:T(8,128)S(1)}, u32[]{:S(2)}, u32[]{:S(2)}) %collective-permute-start.17) | collective-permute-done | bytes 86048 | tf_op jit(solution)/shard_map/ppermute | solution.py:582
  83.0 2.8 %collective-permute-done.18 = f32[1,168,128]{2,1,0:T(8,128)S(1)} collective-permute-done((f32[1,168,128]{2,1,0:T(8,128)S(1)}, f32[1,168,128]{2,1,0:T(8,128)S(1)}, u32[]{:S(2)}, u32[]{:S(2)}) %collective-permute-start.18) | collective-permute-done | bytes 86048 | tf_op jit(solution)/shard_map/ppermute | solution.py:582
  85.9 11.2 %collective-permute-start.20 = (f32[264,128]{1,0:T(8,128)S(1)}, f32[264,128]{1,0:T(8,128)S(1)}, u32[]{:S(2)}, u32[]{:S(2)}) collective-permute-start(f32[264,128]{1,0:T(8,128)S(1)} %bitcast.10), channel_id=1, source_target_pairs={{0,1},{1,0},{2,3},{3,2},{4,5},{5,4},{6,7},{7,6},{8,9},{9,8},{10,11... | collective-permute-start | bytes 405512 | tf_op jit(solution)/shard_map/ppermute | solution.py:598
  98.7 4.5 %shard_map.125 = (f32[128,128]{1,0:T(8,128)}, f32[128,128]{1,0:T(8,128)}, f32[128,128]{1,0:T(8,128)}, f32[8,128]{1,0:T(8,128)}, f32[128,128]{1,0:T(8,128)}) custom-call(f32[264,128]{1,0:T(8,128)} %bitcast.11, f32[264,128]{1,0:T(8,128)} %copy-done.4, s32[5]{0:T(128)} %compare_select_fusion.3.refs_1_.refs_2_.place_ref, f32[128,256]{1,0:T(8,128)} %constant.93.clone.lanes_ref, ...), custom_call_target="tpu_custom_call" | custom-call | tf_op jit(solution)/shard_map/pallas_call | solution.py:573
  103.2 16.3 %all_to_all.10 = f32[128,1,128]{2,1,0:T(1,128)} all-to-all(f32[128,1,128]{2,1,0:T(1,128)} %bitcast.13), channel_id=1, replica_groups=mesh['dp'=4,'grid'=32] {'dp','grid'}, dimensions={0} | all-to-all | bytes 131072 | tf_op jit(solution)/shard_map/all_to_all | solution.py:644
  119.5 5.2 %shard_map.126 = (f32[1024,128]{1,0:T(8,128)}, f32[8,128]{1,0:T(8,128)}) custom-call(f32[128,128]{1,0:T(8,128)} %bitcast.12, f32[8,128]{1,0:T(8,128)} %get-tuple-element.44.range_ref, f32[128,128]{1,0:T(8,128)} %get-tuple-element.45.scaled_ref, f32[128,128]{1,0:T(8,128)} %get-tuple-element.46.real_ref, f32[128,128]{1,0:T(8,128)} %get-tuple-element.47.imag_ref, ...), custom_call_target="tpu_custom_call" | custom-call | tf_op jit(solution)/shard_map/pallas_call | solution.py:573
  124.7 18.9 %all_to_all.11 = f32[128,8,128]{2,1,0:T(8,128)} all-to-all(f32[128,8,128]{2,1,0:T(8,128)} %bitcast.9), channel_id=1, replica_groups=mesh['dp'=4,'grid'=32] {'dp','grid'}, dimensions={0} | all-to-all | bytes 1048576 | tf_op jit(solution)/shard_map/all_to_all | solution.py:649
  143.6 2.4 %shard_map.127 = (f32[4,128,128]{2,1,0:T(8,128)}, f32[4,128,128]{2,1,0:T(8,128)}) custom-call(f32[1024,128]{1,0:T(8,128)} %bitcast.8, f32[8,128]{1,0:T(8,128)} %get-tuple-element.49.gain_ref, bf16[768,256]{1,0:T(8,128)(2,1)} %constant.98.clone.back_ref), custom_call_target="tpu_custom_call" | custom-call | tf_op jit(solution)/shard_map/pallas_call | solution.py:573
  (68 shorter events, 17.9 us)
Async XLA Ops:
  9.7 5.6 %collective-permute-start = (f32[64,64,128]{2,1,0:T(8,128)}, f32[64,64,128]{2,1,0:T(8,128)}, u32[]{:S(2)}, u32[]{:S(2)}) collective-permute-start(f32[64,64,128]{2,1,0:T(8,128)} %get-tuple-element.29), channel_id=1, source_target_pairs={{0,1},{1,0},{2,3},{3,2},{4,5},{5,4},{6,7},{7,6},{8,9},{9,8},{10,11... | collective-permute-start | bytes 6291464 | tf_op jit(solution)/shard_map/ppermute | solution.py:598
  11.1 27.8 %collective-permute-start.7 = (f32[64,64,128]{2,1,0:T(8,128)}, f32[64,64,128]{2,1,0:T(8,128)S(1)}, u32[]{:S(2)}, u32[]{:S(2)}) collective-permute-start(f32[64,64,128]{2,1,0:T(8,128)} %get-tuple-element.34), channel_id=1, source_target_pairs={{0,1},{1,0},{2,3},{3,2},{4,5},{5,4},{6,7},{7,6},{8,9},{9,8},{10,11... | collective-permute-start | bytes 6291464 | tf_op jit(solution)/shard_map/ppermute | solution.py:598
  15.3 14.8 %copy-start.9 = (f32[128,128]{1,0:T(8,128)S(1)}, f32[128,128]{1,0:T(8,128)}, u32[]{:S(2)}) copy-start(f32[128,128]{1,0:T(8,128)} %get-tuple-element.37) | copy-start | bytes 196612
  15.3 20.6 %copy-start.8 = (f32[128,128]{1,0:T(8,128)S(1)}, f32[128,128]{1,0:T(8,128)}, u32[]{:S(2)}) copy-start(f32[128,128]{1,0:T(8,128)} %get-tuple-element.38) | copy-start | bytes 196612
  19.7 29.2 %collective-permute-start.1 = (f32[16,64,128]{2,1,0:T(8,128)}, f32[16,64,128]{2,1,0:T(8,128)S(1)}, u32[]{:S(2)}, u32[]{:S(2)}) collective-permute-start(f32[16,64,128]{2,1,0:T(8,128)} %get-tuple-element.31), channel_id=1, source_target_pairs={{0,32},{1,3},{2,34},{3,5},{4,36},{5,7},{6,38},{7,1},{8,40},{9,11},... | collective-permute-start | bytes 1572872 | tf_op jit(solution)/shard_map/ppermute | solution.py:582
  21.1 28.9 %collective-permute-start.2 = (f32[16,64,128]{2,1,0:T(8,128)}, f32[16,64,128]{2,1,0:T(8,128)}, u32[]{:S(2)}, u32[]{:S(2)}) collective-permute-start(f32[16,64,128]{2,1,0:T(8,128)} %get-tuple-element.32), channel_id=1, source_target_pairs={{0,64},{1,5},{2,66},{3,7},{4,68},{5,1},{6,70},{7,3},{8,72},{9,13},... | collective-permute-start | bytes 1572872 | tf_op jit(solution)/shard_map/ppermute | solution.py:582
  23.7 26.3 %collective-permute-start.3 = (f32[16,64,128]{2,1,0:T(8,128)}, f32[16,64,128]{2,1,0:T(8,128)}, u32[]{:S(2)}, u32[]{:S(2)}) collective-permute-start(f32[16,64,128]{2,1,0:T(8,128)} %get-tuple-element.33), channel_id=1, source_target_pairs={{0,96},{1,7},{2,98},{3,1},{4,100},{5,3},{6,102},{7,5},{8,104},{9,1... | collective-permute-start | bytes 1572872 | tf_op jit(solution)/shard_map/ppermute | solution.py:582
  24.8 5.3 %collective-permute-start.8 = (f32[128,128]{1,0:T(8,128)S(1)}, f32[128,128]{1,0:T(8,128)S(1)}, u32[]{:S(2)}, u32[]{:S(2)}) collective-permute-start(f32[128,128]{1,0:T(8,128)S(1)} %copy-done.10), channel_id=1, source_target_pairs={{0,32},{1,33},{2,34},{3,35},{4,36},{5,37},{6,38},{7,39},{8,40},{9,... | collective-permute-start | bytes 196616 | tf_op jit(solution)/shard_map/ppermute | solution.py:582
  30.1 5.7 %collective-permute-start.9 = (f32[128,128]{1,0:T(8,128)S(1)}, f32[128,128]{1,0:T(8,128)S(1)}, u32[]{:S(2)}, u32[]{:S(2)}) collective-permute-start(f32[128,128]{1,0:T(8,128)S(1)} %copy-done.9), channel_id=1, source_target_pairs={{0,64},{1,65},{2,66},{3,67},{4,68},{5,69},{6,70},{7,71},{8,72},{9,... | collective-permute-start | bytes 196616 | tf_op jit(solution)/shard_map/ppermute | solution.py:582
  35.8 3.1 %collective-permute-start.10 = (f32[128,128]{1,0:T(8,128)S(1)}, f32[128,128]{1,0:T(8,128)S(1)}, u32[]{:S(2)}, u32[]{:S(2)}) collective-permute-start(f32[128,128]{1,0:T(8,128)S(1)} %copy-done.8), channel_id=1, source_target_pairs={{0,96},{1,97},{2,98},{3,99},{4,100},{5,101},{6,102},{7,103},{8,104... | collective-permute-start | bytes 196616 | tf_op jit(solution)/shard_map/ppermute | solution.py:582
  46.5 21.8 %copy-start.1 = (f32[16,80,128]{2,1,0:T(8,128)S(1)}, f32[16,80,128]{2,1,0:T(8,128)}, u32[]{:S(2)}) copy-start(f32[16,80,128]{2,1,0:T(8,128)} %get-tuple-element.39) | copy-start | bytes 1966084
  46.5 18.2 %collective-permute-start.11 = (f32[16,80,128]{2,1,0:T(8,128)}, f32[16,80,128]{2,1,0:T(8,128)S(1)}, u32[]{:S(2)}, u32[]{:S(2)}) collective-permute-start(f32[16,80,128]{2,1,0:T(8,128)} %get-tuple-element.40), channel_id=1, source_target_pairs={{0,32},{1,3},{2,34},{3,5},{4,36},{5,7},{6,38},{7,1},{8,40},{9,11},... | collective-permute-start | bytes 1966088 | tf_op jit(solution)/shard_map/ppermute | solution.py:582
  47.4 21.0 %collective-permute-start.12 = (f32[16,80,128]{2,1,0:T(8,128)}, f32[16,80,128]{2,1,0:T(8,128)S(1)}, u32[]{:S(2)}, u32[]{:S(2)}) collective-permute-start(f32[16,80,128]{2,1,0:T(8,128)} %get-tuple-element.41), channel_id=1, source_target_pairs={{0,64},{1,5},{2,66},{3,7},{4,68},{5,1},{6,70},{7,3},{8,72},{9,13},... | collective-permute-start | bytes 1966088 | tf_op jit(solution)/shard_map/ppermute | solution.py:582
  48.9 19.5 %collective-permute-start.13 = (f32[16,80,128]{2,1,0:T(8,128)}, f32[16,80,128]{2,1,0:T(8,128)S(1)}, u32[]{:S(2)}, u32[]{:S(2)}) collective-permute-start(f32[16,80,128]{2,1,0:T(8,128)} %get-tuple-element.42), channel_id=1, source_target_pairs={{0,96},{1,7},{2,98},{3,1},{4,100},{5,3},{6,102},{7,5},{8,104},{9,1... | collective-permute-start | bytes 1966088 | tf_op jit(solution)/shard_map/ppermute | solution.py:582
  51.4 19.2 %collective-permute-start.4 = (f32[4,64,128]{2,1,0:T(8,128)S(1)}, f32[4,64,128]{2,1,0:T(8,128)S(1)}, u32[]{:S(2)}, u32[]{:S(2)}) collective-permute-start(f32[4,64,128]{2,1,0:T(8,128)S(1)} %get-tuple-element.61), channel_id=1, source_target_pairs={{0,8},{1,9},{2,10},{3,11},{4,12},{5,13},{6,14},{7,15},{8,16},{9,17... | collective-permute-start | bytes 393224 | tf_op jit(solution)/shard_map/ppermute | solution.py:582
  53.1 18.8 %collective-permute-start.6 = (f32[4,64,128]{2,1,0:T(8,128)S(1)}, f32[4,64,128]{2,1,0:T(8,128)S(1)}, u32[]{:S(2)}, u32[]{:S(2)}) collective-permute-start(f32[4,64,128]{2,1,0:T(8,128)S(1)} %get-tuple-element.62), channel_id=1, source_target_pairs={{0,24},{1,25},{2,26},{3,27},{4,28},{5,29},{6,30},{7,31},{8,0},{9,1... | collective-permute-start | bytes 393224 | tf_op jit(solution)/shard_map/ppermute | solution.py:582
  64.7 7.1 %collective-permute-start.5 = (f32[4,64,128]{2,1,0:T(8,128)S(1)}, f32[4,64,128]{2,1,0:T(8,128)S(1)}, u32[]{:S(2)}, u32[]{:S(2)}) collective-permute-start(f32[4,64,128]{2,1,0:T(8,128)S(1)} %get-tuple-element.63), channel_id=1, source_target_pairs={{0,16},{1,17},{2,18},{3,19},{4,20},{5,21},{6,22},{7,23},{8,24},{9,... | collective-permute-start | bytes 393224 | tf_op jit(solution)/shard_map/ppermute | solution.py:582
  68.5 8.6 %collective-permute-start.14 = (f32[4,80,128]{2,1,0:T(8,128)S(1)}, f32[4,80,128]{2,1,0:T(8,128)S(1)}, u32[]{:S(2)}, u32[]{:S(2)}) collective-permute-start(f32[4,80,128]{2,1,0:T(8,128)S(1)} %get-tuple-element.56), channel_id=1, source_target_pairs={{0,8},{1,9},{2,10},{3,11},{4,12},{5,13},{6,14},{7,15},{8,16},{9,17... | collective-permute-start | bytes 491528 | tf_op jit(solution)/shard_map/ppermute | solution.py:582
  69.4 7.8 %collective-permute-start.15 = (f32[4,80,128]{2,1,0:T(8,128)S(1)}, f32[4,80,128]{2,1,0:T(8,128)S(1)}, u32[]{:S(2)}, u32[]{:S(2)}) collective-permute-start(f32[4,80,128]{2,1,0:T(8,128)S(1)} %get-tuple-element.57), channel_id=1, source_target_pairs={{0,16},{1,17},{2,18},{3,19},{4,20},{5,21},{6,22},{7,23},{8,24},{9,... | collective-permute-start | bytes 491528 | tf_op jit(solution)/shard_map/ppermute | solution.py:582
  70.6 7.2 %collective-permute-start.16 = (f32[4,80,128]{2,1,0:T(8,128)S(1)}, f32[4,80,128]{2,1,0:T(8,128)S(1)}, u32[]{:S(2)}, u32[]{:S(2)}) collective-permute-start(f32[4,80,128]{2,1,0:T(8,128)S(1)} %get-tuple-element.58), channel_id=1, source_target_pairs={{0,24},{1,25},{2,26},{3,27},{4,28},{5,29},{6,30},{7,31},{8,0},{9,1... | collective-permute-start | bytes 491528 | tf_op jit(solution)/shard_map/ppermute | solution.py:582
  77.9 4.9 %collective-permute-start.17 = (f32[1,168,128]{2,1,0:T(8,128)S(1)}, f32[1,168,128]{2,1,0:T(8,128)S(1)}, u32[]{:S(2)}, u32[]{:S(2)}) collective-permute-start(f32[1,168,128]{2,1,0:T(8,128)S(1)} %get-tuple-element.64), channel_id=1, source_target_pairs={{0,2},{1,33},{2,4},{3,35},{4,6},{5,37},{6,0},{7,39},{8,10},{9,41},... | collective-permute-start | bytes 258056 | tf_op jit(solution)/shard_map/ppermute | solution.py:582
  78.0 5.0 %collective-permute-start.19 = (f32[1,168,128]{2,1,0:T(8,128)S(1)}, f32[1,168,128]{2,1,0:T(8,128)S(1)}, u32[]{:S(2)}, u32[]{:S(2)}) collective-permute-start(f32[1,168,128]{2,1,0:T(8,128)S(1)} %get-tuple-element.65), channel_id=1, source_target_pairs={{0,6},{1,97},{2,0},{3,99},{4,2},{5,101},{6,4},{7,103},{8,14},{9,10... | collective-permute-start | bytes 258056 | tf_op jit(solution)/shard_map/ppermute | solution.py:582
  80.6 5.1 %collective-permute-start.18 = (f32[1,168,128]{2,1,0:T(8,128)S(1)}, f32[1,168,128]{2,1,0:T(8,128)S(1)}, u32[]{:S(2)}, u32[]{:S(2)}) collective-permute-start(f32[1,168,128]{2,1,0:T(8,128)S(1)} %get-tuple-element.66), channel_id=1, source_target_pairs={{0,4},{1,65},{2,6},{3,67},{4,0},{5,69},{6,2},{7,71},{8,12},{9,73},... | collective-permute-start | bytes 258056 | tf_op jit(solution)/shard_map/ppermute | solution.py:582
  85.9 12.1 %collective-permute-start.20 = (f32[264,128]{1,0:T(8,128)S(1)}, f32[264,128]{1,0:T(8,128)S(1)}, u32[]{:S(2)}, u32[]{:S(2)}) collective-permute-start(f32[264,128]{1,0:T(8,128)S(1)} %bitcast.10), channel_id=1, source_target_pairs={{0,1},{1,0},{2,3},{3,2},{4,5},{5,4},{6,7},{7,6},{8,9},{9,8},{10,11... | collective-permute-start | bytes 405512 | tf_op jit(solution)/shard_map/ppermute | solution.py:598
  (8 other events, 46.0 us)

commit v7 on v4

--- a/solution.py
+++ b/solution.py
@@ -193,10 +193,12 @@
 def grid_kernel(*refs, kept, part, capacity):
     if kept:
         count_ref, list_ref, place_ref, wave_ref, matrix_ref, other_ref = refs[:6]
-        outs = refs[6:]
+        weight_refs = refs[6 : 6 + SIDE] if part else ()
+        outs, row_refs = refs[6 + len(weight_refs) :][:SIDE], refs[6 + len(weight_refs) :][SIDE:]
     else:
-        dest_ref, place_ref, values_ref, matrix_ref, packed_ref, weights_ref = refs[:6]
-        out_refs, (kept_wave_ref, count_ref, list_ref), wave_ref = refs[6:8], refs[8:11], refs[-1]
+        dest_ref, place_ref, values_ref, source_ref, packed_ref, weights_ref = refs[:6]
+        out_refs, (kept_wave_ref, count_ref, list_ref), slice_refs = refs[6:8], refs[8:11], refs[11 : 11 + SIDE]
+        wave_ref, matrix_ref, fetched = refs[-3:]
     nent, rows, width = matrix_ref.shape
     size = width // SIDE
     half = size // 2
@@ -215,9 +217,11 @@
         return 0
 
     def prepare():
+        fetch = pltpu.make_async_copy(source_ref, matrix_ref, fetched)
+        fetch.start()
         lax.fori_loop(0, nslab, clear, 0)
         lax.fori_loop(0, nent, enter, 0)
-        for r, slice_ref in enumerate(refs[11:-1]):
+        for r, slice_ref in enumerate(slice_refs):
             slice_ref[...] = weights_ref[0, :, (place_ref[0] + r) % SIDE, :]
         chip = lax.broadcasted_iota(jnp.int32, (half, half), 0)
         slot = lax.broadcasted_iota(jnp.int32, (half, half), 1)
@@ -239,6 +243,7 @@
             high = wave.astype(jnp.bfloat16)
             low = (wave - high.astype(jnp.float32)).astype(jnp.bfloat16)
             target_ref[...] = jnp.concatenate([high, low], 1).reshape(nent, rows, size)
+        fetch.wait()
 
     if not kept:
         pl.when(step == 0)(prepare)
@@ -285,6 +290,8 @@
 
     if kept:
         products(keep)
+        if part:
+            pl.when(step == STEPS // HALVES - 1)(lambda: weight_kernel(*weight_refs, place_ref, *row_refs))
     else:
         pl.when(step < STEPS // HALVES)(lambda: products(send(out_refs[0])))
         pl.when(step >= STEPS // HALVES)(lambda: products(send(out_refs[1])))
@@ -302,7 +309,11 @@
     in_specs = [scalars if a.dtype == jnp.int32 else fixed(a.shape) for a in args]
     if kept:
         out_shape, out_specs = [f32(SIDE**2, size // HALVES, size)] * SIDE, [moving(SIDE**2)] * SIDE
-        in_specs[-1] = moving(blocks)
+        in_specs[5] = moving(blocks)
+        if part:
+            rows_shape = (SIDE**2 * 8 + 8, size)
+            out_shape = out_shape + [f32(*rows_shape)] * SIDE
+            out_specs = out_specs + [fixed(rows_shape)] * SIDE
         scratch = []
     else:
         wave = (nent, rows, size)
@@ -316,7 +327,8 @@
             pl.BlockSpec(block, lambda i: (0, jnp.minimum(i, STEPS // HALVES - 1), 0)),
             pl.BlockSpec(block, lambda i: (0, jnp.maximum(i - STEPS // HALVES, 0), 0)),
         ] + [fixed(wave), scalars, scalars] + [fixed((size, size))] * SIDE
-        scratch = [pltpu.VMEM(wave, jnp.bfloat16)]
+        in_specs[3] = pl.BlockSpec(memory_space=pl.ANY)
+        scratch = [pltpu.VMEM(wave, jnp.bfloat16), pltpu.VMEM(matrix.shape, jnp.bfloat16), pltpu.SemaphoreType.DMA]
     return pl.pallas_call(
         functools.partial(grid_kernel, kept=kept, part=part, capacity=capacity),
         grid=(steps,),
@@ -482,9 +494,12 @@
     return pick(a[0]), pick(a[1])
 
 
-def solve_kernel(
-    sums_ref, range_ref, scaled_ref, real_ref, imag_ref, lanes_ref, rows_ref, out_ref, gain_ref, *, scale
-):
+def solve_kernel(sums_ref, range_ref, *refs, scale):
+    sources, (out_ref, gain_ref), held, (result_ref, fetched, sent) = refs[:5], refs[5:7], refs[7:12], refs[12:]
+    fetches = [pltpu.make_async_copy(a, b, fetched.at[i]) for i, (a, b) in enumerate(zip(sources, held))]
+    for fetch in fetches:
+        fetch.start()
+    scaled_ref, real_ref, imag_ref, lanes_ref, rows_ref = held
     size = scaled_ref.shape[0]
     given = sums_ref[...]
     low = pltpu.roll(given, size - LOW_LANE, 1)
@@ -518,6 +533,8 @@
         decay = decay * beta[0][0:1]
     gain = lax.rsqrt(jnp.maximum(jnp.abs(decay), 1e-30)) / centre[0][0:1]
     gain_ref[...] = jnp.broadcast_to(gain, gain_ref.shape)
+    for fetch in fetches:
+        fetch.wait()
     scaled = scaled_ref[...]
     field = steps[0]
     solved = jnp.broadcast_to(field, scaled.shape)
@@ -539,9 +556,35 @@
     both = dot_pieces(rows_ref[...], stacked(jnp.concatenate([mid_real, mid_imag], 1), 0), 1, 0)
     real = both[:size, :size] - both[size:, size:]
     imag = both[:size, size:] + both[size:, :size]
-    for copy in range(out_ref.shape[0] // (2 * size)):
-        out_ref[pl.ds(copy * 2 * size, size, stride=2), :] = real
-        out_ref[pl.ds(copy * 2 * size + 1, size, stride=2), :] = imag
+    result_ref[pl.ds(0, size, stride=2), :] = real
+    result_ref[pl.ds(1, size, stride=2), :] = imag
+    copies = [pltpu.make_async_copy(result_ref, out_ref.at[i], sent.at[i]) for i in range(out_ref.shape[0])]
+    for copy in copies:
+        copy.start()
+    for copy in copies:
+        copy.wait()
+
+
+def solve_call(copies, scale, *args):
+    whole = pl.BlockSpec(memory_space=pltpu.VMEM)
+    apart = pl.BlockSpec(memory_space=pl.ANY)
+    size = args[0].shape[1]
+    return pl.pallas_call(
+        functools.partial(solve_kernel, scale=scale),
+        out_shape=[
+            jax.ShapeDtypeStruct((copies, 2 * size, size), jnp.float32),
+            jax.ShapeDtypeStruct((8, size), jnp.float32),
+        ],
+        in_specs=[whole] * 2 + [apart] * (len(args) - 2),
+        out_specs=[apart, whole],
+        scratch_shapes=[pltpu.VMEM(a.shape, a.dtype) for a in args[2:]]
+        + [
+            pltpu.VMEM((2 * size, size), jnp.float32),
+            pltpu.SemaphoreType.DMA((len(args) - 2,)),
+            pltpu.SemaphoreType.DMA((copies,)),
+        ],
+        name="solve",
+    )(*args)
 
 
 def output_kernel(given_ref, gain_ref, back_ref, field_ref, resid_ref):
@@ -593,7 +636,6 @@
         step == 0, x, jnp.where(step == 1, y, jnp.where(step == 2, z, jnp.where(step == 3, core, chip == 0)))
     ).astype(jnp.int32)
 
-    together = lax.optimization_barrier
     *away, wave, counts, lists, p0, p1, p2, p3 = grid_call(
         False, 0, ngrid, capacity, dest_slab[:, 0], place, intensities, gridding, table["packed"], spectral_weights
     )
@@ -605,10 +647,9 @@
     least = lambda parts: functools.reduce(jnp.minimum, parts)
     data = []
     for part in range(HALVES):
-        kept = grid_call(True, part, ngrid, capacity, *members, arrived[part])
+        kept = grid_call(True, part, ngrid, capacity, *members, arrived[part], *(weights if part else ()))
+        kept, rows = kept[:SIDE], kept[SIDE:]
         data.append(exchange(kept, axes[0]))
-    kept, weights = together((kept, weights))
-    rows = call(weight_kernel, [(SIDE**2 * 8 + 8, size)] * SIDE, *weights, place)
     rows = exchange(rows, axes[0])
     parts = quarter(summed(data[0]))
     early = exchange(parts, axes[1])
@@ -634,9 +675,8 @@
         parts, swap(parts), place, table["lanes"], table["rows"], table["mirror"],
     )
     sums = lax.all_to_all(send.reshape(count, 1, size), ALL, 0, 0, tiled=True).reshape(count, size)
-    back, gain = call(
-        functools.partial(solve_kernel, scale=1.0 / size**3), [(ndp * 2 * size, size), (8, size)],
-        sums, ends, scaled, real, imag, table["lanes_pieces"], table["rows_pieces"],
+    back, gain = solve_call(
+        ndp, 1.0 / size**3, sums, ends, scaled, real, imag, table["lanes_pieces"], table["rows_pieces"]
     )
     landed = lax.all_to_all(back.reshape(count, 2 * planes, size), ALL, 0, 0, tiled=True)
     return tuple(

time: 134 us -> 136 us (1.015)
  waiting for transfers between devices: 27.6 us -> 32.6 us
  Pallas kernels: 31.2 us -> 29.5 us
    pallas_call x4 -> x2, Pallas kernels: 14.1 us -> 6.87 us  [call(): pl.pallas_call(kernel, out_shape=[jax.ShapeDtypeStruct(s, jnp.float32) fo...]
    pallas_call x0 -> x1, Pallas kernels: none -> 5.63 us  [solve_call(): pl.pallas_call(functools.partial(solve_kernel, scale=scale), out_shape=[j...]
    ppermute x21, waiting for transfers between devices: 26.6 us -> 31.6 us  [exchange(): lax.ppermute(parts[r], ALL, shift_pairs(axes, r))]
    ppermute x21, starting transfers between devices: 30.3 us -> 28.7 us  [exchange(): lax.ppermute(parts[r], ALL, shift_pairs(axes, r))]
  transfers between devices with their start and end apart: 24 -> 24, of which waited for: 9 -> 12; matrix products, arithmetic and copies ran while one was open for 1% -> 1% of each run, Pallas kernels for 8% -> 7%
where the time goes in v7:
time: 136 us; the launch traced here: 135 us
  starting transfers between devices  34 us (25%)
  blocking collectives  33.6 us (25%)
  waiting for transfers between devices  32.6 us (24%)
  Pallas kernels  29.5 us (22%)
  local copies, waits for them, and re-layouts  2.72 us (2%)
  other arithmetic  2.05 us (2%)
    ppermute x21, waiting for transfers between devices, exchange(): lax.ppermute(parts[r], ALL, shift_pairs(axes, r))  31.6 us
    ppermute x21, starting transfers between devices, exchange(): lax.ppermute(parts[r], ALL, shift_pairs(axes, r))  28.7 us
    all_to_all x1, blocking collectives, body(): lax.all_to_all(back.reshape(count, 2 * planes, size), ALL, 0, 0, tiled=True)  19.2 us
    pallas_call x3, Pallas kernels, grid_call(): pl.pallas_call(functools.partial(grid_kernel, kept=kept, part=part, capac...  17 us
    all_to_all x1, blocking collectives, body(): lax.all_to_all(send.reshape(count, 1, size), ALL, 0, 0, tiled=True)  14.4 us
    pallas_call x2, Pallas kernels, call(): pl.pallas_call(kernel, out_shape=[jax.ShapeDtypeStruct(s, jnp.float32) fo...  6.87 us
    pallas_call x1, Pallas kernels, solve_call(): pl.pallas_call(functools.partial(solve_kernel, scale=scale), out_shape=[j...  5.63 us
    ppermute x3, starting transfers between devices, body(): swap = lambda a: lax.ppermute(a, ALL, shift_pairs((3, 3), 1))  5.3 us
  transfers between devices with their start and end apart: 24, of which 12 were waited for; matrix products, arithmetic and copies ran while one was open for 1% of the time, Pallas kernels for 7%

profile of v7, /device:TPU:1, one launch (start us, length us, event | category | flops | bytes accessed | tf_op | source)
XLA Modules:
  0.0 135.3 jit_solution(15490647693094135551)
XLA Ops:
  1.3 7.8 %shard_map.122 = (f32[64,64,128]{2,1,0:T(8,128)}, f32[64,64,128]{2,1,0:T(8,128)}, bf16[64,32,128]{2,1,0:T(8,128)(2,1)}, s32[32]{0:T(128)}, s32[128]{0:T(128)}, /...) custom-call(s32[64]{0:T(128)} %bitcast.20, ...), custom_call_target="tpu_custom_call" | custom-call | tf_op jit(solution)/shard_map/pallas_call | solution.py:332
  12.0 2.4 %collective-permute-start.9 = (f32[128,128]{1,0:T(8,128)}, f32[128,128]{1,0:T(8,128)S(1)}, u32[]{:S(2)}, u32[]{:S(2)}) collective-permute-start(f32[128,128]{1,0:T(8,128)} %get-tuple-element.41), channel_id=1, source_target_pairs={{0,64},{1,65},{2,66},{3,67},{4,68},{5,69},{6,70},{7,71},{8,72},{9,... | collective-permute-start | bytes 196616 | tf_op jit(solution)/shard_map/ppermute | solution.py:613
  15.6 1.9 %collective-permute-done.9.refs_8_ = f32[128,128]{1,0:T(8,128)S(1)} collective-permute-done((f32[128,128]{1,0:T(8,128)}, f32[128,128]{1,0:T(8,128)S(1)}, u32[]{:S(2)}, u32[]{:S(2)}) %collective-permute-start.9) | collective-permute-done | bytes 65568 | tf_op jit(solution)/shard_map/ppermute | solution.py:613
  18.6 4.8 %shard_map.124 = (f32[16,64,128]{2,1,0:T(8,128)}, f32[16,64,128]{2,1,0:T(8,128)}, f32[16,64,128]{2,1,0:T(8,128)}, f32[16,64,128]{2,1,0:T(8,128)}, f32[136,128]{1...) custom-call(s32[32]{0:T(128)} %get-tuple-element.30.refs_0_, ...), custom_call_target="tpu_custom_call" | custom-call | tf_op jit(solution)/shard_map/pallas_call | solution.py:332
  24.8 2.6 %collective-permute-start.15 = (f32[136,128]{1,0:T(8,128)}, f32[136,128]{1,0:T(8,128)S(1)}, u32[]{:S(2)}, u32[]{:S(2)}) collective-permute-start(f32[136,128]{1,0:T(8,128)} %get-tuple-element.49), channel_id=1, source_target_pairs={{0,64},{1,5},{2,66},{3,7},{4,68},{5,1},{6,70},{7,3},{8,72},{9,13},... | collective-permute-start | bytes 208904 | tf_op jit(solution)/shard_map/ppermute | solution.py:613
  29.9 4.4 %shard_map.123 = (f32[16,64,128]{2,1,0:T(8,128)}, f32[16,64,128]{2,1,0:T(8,128)}, f32[16,64,128]{2,1,0:T(8,128)}, f32[16,64,128]{2,1,0:T(8,128)}) custom-call(s32[32]{0:T(128)} %get-tuple-element.30.refs_0_, s32[128]{0:T(128)} %get-tuple-element.31.refs_1_, s32[5]{0:T(128)} %compare_select_fusion.3.refs_1_.refs_2_.place_ref, ...), custom_call_target="tpu_custom_call" | custom-call | tf_op jit(solution)/shard_map/pallas_call | solution.py:332
  35.5 1.7 %collective-permute-start.3 = (f32[16,64,128]{2,1,0:T(8,128)}, f32[16,64,128]{2,1,0:T(8,128)S(1)}, u32[]{:S(2)}, u32[]{:S(2)}) collective-permute-start(f32[16,64,128]{2,1,0:T(8,128)} %get-tuple-element.37), channel_id=1, source_target_pairs={{0,96},{1,7},{2,98},{3,1},{4,100},{5,3},{6,102},{7,5},{8,104},{9,1... | collective-permute-start | bytes 1572872 | tf_op jit(solution)/shard_map/ppermute | solution.py:613
  37.7 1.8 %collective-permute-start.12 = (f32[16,64,128]{2,1,0:T(8,128)S(1)}, f32[16,64,128]{2,1,0:T(8,128)S(1)}, u32[]{:S(2)}, u32[]{:S(2)}) collective-permute-start(f32[16,64,128]{2,1,0:T(8,128)S(1)} %copy-done.9), channel_id=1, source_target_pairs={{0,64},{1,5},{2,66},{3,7},{4,68},{5,1},{6,70},{7,3},{8,72},{9,13},... | collective-permute-start | bytes 1572872 | tf_op jit(solution)/shard_map/ppermute | solution.py:613
  39.5 10.2 %collective-permute-done.1 = f32[16,64,128]{2,1,0:T(8,128)S(1)} collective-permute-done((f32[16,64,128]{2,1,0:T(8,128)}, f32[16,64,128]{2,1,0:T(8,128)S(1)}, u32[]{:S(2)}, u32[]{:S(2)}) %collective-permute-start.1) | collective-permute-done | bytes 524320 | tf_op jit(solution)/shard_map/ppermute | solution.py:613
  51.5 1.7 %collective-permute-start.4 = (f32[4,64,128]{2,1,0:T(8,128)S(1)}, f32[4,64,128]{2,1,0:T(8,128)S(1)}, u32[]{:S(2)}, u32[]{:S(2)}) collective-permute-start(f32[4,64,128]{2,1,0:T(8,128)S(1)} %get-tuple-element.67), channel_id=1, source_target_pairs={{0,8},{1,9},{2,10},{3,11},{4,12},{5,13},{6,14},{7,15},{8,16},{9,17... | collective-permute-start | bytes 393224 | tf_op jit(solution)/shard_map/ppermute | solution.py:613
  53.2 2.2 %collective-permute-start.6 = (f32[4,64,128]{2,1,0:T(8,128)S(1)}, f32[4,64,128]{2,1,0:T(8,128)S(1)}, u32[]{:S(2)}, u32[]{:S(2)}) collective-permute-start(f32[4,64,128]{2,1,0:T(8,128)S(1)} %get-tuple-element.68), channel_id=1, source_target_pairs={{0,24},{1,25},{2,26},{3,27},{4,28},{5,29},{6,30},{7,31},{8,0},{9,1... | collective-permute-start | bytes 393224 | tf_op jit(solution)/shard_map/ppermute | solution.py:613
  55.4 5.5 %collective-permute-done.11 = f32[16,64,128]{2,1,0:T(8,128)S(1)} collective-permute-done((f32[16,64,128]{2,1,0:T(8,128)}, f32[16,64,128]{2,1,0:T(8,128)S(1)}, u32[]{:S(2)}, u32[]{:S(2)}) %collective-permute-start.11) | collective-permute-done | bytes 524320 | tf_op jit(solution)/shard_map/ppermute | solution.py:613
  60.9 3.5 %collective-permute-start.5 = (f32[4,64,128]{2,1,0:T(8,128)S(1)}, f32[4,64,128]{2,1,0:T(8,128)S(1)}, u32[]{:S(2)}, u32[]{:S(2)}) collective-permute-start(f32[4,64,128]{2,1,0:T(8,128)S(1)} %get-tuple-element.69), channel_id=1, source_target_pairs={{0,16},{1,17},{2,18},{3,19},{4,20},{5,21},{6,22},{7,23},{8,24},{9,... | collective-permute-start | bytes 393224 | tf_op jit(solution)/shard_map/ppermute | solution.py:613
  68.1 3.2 %collective-permute-done.17 = f32[4,80,128]{2,1,0:T(8,128)S(1)} collective-permute-done((f32[4,80,128]{2,1,0:T(8,128)S(1)}, f32[4,80,128]{2,1,0:T(8,128)S(1)}, u32[]{:S(2)}, u32[]{:S(2)}) %collective-permute-start.17) | collective-permute-done | bytes 163872 | tf_op jit(solution)/shard_map/ppermute | solution.py:613
  71.3 3.7 %collective-permute-done.18 = f32[4,80,128]{2,1,0:T(8,128)S(1)} collective-permute-done((f32[4,80,128]{2,1,0:T(8,128)S(1)}, f32[4,80,128]{2,1,0:T(8,128)S(1)}, u32[]{:S(2)}, u32[]{:S(2)}) %collective-permute-start.18) | collective-permute-done | bytes 163872 | tf_op jit(solution)/shard_map/ppermute | solution.py:613
  76.2 2.7 %collective-permute-start.22 = (f32[1,168,128]{2,1,0:T(8,128)S(1)}, f32[1,168,128]{2,1,0:T(8,128)S(1)}, u32[]{:S(2)}, u32[]{:S(2)}) collective-permute-start(f32[1,168,128]{2,1,0:T(8,128)S(1)} %get-tuple-element.71), channel_id=1, source_target_pairs={{0,6},{1,97},{2,0},{3,99},{4,2},{5,101},{6,4},{7,103},{8,14},{9,10... | collective-permute-start | bytes 258056 | tf_op jit(solution)/shard_map/ppermute | solution.py:613
  78.9 1.9 %collective-permute-done.20 = f32[1,168,128]{2,1,0:T(8,128)S(1)} collective-permute-done((f32[1,168,128]{2,1,0:T(8,128)S(1)}, f32[1,168,128]{2,1,0:T(8,128)S(1)}, u32[]{:S(2)}, u32[]{:S(2)}) %collective-permute-start.20) | collective-permute-done | bytes 86048 | tf_op jit(solution)/shard_map/ppermute | solution.py:613
  81.3 2.5 %collective-permute-done.21 = f32[1,168,128]{2,1,0:T(8,128)S(1)} collective-permute-done((f32[1,168,128]{2,1,0:T(8,128)S(1)}, f32[1,168,128]{2,1,0:T(8,128)S(1)}, u32[]{:S(2)}, u32[]{:S(2)}) %collective-permute-start.21) | collective-permute-done | bytes 86048 | tf_op jit(solution)/shard_map/ppermute | solution.py:613
  83.8 3.7 %collective-permute-start.23 = (f32[264,128]{1,0:T(8,128)S(1)}, f32[264,128]{1,0:T(8,128)S(1)}, u32[]{:S(2)}, u32[]{:S(2)}) collective-permute-start(f32[264,128]{1,0:T(8,128)S(1)} %bitcast.16), channel_id=1, source_target_pairs={{0,1},{1,0},{2,3},{3,2},{4,5},{5,4},{6,7},{7,6},{8,9},{9,8},{10,11... | collective-permute-start | bytes 405512 | tf_op jit(solution)/shard_map/ppermute | solution.py:629
  89.2 4.5 %shard_map.125 = (f32[128,128]{1,0:T(8,128)}, f32[128,128]{1,0:T(8,128)}, f32[128,128]{1,0:T(8,128)}, f32[8,128]{1,0:T(8,128)}, f32[128,128]{1,0:T(8,128)}) custom-call(f32[264,128]{1,0:T(8,128)} %bitcast.17, f32[264,128]{1,0:T(8,128)} %copy-done.3, s32[5]{0:T(128)} %compare_select_fusion.3.refs_1_.refs_2_.place_ref, f32[128,256]{1,0:T(8,128)} %constant.93.clone.lanes_ref, ...), custom_call_target="tpu_custom_call" | custom-call | tf_op jit(solution)/shard_map/pallas_call | solution.py:604
  93.7 14.4 %all_to_all.10 = f32[128,1,128]{2,1,0:T(1,128)} all-to-all(f32[128,1,128]{2,1,0:T(1,128)} %bitcast.19), channel_id=1, replica_groups=mesh['dp'=4,'grid'=32] {'dp','grid'}, dimensions={0} | all-to-all | bytes 131072 | tf_op jit(solution)/shard_map/all_to_all | solution.py:677
  108.1 5.6 %solve.1 = (f32[4,256,128]{2,1,0:T(8,128)}, f32[8,128]{1,0:T(8,128)}) custom-call(f32[128,128]{1,0:T(8,128)} %bitcast.18, f32[8,128]{1,0:T(8,128)} %get-tuple-element.52.range_ref, f32[128,128]{1,0:T(8,128)} %get-tuple-element.53.refs_0_, f32[128,128]{1,0:T(8,128)} %get-tuple-element.54.refs_1_, f32[128,128]{1,0:T(8,128)} %get-tuple-element.55.refs_2_, ...), custom_call_target="tpu_custom_call" | custom-call | tf_op jit(solution)/shard_map/solve/pallas_call | solution.py:572
  113.8 19.2 %all_to_all.11 = f32[128,8,128]{2,1,0:T(8,128)} all-to-all(f32[128,8,128]{2,1,0:T(8,128)} %bitcast.14), channel_id=1, replica_groups=mesh['dp'=4,'grid'=32] {'dp','grid'}, dimensions={0} | all-to-all | bytes 1048576 | tf_op jit(solution)/shard_map/all_to_all | solution.py:681
  132.9 2.4 %shard_map.126 = (f32[4,128,128]{2,1,0:T(8,128)}, f32[4,128,128]{2,1,0:T(8,128)}) custom-call(f32[1024,128]{1,0:T(8,128)} %bitcast.13, f32[8,128]{1,0:T(8,128)} %get-tuple-element.57.gain_ref, bf16[768,256]{1,0:T(8,128)(2,1)} %constant.98.clone.back_ref), custom_call_target="tpu_custom_call" | custom-call | tf_op jit(solution)/shard_map/pallas_call | solution.py:604
  (75 shorter events, 20.0 us)
Async XLA Ops:
  9.1 8.9 %collective-permute-start.7 = (f32[64,64,128]{2,1,0:T(8,128)}, f32[64,64,128]{2,1,0:T(8,128)}, u32[]{:S(2)}, u32[]{:S(2)}) collective-permute-start(f32[64,64,128]{2,1,0:T(8,128)} %get-tuple-element.38), channel_id=1, source_target_pairs={{0,1},{1,0},{2,3},{3,2},{4,5},{5,4},{6,7},{7,6},{8,9},{9,8},{10,11... | collective-permute-start | bytes 6291464 | tf_op jit(solution)/shard_map/ppermute | solution.py:629
  10.6 18.0 %collective-permute-start = (f32[64,64,128]{2,1,0:T(8,128)}, f32[64,64,128]{2,1,0:T(8,128)S(1)}, u32[]{:S(2)}, u32[]{:S(2)}) collective-permute-start(f32[64,64,128]{2,1,0:T(8,128)} %get-tuple-element.33), channel_id=1, source_target_pairs={{0,1},{1,0},{2,3},{3,2},{4,5},{5,4},{6,7},{7,6},{8,9},{9,8},{10,11... | collective-permute-start | bytes 6291464 | tf_op jit(solution)/shard_map/ppermute | solution.py:629
  10.7 4.9 %collective-permute-start.8 = (f32[128,128]{1,0:T(8,128)}, f32[128,128]{1,0:T(8,128)S(1)}, u32[]{:S(2)}, u32[]{:S(2)}) collective-permute-start(f32[128,128]{1,0:T(8,128)} %get-tuple-element.40), channel_id=1, source_target_pairs={{0,32},{1,33},{2,34},{3,35},{4,36},{5,37},{6,38},{7,39},{8,40},{9,... | collective-permute-start | bytes 196616 | tf_op jit(solution)/shard_map/ppermute | solution.py:613
  12.0 5.5 %collective-permute-start.9 = (f32[128,128]{1,0:T(8,128)}, f32[128,128]{1,0:T(8,128)S(1)}, u32[]{:S(2)}, u32[]{:S(2)}) collective-permute-start(f32[128,128]{1,0:T(8,128)} %get-tuple-element.41), channel_id=1, source_target_pairs={{0,64},{1,65},{2,66},{3,67},{4,68},{5,69},{6,70},{7,71},{8,72},{9,... | collective-permute-start | bytes 196616 | tf_op jit(solution)/shard_map/ppermute | solution.py:613
  14.4 3.6 %collective-permute-start.10 = (f32[128,128]{1,0:T(8,128)}, f32[128,128]{1,0:T(8,128)S(1)}, u32[]{:S(2)}, u32[]{:S(2)}) collective-permute-start(f32[128,128]{1,0:T(8,128)} %get-tuple-element.42), channel_id=1, source_target_pairs={{0,96},{1,97},{2,98},{3,99},{4,100},{5,101},{6,102},{7,103},{8,104... | collective-permute-start | bytes 196616 | tf_op jit(solution)/shard_map/ppermute | solution.py:613
  23.4 12.1 %collective-permute-start.14 = (f32[136,128]{1,0:T(8,128)}, f32[136,128]{1,0:T(8,128)S(1)}, u32[]{:S(2)}, u32[]{:S(2)}) collective-permute-start(f32[136,128]{1,0:T(8,128)} %get-tuple-element.48), channel_id=1, source_target_pairs={{0,32},{1,3},{2,34},{3,5},{4,36},{5,7},{6,38},{7,1},{8,40},{9,11},... | collective-permute-start | bytes 208904 | tf_op jit(solution)/shard_map/ppermute | solution.py:613
  24.8 12.4 %collective-permute-start.15 = (f32[136,128]{1,0:T(8,128)}, f32[136,128]{1,0:T(8,128)S(1)}, u32[]{:S(2)}, u32[]{:S(2)}) collective-permute-start(f32[136,128]{1,0:T(8,128)} %get-tuple-element.49), channel_id=1, source_target_pairs={{0,64},{1,5},{2,66},{3,7},{4,68},{5,1},{6,70},{7,3},{8,72},{9,13},... | collective-permute-start | bytes 208904 | tf_op jit(solution)/shard_map/ppermute | solution.py:613
  27.5 10.2 %collective-permute-start.16 = (f32[136,128]{1,0:T(8,128)}, f32[136,128]{1,0:T(8,128)S(1)}, u32[]{:S(2)}, u32[]{:S(2)}) collective-permute-start(f32[136,128]{1,0:T(8,128)} %get-tuple-element.50), channel_id=1, source_target_pairs={{0,96},{1,7},{2,98},{3,1},{4,100},{5,3},{6,102},{7,5},{8,104},{9,1... | collective-permute-start | bytes 208904 | tf_op jit(solution)/shard_map/ppermute | solution.py:613
  34.3 15.4 %collective-permute-start.1 = (f32[16,64,128]{2,1,0:T(8,128)}, f32[16,64,128]{2,1,0:T(8,128)S(1)}, u32[]{:S(2)}, u32[]{:S(2)}) collective-permute-start(f32[16,64,128]{2,1,0:T(8,128)} %get-tuple-element.35), channel_id=1, source_target_pairs={{0,32},{1,3},{2,34},{3,5},{4,36},{5,7},{6,38},{7,1},{8,40},{9,11},... | collective-permute-start | bytes 1572872 | tf_op jit(solution)/shard_map/ppermute | solution.py:613
  34.7 15.0 %collective-permute-start.2 = (f32[16,64,128]{2,1,0:T(8,128)}, f32[16,64,128]{2,1,0:T(8,128)S(1)}, u32[]{:S(2)}, u32[]{:S(2)}) collective-permute-start(f32[16,64,128]{2,1,0:T(8,128)} %get-tuple-element.36), channel_id=1, source_target_pairs={{0,64},{1,5},{2,66},{3,7},{4,68},{5,1},{6,70},{7,3},{8,72},{9,13},... | collective-permute-start | bytes 1572872 | tf_op jit(solution)/shard_map/ppermute | solution.py:613
  35.5 14.8 %collective-permute-start.3 = (f32[16,64,128]{2,1,0:T(8,128)}, f32[16,64,128]{2,1,0:T(8,128)S(1)}, u32[]{:S(2)}, u32[]{:S(2)}) collective-permute-start(f32[16,64,128]{2,1,0:T(8,128)} %get-tuple-element.37), channel_id=1, source_target_pairs={{0,96},{1,7},{2,98},{3,1},{4,100},{5,3},{6,102},{7,5},{8,104},{9,1... | collective-permute-start | bytes 1572872 | tf_op jit(solution)/shard_map/ppermute | solution.py:613
  37.2 23.7 %collective-permute-start.11 = (f32[16,64,128]{2,1,0:T(8,128)}, f32[16,64,128]{2,1,0:T(8,128)S(1)}, u32[]{:S(2)}, u32[]{:S(2)}) collective-permute-start(f32[16,64,128]{2,1,0:T(8,128)} %get-tuple-element.44), channel_id=1, source_target_pairs={{0,32},{1,3},{2,34},{3,5},{4,36},{5,7},{6,38},{7,1},{8,40},{9,11},... | collective-permute-start | bytes 1572872 | tf_op jit(solution)/shard_map/ppermute | solution.py:613
  37.7 26.8 %collective-permute-start.12 = (f32[16,64,128]{2,1,0:T(8,128)S(1)}, f32[16,64,128]{2,1,0:T(8,128)S(1)}, u32[]{:S(2)}, u32[]{:S(2)}) collective-permute-start(f32[16,64,128]{2,1,0:T(8,128)S(1)} %copy-done.9), channel_id=1, source_target_pairs={{0,64},{1,5},{2,66},{3,7},{4,68},{5,1},{6,70},{7,3},{8,72},{9,13},... | collective-permute-start | bytes 1572872 | tf_op jit(solution)/shard_map/ppermute | solution.py:613
  49.7 14.8 %collective-permute-start.13 = (f32[16,64,128]{2,1,0:T(8,128)S(1)}, f32[16,64,128]{2,1,0:T(8,128)S(1)}, u32[]{:S(2)}, u32[]{:S(2)}) collective-permute-start(f32[16,64,128]{2,1,0:T(8,128)S(1)} %copy-done.8), channel_id=1, source_target_pairs={{0,96},{1,7},{2,98},{3,1},{4,100},{5,3},{6,102},{7,5},{8,104},{9,1... | collective-permute-start | bytes 1572872 | tf_op jit(solution)/shard_map/ppermute | solution.py:613
  51.5 15.3 %collective-permute-start.4 = (f32[4,64,128]{2,1,0:T(8,128)S(1)}, f32[4,64,128]{2,1,0:T(8,128)S(1)}, u32[]{:S(2)}, u32[]{:S(2)}) collective-permute-start(f32[4,64,128]{2,1,0:T(8,128)S(1)} %get-tuple-element.67), channel_id=1, source_target_pairs={{0,8},{1,9},{2,10},{3,11},{4,12},{5,13},{6,14},{7,15},{8,16},{9,17... | collective-permute-start | bytes 393224 | tf_op jit(solution)/shard_map/ppermute | solution.py:613
  53.2 14.8 %collective-permute-start.6 = (f32[4,64,128]{2,1,0:T(8,128)S(1)}, f32[4,64,128]{2,1,0:T(8,128)S(1)}, u32[]{:S(2)}, u32[]{:S(2)}) collective-permute-start(f32[4,64,128]{2,1,0:T(8,128)S(1)} %get-tuple-element.68), channel_id=1, source_target_pairs={{0,24},{1,25},{2,26},{3,27},{4,28},{5,29},{6,30},{7,31},{8,0},{9,1... | collective-permute-start | bytes 393224 | tf_op jit(solution)/shard_map/ppermute | solution.py:613
  60.9 7.1 %collective-permute-start.5 = (f32[4,64,128]{2,1,0:T(8,128)S(1)}, f32[4,64,128]{2,1,0:T(8,128)S(1)}, u32[]{:S(2)}, u32[]{:S(2)}) collective-permute-start(f32[4,64,128]{2,1,0:T(8,128)S(1)} %get-tuple-element.69), channel_id=1, source_target_pairs={{0,16},{1,17},{2,18},{3,19},{4,20},{5,21},{6,22},{7,23},{8,24},{9,... | collective-permute-start | bytes 393224 | tf_op jit(solution)/shard_map/ppermute | solution.py:613
  64.7 6.6 %collective-permute-start.17 = (f32[4,80,128]{2,1,0:T(8,128)S(1)}, f32[4,80,128]{2,1,0:T(8,128)S(1)}, u32[]{:S(2)}, u32[]{:S(2)}) collective-permute-start(f32[4,80,128]{2,1,0:T(8,128)S(1)} %get-tuple-element.64), channel_id=1, source_target_pairs={{0,8},{1,9},{2,10},{3,11},{4,12},{5,13},{6,14},{7,15},{8,16},{9,17... | collective-permute-start | bytes 491528 | tf_op jit(solution)/shard_map/ppermute | solution.py:613
  65.5 9.4 %collective-permute-start.18 = (f32[4,80,128]{2,1,0:T(8,128)S(1)}, f32[4,80,128]{2,1,0:T(8,128)S(1)}, u32[]{:S(2)}, u32[]{:S(2)}) collective-permute-start(f32[4,80,128]{2,1,0:T(8,128)S(1)} %get-tuple-element.65), channel_id=1, source_target_pairs={{0,16},{1,17},{2,18},{3,19},{4,20},{5,21},{6,22},{7,23},{8,24},{9,... | collective-permute-start | bytes 491528 | tf_op jit(solution)/shard_map/ppermute | solution.py:613
  66.8 9.2 %collective-permute-start.19 = (f32[4,80,128]{2,1,0:T(8,128)S(1)}, f32[4,80,128]{2,1,0:T(8,128)S(1)}, u32[]{:S(2)}, u32[]{:S(2)}) collective-permute-start(f32[4,80,128]{2,1,0:T(8,128)S(1)} %get-tuple-element.66), channel_id=1, source_target_pairs={{0,24},{1,25},{2,26},{3,27},{4,28},{5,29},{6,30},{7,31},{8,0},{9,1... | collective-permute-start | bytes 491528 | tf_op jit(solution)/shard_map/ppermute | solution.py:613
  76.2 4.6 %collective-permute-start.20 = (f32[1,168,128]{2,1,0:T(8,128)S(1)}, f32[1,168,128]{2,1,0:T(8,128)S(1)}, u32[]{:S(2)}, u32[]{:S(2)}) collective-permute-start(f32[1,168,128]{2,1,0:T(8,128)S(1)} %get-tuple-element.70), channel_id=1, source_target_pairs={{0,2},{1,33},{2,4},{3,35},{4,6},{5,37},{6,0},{7,39},{8,10},{9,41},... | collective-permute-start | bytes 258056 | tf_op jit(solution)/shard_map/ppermute | solution.py:613
  76.2 5.0 %collective-permute-start.22 = (f32[1,168,128]{2,1,0:T(8,128)S(1)}, f32[1,168,128]{2,1,0:T(8,128)S(1)}, u32[]{:S(2)}, u32[]{:S(2)}) collective-permute-start(f32[1,168,128]{2,1,0:T(8,128)S(1)} %get-tuple-element.71), channel_id=1, source_target_pairs={{0,6},{1,97},{2,0},{3,99},{4,2},{5,101},{6,4},{7,103},{8,14},{9,10... | collective-permute-start | bytes 258056 | tf_op jit(solution)/shard_map/ppermute | solution.py:613
  78.9 4.8 %collective-permute-start.21 = (f32[1,168,128]{2,1,0:T(8,128)S(1)}, f32[1,168,128]{2,1,0:T(8,128)S(1)}, u32[]{:S(2)}, u32[]{:S(2)}) collective-permute-start(f32[1,168,128]{2,1,0:T(8,128)S(1)} %get-tuple-element.72), channel_id=1, source_target_pairs={{0,4},{1,65},{2,6},{3,67},{4,0},{5,69},{6,2},{7,71},{8,12},{9,73},... | collective-permute-start | bytes 258056 | tf_op jit(solution)/shard_map/ppermute | solution.py:613
  83.8 4.7 %collective-permute-start.23 = (f32[264,128]{1,0:T(8,128)S(1)}, f32[264,128]{1,0:T(8,128)S(1)}, u32[]{:S(2)}, u32[]{:S(2)}) collective-permute-start(f32[264,128]{1,0:T(8,128)S(1)} %bitcast.16), channel_id=1, source_target_pairs={{0,1},{1,0},{2,3},{3,2},{4,5},{5,4},{6,7},{7,6},{8,9},{9,8},{10,11... | collective-permute-start | bytes 405512 | tf_op jit(solution)/shard_map/ppermute | solution.py:629
  (10 other events, 85.2 us)

commit v8 on v4

--- a/solution.py
+++ b/solution.py
@@ -78,7 +78,7 @@
 
 SIDE = 4
 CORES = 2
-ORDERS = ((0, 2, 1), (1, 2, 0))
+ORDERS = ((0, 2, 1), (1, 0, 2))
 
 
 def place_of(device):
@@ -193,10 +193,12 @@
 def grid_kernel(*refs, kept, part, capacity):
     if kept:
         count_ref, list_ref, place_ref, wave_ref, matrix_ref, other_ref = refs[:6]
-        outs = refs[6:]
+        weight_refs = refs[6 : 6 + SIDE] if part else ()
+        outs, row_refs = refs[6 + len(weight_refs) :][:SIDE], refs[6 + len(weight_refs) :][SIDE:]
     else:
-        dest_ref, place_ref, values_ref, matrix_ref, packed_ref, weights_ref = refs[:6]
-        out_refs, (kept_wave_ref, count_ref, list_ref), wave_ref = refs[6:8], refs[8:11], refs[-1]
+        dest_ref, place_ref, values_ref, source_ref, packed_ref, weights_ref = refs[:6]
+        out_refs, (kept_wave_ref, count_ref, list_ref), slice_refs = refs[6:8], refs[8:11], refs[11 : 11 + SIDE]
+        wave_ref, matrix_ref, fetched = refs[-3:]
     nent, rows, width = matrix_ref.shape
     size = width // SIDE
     half = size // 2
@@ -215,9 +217,11 @@
         return 0
 
     def prepare():
+        fetch = pltpu.make_async_copy(source_ref, matrix_ref, fetched)
+        fetch.start()
         lax.fori_loop(0, nslab, clear, 0)
         lax.fori_loop(0, nent, enter, 0)
-        for r, slice_ref in enumerate(refs[11:-1]):
+        for r, slice_ref in enumerate(slice_refs):
             slice_ref[...] = weights_ref[0, :, (place_ref[0] + r) % SIDE, :]
         chip = lax.broadcasted_iota(jnp.int32, (half, half), 0)
         slot = lax.broadcasted_iota(jnp.int32, (half, half), 1)
@@ -239,6 +243,7 @@
             high = wave.astype(jnp.bfloat16)
             low = (wave - high.astype(jnp.float32)).astype(jnp.bfloat16)
             target_ref[...] = jnp.concatenate([high, low], 1).reshape(nent, rows, size)
+        fetch.wait()
 
     if not kept:
         pl.when(step == 0)(prepare)
@@ -285,6 +290,8 @@
 
     if kept:
         products(keep)
+        if part:
+            pl.when(step == STEPS // HALVES - 1)(lambda: weight_kernel(*weight_refs, place_ref, *row_refs))
     else:
         pl.when(step < STEPS // HALVES)(lambda: products(send(out_refs[0])))
         pl.when(step >= STEPS // HALVES)(lambda: products(send(out_refs[1])))
@@ -302,7 +309,11 @@
     in_specs = [scalars if a.dtype == jnp.int32 else fixed(a.shape) for a in args]
     if kept:
         out_shape, out_specs = [f32(SIDE**2, size // HALVES, size)] * SIDE, [moving(SIDE**2)] * SIDE
-        in_specs[-1] = moving(blocks)
+        in_specs[5] = moving(blocks)
+        if part:
+            rows_shape = (SIDE**2 * 8 + 8, size)
+            out_shape = out_shape + [f32(*rows_shape)] * SIDE
+            out_specs = out_specs + [fixed(rows_shape)] * SIDE
         scratch = []
     else:
         wave = (nent, rows, size)
@@ -316,7 +327,8 @@
             pl.BlockSpec(block, lambda i: (0, jnp.minimum(i, STEPS // HALVES - 1), 0)),
             pl.BlockSpec(block, lambda i: (0, jnp.maximum(i - STEPS // HALVES, 0), 0)),
         ] + [fixed(wave), scalars, scalars] + [fixed((size, size))] * SIDE
-        scratch = [pltpu.VMEM(wave, jnp.bfloat16)]
+        in_specs[3] = pl.BlockSpec(memory_space=pl.ANY)
+        scratch = [pltpu.VMEM(wave, jnp.bfloat16), pltpu.VMEM(matrix.shape, jnp.bfloat16), pltpu.SemaphoreType.DMA]
     return pl.pallas_call(
         functools.partial(grid_kernel, kept=kept, part=part, capacity=capacity),
         grid=(steps,),
@@ -593,7 +605,6 @@
         step == 0, x, jnp.where(step == 1, y, jnp.where(step == 2, z, jnp.where(step == 3, core, chip == 0)))
     ).astype(jnp.int32)
 
-    together = lax.optimization_barrier
     *away, wave, counts, lists, p0, p1, p2, p3 = grid_call(
         False, 0, ngrid, capacity, dest_slab[:, 0], place, intensities, gridding, table["packed"], spectral_weights
     )
@@ -605,10 +616,9 @@
     least = lambda parts: functools.reduce(jnp.minimum, parts)
     data = []
     for part in range(HALVES):
-        kept = grid_call(True, part, ngrid, capacity, *members, arrived[part])
+        kept = grid_call(True, part, ngrid, capacity, *members, arrived[part], *(weights if part else ()))
+        kept, rows = kept[:SIDE], kept[SIDE:]
         data.append(exchange(kept, axes[0]))
-    kept, weights = together((kept, weights))
-    rows = call(weight_kernel, [(SIDE**2 * 8 + 8, size)] * SIDE, *weights, place)
     rows = exchange(rows, axes[0])
     parts = quarter(summed(data[0]))
     early = exchange(parts, axes[1])

time: 134 us -> 142 us (1.060)
  starting transfers between devices: 35.3 us -> 40.5 us
  blocking collectives: 34.1 us -> 37.4 us
  Pallas kernels: 31.2 us -> 29 us
    ppermute x3, starting transfers between devices: 5.08 us -> 12.2 us  [body(): swap = lambda a: lax.ppermute(a, ALL, shift_pairs((3, 3), 1))]
    all_to_all x1, blocking collectives: 15.2 us -> 18.2 us  [body(): lax.all_to_all(send.reshape(count, 1, size), ALL, 0, 0, tiled=True)]
    pallas_call x4 -> x3, Pallas kernels: 14.1 us -> 12 us  [call(): pl.pallas_call(kernel, out_shape=[jax.ShapeDtypeStruct(s, jnp.float32) fo...]
    ppermute x21, starting transfers between devices: 30.3 us -> 28.3 us  [exchange(): lax.ppermute(parts[r], ALL, shift_pairs(axes, r))]
  transfers between devices with their start and end apart: 24 -> 24, of which waited for: 9 -> 11; matrix products, arithmetic and copies ran while one was open for 1% -> 1% of each run, Pallas kernels for 8% -> 6%
where the time goes in v8:
time: 142 us; the launch traced here: 141 us
  starting transfers between devices  40.5 us (29%)
  blocking collectives  37.4 us (26%)
  Pallas kernels  29 us (20%)
  waiting for transfers between devices  28.9 us (20%)
  local copies, waits for them, and re-layouts  2.72 us (2%)
  other arithmetic  2.05 us (1%)
    ppermute x21, starting transfers between devices, exchange(): lax.ppermute(parts[r], ALL, shift_pairs(axes, r))  28.3 us
    ppermute x21, waiting for transfers between devices, exchange(): lax.ppermute(parts[r], ALL, shift_pairs(axes, r))  27.9 us
    all_to_all x1, blocking collectives, body(): lax.all_to_all(back.reshape(count, 2 * planes, size), ALL, 0, 0, tiled=True)  19.2 us
    all_to_all x1, blocking collectives, body(): lax.all_to_all(send.reshape(count, 1, size), ALL, 0, 0, tiled=True)  18.2 us
    pallas_call x3, Pallas kernels, grid_call(): pl.pallas_call(functools.partial(grid_kernel, kept=kept, part=part, capac...  17 us
    ppermute x3, starting transfers between devices, body(): swap = lambda a: lax.ppermute(a, ALL, shift_pairs((3, 3), 1))  12.2 us
    pallas_call x3, Pallas kernels, call(): pl.pallas_call(kernel, out_shape=[jax.ShapeDtypeStruct(s, jnp.float32) fo...  12 us
  transfers between devices with their start and end apart: 24, of which 11 were waited for; matrix products, arithmetic and copies ran while one was open for 1% of the time, Pallas kernels for 6%

profile of v8, /device:TPU:1, one launch (start us, length us, event | category | flops | bytes accessed | tf_op | source)
XLA Modules:
  0.0 141.5 jit_solution(10497057229208751705)
XLA Ops:
  1.3 7.8 %shard_map.122 = (f32[64,64,128]{2,1,0:T(8,128)}, f32[64,64,128]{2,1,0:T(8,128)}, bf16[64,32,128]{2,1,0:T(8,128)(2,1)}, s32[32]{0:T(128)}, s32[128]{0:T(128)}, /...) custom-call(s32[64]{0:T(128)} %bitcast.20, ...), custom_call_target="tpu_custom_call" | custom-call | tf_op jit(solution)/shard_map/pallas_call | solution.py:332
  9.1 1.4 %collective-permute-start.7 = (f32[64,64,128]{2,1,0:T(8,128)}, f32[64,64,128]{2,1,0:T(8,128)}, u32[]{:S(2)}, u32[]{:S(2)}) collective-permute-start(f32[64,64,128]{2,1,0:T(8,128)} %get-tuple-element.38), channel_id=1, source_target_pairs={{0,1},{1,0},{2,3},{3,2},{4,5},{5,4},{6,7},{7,6},{8,9},{9,8},{10,11... | collective-permute-start | bytes 6291464 | tf_op jit(solution)/shard_map/ppermute | solution.py:598
  12.0 2.4 %collective-permute-start.9 = (f32[128,128]{1,0:T(8,128)}, f32[128,128]{1,0:T(8,128)S(1)}, u32[]{:S(2)}, u32[]{:S(2)}) collective-permute-start(f32[128,128]{1,0:T(8,128)} %get-tuple-element.41), channel_id=1, source_target_pairs={{0,64},{1,65},{2,66},{3,67},{4,68},{5,69},{6,70},{7,71},{8,72},{9,... | collective-permute-start | bytes 196616 | tf_op jit(solution)/shard_map/ppermute | solution.py:582
  15.6 1.9 %collective-permute-done.9.refs_8_ = f32[128,128]{1,0:T(8,128)S(1)} collective-permute-done((f32[128,128]{1,0:T(8,128)}, f32[128,128]{1,0:T(8,128)S(1)}, u32[]{:S(2)}, u32[]{:S(2)}) %collective-permute-start.9) | collective-permute-done | bytes 65568 | tf_op jit(solution)/shard_map/ppermute | solution.py:582
  18.6 4.8 %shard_map.124 = (f32[16,64,128]{2,1,0:T(8,128)}, f32[16,64,128]{2,1,0:T(8,128)}, f32[16,64,128]{2,1,0:T(8,128)}, f32[16,64,128]{2,1,0:T(8,128)}, f32[136,128]{1...) custom-call(s32[32]{0:T(128)} %get-tuple-element.30.refs_0_, ...), custom_call_target="tpu_custom_call" | custom-call | tf_op jit(solution)/shard_map/pallas_call | solution.py:332
  23.5 1.4 collective-permute-start.14
  24.8 2.6 %collective-permute-start.15 = (f32[136,128]{1,0:T(8,128)}, f32[136,128]{1,0:T(8,128)S(1)}, u32[]{:S(2)}, u32[]{:S(2)}) collective-permute-start(f32[136,128]{1,0:T(8,128)} %get-tuple-element.49), channel_id=1, source_target_pairs={{0,64},{1,5},{2,66},{3,7},{4,68},{5,1},{6,70},{7,3},{8,72},{9,13},... | collective-permute-start | bytes 208904 | tf_op jit(solution)/shard_map/ppermute | solution.py:582
  29.9 4.4 %shard_map.123 = (f32[16,64,128]{2,1,0:T(8,128)}, f32[16,64,128]{2,1,0:T(8,128)}, f32[16,64,128]{2,1,0:T(8,128)}, f32[16,64,128]{2,1,0:T(8,128)}) custom-call(s32[32]{0:T(128)} %get-tuple-element.30.refs_0_, s32[128]{0:T(128)} %get-tuple-element.31.refs_1_, s32[5]{0:T(128)} %compare_select_fusion.3.refs_1_.refs_2_.place_ref, ...), custom_call_target="tpu_custom_call" | custom-call | tf_op jit(solution)/shard_map/pallas_call | solution.py:332
  35.6 1.7 %collective-permute-start.3 = (f32[16,64,128]{2,1,0:T(8,128)}, f32[16,64,128]{2,1,0:T(8,128)S(1)}, u32[]{:S(2)}, u32[]{:S(2)}) collective-permute-start(f32[16,64,128]{2,1,0:T(8,128)} %get-tuple-element.37), channel_id=1, source_target_pairs={{0,96},{1,7},{2,98},{3,1},{4,100},{5,3},{6,102},{7,5},{8,104},{9,1... | collective-permute-start | bytes 1572872 | tf_op jit(solution)/shard_map/ppermute | solution.py:582
  37.7 1.8 %collective-permute-start.12 = (f32[16,64,128]{2,1,0:T(8,128)S(1)}, f32[16,64,128]{2,1,0:T(8,128)S(1)}, u32[]{:S(2)}, u32[]{:S(2)}) collective-permute-start(f32[16,64,128]{2,1,0:T(8,128)S(1)} %copy-done.9), channel_id=1, source_target_pairs={{0,64},{1,5},{2,66},{3,7},{4,68},{5,1},{6,70},{7,3},{8,72},{9,13},... | collective-permute-start | bytes 1572872 | tf_op jit(solution)/shard_map/ppermute | solution.py:582
  39.5 10.2 %collective-permute-done.1 = f32[16,64,128]{2,1,0:T(8,128)S(1)} collective-permute-done((f32[16,64,128]{2,1,0:T(8,128)}, f32[16,64,128]{2,1,0:T(8,128)S(1)}, u32[]{:S(2)}, u32[]{:S(2)}) %collective-permute-start.1) | collective-permute-done | bytes 524320 | tf_op jit(solution)/shard_map/ppermute | solution.py:582
  51.7 2.6 %collective-permute-start.6 = (f32[4,64,128]{2,1,0:T(8,128)S(1)}, f32[4,64,128]{2,1,0:T(8,128)S(1)}, u32[]{:S(2)}, u32[]{:S(2)}) collective-permute-start(f32[4,64,128]{2,1,0:T(8,128)S(1)} %get-tuple-element.68), channel_id=1, source_target_pairs={{0,24},{1,97},{2,26},{3,99},{4,28},{5,101},{6,30},{7,103},{8,0},{9... | collective-permute-start | bytes 393224 | tf_op jit(solution)/shard_map/ppermute | solution.py:582
  54.3 6.6 %collective-permute-done.11 = f32[16,64,128]{2,1,0:T(8,128)S(1)} collective-permute-done((f32[16,64,128]{2,1,0:T(8,128)}, f32[16,64,128]{2,1,0:T(8,128)S(1)}, u32[]{:S(2)}, u32[]{:S(2)}) %collective-permute-start.11) | collective-permute-done | bytes 524320 | tf_op jit(solution)/shard_map/ppermute | solution.py:582
  66.4 1.6 %collective-permute-done.17 = f32[4,80,128]{2,1,0:T(8,128)S(1)} collective-permute-done((f32[4,80,128]{2,1,0:T(8,128)S(1)}, f32[4,80,128]{2,1,0:T(8,128)S(1)}, u32[]{:S(2)}, u32[]{:S(2)}) %collective-permute-start.17) | collective-permute-done | bytes 163872 | tf_op jit(solution)/shard_map/ppermute | solution.py:582
  68.0 2.0 %collective-permute-done.18 = f32[4,80,128]{2,1,0:T(8,128)S(1)} collective-permute-done((f32[4,80,128]{2,1,0:T(8,128)S(1)}, f32[4,80,128]{2,1,0:T(8,128)S(1)}, u32[]{:S(2)}, u32[]{:S(2)}) %collective-permute-start.18) | collective-permute-done | bytes 163872 | tf_op jit(solution)/shard_map/ppermute | solution.py:582
  70.7 1.7 %collective-permute-start.20 = (f32[1,168,128]{2,1,0:T(8,128)S(1)}, f32[1,168,128]{2,1,0:T(8,128)S(1)}, u32[]{:S(2)}, u32[]{:S(2)}) collective-permute-start(f32[1,168,128]{2,1,0:T(8,128)S(1)} %get-tuple-element.70), channel_id=1, source_target_pairs={{0,2},{1,9},{2,4},{3,11},{4,6},{5,13},{6,0},{7,15},{8,10},{9,17},{... | collective-permute-start | bytes 258056 | tf_op jit(solution)/shard_map/ppermute | solution.py:582
  72.4 2.4 %collective-permute-start.22 = (f32[1,168,128]{2,1,0:T(8,128)S(1)}, f32[1,168,128]{2,1,0:T(8,128)S(1)}, u32[]{:S(2)}, u32[]{:S(2)}) collective-permute-start(f32[1,168,128]{2,1,0:T(8,128)S(1)} %get-tuple-element.71), channel_id=1, source_target_pairs={{0,6},{1,25},{2,0},{3,27},{4,2},{5,29},{6,4},{7,31},{8,14},{9,1},{... | collective-permute-start | bytes 258056 | tf_op jit(solution)/shard_map/ppermute | solution.py:582
  77.2 2.5 %collective-permute-done.21 = f32[1,168,128]{2,1,0:T(8,128)S(1)} collective-permute-done((f32[1,168,128]{2,1,0:T(8,128)S(1)}, f32[1,168,128]{2,1,0:T(8,128)S(1)}, u32[]{:S(2)}, u32[]{:S(2)}) %collective-permute-start.21) | collective-permute-done | bytes 86048 | tf_op jit(solution)/shard_map/ppermute | solution.py:582
  79.8 10.7 %collective-permute-start.23 = (f32[264,128]{1,0:T(8,128)S(1)}, f32[264,128]{1,0:T(8,128)S(1)}, u32[]{:S(2)}, u32[]{:S(2)}) collective-permute-start(f32[264,128]{1,0:T(8,128)S(1)} %bitcast.16), channel_id=1, source_target_pairs={{0,1},{1,0},{2,3},{3,2},{4,5},{5,4},{6,7},{7,6},{8,9},{9,8},{10,11... | collective-permute-start | bytes 405512 | tf_op jit(solution)/shard_map/ppermute | solution.py:598
  92.1 4.5 %shard_map.125 = (f32[128,128]{1,0:T(8,128)}, f32[128,128]{1,0:T(8,128)}, f32[128,128]{1,0:T(8,128)}, f32[8,128]{1,0:T(8,128)}, f32[128,128]{1,0:T(8,128)}) custom-call(f32[264,128]{1,0:T(8,128)} %bitcast.17, f32[264,128]{1,0:T(8,128)} %copy-done.3, s32[5]{0:T(128)} %compare_select_fusion.3.refs_1_.refs_2_.place_ref, f32[128,256]{1,0:T(8,128)} %constant.93.clone.lanes_ref, ...), custom_call_target="tpu_custom_call" | custom-call | tf_op jit(solution)/shard_map/pallas_call | solution.py:573
  96.6 18.2 %all_to_all.10 = f32[128,1,128]{2,1,0:T(1,128)} all-to-all(f32[128,1,128]{2,1,0:T(1,128)} %bitcast.19), channel_id=1, replica_groups=mesh['dp'=4,'grid'=32] {'dp','grid'}, dimensions={0} | all-to-all | bytes 131072 | tf_op jit(solution)/shard_map/all_to_all | solution.py:646
  114.8 5.2 %shard_map.126 = (f32[1024,128]{1,0:T(8,128)}, f32[8,128]{1,0:T(8,128)}) custom-call(f32[128,128]{1,0:T(8,128)} %bitcast.18, f32[8,128]{1,0:T(8,128)} %get-tuple-element.52.range_ref, f32[128,128]{1,0:T(8,128)} %get-tuple-element.53.scaled_ref, f32[128,128]{1,0:T(8,128)} %get-tuple-element.54.real_ref, f32[128,128]{1,0:T(8,128)} %get-tuple-element.55.imag_ref, ...), custom_call_target="tpu_custom_call" | custom-call | tf_op jit(solution)/shard_map/pallas_call | solution.py:573
  119.9 19.2 %all_to_all.11 = f32[128,8,128]{2,1,0:T(8,128)} all-to-all(f32[128,8,128]{2,1,0:T(8,128)} %bitcast.14), channel_id=1, replica_groups=mesh['dp'=4,'grid'=32] {'dp','grid'}, dimensions={0} | all-to-all | bytes 1048576 | tf_op jit(solution)/shard_map/all_to_all | solution.py:651
  139.1 2.4 %shard_map.127 = (f32[4,128,128]{2,1,0:T(8,128)}, f32[4,128,128]{2,1,0:T(8,128)}) custom-call(f32[1024,128]{1,0:T(8,128)} %bitcast.13, f32[8,128]{1,0:T(8,128)} %get-tuple-element.57.gain_ref, bf16[768,256]{1,0:T(8,128)(2,1)} %constant.98.clone.back_ref), custom_call_target="tpu_custom_call" | custom-call | tf_op jit(solution)/shard_map/pallas_call | solution.py:573
  (75 shorter events, 20.6 us)
Async XLA Ops:
  9.1 8.9 %collective-permute-start.7 = (f32[64,64,128]{2,1,0:T(8,128)}, f32[64,64,128]{2,1,0:T(8,128)}, u32[]{:S(2)}, u32[]{:S(2)}) collective-permute-start(f32[64,64,128]{2,1,0:T(8,128)} %get-tuple-element.38), channel_id=1, source_target_pairs={{0,1},{1,0},{2,3},{3,2},{4,5},{5,4},{6,7},{7,6},{8,9},{9,8},{10,11... | collective-permute-start | bytes 6291464 | tf_op jit(solution)/shard_map/ppermute | solution.py:598
  10.6 18.0 %collective-permute-start = (f32[64,64,128]{2,1,0:T(8,128)}, f32[64,64,128]{2,1,0:T(8,128)S(1)}, u32[]{:S(2)}, u32[]{:S(2)}) collective-permute-start(f32[64,64,128]{2,1,0:T(8,128)} %get-tuple-element.33), channel_id=1, source_target_pairs={{0,1},{1,0},{2,3},{3,2},{4,5},{5,4},{6,7},{7,6},{8,9},{9,8},{10,11... | collective-permute-start | bytes 6291464 | tf_op jit(solution)/shard_map/ppermute | solution.py:598
  10.6 4.9 %collective-permute-start.8 = (f32[128,128]{1,0:T(8,128)}, f32[128,128]{1,0:T(8,128)S(1)}, u32[]{:S(2)}, u32[]{:S(2)}) collective-permute-start(f32[128,128]{1,0:T(8,128)} %get-tuple-element.40), channel_id=1, source_target_pairs={{0,32},{1,33},{2,34},{3,35},{4,36},{5,37},{6,38},{7,39},{8,40},{9,... | collective-permute-start | bytes 196616 | tf_op jit(solution)/shard_map/ppermute | solution.py:582
  12.0 5.5 %collective-permute-start.9 = (f32[128,128]{1,0:T(8,128)}, f32[128,128]{1,0:T(8,128)S(1)}, u32[]{:S(2)}, u32[]{:S(2)}) collective-permute-start(f32[128,128]{1,0:T(8,128)} %get-tuple-element.41), channel_id=1, source_target_pairs={{0,64},{1,65},{2,66},{3,67},{4,68},{5,69},{6,70},{7,71},{8,72},{9,... | collective-permute-start | bytes 196616 | tf_op jit(solution)/shard_map/ppermute | solution.py:582
  14.4 3.6 %collective-permute-start.10 = (f32[128,128]{1,0:T(8,128)}, f32[128,128]{1,0:T(8,128)S(1)}, u32[]{:S(2)}, u32[]{:S(2)}) collective-permute-start(f32[128,128]{1,0:T(8,128)} %get-tuple-element.42), channel_id=1, source_target_pairs={{0,96},{1,97},{2,98},{3,99},{4,100},{5,101},{6,102},{7,103},{8,104... | collective-permute-start | bytes 196616 | tf_op jit(solution)/shard_map/ppermute | solution.py:582
  23.5 12.1 %collective-permute-start.14 = (f32[136,128]{1,0:T(8,128)}, f32[136,128]{1,0:T(8,128)S(1)}, u32[]{:S(2)}, u32[]{:S(2)}) collective-permute-start(f32[136,128]{1,0:T(8,128)} %get-tuple-element.48), channel_id=1, source_target_pairs={{0,32},{1,3},{2,34},{3,5},{4,36},{5,7},{6,38},{7,1},{8,40},{9,11},... | collective-permute-start | bytes 208904 | tf_op jit(solution)/shard_map/ppermute | solution.py:582
  24.8 12.4 %collective-permute-start.15 = (f32[136,128]{1,0:T(8,128)}, f32[136,128]{1,0:T(8,128)S(1)}, u32[]{:S(2)}, u32[]{:S(2)}) collective-permute-start(f32[136,128]{1,0:T(8,128)} %get-tuple-element.49), channel_id=1, source_target_pairs={{0,64},{1,5},{2,66},{3,7},{4,68},{5,1},{6,70},{7,3},{8,72},{9,13},... | collective-permute-start | bytes 208904 | tf_op jit(solution)/shard_map/ppermute | solution.py:582
  27.5 10.2 %collective-permute-start.16 = (f32[136,128]{1,0:T(8,128)}, f32[136,128]{1,0:T(8,128)S(1)}, u32[]{:S(2)}, u32[]{:S(2)}) collective-permute-start(f32[136,128]{1,0:T(8,128)} %get-tuple-element.50), channel_id=1, source_target_pairs={{0,96},{1,7},{2,98},{3,1},{4,100},{5,3},{6,102},{7,5},{8,104},{9,1... | collective-permute-start | bytes 208904 | tf_op jit(solution)/shard_map/ppermute | solution.py:582
  34.3 15.4 %collective-permute-start.1 = (f32[16,64,128]{2,1,0:T(8,128)}, f32[16,64,128]{2,1,0:T(8,128)S(1)}, u32[]{:S(2)}, u32[]{:S(2)}) collective-permute-start(f32[16,64,128]{2,1,0:T(8,128)} %get-tuple-element.35), channel_id=1, source_target_pairs={{0,32},{1,3},{2,34},{3,5},{4,36},{5,7},{6,38},{7,1},{8,40},{9,11},... | collective-permute-start | bytes 1572872 | tf_op jit(solution)/shard_map/ppermute | solution.py:582
  34.7 15.0 %collective-permute-start.2 = (f32[16,64,128]{2,1,0:T(8,128)}, f32[16,64,128]{2,1,0:T(8,128)S(1)}, u32[]{:S(2)}, u32[]{:S(2)}) collective-permute-start(f32[16,64,128]{2,1,0:T(8,128)} %get-tuple-element.36), channel_id=1, source_target_pairs={{0,64},{1,5},{2,66},{3,7},{4,68},{5,1},{6,70},{7,3},{8,72},{9,13},... | collective-permute-start | bytes 1572872 | tf_op jit(solution)/shard_map/ppermute | solution.py:582
  35.6 14.8 %collective-permute-start.3 = (f32[16,64,128]{2,1,0:T(8,128)}, f32[16,64,128]{2,1,0:T(8,128)S(1)}, u32[]{:S(2)}, u32[]{:S(2)}) collective-permute-start(f32[16,64,128]{2,1,0:T(8,128)} %get-tuple-element.37), channel_id=1, source_target_pairs={{0,96},{1,7},{2,98},{3,1},{4,100},{5,3},{6,102},{7,5},{8,104},{9,1... | collective-permute-start | bytes 1572872 | tf_op jit(solution)/shard_map/ppermute | solution.py:582
  37.2 23.7 %collective-permute-start.11 = (f32[16,64,128]{2,1,0:T(8,128)}, f32[16,64,128]{2,1,0:T(8,128)S(1)}, u32[]{:S(2)}, u32[]{:S(2)}) collective-permute-start(f32[16,64,128]{2,1,0:T(8,128)} %get-tuple-element.44), channel_id=1, source_target_pairs={{0,32},{1,3},{2,34},{3,5},{4,36},{5,7},{6,38},{7,1},{8,40},{9,11},... | collective-permute-start | bytes 1572872 | tf_op jit(solution)/shard_map/ppermute | solution.py:582
  37.7 24.6 %collective-permute-start.12 = (f32[16,64,128]{2,1,0:T(8,128)S(1)}, f32[16,64,128]{2,1,0:T(8,128)S(1)}, u32[]{:S(2)}, u32[]{:S(2)}) collective-permute-start(f32[16,64,128]{2,1,0:T(8,128)S(1)} %copy-done.9), channel_id=1, source_target_pairs={{0,64},{1,5},{2,66},{3,7},{4,68},{5,1},{6,70},{7,3},{8,72},{9,13},... | collective-permute-start | bytes 1572872 | tf_op jit(solution)/shard_map/ppermute | solution.py:582
  49.7 12.6 %collective-permute-start.13 = (f32[16,64,128]{2,1,0:T(8,128)S(1)}, f32[16,64,128]{2,1,0:T(8,128)S(1)}, u32[]{:S(2)}, u32[]{:S(2)}) collective-permute-start(f32[16,64,128]{2,1,0:T(8,128)S(1)} %copy-done.8), channel_id=1, source_target_pairs={{0,96},{1,7},{2,98},{3,1},{4,100},{5,3},{6,102},{7,5},{8,104},{9,1... | collective-permute-start | bytes 1572872 | tf_op jit(solution)/shard_map/ppermute | solution.py:582
  51.5 13.6 %collective-permute-start.4 = (f32[4,64,128]{2,1,0:T(8,128)S(1)}, f32[4,64,128]{2,1,0:T(8,128)S(1)}, u32[]{:S(2)}, u32[]{:S(2)}) collective-permute-start(f32[4,64,128]{2,1,0:T(8,128)S(1)} %get-tuple-element.67), channel_id=1, source_target_pairs={{0,8},{1,33},{2,10},{3,35},{4,12},{5,37},{6,14},{7,39},{8,16},{9,4... | collective-permute-start | bytes 393224 | tf_op jit(solution)/shard_map/ppermute | solution.py:582
  51.7 14.7 %collective-permute-start.6 = (f32[4,64,128]{2,1,0:T(8,128)S(1)}, f32[4,64,128]{2,1,0:T(8,128)S(1)}, u32[]{:S(2)}, u32[]{:S(2)}) collective-permute-start(f32[4,64,128]{2,1,0:T(8,128)S(1)} %get-tuple-element.68), channel_id=1, source_target_pairs={{0,24},{1,97},{2,26},{3,99},{4,28},{5,101},{6,30},{7,103},{8,0},{9... | collective-permute-start | bytes 393224 | tf_op jit(solution)/shard_map/ppermute | solution.py:582
  60.9 5.5 %collective-permute-start.5 = (f32[4,64,128]{2,1,0:T(8,128)S(1)}, f32[4,64,128]{2,1,0:T(8,128)S(1)}, u32[]{:S(2)}, u32[]{:S(2)}) collective-permute-start(f32[4,64,128]{2,1,0:T(8,128)S(1)} %get-tuple-element.69), channel_id=1, source_target_pairs={{0,16},{1,65},{2,18},{3,67},{4,20},{5,69},{6,22},{7,71},{8,24},{9,... | collective-permute-start | bytes 393224 | tf_op jit(solution)/shard_map/ppermute | solution.py:582
  62.5 5.5 %collective-permute-start.17 = (f32[4,80,128]{2,1,0:T(8,128)S(1)}, f32[4,80,128]{2,1,0:T(8,128)S(1)}, u32[]{:S(2)}, u32[]{:S(2)}) collective-permute-start(f32[4,80,128]{2,1,0:T(8,128)S(1)} %get-tuple-element.64), channel_id=1, source_target_pairs={{0,8},{1,33},{2,10},{3,35},{4,12},{5,37},{6,14},{7,39},{8,16},{9,4... | collective-permute-start | bytes 491528 | tf_op jit(solution)/shard_map/ppermute | solution.py:582
  63.9 6.2 %collective-permute-start.18 = (f32[4,80,128]{2,1,0:T(8,128)S(1)}, f32[4,80,128]{2,1,0:T(8,128)S(1)}, u32[]{:S(2)}, u32[]{:S(2)}) collective-permute-start(f32[4,80,128]{2,1,0:T(8,128)S(1)} %get-tuple-element.65), channel_id=1, source_target_pairs={{0,16},{1,65},{2,18},{3,67},{4,20},{5,69},{6,22},{7,71},{8,24},{9,... | collective-permute-start | bytes 491528 | tf_op jit(solution)/shard_map/ppermute | solution.py:582
  65.2 5.5 %collective-permute-start.19 = (f32[4,80,128]{2,1,0:T(8,128)S(1)}, f32[4,80,128]{2,1,0:T(8,128)S(1)}, u32[]{:S(2)}, u32[]{:S(2)}) collective-permute-start(f32[4,80,128]{2,1,0:T(8,128)S(1)} %get-tuple-element.66), channel_id=1, source_target_pairs={{0,24},{1,97},{2,26},{3,99},{4,28},{5,101},{6,30},{7,103},{8,0},{9... | collective-permute-start | bytes 491528 | tf_op jit(solution)/shard_map/ppermute | solution.py:582
  70.7 6.5 %collective-permute-start.20 = (f32[1,168,128]{2,1,0:T(8,128)S(1)}, f32[1,168,128]{2,1,0:T(8,128)S(1)}, u32[]{:S(2)}, u32[]{:S(2)}) collective-permute-start(f32[1,168,128]{2,1,0:T(8,128)S(1)} %get-tuple-element.70), channel_id=1, source_target_pairs={{0,2},{1,9},{2,4},{3,11},{4,6},{5,13},{6,0},{7,15},{8,10},{9,17},{... | collective-permute-start | bytes 258056 | tf_op jit(solution)/shard_map/ppermute | solution.py:582
  72.4 4.8 %collective-permute-start.22 = (f32[1,168,128]{2,1,0:T(8,128)S(1)}, f32[1,168,128]{2,1,0:T(8,128)S(1)}, u32[]{:S(2)}, u32[]{:S(2)}) collective-permute-start(f32[1,168,128]{2,1,0:T(8,128)S(1)} %get-tuple-element.71), channel_id=1, source_target_pairs={{0,6},{1,25},{2,0},{3,27},{4,2},{5,29},{6,4},{7,31},{8,14},{9,1},{... | collective-permute-start | bytes 258056 | tf_op jit(solution)/shard_map/ppermute | solution.py:582
  74.8 4.8 %collective-permute-start.21 = (f32[1,168,128]{2,1,0:T(8,128)S(1)}, f32[1,168,128]{2,1,0:T(8,128)S(1)}, u32[]{:S(2)}, u32[]{:S(2)}) collective-permute-start(f32[1,168,128]{2,1,0:T(8,128)S(1)} %get-tuple-element.72), channel_id=1, source_target_pairs={{0,4},{1,17},{2,6},{3,19},{4,0},{5,21},{6,2},{7,23},{8,12},{9,25},... | collective-permute-start | bytes 258056 | tf_op jit(solution)/shard_map/ppermute | solution.py:582
  79.8 11.7 %collective-permute-start.23 = (f32[264,128]{1,0:T(8,128)S(1)}, f32[264,128]{1,0:T(8,128)S(1)}, u32[]{:S(2)}, u32[]{:S(2)}) collective-permute-start(f32[264,128]{1,0:T(8,128)S(1)} %bitcast.16), channel_id=1, source_target_pairs={{0,1},{1,0},{2,3},{3,2},{4,5},{5,4},{6,7},{7,6},{8,9},{9,8},{10,11... | collective-permute-start | bytes 405512 | tf_op jit(solution)/shard_map/ppermute | solution.py:598
  (10 other events, 89.8 us)

commit v9 on v8

--- a/solution.py
+++ b/solution.py
@@ -78,7 +78,7 @@
 
 SIDE = 4
 CORES = 2
-ORDERS = ((0, 2, 1), (1, 0, 2))
+ORDERS = ((0, 2, 1), (1, 2, 0))
 
 
 def place_of(device):
@@ -579,7 +579,8 @@
 
 
 def exchange(parts, axes):
-    return [parts[0]] + [lax.ppermute(parts[r], ALL, shift_pairs(axes, r)) for r in range(1, SIDE)]
+    arrived = {r: lax.ppermute(parts[r], ALL, shift_pairs(axes, r)) for r in (2, 1, 3)}
+    return [parts[0], arrived[1], arrived[2], arrived[3]]
 
 
 def summed(parts):

time: 142 us -> 135 us (0.951)
  starting transfers between devices: 40.5 us -> 34 us
  blocking collectives: 37.4 us -> 33.6 us
  waiting for transfers between devices: 28.9 us -> 32.6 us
    ppermute x3, starting transfers between devices: 12.2 us -> 5.3 us  [body(): swap = lambda a: lax.ppermute(a, ALL, shift_pairs((3, 3), 1))]
    all_to_all x1, blocking collectives: 18.2 us -> 14.4 us  [body(): lax.all_to_all(send.reshape(count, 1, size), ALL, 0, 0, tiled=True)]
    ppermute x21, waiting for transfers between devices: 27.9 us -> 31.6 us  [exchange(): lax.ppermute(parts[r], ALL, shift_pairs(axes, r))]
  transfers between devices with their start and end apart: 24 -> 24, of which waited for: 11 -> 12; matrix products, arithmetic and copies ran while one was open for 1% -> 1% of each run, Pallas kernels for 6% -> 7%
where the time goes in v9:
time: 135 us
  starting transfers between devices  34 us (25%)
  blocking collectives  33.6 us (25%)
  waiting for transfers between devices  32.6 us (24%)
  Pallas kernels  29 us (21%)
  local copies, waits for them, and re-layouts  2.72 us (2%)
  other arithmetic  2.05 us (2%)
    ppermute x21, waiting for transfers between devices, exchange(): lax.ppermute(parts[r], ALL, shift_pairs(axes, r))  31.6 us
    ppermute x21, starting transfers between devices, exchange(): lax.ppermute(parts[r], ALL, shift_pairs(axes, r))  28.7 us
    all_to_all x1, blocking collectives, body(): lax.all_to_all(back.reshape(count, 2 * planes, size), ALL, 0, 0, tiled=True)  19.2 us
    pallas_call x3, Pallas kernels, grid_call(): pl.pallas_call(functools.partial(grid_kernel, kept=kept, part=part, capac...  17 us
    all_to_all x1, blocking collectives, body(): lax.all_to_all(send.reshape(count, 1, size), ALL, 0, 0, tiled=True)  14.4 us
    pallas_call x3, Pallas kernels, call(): pl.pallas_call(kernel, out_shape=[jax.ShapeDtypeStruct(s, jnp.float32) fo...  12 us
    ppermute x3, starting transfers between devices, body(): swap = lambda a: lax.ppermute(a, ALL, shift_pairs((3, 3), 1))  5.3 us
  transfers between devices with their start and end apart: 24, of which 12 were waited for; matrix products, arithmetic and copies ran while one was open for 1% of the time, Pallas kernels for 7%

profile of v9, /device:TPU:1, one launch (start us, length us, event | category | flops | bytes accessed | tf_op | source)
XLA Modules:
  0.0 134.8 jit_solution(15318651125855214493)
XLA Ops:
  1.3 7.8 %shard_map.122 = (f32[64,64,128]{2,1,0:T(8,128)}, f32[64,64,128]{2,1,0:T(8,128)}, bf16[64,32,128]{2,1,0:T(8,128)(2,1)}, s32[32]{0:T(128)}, s32[128]{0:T(128)}, /...) custom-call(s32[64]{0:T(128)} %bitcast.20, ...), custom_call_target="tpu_custom_call" | custom-call | tf_op jit(solution)/shard_map/pallas_call | solution.py:332
  12.0 2.4 %collective-permute-start.9 = (f32[128,128]{1,0:T(8,128)}, f32[128,128]{1,0:T(8,128)S(1)}, u32[]{:S(2)}, u32[]{:S(2)}) collective-permute-start(f32[128,128]{1,0:T(8,128)} %get-tuple-element.41), channel_id=1, source_target_pairs={{0,64},{1,65},{2,66},{3,67},{4,68},{5,69},{6,70},{7,71},{8,72},{9,... | collective-permute-start | bytes 196616 | tf_op jit(solution)/shard_map/ppermute | solution.py:582
  15.6 1.9 %collective-permute-done.9.refs_8_ = f32[128,128]{1,0:T(8,128)S(1)} collective-permute-done((f32[128,128]{1,0:T(8,128)}, f32[128,128]{1,0:T(8,128)S(1)}, u32[]{:S(2)}, u32[]{:S(2)}) %collective-permute-start.9) | collective-permute-done | bytes 65568 | tf_op jit(solution)/shard_map/ppermute | solution.py:582
  18.6 4.8 %shard_map.124 = (f32[16,64,128]{2,1,0:T(8,128)}, f32[16,64,128]{2,1,0:T(8,128)}, f32[16,64,128]{2,1,0:T(8,128)}, f32[16,64,128]{2,1,0:T(8,128)}, f32[136,128]{1...) custom-call(s32[32]{0:T(128)} %get-tuple-element.30.refs_0_, ...), custom_call_target="tpu_custom_call" | custom-call | tf_op jit(solution)/shard_map/pallas_call | solution.py:332
  24.8 2.6 %collective-permute-start.15 = (f32[136,128]{1,0:T(8,128)}, f32[136,128]{1,0:T(8,128)S(1)}, u32[]{:S(2)}, u32[]{:S(2)}) collective-permute-start(f32[136,128]{1,0:T(8,128)} %get-tuple-element.49), channel_id=1, source_target_pairs={{0,64},{1,5},{2,66},{3,7},{4,68},{5,1},{6,70},{7,3},{8,72},{9,13},... | collective-permute-start | bytes 208904 | tf_op jit(solution)/shard_map/ppermute | solution.py:582
  29.9 4.4 %shard_map.123 = (f32[16,64,128]{2,1,0:T(8,128)}, f32[16,64,128]{2,1,0:T(8,128)}, f32[16,64,128]{2,1,0:T(8,128)}, f32[16,64,128]{2,1,0:T(8,128)}) custom-call(s32[32]{0:T(128)} %get-tuple-element.30.refs_0_, s32[128]{0:T(128)} %get-tuple-element.31.refs_1_, s32[5]{0:T(128)} %compare_select_fusion.3.refs_1_.refs_2_.place_ref, ...), custom_call_target="tpu_custom_call" | custom-call | tf_op jit(solution)/shard_map/pallas_call | solution.py:332
  35.5 1.7 %collective-permute-start.3 = (f32[16,64,128]{2,1,0:T(8,128)}, f32[16,64,128]{2,1,0:T(8,128)S(1)}, u32[]{:S(2)}, u32[]{:S(2)}) collective-permute-start(f32[16,64,128]{2,1,0:T(8,128)} %get-tuple-element.37), channel_id=1, source_target_pairs={{0,96},{1,7},{2,98},{3,1},{4,100},{5,3},{6,102},{7,5},{8,104},{9,1... | collective-permute-start | bytes 1572872 | tf_op jit(solution)/shard_map/ppermute | solution.py:582
  37.7 1.8 %collective-permute-start.12 = (f32[16,64,128]{2,1,0:T(8,128)S(1)}, f32[16,64,128]{2,1,0:T(8,128)S(1)}, u32[]{:S(2)}, u32[]{:S(2)}) collective-permute-start(f32[16,64,128]{2,1,0:T(8,128)S(1)} %copy-done.9), channel_id=1, source_target_pairs={{0,64},{1,5},{2,66},{3,7},{4,68},{5,1},{6,70},{7,3},{8,72},{9,13},... | collective-permute-start | bytes 1572872 | tf_op jit(solution)/shard_map/ppermute | solution.py:582
  39.5 10.2 %collective-permute-done.1 = f32[16,64,128]{2,1,0:T(8,128)S(1)} collective-permute-done((f32[16,64,128]{2,1,0:T(8,128)}, f32[16,64,128]{2,1,0:T(8,128)S(1)}, u32[]{:S(2)}, u32[]{:S(2)}) %collective-permute-start.1) | collective-permute-done | bytes 524320 | tf_op jit(solution)/shard_map/ppermute | solution.py:582
  51.5 1.7 %collective-permute-start.4 = (f32[4,64,128]{2,1,0:T(8,128)S(1)}, f32[4,64,128]{2,1,0:T(8,128)S(1)}, u32[]{:S(2)}, u32[]{:S(2)}) collective-permute-start(f32[4,64,128]{2,1,0:T(8,128)S(1)} %get-tuple-element.67), channel_id=1, source_target_pairs={{0,8},{1,9},{2,10},{3,11},{4,12},{5,13},{6,14},{7,15},{8,16},{9,17... | collective-permute-start | bytes 393224 | tf_op jit(solution)/shard_map/ppermute | solution.py:582
  53.2 2.2 %collective-permute-start.6 = (f32[4,64,128]{2,1,0:T(8,128)S(1)}, f32[4,64,128]{2,1,0:T(8,128)S(1)}, u32[]{:S(2)}, u32[]{:S(2)}) collective-permute-start(f32[4,64,128]{2,1,0:T(8,128)S(1)} %get-tuple-element.68), channel_id=1, source_target_pairs={{0,24},{1,25},{2,26},{3,27},{4,28},{5,29},{6,30},{7,31},{8,0},{9,1... | collective-permute-start | bytes 393224 | tf_op jit(solution)/shard_map/ppermute | solution.py:582
  55.4 5.5 %collective-permute-done.11 = f32[16,64,128]{2,1,0:T(8,128)S(1)} collective-permute-done((f32[16,64,128]{2,1,0:T(8,128)}, f32[16,64,128]{2,1,0:T(8,128)S(1)}, u32[]{:S(2)}, u32[]{:S(2)}) %collective-permute-start.11) | collective-permute-done | bytes 524320 | tf_op jit(solution)/shard_map/ppermute | solution.py:582
  60.9 3.5 %collective-permute-start.5 = (f32[4,64,128]{2,1,0:T(8,128)S(1)}, f32[4,64,128]{2,1,0:T(8,128)S(1)}, u32[]{:S(2)}, u32[]{:S(2)}) collective-permute-start(f32[4,64,128]{2,1,0:T(8,128)S(1)} %get-tuple-element.69), channel_id=1, source_target_pairs={{0,16},{1,17},{2,18},{3,19},{4,20},{5,21},{6,22},{7,23},{8,24},{9,... | collective-permute-start | bytes 393224 | tf_op jit(solution)/shard_map/ppermute | solution.py:582
  68.1 3.2 %collective-permute-done.17 = f32[4,80,128]{2,1,0:T(8,128)S(1)} collective-permute-done((f32[4,80,128]{2,1,0:T(8,128)S(1)}, f32[4,80,128]{2,1,0:T(8,128)S(1)}, u32[]{:S(2)}, u32[]{:S(2)}) %collective-permute-start.17) | collective-permute-done | bytes 163872 | tf_op jit(solution)/shard_map/ppermute | solution.py:582
  71.3 3.7 %collective-permute-done.18 = f32[4,80,128]{2,1,0:T(8,128)S(1)} collective-permute-done((f32[4,80,128]{2,1,0:T(8,128)S(1)}, f32[4,80,128]{2,1,0:T(8,128)S(1)}, u32[]{:S(2)}, u32[]{:S(2)}) %collective-permute-start.18) | collective-permute-done | bytes 163872 | tf_op jit(solution)/shard_map/ppermute | solution.py:582
  76.2 2.7 %collective-permute-start.22 = (f32[1,168,128]{2,1,0:T(8,128)S(1)}, f32[1,168,128]{2,1,0:T(8,128)S(1)}, u32[]{:S(2)}, u32[]{:S(2)}) collective-permute-start(f32[1,168,128]{2,1,0:T(8,128)S(1)} %get-tuple-element.71), channel_id=1, source_target_pairs={{0,6},{1,97},{2,0},{3,99},{4,2},{5,101},{6,4},{7,103},{8,14},{9,10... | collective-permute-start | bytes 258056 | tf_op jit(solution)/shard_map/ppermute | solution.py:582
  78.9 1.9 %collective-permute-done.20 = f32[1,168,128]{2,1,0:T(8,128)S(1)} collective-permute-done((f32[1,168,128]{2,1,0:T(8,128)S(1)}, f32[1,168,128]{2,1,0:T(8,128)S(1)}, u32[]{:S(2)}, u32[]{:S(2)}) %collective-permute-start.20) | collective-permute-done | bytes 86048 | tf_op jit(solution)/shard_map/ppermute | solution.py:582
  81.3 2.5 %collective-permute-done.21 = f32[1,168,128]{2,1,0:T(8,128)S(1)} collective-permute-done((f32[1,168,128]{2,1,0:T(8,128)S(1)}, f32[1,168,128]{2,1,0:T(8,128)S(1)}, u32[]{:S(2)}, u32[]{:S(2)}) %collective-permute-start.21) | collective-permute-done | bytes 86048 | tf_op jit(solution)/shard_map/ppermute | solution.py:582
  83.8 3.7 %collective-permute-start.23 = (f32[264,128]{1,0:T(8,128)S(1)}, f32[264,128]{1,0:T(8,128)S(1)}, u32[]{:S(2)}, u32[]{:S(2)}) collective-permute-start(f32[264,128]{1,0:T(8,128)S(1)} %bitcast.16), channel_id=1, source_target_pairs={{0,1},{1,0},{2,3},{3,2},{4,5},{5,4},{6,7},{7,6},{8,9},{9,8},{10,11... | collective-permute-start | bytes 405512 | tf_op jit(solution)/shard_map/ppermute | solution.py:599
  89.2 4.5 %shard_map.125 = (f32[128,128]{1,0:T(8,128)}, f32[128,128]{1,0:T(8,128)}, f32[128,128]{1,0:T(8,128)}, f32[8,128]{1,0:T(8,128)}, f32[128,128]{1,0:T(8,128)}) custom-call(f32[264,128]{1,0:T(8,128)} %bitcast.17, f32[264,128]{1,0:T(8,128)} %copy-done.3, s32[5]{0:T(128)} %compare_select_fusion.3.refs_1_.refs_2_.place_ref, f32[128,256]{1,0:T(8,128)} %constant.93.clone.lanes_ref, ...), custom_call_target="tpu_custom_call" | custom-call | tf_op jit(solution)/shard_map/pallas_call | solution.py:573
  93.7 14.4 %all_to_all.10 = f32[128,1,128]{2,1,0:T(1,128)} all-to-all(f32[128,1,128]{2,1,0:T(1,128)} %bitcast.19), channel_id=1, replica_groups=mesh['dp'=4,'grid'=32] {'dp','grid'}, dimensions={0} | all-to-all | bytes 131072 | tf_op jit(solution)/shard_map/all_to_all | solution.py:647
  108.1 5.2 %shard_map.126 = (f32[1024,128]{1,0:T(8,128)}, f32[8,128]{1,0:T(8,128)}) custom-call(f32[128,128]{1,0:T(8,128)} %bitcast.18, f32[8,128]{1,0:T(8,128)} %get-tuple-element.52.range_ref, f32[128,128]{1,0:T(8,128)} %get-tuple-element.53.scaled_ref, f32[128,128]{1,0:T(8,128)} %get-tuple-element.54.real_ref, f32[128,128]{1,0:T(8,128)} %get-tuple-element.55.imag_ref, ...), custom_call_target="tpu_custom_call" | custom-call | tf_op jit(solution)/shard_map/pallas_call | solution.py:573
  113.3 19.2 %all_to_all.11 = f32[128,8,128]{2,1,0:T(8,128)} all-to-all(f32[128,8,128]{2,1,0:T(8,128)} %bitcast.14), channel_id=1, replica_groups=mesh['dp'=4,'grid'=32] {'dp','grid'}, dimensions={0} | all-to-all | bytes 1048576 | tf_op jit(solution)/shard_map/all_to_all | solution.py:652
  132.4 2.4 %shard_map.127 = (f32[4,128,128]{2,1,0:T(8,128)}, f32[4,128,128]{2,1,0:T(8,128)}) custom-call(f32[1024,128]{1,0:T(8,128)} %bitcast.13, f32[8,128]{1,0:T(8,128)} %get-tuple-element.57.gain_ref, bf16[768,256]{1,0:T(8,128)(2,1)} %constant.98.clone.back_ref), custom_call_target="tpu_custom_call" | custom-call | tf_op jit(solution)/shard_map/pallas_call | solution.py:573
  (75 shorter events, 20.0 us)
Async XLA Ops:
  9.1 8.9 %collective-permute-start.7 = (f32[64,64,128]{2,1,0:T(8,128)}, f32[64,64,128]{2,1,0:T(8,128)}, u32[]{:S(2)}, u32[]{:S(2)}) collective-permute-start(f32[64,64,128]{2,1,0:T(8,128)} %get-tuple-element.38), channel_id=1, source_target_pairs={{0,1},{1,0},{2,3},{3,2},{4,5},{5,4},{6,7},{7,6},{8,9},{9,8},{10,11... | collective-permute-start | bytes 6291464 | tf_op jit(solution)/shard_map/ppermute | solution.py:599
  10.6 18.0 %collective-permute-start = (f32[64,64,128]{2,1,0:T(8,128)}, f32[64,64,128]{2,1,0:T(8,128)S(1)}, u32[]{:S(2)}, u32[]{:S(2)}) collective-permute-start(f32[64,64,128]{2,1,0:T(8,128)} %get-tuple-element.33), channel_id=1, source_target_pairs={{0,1},{1,0},{2,3},{3,2},{4,5},{5,4},{6,7},{7,6},{8,9},{9,8},{10,11... | collective-permute-start | bytes 6291464 | tf_op jit(solution)/shard_map/ppermute | solution.py:599
  10.7 4.9 %collective-permute-start.8 = (f32[128,128]{1,0:T(8,128)}, f32[128,128]{1,0:T(8,128)S(1)}, u32[]{:S(2)}, u32[]{:S(2)}) collective-permute-start(f32[128,128]{1,0:T(8,128)} %get-tuple-element.40), channel_id=1, source_target_pairs={{0,32},{1,33},{2,34},{3,35},{4,36},{5,37},{6,38},{7,39},{8,40},{9,... | collective-permute-start | bytes 196616 | tf_op jit(solution)/shard_map/ppermute | solution.py:582
  12.0 5.5 %collective-permute-start.9 = (f32[128,128]{1,0:T(8,128)}, f32[128,128]{1,0:T(8,128)S(1)}, u32[]{:S(2)}, u32[]{:S(2)}) collective-permute-start(f32[128,128]{1,0:T(8,128)} %get-tuple-element.41), channel_id=1, source_target_pairs={{0,64},{1,65},{2,66},{3,67},{4,68},{5,69},{6,70},{7,71},{8,72},{9,... | collective-permute-start | bytes 196616 | tf_op jit(solution)/shard_map/ppermute | solution.py:582
  14.4 3.6 %collective-permute-start.10 = (f32[128,128]{1,0:T(8,128)}, f32[128,128]{1,0:T(8,128)S(1)}, u32[]{:S(2)}, u32[]{:S(2)}) collective-permute-start(f32[128,128]{1,0:T(8,128)} %get-tuple-element.42), channel_id=1, source_target_pairs={{0,96},{1,97},{2,98},{3,99},{4,100},{5,101},{6,102},{7,103},{8,104... | collective-permute-start | bytes 196616 | tf_op jit(solution)/shard_map/ppermute | solution.py:582
  23.4 12.1 %collective-permute-start.14 = (f32[136,128]{1,0:T(8,128)}, f32[136,128]{1,0:T(8,128)S(1)}, u32[]{:S(2)}, u32[]{:S(2)}) collective-permute-start(f32[136,128]{1,0:T(8,128)} %get-tuple-element.48), channel_id=1, source_target_pairs={{0,32},{1,3},{2,34},{3,5},{4,36},{5,7},{6,38},{7,1},{8,40},{9,11},... | collective-permute-start | bytes 208904 | tf_op jit(solution)/shard_map/ppermute | solution.py:582
  24.8 12.4 %collective-permute-start.15 = (f32[136,128]{1,0:T(8,128)}, f32[136,128]{1,0:T(8,128)S(1)}, u32[]{:S(2)}, u32[]{:S(2)}) collective-permute-start(f32[136,128]{1,0:T(8,128)} %get-tuple-element.49), channel_id=1, source_target_pairs={{0,64},{1,5},{2,66},{3,7},{4,68},{5,1},{6,70},{7,3},{8,72},{9,13},... | collective-permute-start | bytes 208904 | tf_op jit(solution)/shard_map/ppermute | solution.py:582
  27.5 10.2 %collective-permute-start.16 = (f32[136,128]{1,0:T(8,128)}, f32[136,128]{1,0:T(8,128)S(1)}, u32[]{:S(2)}, u32[]{:S(2)}) collective-permute-start(f32[136,128]{1,0:T(8,128)} %get-tuple-element.50), channel_id=1, source_target_pairs={{0,96},{1,7},{2,98},{3,1},{4,100},{5,3},{6,102},{7,5},{8,104},{9,1... | collective-permute-start | bytes 208904 | tf_op jit(solution)/shard_map/ppermute | solution.py:582
  34.3 15.4 %collective-permute-start.1 = (f32[16,64,128]{2,1,0:T(8,128)}, f32[16,64,128]{2,1,0:T(8,128)S(1)}, u32[]{:S(2)}, u32[]{:S(2)}) collective-permute-start(f32[16,64,128]{2,1,0:T(8,128)} %get-tuple-element.35), channel_id=1, source_target_pairs={{0,32},{1,3},{2,34},{3,5},{4,36},{5,7},{6,38},{7,1},{8,40},{9,11},... | collective-permute-start | bytes 1572872 | tf_op jit(solution)/shard_map/ppermute | solution.py:582
  34.7 15.0 %collective-permute-start.2 = (f32[16,64,128]{2,1,0:T(8,128)}, f32[16,64,128]{2,1,0:T(8,128)S(1)}, u32[]{:S(2)}, u32[]{:S(2)}) collective-permute-start(f32[16,64,128]{2,1,0:T(8,128)} %get-tuple-element.36), channel_id=1, source_target_pairs={{0,64},{1,5},{2,66},{3,7},{4,68},{5,1},{6,70},{7,3},{8,72},{9,13},... | collective-permute-start | bytes 1572872 | tf_op jit(solution)/shard_map/ppermute | solution.py:582
  35.5 14.8 %collective-permute-start.3 = (f32[16,64,128]{2,1,0:T(8,128)}, f32[16,64,128]{2,1,0:T(8,128)S(1)}, u32[]{:S(2)}, u32[]{:S(2)}) collective-permute-start(f32[16,64,128]{2,1,0:T(8,128)} %get-tuple-element.37), channel_id=1, source_target_pairs={{0,96},{1,7},{2,98},{3,1},{4,100},{5,3},{6,102},{7,5},{8,104},{9,1... | collective-permute-start | bytes 1572872 | tf_op jit(solution)/shard_map/ppermute | solution.py:582
  37.2 23.7 %collective-permute-start.11 = (f32[16,64,128]{2,1,0:T(8,128)}, f32[16,64,128]{2,1,0:T(8,128)S(1)}, u32[]{:S(2)}, u32[]{:S(2)}) collective-permute-start(f32[16,64,128]{2,1,0:T(8,128)} %get-tuple-element.44), channel_id=1, source_target_pairs={{0,32},{1,3},{2,34},{3,5},{4,36},{5,7},{6,38},{7,1},{8,40},{9,11},... | collective-permute-start | bytes 1572872 | tf_op jit(solution)/shard_map/ppermute | solution.py:582
  37.7 26.8 %collective-permute-start.12 = (f32[16,64,128]{2,1,0:T(8,128)S(1)}, f32[16,64,128]{2,1,0:T(8,128)S(1)}, u32[]{:S(2)}, u32[]{:S(2)}) collective-permute-start(f32[16,64,128]{2,1,0:T(8,128)S(1)} %copy-done.9), channel_id=1, source_target_pairs={{0,64},{1,5},{2,66},{3,7},{4,68},{5,1},{6,70},{7,3},{8,72},{9,13},... | collective-permute-start | bytes 1572872 | tf_op jit(solution)/shard_map/ppermute | solution.py:582
  49.7 14.8 %collective-permute-start.13 = (f32[16,64,128]{2,1,0:T(8,128)S(1)}, f32[16,64,128]{2,1,0:T(8,128)S(1)}, u32[]{:S(2)}, u32[]{:S(2)}) collective-permute-start(f32[16,64,128]{2,1,0:T(8,128)S(1)} %copy-done.8), channel_id=1, source_target_pairs={{0,96},{1,7},{2,98},{3,1},{4,100},{5,3},{6,102},{7,5},{8,104},{9,1... | collective-permute-start | bytes 1572872 | tf_op jit(solution)/shard_map/ppermute | solution.py:582
  51.5 15.3 %collective-permute-start.4 = (f32[4,64,128]{2,1,0:T(8,128)S(1)}, f32[4,64,128]{2,1,0:T(8,128)S(1)}, u32[]{:S(2)}, u32[]{:S(2)}) collective-permute-start(f32[4,64,128]{2,1,0:T(8,128)S(1)} %get-tuple-element.67), channel_id=1, source_target_pairs={{0,8},{1,9},{2,10},{3,11},{4,12},{5,13},{6,14},{7,15},{8,16},{9,17... | collective-permute-start | bytes 393224 | tf_op jit(solution)/shard_map/ppermute | solution.py:582
  53.2 14.8 %collective-permute-start.6 = (f32[4,64,128]{2,1,0:T(8,128)S(1)}, f32[4,64,128]{2,1,0:T(8,128)S(1)}, u32[]{:S(2)}, u32[]{:S(2)}) collective-permute-start(f32[4,64,128]{2,1,0:T(8,128)S(1)} %get-tuple-element.68), channel_id=1, source_target_pairs={{0,24},{1,25},{2,26},{3,27},{4,28},{5,29},{6,30},{7,31},{8,0},{9,1... | collective-permute-start | bytes 393224 | tf_op jit(solution)/shard_map/ppermute | solution.py:582
  60.9 7.1 %collective-permute-start.5 = (f32[4,64,128]{2,1,0:T(8,128)S(1)}, f32[4,64,128]{2,1,0:T(8,128)S(1)}, u32[]{:S(2)}, u32[]{:S(2)}) collective-permute-start(f32[4,64,128]{2,1,0:T(8,128)S(1)} %get-tuple-element.69), channel_id=1, source_target_pairs={{0,16},{1,17},{2,18},{3,19},{4,20},{5,21},{6,22},{7,23},{8,24},{9,... | collective-permute-start | bytes 393224 | tf_op jit(solution)/shard_map/ppermute | solution.py:582
  64.7 6.6 %collective-permute-start.17 = (f32[4,80,128]{2,1,0:T(8,128)S(1)}, f32[4,80,128]{2,1,0:T(8,128)S(1)}, u32[]{:S(2)}, u32[]{:S(2)}) collective-permute-start(f32[4,80,128]{2,1,0:T(8,128)S(1)} %get-tuple-element.64), channel_id=1, source_target_pairs={{0,8},{1,9},{2,10},{3,11},{4,12},{5,13},{6,14},{7,15},{8,16},{9,17... | collective-permute-start | bytes 491528 | tf_op jit(solution)/shard_map/ppermute | solution.py:582
  65.5 9.4 %collective-permute-start.18 = (f32[4,80,128]{2,1,0:T(8,128)S(1)}, f32[4,80,128]{2,1,0:T(8,128)S(1)}, u32[]{:S(2)}, u32[]{:S(2)}) collective-permute-start(f32[4,80,128]{2,1,0:T(8,128)S(1)} %get-tuple-element.65), channel_id=1, source_target_pairs={{0,16},{1,17},{2,18},{3,19},{4,20},{5,21},{6,22},{7,23},{8,24},{9,... | collective-permute-start | bytes 491528 | tf_op jit(solution)/shard_map/ppermute | solution.py:582
  66.8 9.2 %collective-permute-start.19 = (f32[4,80,128]{2,1,0:T(8,128)S(1)}, f32[4,80,128]{2,1,0:T(8,128)S(1)}, u32[]{:S(2)}, u32[]{:S(2)}) collective-permute-start(f32[4,80,128]{2,1,0:T(8,128)S(1)} %get-tuple-element.66), channel_id=1, source_target_pairs={{0,24},{1,25},{2,26},{3,27},{4,28},{5,29},{6,30},{7,31},{8,0},{9,1... | collective-permute-start | bytes 491528 | tf_op jit(solution)/shard_map/ppermute | solution.py:582
  76.2 4.6 %collective-permute-start.20 = (f32[1,168,128]{2,1,0:T(8,128)S(1)}, f32[1,168,128]{2,1,0:T(8,128)S(1)}, u32[]{:S(2)}, u32[]{:S(2)}) collective-permute-start(f32[1,168,128]{2,1,0:T(8,128)S(1)} %get-tuple-element.70), channel_id=1, source_target_pairs={{0,2},{1,33},{2,4},{3,35},{4,6},{5,37},{6,0},{7,39},{8,10},{9,41},... | collective-permute-start | bytes 258056 | tf_op jit(solution)/shard_map/ppermute | solution.py:582
  76.2 5.0 %collective-permute-start.22 = (f32[1,168,128]{2,1,0:T(8,128)S(1)}, f32[1,168,128]{2,1,0:T(8,128)S(1)}, u32[]{:S(2)}, u32[]{:S(2)}) collective-permute-start(f32[1,168,128]{2,1,0:T(8,128)S(1)} %get-tuple-element.71), channel_id=1, source_target_pairs={{0,6},{1,97},{2,0},{3,99},{4,2},{5,101},{6,4},{7,103},{8,14},{9,10... | collective-permute-start | bytes 258056 | tf_op jit(solution)/shard_map/ppermute | solution.py:582
  78.9 4.8 %collective-permute-start.21 = (f32[1,168,128]{2,1,0:T(8,128)S(1)}, f32[1,168,128]{2,1,0:T(8,128)S(1)}, u32[]{:S(2)}, u32[]{:S(2)}) collective-permute-start(f32[1,168,128]{2,1,0:T(8,128)S(1)} %get-tuple-element.72), channel_id=1, source_target_pairs={{0,4},{1,65},{2,6},{3,67},{4,0},{5,69},{6,2},{7,71},{8,12},{9,73},... | collective-permute-start | bytes 258056 | tf_op jit(solution)/shard_map/ppermute | solution.py:582
  83.8 4.7 %collective-permute-start.23 = (f32[264,128]{1,0:T(8,128)S(1)}, f32[264,128]{1,0:T(8,128)S(1)}, u32[]{:S(2)}, u32[]{:S(2)}) collective-permute-start(f32[264,128]{1,0:T(8,128)S(1)} %bitcast.16), channel_id=1, source_target_pairs={{0,1},{1,0},{2,3},{3,2},{4,5},{5,4},{6,7},{7,6},{8,9},{9,8},{10,11... | collective-permute-start | bytes 405512 | tf_op jit(solution)/shard_map/ppermute | solution.py:599
  (10 other events, 85.2 us)

commit v10 on v9

--- a/solution.py
+++ b/solution.py
@@ -579,7 +579,9 @@
 
 
 def exchange(parts, axes):
-    arrived = {r: lax.ppermute(parts[r], ALL, shift_pairs(axes, r)) for r in (2, 1, 3)}
+    arrived = {}
+    for r in (2, 1, 3):
+        arrived[r] = lax.ppermute(parts[r], ALL, shift_pairs(axes, r))
     return [parts[0], arrived[1], arrived[2], arrived[3]]
 
 
@@ -625,7 +627,8 @@
     early = exchange(parts, axes[1])
     held = summed([a[: SIDE**2 * 8] for a in rows]).reshape(SIDE**2, 8, size)
     ends = jnp.broadcast_to(least([a[SIDE**2 * 8 :] for a in rows])[None], (SIDE**2, 8, size))
-    parts = exchange(quarter(jnp.concatenate([summed(data[1]), held, ends], 1)), axes[1])
+    parts = quarter(jnp.concatenate([summed(data[1]), held, ends], 1))
+    parts = exchange(parts, axes[1])
     late = size // HALVES
     for stage in (1, 2):
         if stage == 2:

time: 135 us -> 135 us (level)
  no operation moved by 1% of the time
where the time goes in v10:
time: 135 us
  starting transfers between devices  34 us (25%)
  blocking collectives  33.6 us (25%)
  waiting for transfers between devices  32.6 us (24%)
  Pallas kernels  29 us (21%)
  local copies, waits for them, and re-layouts  2.72 us (2%)
  other arithmetic  2.05 us (2%)
    ppermute x21, waiting for transfers between devices, exchange(): arrived[r] = lax.ppermute(parts[r], ALL, shift_pairs(axes, r))  31.6 us
    ppermute x21, starting transfers between devices, exchange(): arrived[r] = lax.ppermute(parts[r], ALL, shift_pairs(axes, r))  28.7 us
    all_to_all x1, blocking collectives, body(): lax.all_to_all(back.reshape(count, 2 * planes, size), ALL, 0, 0, tiled=True)  19.2 us
    pallas_call x3, Pallas kernels, grid_call(): pl.pallas_call(functools.partial(grid_kernel, kept=kept, part=part, capac...  17 us
    all_to_all x1, blocking collectives, body(): lax.all_to_all(send.reshape(count, 1, size), ALL, 0, 0, tiled=True)  14.4 us
    pallas_call x3, Pallas kernels, call(): pl.pallas_call(kernel, out_shape=[jax.ShapeDtypeStruct(s, jnp.float32) fo...  12 us
    ppermute x3, starting transfers between devices, body(): swap = lambda a: lax.ppermute(a, ALL, shift_pairs((3, 3), 1))  5.3 us
  transfers between devices with their start and end apart: 24, of which 12 were waited for; matrix products, arithmetic and copies ran while one was open for 1% of the time, Pallas kernels for 7%

profile of v10, /device:TPU:1, one launch (start us, length us, event | category | flops | bytes accessed | tf_op | source)
XLA Modules:
  0.0 134.8 jit_solution(15318651125855214493)
XLA Ops:
  1.3 7.8 %shard_map.122 = (f32[64,64,128]{2,1,0:T(8,128)}, f32[64,64,128]{2,1,0:T(8,128)}, bf16[64,32,128]{2,1,0:T(8,128)(2,1)}, s32[32]{0:T(128)}, s32[128]{0:T(128)}, /...) custom-call(s32[64]{0:T(128)} %bitcast.20, ...), custom_call_target="tpu_custom_call" | custom-call | tf_op jit(solution)/shard_map/pallas_call | solution.py:332
  12.0 2.4 %collective-permute-start.9 = (f32[128,128]{1,0:T(8,128)}, f32[128,128]{1,0:T(8,128)S(1)}, u32[]{:S(2)}, u32[]{:S(2)}) collective-permute-start(f32[128,128]{1,0:T(8,128)} %get-tuple-element.41), channel_id=1, source_target_pairs={{0,64},{1,65},{2,66},{3,67},{4,68},{5,69},{6,70},{7,71},{8,72},{9,... | collective-permute-start | bytes 196616 | tf_op jit(solution)/shard_map/ppermute | solution.py:584
  15.6 1.9 %collective-permute-done.9.refs_8_ = f32[128,128]{1,0:T(8,128)S(1)} collective-permute-done((f32[128,128]{1,0:T(8,128)}, f32[128,128]{1,0:T(8,128)S(1)}, u32[]{:S(2)}, u32[]{:S(2)}) %collective-permute-start.9) | collective-permute-done | bytes 65568 | tf_op jit(solution)/shard_map/ppermute | solution.py:584
  18.6 4.8 %shard_map.124 = (f32[16,64,128]{2,1,0:T(8,128)}, f32[16,64,128]{2,1,0:T(8,128)}, f32[16,64,128]{2,1,0:T(8,128)}, f32[16,64,128]{2,1,0:T(8,128)}, f32[136,128]{1...) custom-call(s32[32]{0:T(128)} %get-tuple-element.30.refs_0_, ...), custom_call_target="tpu_custom_call" | custom-call | tf_op jit(solution)/shard_map/pallas_call | solution.py:332
  24.8 2.6 %collective-permute-start.15 = (f32[136,128]{1,0:T(8,128)}, f32[136,128]{1,0:T(8,128)S(1)}, u32[]{:S(2)}, u32[]{:S(2)}) collective-permute-start(f32[136,128]{1,0:T(8,128)} %get-tuple-element.49), channel_id=1, source_target_pairs={{0,64},{1,5},{2,66},{3,7},{4,68},{5,1},{6,70},{7,3},{8,72},{9,13},... | collective-permute-start | bytes 208904 | tf_op jit(solution)/shard_map/ppermute | solution.py:584
  29.9 4.4 %shard_map.123 = (f32[16,64,128]{2,1,0:T(8,128)}, f32[16,64,128]{2,1,0:T(8,128)}, f32[16,64,128]{2,1,0:T(8,128)}, f32[16,64,128]{2,1,0:T(8,128)}) custom-call(s32[32]{0:T(128)} %get-tuple-element.30.refs_0_, s32[128]{0:T(128)} %get-tuple-element.31.refs_1_, s32[5]{0:T(128)} %compare_select_fusion.3.refs_1_.refs_2_.place_ref, ...), custom_call_target="tpu_custom_call" | custom-call | tf_op jit(solution)/shard_map/pallas_call | solution.py:332
  35.5 1.7 %collective-permute-start.3 = (f32[16,64,128]{2,1,0:T(8,128)}, f32[16,64,128]{2,1,0:T(8,128)S(1)}, u32[]{:S(2)}, u32[]{:S(2)}) collective-permute-start(f32[16,64,128]{2,1,0:T(8,128)} %get-tuple-element.37), channel_id=1, source_target_pairs={{0,96},{1,7},{2,98},{3,1},{4,100},{5,3},{6,102},{7,5},{8,104},{9,1... | collective-permute-start | bytes 1572872 | tf_op jit(solution)/shard_map/ppermute | solution.py:584
  37.7 1.8 %collective-permute-start.12 = (f32[16,64,128]{2,1,0:T(8,128)S(1)}, f32[16,64,128]{2,1,0:T(8,128)S(1)}, u32[]{:S(2)}, u32[]{:S(2)}) collective-permute-start(f32[16,64,128]{2,1,0:T(8,128)S(1)} %copy-done.9), channel_id=1, source_target_pairs={{0,64},{1,5},{2,66},{3,7},{4,68},{5,1},{6,70},{7,3},{8,72},{9,13},... | collective-permute-start | bytes 1572872 | tf_op jit(solution)/shard_map/ppermute | solution.py:584
  39.5 10.2 %collective-permute-done.1 = f32[16,64,128]{2,1,0:T(8,128)S(1)} collective-permute-done((f32[16,64,128]{2,1,0:T(8,128)}, f32[16,64,128]{2,1,0:T(8,128)S(1)}, u32[]{:S(2)}, u32[]{:S(2)}) %collective-permute-start.1) | collective-permute-done | bytes 524320 | tf_op jit(solution)/shard_map/ppermute | solution.py:584
  51.5 1.7 %collective-permute-start.4 = (f32[4,64,128]{2,1,0:T(8,128)S(1)}, f32[4,64,128]{2,1,0:T(8,128)S(1)}, u32[]{:S(2)}, u32[]{:S(2)}) collective-permute-start(f32[4,64,128]{2,1,0:T(8,128)S(1)} %get-tuple-element.67), channel_id=1, source_target_pairs={{0,8},{1,9},{2,10},{3,11},{4,12},{5,13},{6,14},{7,15},{8,16},{9,17... | collective-permute-start | bytes 393224 | tf_op jit(solution)/shard_map/ppermute | solution.py:584
  53.2 2.2 %collective-permute-start.6 = (f32[4,64,128]{2,1,0:T(8,128)S(1)}, f32[4,64,128]{2,1,0:T(8,128)S(1)}, u32[]{:S(2)}, u32[]{:S(2)}) collective-permute-start(f32[4,64,128]{2,1,0:T(8,128)S(1)} %get-tuple-element.68), channel_id=1, source_target_pairs={{0,24},{1,25},{2,26},{3,27},{4,28},{5,29},{6,30},{7,31},{8,0},{9,1... | collective-permute-start | bytes 393224 | tf_op jit(solution)/shard_map/ppermute | solution.py:584
  55.4 5.5 %collective-permute-done.11 = f32[16,64,128]{2,1,0:T(8,128)S(1)} collective-permute-done((f32[16,64,128]{2,1,0:T(8,128)}, f32[16,64,128]{2,1,0:T(8,128)S(1)}, u32[]{:S(2)}, u32[]{:S(2)}) %collective-permute-start.11) | collective-permute-done | bytes 524320 | tf_op jit(solution)/shard_map/ppermute | solution.py:584
  60.9 3.5 %collective-permute-start.5 = (f32[4,64,128]{2,1,0:T(8,128)S(1)}, f32[4,64,128]{2,1,0:T(8,128)S(1)}, u32[]{:S(2)}, u32[]{:S(2)}) collective-permute-start(f32[4,64,128]{2,1,0:T(8,128)S(1)} %get-tuple-element.69), channel_id=1, source_target_pairs={{0,16},{1,17},{2,18},{3,19},{4,20},{5,21},{6,22},{7,23},{8,24},{9,... | collective-permute-start | bytes 393224 | tf_op jit(solution)/shard_map/ppermute | solution.py:584
  68.1 3.2 %collective-permute-done.17 = f32[4,80,128]{2,1,0:T(8,128)S(1)} collective-permute-done((f32[4,80,128]{2,1,0:T(8,128)S(1)}, f32[4,80,128]{2,1,0:T(8,128)S(1)}, u32[]{:S(2)}, u32[]{:S(2)}) %collective-permute-start.17) | collective-permute-done | bytes 163872 | tf_op jit(solution)/shard_map/ppermute | solution.py:584
  71.3 3.7 %collective-permute-done.18 = f32[4,80,128]{2,1,0:T(8,128)S(1)} collective-permute-done((f32[4,80,128]{2,1,0:T(8,128)S(1)}, f32[4,80,128]{2,1,0:T(8,128)S(1)}, u32[]{:S(2)}, u32[]{:S(2)}) %collective-permute-start.18) | collective-permute-done | bytes 163872 | tf_op jit(solution)/shard_map/ppermute | solution.py:584
  76.2 2.7 %collective-permute-start.22 = (f32[1,168,128]{2,1,0:T(8,128)S(1)}, f32[1,168,128]{2,1,0:T(8,128)S(1)}, u32[]{:S(2)}, u32[]{:S(2)}) collective-permute-start(f32[1,168,128]{2,1,0:T(8,128)S(1)} %get-tuple-element.71), channel_id=1, source_target_pairs={{0,6},{1,97},{2,0},{3,99},{4,2},{5,101},{6,4},{7,103},{8,14},{9,10... | collective-permute-start | bytes 258056 | tf_op jit(solution)/shard_map/ppermute | solution.py:584
  78.9 1.9 %collective-permute-done.20 = f32[1,168,128]{2,1,0:T(8,128)S(1)} collective-permute-done((f32[1,168,128]{2,1,0:T(8,128)S(1)}, f32[1,168,128]{2,1,0:T(8,128)S(1)}, u32[]{:S(2)}, u32[]{:S(2)}) %collective-permute-start.20) | collective-permute-done | bytes 86048 | tf_op jit(solution)/shard_map/ppermute | solution.py:584
  81.3 2.5 %collective-permute-done.21 = f32[1,168,128]{2,1,0:T(8,128)S(1)} collective-permute-done((f32[1,168,128]{2,1,0:T(8,128)S(1)}, f32[1,168,128]{2,1,0:T(8,128)S(1)}, u32[]{:S(2)}, u32[]{:S(2)}) %collective-permute-start.21) | collective-permute-done | bytes 86048 | tf_op jit(solution)/shard_map/ppermute | solution.py:584
  83.8 3.7 %collective-permute-start.23 = (f32[264,128]{1,0:T(8,128)S(1)}, f32[264,128]{1,0:T(8,128)S(1)}, u32[]{:S(2)}, u32[]{:S(2)}) collective-permute-start(f32[264,128]{1,0:T(8,128)S(1)} %bitcast.16), channel_id=1, source_target_pairs={{0,1},{1,0},{2,3},{3,2},{4,5},{5,4},{6,7},{7,6},{8,9},{9,8},{10,11... | collective-permute-start | bytes 405512 | tf_op jit(solution)/shard_map/ppermute | solution.py:601
  89.2 4.5 %shard_map.125 = (f32[128,128]{1,0:T(8,128)}, f32[128,128]{1,0:T(8,128)}, f32[128,128]{1,0:T(8,128)}, f32[8,128]{1,0:T(8,128)}, f32[128,128]{1,0:T(8,128)}) custom-call(f32[264,128]{1,0:T(8,128)} %bitcast.17, f32[264,128]{1,0:T(8,128)} %copy-done.3, s32[5]{0:T(128)} %compare_select_fusion.3.refs_1_.refs_2_.place_ref, f32[128,256]{1,0:T(8,128)} %constant.93.clone.lanes_ref, ...), custom_call_target="tpu_custom_call" | custom-call | tf_op jit(solution)/shard_map/pallas_call | solution.py:573
  93.7 14.4 %all_to_all.10 = f32[128,1,128]{2,1,0:T(1,128)} all-to-all(f32[128,1,128]{2,1,0:T(1,128)} %bitcast.19), channel_id=1, replica_groups=mesh['dp'=4,'grid'=32] {'dp','grid'}, dimensions={0} | all-to-all | bytes 131072 | tf_op jit(solution)/shard_map/all_to_all | solution.py:650
  108.1 5.2 %shard_map.126 = (f32[1024,128]{1,0:T(8,128)}, f32[8,128]{1,0:T(8,128)}) custom-call(f32[128,128]{1,0:T(8,128)} %bitcast.18, f32[8,128]{1,0:T(8,128)} %get-tuple-element.52.range_ref, f32[128,128]{1,0:T(8,128)} %get-tuple-element.53.scaled_ref, f32[128,128]{1,0:T(8,128)} %get-tuple-element.54.real_ref, f32[128,128]{1,0:T(8,128)} %get-tuple-element.55.imag_ref, ...), custom_call_target="tpu_custom_call" | custom-call | tf_op jit(solution)/shard_map/pallas_call | solution.py:573
  113.3 19.2 %all_to_all.11 = f32[128,8,128]{2,1,0:T(8,128)} all-to-all(f32[128,8,128]{2,1,0:T(8,128)} %bitcast.14), channel_id=1, replica_groups=mesh['dp'=4,'grid'=32] {'dp','grid'}, dimensions={0} | all-to-all | bytes 1048576 | tf_op jit(solution)/shard_map/all_to_all | solution.py:655
  132.4 2.4 %shard_map.127 = (f32[4,128,128]{2,1,0:T(8,128)}, f32[4,128,128]{2,1,0:T(8,128)}) custom-call(f32[1024,128]{1,0:T(8,128)} %bitcast.13, f32[8,128]{1,0:T(8,128)} %get-tuple-element.57.gain_ref, bf16[768,256]{1,0:T(8,128)(2,1)} %constant.98.clone.back_ref), custom_call_target="tpu_custom_call" | custom-call | tf_op jit(solution)/shard_map/pallas_call | solution.py:573
  (75 shorter events, 20.0 us)
Async XLA Ops:
  9.1 8.9 %collective-permute-start.7 = (f32[64,64,128]{2,1,0:T(8,128)}, f32[64,64,128]{2,1,0:T(8,128)}, u32[]{:S(2)}, u32[]{:S(2)}) collective-permute-start(f32[64,64,128]{2,1,0:T(8,128)} %get-tuple-element.38), channel_id=1, source_target_pairs={{0,1},{1,0},{2,3},{3,2},{4,5},{5,4},{6,7},{7,6},{8,9},{9,8},{10,11... | collective-permute-start | bytes 6291464 | tf_op jit(solution)/shard_map/ppermute | solution.py:601
  10.6 18.0 %collective-permute-start = (f32[64,64,128]{2,1,0:T(8,128)}, f32[64,64,128]{2,1,0:T(8,128)S(1)}, u32[]{:S(2)}, u32[]{:S(2)}) collective-permute-start(f32[64,64,128]{2,1,0:T(8,128)} %get-tuple-element.33), channel_id=1, source_target_pairs={{0,1},{1,0},{2,3},{3,2},{4,5},{5,4},{6,7},{7,6},{8,9},{9,8},{10,11... | collective-permute-start | bytes 6291464 | tf_op jit(solution)/shard_map/ppermute | solution.py:601
  10.7 4.9 %collective-permute-start.8 = (f32[128,128]{1,0:T(8,128)}, f32[128,128]{1,0:T(8,128)S(1)}, u32[]{:S(2)}, u32[]{:S(2)}) collective-permute-start(f32[128,128]{1,0:T(8,128)} %get-tuple-element.40), channel_id=1, source_target_pairs={{0,32},{1,33},{2,34},{3,35},{4,36},{5,37},{6,38},{7,39},{8,40},{9,... | collective-permute-start | bytes 196616 | tf_op jit(solution)/shard_map/ppermute | solution.py:584
  12.0 5.5 %collective-permute-start.9 = (f32[128,128]{1,0:T(8,128)}, f32[128,128]{1,0:T(8,128)S(1)}, u32[]{:S(2)}, u32[]{:S(2)}) collective-permute-start(f32[128,128]{1,0:T(8,128)} %get-tuple-element.41), channel_id=1, source_target_pairs={{0,64},{1,65},{2,66},{3,67},{4,68},{5,69},{6,70},{7,71},{8,72},{9,... | collective-permute-start | bytes 196616 | tf_op jit(solution)/shard_map/ppermute | solution.py:584
  14.4 3.6 %collective-permute-start.10 = (f32[128,128]{1,0:T(8,128)}, f32[128,128]{1,0:T(8,128)S(1)}, u32[]{:S(2)}, u32[]{:S(2)}) collective-permute-start(f32[128,128]{1,0:T(8,128)} %get-tuple-element.42), channel_id=1, source_target_pairs={{0,96},{1,97},{2,98},{3,99},{4,100},{5,101},{6,102},{7,103},{8,104... | collective-permute-start | bytes 196616 | tf_op jit(solution)/shard_map/ppermute | solution.py:584
  23.4 12.1 %collective-permute-start.14 = (f32[136,128]{1,0:T(8,128)}, f32[136,128]{1,0:T(8,128)S(1)}, u32[]{:S(2)}, u32[]{:S(2)}) collective-permute-start(f32[136,128]{1,0:T(8,128)} %get-tuple-element.48), channel_id=1, source_target_pairs={{0,32},{1,3},{2,34},{3,5},{4,36},{5,7},{6,38},{7,1},{8,40},{9,11},... | collective-permute-start | bytes 208904 | tf_op jit(solution)/shard_map/ppermute | solution.py:584
  24.8 12.4 %collective-permute-start.15 = (f32[136,128]{1,0:T(8,128)}, f32[136,128]{1,0:T(8,128)S(1)}, u32[]{:S(2)}, u32[]{:S(2)}) collective-permute-start(f32[136,128]{1,0:T(8,128)} %get-tuple-element.49), channel_id=1, source_target_pairs={{0,64},{1,5},{2,66},{3,7},{4,68},{5,1},{6,70},{7,3},{8,72},{9,13},... | collective-permute-start | bytes 208904 | tf_op jit(solution)/shard_map/ppermute | solution.py:584
  27.5 10.2 %collective-permute-start.16 = (f32[136,128]{1,0:T(8,128)}, f32[136,128]{1,0:T(8,128)S(1)}, u32[]{:S(2)}, u32[]{:S(2)}) collective-permute-start(f32[136,128]{1,0:T(8,128)} %get-tuple-element.50), channel_id=1, source_target_pairs={{0,96},{1,7},{2,98},{3,1},{4,100},{5,3},{6,102},{7,5},{8,104},{9,1... | collective-permute-start | bytes 208904 | tf_op jit(solution)/shard_map/ppermute | solution.py:584
  34.3 15.4 %collective-permute-start.1 = (f32[16,64,128]{2,1,0:T(8,128)}, f32[16,64,128]{2,1,0:T(8,128)S(1)}, u32[]{:S(2)}, u32[]{:S(2)}) collective-permute-start(f32[16,64,128]{2,1,0:T(8,128)} %get-tuple-element.35), channel_id=1, source_target_pairs={{0,32},{1,3},{2,34},{3,5},{4,36},{5,7},{6,38},{7,1},{8,40},{9,11},... | collective-permute-start | bytes 1572872 | tf_op jit(solution)/shard_map/ppermute | solution.py:584
  34.7 15.0 %collective-permute-start.2 = (f32[16,64,128]{2,1,0:T(8,128)}, f32[16,64,128]{2,1,0:T(8,128)S(1)}, u32[]{:S(2)}, u32[]{:S(2)}) collective-permute-start(f32[16,64,128]{2,1,0:T(8,128)} %get-tuple-element.36), channel_id=1, source_target_pairs={{0,64},{1,5},{2,66},{3,7},{4,68},{5,1},{6,70},{7,3},{8,72},{9,13},... | collective-permute-start | bytes 1572872 | tf_op jit(solution)/shard_map/ppermute | solution.py:584
  35.5 14.8 %collective-permute-start.3 = (f32[16,64,128]{2,1,0:T(8,128)}, f32[16,64,128]{2,1,0:T(8,128)S(1)}, u32[]{:S(2)}, u32[]{:S(2)}) collective-permute-start(f32[16,64,128]{2,1,0:T(8,128)} %get-tuple-element.37), channel_id=1, source_target_pairs={{0,96},{1,7},{2,98},{3,1},{4,100},{5,3},{6,102},{7,5},{8,104},{9,1... | collective-permute-start | bytes 1572872 | tf_op jit(solution)/shard_map/ppermute | solution.py:584
  37.2 23.7 %collective-permute-start.11 = (f32[16,64,128]{2,1,0:T(8,128)}, f32[16,64,128]{2,1,0:T(8,128)S(1)}, u32[]{:S(2)}, u32[]{:S(2)}) collective-permute-start(f32[16,64,128]{2,1,0:T(8,128)} %get-tuple-element.44), channel_id=1, source_target_pairs={{0,32},{1,3},{2,34},{3,5},{4,36},{5,7},{6,38},{7,1},{8,40},{9,11},... | collective-permute-start | bytes 1572872 | tf_op jit(solution)/shard_map/ppermute | solution.py:584
  37.7 26.8 %collective-permute-start.12 = (f32[16,64,128]{2,1,0:T(8,128)S(1)}, f32[16,64,128]{2,1,0:T(8,128)S(1)}, u32[]{:S(2)}, u32[]{:S(2)}) collective-permute-start(f32[16,64,128]{2,1,0:T(8,128)S(1)} %copy-done.9), channel_id=1, source_target_pairs={{0,64},{1,5},{2,66},{3,7},{4,68},{5,1},{6,70},{7,3},{8,72},{9,13},... | collective-permute-start | bytes 1572872 | tf_op jit(solution)/shard_map/ppermute | solution.py:584
  49.7 14.8 %collective-permute-start.13 = (f32[16,64,128]{2,1,0:T(8,128)S(1)}, f32[16,64,128]{2,1,0:T(8,128)S(1)}, u32[]{:S(2)}, u32[]{:S(2)}) collective-permute-start(f32[16,64,128]{2,1,0:T(8,128)S(1)} %copy-done.8), channel_id=1, source_target_pairs={{0,96},{1,7},{2,98},{3,1},{4,100},{5,3},{6,102},{7,5},{8,104},{9,1... | collective-permute-start | bytes 1572872 | tf_op jit(solution)/shard_map/ppermute | solution.py:584
  51.5 15.3 %collective-permute-start.4 = (f32[4,64,128]{2,1,0:T(8,128)S(1)}, f32[4,64,128]{2,1,0:T(8,128)S(1)}, u32[]{:S(2)}, u32[]{:S(2)}) collective-permute-start(f32[4,64,128]{2,1,0:T(8,128)S(1)} %get-tuple-element.67), channel_id=1, source_target_pairs={{0,8},{1,9},{2,10},{3,11},{4,12},{5,13},{6,14},{7,15},{8,16},{9,17... | collective-permute-start | bytes 393224 | tf_op jit(solution)/shard_map/ppermute | solution.py:584
  53.2 14.8 %collective-permute-start.6 = (f32[4,64,128]{2,1,0:T(8,128)S(1)}, f32[4,64,128]{2,1,0:T(8,128)S(1)}, u32[]{:S(2)}, u32[]{:S(2)}) collective-permute-start(f32[4,64,128]{2,1,0:T(8,128)S(1)} %get-tuple-element.68), channel_id=1, source_target_pairs={{0,24},{1,25},{2,26},{3,27},{4,28},{5,29},{6,30},{7,31},{8,0},{9,1... | collective-permute-start | bytes 393224 | tf_op jit(solution)/shard_map/ppermute | solution.py:584
  60.9 7.1 %collective-permute-start.5 = (f32[4,64,128]{2,1,0:T(8,128)S(1)}, f32[4,64,128]{2,1,0:T(8,128)S(1)}, u32[]{:S(2)}, u32[]{:S(2)}) collective-permute-start(f32[4,64,128]{2,1,0:T(8,128)S(1)} %get-tuple-element.69), channel_id=1, source_target_pairs={{0,16},{1,17},{2,18},{3,19},{4,20},{5,21},{6,22},{7,23},{8,24},{9,... | collective-permute-start | bytes 393224 | tf_op jit(solution)/shard_map/ppermute | solution.py:584
  64.7 6.6 %collective-permute-start.17 = (f32[4,80,128]{2,1,0:T(8,128)S(1)}, f32[4,80,128]{2,1,0:T(8,128)S(1)}, u32[]{:S(2)}, u32[]{:S(2)}) collective-permute-start(f32[4,80,128]{2,1,0:T(8,128)S(1)} %get-tuple-element.64), channel_id=1, source_target_pairs={{0,8},{1,9},{2,10},{3,11},{4,12},{5,13},{6,14},{7,15},{8,16},{9,17... | collective-permute-start | bytes 491528 | tf_op jit(solution)/shard_map/ppermute | solution.py:584
  65.5 9.4 %collective-permute-start.18 = (f32[4,80,128]{2,1,0:T(8,128)S(1)}, f32[4,80,128]{2,1,0:T(8,128)S(1)}, u32[]{:S(2)}, u32[]{:S(2)}) collective-permute-start(f32[4,80,128]{2,1,0:T(8,128)S(1)} %get-tuple-element.65), channel_id=1, source_target_pairs={{0,16},{1,17},{2,18},{3,19},{4,20},{5,21},{6,22},{7,23},{8,24},{9,... | collective-permute-start | bytes 491528 | tf_op jit(solution)/shard_map/ppermute | solution.py:584
  66.8 9.2 %collective-permute-start.19 = (f32[4,80,128]{2,1,0:T(8,128)S(1)}, f32[4,80,128]{2,1,0:T(8,128)S(1)}, u32[]{:S(2)}, u32[]{:S(2)}) collective-permute-start(f32[4,80,128]{2,1,0:T(8,128)S(1)} %get-tuple-element.66), channel_id=1, source_target_pairs={{0,24},{1,25},{2,26},{3,27},{4,28},{5,29},{6,30},{7,31},{8,0},{9,1... | collective-permute-start | bytes 491528 | tf_op jit(solution)/shard_map/ppermute | solution.py:584
  76.2 4.6 %collective-permute-start.20 = (f32[1,168,128]{2,1,0:T(8,128)S(1)}, f32[1,168,128]{2,1,0:T(8,128)S(1)}, u32[]{:S(2)}, u32[]{:S(2)}) collective-permute-start(f32[1,168,128]{2,1,0:T(8,128)S(1)} %get-tuple-element.70), channel_id=1, source_target_pairs={{0,2},{1,33},{2,4},{3,35},{4,6},{5,37},{6,0},{7,39},{8,10},{9,41},... | collective-permute-start | bytes 258056 | tf_op jit(solution)/shard_map/ppermute | solution.py:584
  76.2 5.0 %collective-permute-start.22 = (f32[1,168,128]{2,1,0:T(8,128)S(1)}, f32[1,168,128]{2,1,0:T(8,128)S(1)}, u32[]{:S(2)}, u32[]{:S(2)}) collective-permute-start(f32[1,168,128]{2,1,0:T(8,128)S(1)} %get-tuple-element.71), channel_id=1, source_target_pairs={{0,6},{1,97},{2,0},{3,99},{4,2},{5,101},{6,4},{7,103},{8,14},{9,10... | collective-permute-start | bytes 258056 | tf_op jit(solution)/shard_map/ppermute | solution.py:584
  78.9 4.8 %collective-permute-start.21 = (f32[1,168,128]{2,1,0:T(8,128)S(1)}, f32[1,168,128]{2,1,0:T(8,128)S(1)}, u32[]{:S(2)}, u32[]{:S(2)}) collective-permute-start(f32[1,168,128]{2,1,0:T(8,128)S(1)} %get-tuple-element.72), channel_id=1, source_target_pairs={{0,4},{1,65},{2,6},{3,67},{4,0},{5,69},{6,2},{7,71},{8,12},{9,73},... | collective-permute-start | bytes 258056 | tf_op jit(solution)/shard_map/ppermute | solution.py:584
  83.8 4.7 %collective-permute-start.23 = (f32[264,128]{1,0:T(8,128)S(1)}, f32[264,128]{1,0:T(8,128)S(1)}, u32[]{:S(2)}, u32[]{:S(2)}) collective-permute-start(f32[264,128]{1,0:T(8,128)S(1)} %bitcast.16), channel_id=1, source_target_pairs={{0,1},{1,0},{2,3},{3,2},{4,5},{5,4},{6,7},{7,6},{8,9},{9,8},{10,11... | collective-permute-start | bytes 405512 | tf_op jit(solution)/shard_map/ppermute | solution.py:601
  (10 other events, 85.2 us)

commit v11 on v9

--- a/solution.py
+++ b/solution.py
@@ -510,6 +510,8 @@
     lane = lax.broadcasted_iota(jnp.int32, moments[0].shape, 1)
     resid, direct = moments, moments
     held = lane_of(resid, 0)
+    least = (1.0 - 1e-4) / (centre[0] + 1.0)
+    most = (1.0 + 1e-4) / jnp.maximum(centre[0] - 1.0, 1e-3)
     steps, turns = [], []
     decay = jnp.ones((1, size), jnp.float32)
     for k in range(ITERS):
@@ -518,17 +520,22 @@
         prior = tuple(jnp.where(lane == 0, a, p) for a, p in zip(after, prior))
         image = dd_add(dd_mul(direct, centre), dd_scale(dd_add(after, prior), 0.5))
         alpha = dd_div(held, lane_of(image, k))
+        inside = jnp.logical_and(alpha[0] >= least, alpha[0] <= most)
+        bound = jnp.where(alpha[0] > most, most, least)
+        alpha = jnp.where(inside, alpha[0], bound), jnp.where(inside, alpha[1], 0.0)
         fresh = dd_add(resid, dd_neg(dd_mul(alpha, image)))
         reached = lane_of(fresh, k + 1)
         beta = dd_mul(alpha, dd_div(reached, held))
         held = reached
         beta = dd_scale(beta, -1.0 if k == 0 else -0.5)
+        sound = jnp.logical_and(beta[0] >= 0.0, beta[0] <= 1e4)
+        beta = tuple(jnp.where(sound, v, 0.0) for v in beta)
         direct = dd_add(fresh, dd_mul(beta, direct))
         resid = fresh
         steps.append(alpha[0][0:1])
         turns.append(beta[0][0:1])
         decay = decay * beta[0][0:1]
-    gain = lax.rsqrt(jnp.maximum(jnp.abs(decay), 1e-30)) / centre[0][0:1]
+    gain = lax.rsqrt(jnp.maximum(jnp.abs(decay), 1e-13)) / centre[0][0:1]
     gain_ref[...] = jnp.broadcast_to(gain, gain_ref.shape)
     scaled = scaled_ref[...]
     field = steps[0]

time: 135 us -> 135 us (level)
  no operation moved by 1% of the time
where the time goes in v11:
time: 135 us
  starting transfers between devices  34 us (25%)
  blocking collectives  33.6 us (25%)
  waiting for transfers between devices  32.6 us (24%)
  Pallas kernels  29 us (21%)
  local copies, waits for them, and re-layouts  2.72 us (2%)
  other arithmetic  2.05 us (2%)
    ppermute x21, waiting for transfers between devices, exchange(): lax.ppermute(parts[r], ALL, shift_pairs(axes, r))  31.6 us
    ppermute x21, starting transfers between devices, exchange(): lax.ppermute(parts[r], ALL, shift_pairs(axes, r))  28.7 us
    all_to_all x1, blocking collectives, body(): lax.all_to_all(back.reshape(count, 2 * planes, size), ALL, 0, 0, tiled=True)  19.2 us
    pallas_call x3, Pallas kernels, grid_call(): pl.pallas_call(functools.partial(grid_kernel, kept=kept, part=part, capac...  17 us
    all_to_all x1, blocking collectives, body(): lax.all_to_all(send.reshape(count, 1, size), ALL, 0, 0, tiled=True)  14.4 us
    pallas_call x3, Pallas kernels, call(): pl.pallas_call(kernel, out_shape=[jax.ShapeDtypeStruct(s, jnp.float32) fo...  12 us
    ppermute x3, starting transfers between devices, body(): swap = lambda a: lax.ppermute(a, ALL, shift_pairs((3, 3), 1))  5.3 us
  transfers between devices with their start and end apart: 24, of which 12 were waited for; matrix products, arithmetic and copies ran while one was open for 1% of the time, Pallas kernels for 7%

profile of v11, /device:TPU:1, one launch (start us, length us, event | category | flops | bytes accessed | tf_op | source)
XLA Modules:
  0.0 134.9 jit_solution(12648066396449903960)
XLA Ops:
  1.3 7.8 %shard_map.122 = (f32[64,64,128]{2,1,0:T(8,128)}, f32[64,64,128]{2,1,0:T(8,128)}, bf16[64,32,128]{2,1,0:T(8,128)(2,1)}, s32[32]{0:T(128)}, s32[128]{0:T(128)}, /...) custom-call(s32[64]{0:T(128)} %bitcast.20, ...), custom_call_target="tpu_custom_call" | custom-call | tf_op jit(solution)/shard_map/pallas_call | solution.py:332
  12.0 2.4 %collective-permute-start.9 = (f32[128,128]{1,0:T(8,128)}, f32[128,128]{1,0:T(8,128)S(1)}, u32[]{:S(2)}, u32[]{:S(2)}) collective-permute-start(f32[128,128]{1,0:T(8,128)} %get-tuple-element.41), channel_id=1, source_target_pairs={{0,64},{1,65},{2,66},{3,67},{4,68},{5,69},{6,70},{7,71},{8,72},{9,... | collective-permute-start | bytes 196616 | tf_op jit(solution)/shard_map/ppermute | solution.py:589
  15.6 1.9 %collective-permute-done.9.refs_8_ = f32[128,128]{1,0:T(8,128)S(1)} collective-permute-done((f32[128,128]{1,0:T(8,128)}, f32[128,128]{1,0:T(8,128)S(1)}, u32[]{:S(2)}, u32[]{:S(2)}) %collective-permute-start.9) | collective-permute-done | bytes 65568 | tf_op jit(solution)/shard_map/ppermute | solution.py:589
  18.6 4.8 %shard_map.124 = (f32[16,64,128]{2,1,0:T(8,128)}, f32[16,64,128]{2,1,0:T(8,128)}, f32[16,64,128]{2,1,0:T(8,128)}, f32[16,64,128]{2,1,0:T(8,128)}, f32[136,128]{1...) custom-call(s32[32]{0:T(128)} %get-tuple-element.30.refs_0_, ...), custom_call_target="tpu_custom_call" | custom-call | tf_op jit(solution)/shard_map/pallas_call | solution.py:332
  24.8 2.6 %collective-permute-start.15 = (f32[136,128]{1,0:T(8,128)}, f32[136,128]{1,0:T(8,128)S(1)}, u32[]{:S(2)}, u32[]{:S(2)}) collective-permute-start(f32[136,128]{1,0:T(8,128)} %get-tuple-element.49), channel_id=1, source_target_pairs={{0,64},{1,5},{2,66},{3,7},{4,68},{5,1},{6,70},{7,3},{8,72},{9,13},... | collective-permute-start | bytes 208904 | tf_op jit(solution)/shard_map/ppermute | solution.py:589
  29.9 4.4 %shard_map.123 = (f32[16,64,128]{2,1,0:T(8,128)}, f32[16,64,128]{2,1,0:T(8,128)}, f32[16,64,128]{2,1,0:T(8,128)}, f32[16,64,128]{2,1,0:T(8,128)}) custom-call(s32[32]{0:T(128)} %get-tuple-element.30.refs_0_, s32[128]{0:T(128)} %get-tuple-element.31.refs_1_, s32[5]{0:T(128)} %compare_select_fusion.3.refs_1_.refs_2_.place_ref, ...), custom_call_target="tpu_custom_call" | custom-call | tf_op jit(solution)/shard_map/pallas_call | solution.py:332
  35.5 1.7 %collective-permute-start.3 = (f32[16,64,128]{2,1,0:T(8,128)}, f32[16,64,128]{2,1,0:T(8,128)S(1)}, u32[]{:S(2)}, u32[]{:S(2)}) collective-permute-start(f32[16,64,128]{2,1,0:T(8,128)} %get-tuple-element.37), channel_id=1, source_target_pairs={{0,96},{1,7},{2,98},{3,1},{4,100},{5,3},{6,102},{7,5},{8,104},{9,1... | collective-permute-start | bytes 1572872 | tf_op jit(solution)/shard_map/ppermute | solution.py:589
  37.7 1.8 %collective-permute-start.12 = (f32[16,64,128]{2,1,0:T(8,128)S(1)}, f32[16,64,128]{2,1,0:T(8,128)S(1)}, u32[]{:S(2)}, u32[]{:S(2)}) collective-permute-start(f32[16,64,128]{2,1,0:T(8,128)S(1)} %copy-done.9), channel_id=1, source_target_pairs={{0,64},{1,5},{2,66},{3,7},{4,68},{5,1},{6,70},{7,3},{8,72},{9,13},... | collective-permute-start | bytes 1572872 | tf_op jit(solution)/shard_map/ppermute | solution.py:589
  39.5 10.2 %collective-permute-done.1 = f32[16,64,128]{2,1,0:T(8,128)S(1)} collective-permute-done((f32[16,64,128]{2,1,0:T(8,128)}, f32[16,64,128]{2,1,0:T(8,128)S(1)}, u32[]{:S(2)}, u32[]{:S(2)}) %collective-permute-start.1) | collective-permute-done | bytes 524320 | tf_op jit(solution)/shard_map/ppermute | solution.py:589
  51.5 1.7 %collective-permute-start.4 = (f32[4,64,128]{2,1,0:T(8,128)S(1)}, f32[4,64,128]{2,1,0:T(8,128)S(1)}, u32[]{:S(2)}, u32[]{:S(2)}) collective-permute-start(f32[4,64,128]{2,1,0:T(8,128)S(1)} %get-tuple-element.67), channel_id=1, source_target_pairs={{0,8},{1,9},{2,10},{3,11},{4,12},{5,13},{6,14},{7,15},{8,16},{9,17... | collective-permute-start | bytes 393224 | tf_op jit(solution)/shard_map/ppermute | solution.py:589
  53.2 2.2 %collective-permute-start.6 = (f32[4,64,128]{2,1,0:T(8,128)S(1)}, f32[4,64,128]{2,1,0:T(8,128)S(1)}, u32[]{:S(2)}, u32[]{:S(2)}) collective-permute-start(f32[4,64,128]{2,1,0:T(8,128)S(1)} %get-tuple-element.68), channel_id=1, source_target_pairs={{0,24},{1,25},{2,26},{3,27},{4,28},{5,29},{6,30},{7,31},{8,0},{9,1... | collective-permute-start | bytes 393224 | tf_op jit(solution)/shard_map/ppermute | solution.py:589
  55.4 5.5 %collective-permute-done.11 = f32[16,64,128]{2,1,0:T(8,128)S(1)} collective-permute-done((f32[16,64,128]{2,1,0:T(8,128)}, f32[16,64,128]{2,1,0:T(8,128)S(1)}, u32[]{:S(2)}, u32[]{:S(2)}) %collective-permute-start.11) | collective-permute-done | bytes 524320 | tf_op jit(solution)/shard_map/ppermute | solution.py:589
  60.9 3.5 %collective-permute-start.5 = (f32[4,64,128]{2,1,0:T(8,128)S(1)}, f32[4,64,128]{2,1,0:T(8,128)S(1)}, u32[]{:S(2)}, u32[]{:S(2)}) collective-permute-start(f32[4,64,128]{2,1,0:T(8,128)S(1)} %get-tuple-element.69), channel_id=1, source_target_pairs={{0,16},{1,17},{2,18},{3,19},{4,20},{5,21},{6,22},{7,23},{8,24},{9,... | collective-permute-start | bytes 393224 | tf_op jit(solution)/shard_map/ppermute | solution.py:589
  68.1 3.2 %collective-permute-done.17 = f32[4,80,128]{2,1,0:T(8,128)S(1)} collective-permute-done((f32[4,80,128]{2,1,0:T(8,128)S(1)}, f32[4,80,128]{2,1,0:T(8,128)S(1)}, u32[]{:S(2)}, u32[]{:S(2)}) %collective-permute-start.17) | collective-permute-done | bytes 163872 | tf_op jit(solution)/shard_map/ppermute | solution.py:589
  71.3 3.7 %collective-permute-done.18 = f32[4,80,128]{2,1,0:T(8,128)S(1)} collective-permute-done((f32[4,80,128]{2,1,0:T(8,128)S(1)}, f32[4,80,128]{2,1,0:T(8,128)S(1)}, u32[]{:S(2)}, u32[]{:S(2)}) %collective-permute-start.18) | collective-permute-done | bytes 163872 | tf_op jit(solution)/shard_map/ppermute | solution.py:589
  76.2 2.7 %collective-permute-start.22 = (f32[1,168,128]{2,1,0:T(8,128)S(1)}, f32[1,168,128]{2,1,0:T(8,128)S(1)}, u32[]{:S(2)}, u32[]{:S(2)}) collective-permute-start(f32[1,168,128]{2,1,0:T(8,128)S(1)} %get-tuple-element.71), channel_id=1, source_target_pairs={{0,6},{1,97},{2,0},{3,99},{4,2},{5,101},{6,4},{7,103},{8,14},{9,10... | collective-permute-start | bytes 258056 | tf_op jit(solution)/shard_map/ppermute | solution.py:589
  78.9 1.9 %collective-permute-done.20 = f32[1,168,128]{2,1,0:T(8,128)S(1)} collective-permute-done((f32[1,168,128]{2,1,0:T(8,128)S(1)}, f32[1,168,128]{2,1,0:T(8,128)S(1)}, u32[]{:S(2)}, u32[]{:S(2)}) %collective-permute-start.20) | collective-permute-done | bytes 86048 | tf_op jit(solution)/shard_map/ppermute | solution.py:589
  81.3 2.5 %collective-permute-done.21 = f32[1,168,128]{2,1,0:T(8,128)S(1)} collective-permute-done((f32[1,168,128]{2,1,0:T(8,128)S(1)}, f32[1,168,128]{2,1,0:T(8,128)S(1)}, u32[]{:S(2)}, u32[]{:S(2)}) %collective-permute-start.21) | collective-permute-done | bytes 86048 | tf_op jit(solution)/shard_map/ppermute | solution.py:589
  83.8 3.7 %collective-permute-start.23 = (f32[264,128]{1,0:T(8,128)S(1)}, f32[264,128]{1,0:T(8,128)S(1)}, u32[]{:S(2)}, u32[]{:S(2)}) collective-permute-start(f32[264,128]{1,0:T(8,128)S(1)} %bitcast.16), channel_id=1, source_target_pairs={{0,1},{1,0},{2,3},{3,2},{4,5},{5,4},{6,7},{7,6},{8,9},{9,8},{10,11... | collective-permute-start | bytes 405512 | tf_op jit(solution)/shard_map/ppermute | solution.py:606
  89.2 4.5 %shard_map.125 = (f32[128,128]{1,0:T(8,128)}, f32[128,128]{1,0:T(8,128)}, f32[128,128]{1,0:T(8,128)}, f32[8,128]{1,0:T(8,128)}, f32[128,128]{1,0:T(8,128)}) custom-call(f32[264,128]{1,0:T(8,128)} %bitcast.17, f32[264,128]{1,0:T(8,128)} %copy-done.3, s32[5]{0:T(128)} %compare_select_fusion.3.refs_1_.refs_2_.place_ref, f32[128,256]{1,0:T(8,128)} %constant.93.clone.lanes_ref, ...), custom_call_target="tpu_custom_call" | custom-call | tf_op jit(solution)/shard_map/pallas_call | solution.py:580
  93.7 14.4 %all_to_all.10 = f32[128,1,128]{2,1,0:T(1,128)} all-to-all(f32[128,1,128]{2,1,0:T(1,128)} %bitcast.19), channel_id=1, replica_groups=mesh['dp'=4,'grid'=32] {'dp','grid'}, dimensions={0} | all-to-all | bytes 131072 | tf_op jit(solution)/shard_map/all_to_all | solution.py:654
  108.1 5.2 %shard_map.126 = (f32[1024,128]{1,0:T(8,128)}, f32[8,128]{1,0:T(8,128)}) custom-call(f32[128,128]{1,0:T(8,128)} %bitcast.18, f32[8,128]{1,0:T(8,128)} %get-tuple-element.52.range_ref, f32[128,128]{1,0:T(8,128)} %get-tuple-element.53.scaled_ref, f32[128,128]{1,0:T(8,128)} %get-tuple-element.54.real_ref, f32[128,128]{1,0:T(8,128)} %get-tuple-element.55.imag_ref, ...), custom_call_target="tpu_custom_call" | custom-call | tf_op jit(solution)/shard_map/pallas_call | solution.py:580
  113.3 19.2 %all_to_all.11 = f32[128,8,128]{2,1,0:T(8,128)} all-to-all(f32[128,8,128]{2,1,0:T(8,128)} %bitcast.14), channel_id=1, replica_groups=mesh['dp'=4,'grid'=32] {'dp','grid'}, dimensions={0} | all-to-all | bytes 1048576 | tf_op jit(solution)/shard_map/all_to_all | solution.py:659
  132.5 2.4 %shard_map.127 = (f32[4,128,128]{2,1,0:T(8,128)}, f32[4,128,128]{2,1,0:T(8,128)}) custom-call(f32[1024,128]{1,0:T(8,128)} %bitcast.13, f32[8,128]{1,0:T(8,128)} %get-tuple-element.57.gain_ref, bf16[768,256]{1,0:T(8,128)(2,1)} %constant.98.clone.back_ref), custom_call_target="tpu_custom_call" | custom-call | tf_op jit(solution)/shard_map/pallas_call | solution.py:580
  (75 shorter events, 20.0 us)
Async XLA Ops:
  9.1 8.9 %collective-permute-start.7 = (f32[64,64,128]{2,1,0:T(8,128)}, f32[64,64,128]{2,1,0:T(8,128)}, u32[]{:S(2)}, u32[]{:S(2)}) collective-permute-start(f32[64,64,128]{2,1,0:T(8,128)} %get-tuple-element.38), channel_id=1, source_target_pairs={{0,1},{1,0},{2,3},{3,2},{4,5},{5,4},{6,7},{7,6},{8,9},{9,8},{10,11... | collective-permute-start | bytes 6291464 | tf_op jit(solution)/shard_map/ppermute | solution.py:606
  10.6 18.0 %collective-permute-start = (f32[64,64,128]{2,1,0:T(8,128)}, f32[64,64,128]{2,1,0:T(8,128)S(1)}, u32[]{:S(2)}, u32[]{:S(2)}) collective-permute-start(f32[64,64,128]{2,1,0:T(8,128)} %get-tuple-element.33), channel_id=1, source_target_pairs={{0,1},{1,0},{2,3},{3,2},{4,5},{5,4},{6,7},{7,6},{8,9},{9,8},{10,11... | collective-permute-start | bytes 6291464 | tf_op jit(solution)/shard_map/ppermute | solution.py:606
  10.7 4.9 %collective-permute-start.8 = (f32[128,128]{1,0:T(8,128)}, f32[128,128]{1,0:T(8,128)S(1)}, u32[]{:S(2)}, u32[]{:S(2)}) collective-permute-start(f32[128,128]{1,0:T(8,128)} %get-tuple-element.40), channel_id=1, source_target_pairs={{0,32},{1,33},{2,34},{3,35},{4,36},{5,37},{6,38},{7,39},{8,40},{9,... | collective-permute-start | bytes 196616 | tf_op jit(solution)/shard_map/ppermute | solution.py:589
  12.0 5.5 %collective-permute-start.9 = (f32[128,128]{1,0:T(8,128)}, f32[128,128]{1,0:T(8,128)S(1)}, u32[]{:S(2)}, u32[]{:S(2)}) collective-permute-start(f32[128,128]{1,0:T(8,128)} %get-tuple-element.41), channel_id=1, source_target_pairs={{0,64},{1,65},{2,66},{3,67},{4,68},{5,69},{6,70},{7,71},{8,72},{9,... | collective-permute-start | bytes 196616 | tf_op jit(solution)/shard_map/ppermute | solution.py:589
  14.4 3.6 %collective-permute-start.10 = (f32[128,128]{1,0:T(8,128)}, f32[128,128]{1,0:T(8,128)S(1)}, u32[]{:S(2)}, u32[]{:S(2)}) collective-permute-start(f32[128,128]{1,0:T(8,128)} %get-tuple-element.42), channel_id=1, source_target_pairs={{0,96},{1,97},{2,98},{3,99},{4,100},{5,101},{6,102},{7,103},{8,104... | collective-permute-start | bytes 196616 | tf_op jit(solution)/shard_map/ppermute | solution.py:589
  23.4 12.1 %collective-permute-start.14 = (f32[136,128]{1,0:T(8,128)}, f32[136,128]{1,0:T(8,128)S(1)}, u32[]{:S(2)}, u32[]{:S(2)}) collective-permute-start(f32[136,128]{1,0:T(8,128)} %get-tuple-element.48), channel_id=1, source_target_pairs={{0,32},{1,3},{2,34},{3,5},{4,36},{5,7},{6,38},{7,1},{8,40},{9,11},... | collective-permute-start | bytes 208904 | tf_op jit(solution)/shard_map/ppermute | solution.py:589
  24.8 12.4 %collective-permute-start.15 = (f32[136,128]{1,0:T(8,128)}, f32[136,128]{1,0:T(8,128)S(1)}, u32[]{:S(2)}, u32[]{:S(2)}) collective-permute-start(f32[136,128]{1,0:T(8,128)} %get-tuple-element.49), channel_id=1, source_target_pairs={{0,64},{1,5},{2,66},{3,7},{4,68},{5,1},{6,70},{7,3},{8,72},{9,13},... | collective-permute-start | bytes 208904 | tf_op jit(solution)/shard_map/ppermute | solution.py:589
  27.5 10.2 %collective-permute-start.16 = (f32[136,128]{1,0:T(8,128)}, f32[136,128]{1,0:T(8,128)S(1)}, u32[]{:S(2)}, u32[]{:S(2)}) collective-permute-start(f32[136,128]{1,0:T(8,128)} %get-tuple-element.50), channel_id=1, source_target_pairs={{0,96},{1,7},{2,98},{3,1},{4,100},{5,3},{6,102},{7,5},{8,104},{9,1... | collective-permute-start | bytes 208904 | tf_op jit(solution)/shard_map/ppermute | solution.py:589
  34.3 15.4 %collective-permute-start.1 = (f32[16,64,128]{2,1,0:T(8,128)}, f32[16,64,128]{2,1,0:T(8,128)S(1)}, u32[]{:S(2)}, u32[]{:S(2)}) collective-permute-start(f32[16,64,128]{2,1,0:T(8,128)} %get-tuple-element.35), channel_id=1, source_target_pairs={{0,32},{1,3},{2,34},{3,5},{4,36},{5,7},{6,38},{7,1},{8,40},{9,11},... | collective-permute-start | bytes 1572872 | tf_op jit(solution)/shard_map/ppermute | solution.py:589
  34.7 15.0 %collective-permute-start.2 = (f32[16,64,128]{2,1,0:T(8,128)}, f32[16,64,128]{2,1,0:T(8,128)S(1)}, u32[]{:S(2)}, u32[]{:S(2)}) collective-permute-start(f32[16,64,128]{2,1,0:T(8,128)} %get-tuple-element.36), channel_id=1, source_target_pairs={{0,64},{1,5},{2,66},{3,7},{4,68},{5,1},{6,70},{7,3},{8,72},{9,13},... | collective-permute-start | bytes 1572872 | tf_op jit(solution)/shard_map/ppermute | solution.py:589
  35.5 14.8 %collective-permute-start.3 = (f32[16,64,128]{2,1,0:T(8,128)}, f32[16,64,128]{2,1,0:T(8,128)S(1)}, u32[]{:S(2)}, u32[]{:S(2)}) collective-permute-start(f32[16,64,128]{2,1,0:T(8,128)} %get-tuple-element.37), channel_id=1, source_target_pairs={{0,96},{1,7},{2,98},{3,1},{4,100},{5,3},{6,102},{7,5},{8,104},{9,1... | collective-permute-start | bytes 1572872 | tf_op jit(solution)/shard_map/ppermute | solution.py:589
  37.2 23.7 %collective-permute-start.11 = (f32[16,64,128]{2,1,0:T(8,128)}, f32[16,64,128]{2,1,0:T(8,128)S(1)}, u32[]{:S(2)}, u32[]{:S(2)}) collective-permute-start(f32[16,64,128]{2,1,0:T(8,128)} %get-tuple-element.44), channel_id=1, source_target_pairs={{0,32},{1,3},{2,34},{3,5},{4,36},{5,7},{6,38},{7,1},{8,40},{9,11},... | collective-permute-start | bytes 1572872 | tf_op jit(solution)/shard_map/ppermute | solution.py:589
  37.7 26.8 %collective-permute-start.12 = (f32[16,64,128]{2,1,0:T(8,128)S(1)}, f32[16,64,128]{2,1,0:T(8,128)S(1)}, u32[]{:S(2)}, u32[]{:S(2)}) collective-permute-start(f32[16,64,128]{2,1,0:T(8,128)S(1)} %copy-done.9), channel_id=1, source_target_pairs={{0,64},{1,5},{2,66},{3,7},{4,68},{5,1},{6,70},{7,3},{8,72},{9,13},... | collective-permute-start | bytes 1572872 | tf_op jit(solution)/shard_map/ppermute | solution.py:589
  49.7 14.8 %collective-permute-start.13 = (f32[16,64,128]{2,1,0:T(8,128)S(1)}, f32[16,64,128]{2,1,0:T(8,128)S(1)}, u32[]{:S(2)}, u32[]{:S(2)}) collective-permute-start(f32[16,64,128]{2,1,0:T(8,128)S(1)} %copy-done.8), channel_id=1, source_target_pairs={{0,96},{1,7},{2,98},{3,1},{4,100},{5,3},{6,102},{7,5},{8,104},{9,1... | collective-permute-start | bytes 1572872 | tf_op jit(solution)/shard_map/ppermute | solution.py:589
  51.5 15.3 %collective-permute-start.4 = (f32[4,64,128]{2,1,0:T(8,128)S(1)}, f32[4,64,128]{2,1,0:T(8,128)S(1)}, u32[]{:S(2)}, u32[]{:S(2)}) collective-permute-start(f32[4,64,128]{2,1,0:T(8,128)S(1)} %get-tuple-element.67), channel_id=1, source_target_pairs={{0,8},{1,9},{2,10},{3,11},{4,12},{5,13},{6,14},{7,15},{8,16},{9,17... | collective-permute-start | bytes 393224 | tf_op jit(solution)/shard_map/ppermute | solution.py:589
  53.2 14.8 %collective-permute-start.6 = (f32[4,64,128]{2,1,0:T(8,128)S(1)}, f32[4,64,128]{2,1,0:T(8,128)S(1)}, u32[]{:S(2)}, u32[]{:S(2)}) collective-permute-start(f32[4,64,128]{2,1,0:T(8,128)S(1)} %get-tuple-element.68), channel_id=1, source_target_pairs={{0,24},{1,25},{2,26},{3,27},{4,28},{5,29},{6,30},{7,31},{8,0},{9,1... | collective-permute-start | bytes 393224 | tf_op jit(solution)/shard_map/ppermute | solution.py:589
  60.9 7.1 %collective-permute-start.5 = (f32[4,64,128]{2,1,0:T(8,128)S(1)}, f32[4,64,128]{2,1,0:T(8,128)S(1)}, u32[]{:S(2)}, u32[]{:S(2)}) collective-permute-start(f32[4,64,128]{2,1,0:T(8,128)S(1)} %get-tuple-element.69), channel_id=1, source_target_pairs={{0,16},{1,17},{2,18},{3,19},{4,20},{5,21},{6,22},{7,23},{8,24},{9,... | collective-permute-start | bytes 393224 | tf_op jit(solution)/shard_map/ppermute | solution.py:589
  64.7 6.6 %collective-permute-start.17 = (f32[4,80,128]{2,1,0:T(8,128)S(1)}, f32[4,80,128]{2,1,0:T(8,128)S(1)}, u32[]{:S(2)}, u32[]{:S(2)}) collective-permute-start(f32[4,80,128]{2,1,0:T(8,128)S(1)} %get-tuple-element.64), channel_id=1, source_target_pairs={{0,8},{1,9},{2,10},{3,11},{4,12},{5,13},{6,14},{7,15},{8,16},{9,17... | collective-permute-start | bytes 491528 | tf_op jit(solution)/shard_map/ppermute | solution.py:589
  65.5 9.4 %collective-permute-start.18 = (f32[4,80,128]{2,1,0:T(8,128)S(1)}, f32[4,80,128]{2,1,0:T(8,128)S(1)}, u32[]{:S(2)}, u32[]{:S(2)}) collective-permute-start(f32[4,80,128]{2,1,0:T(8,128)S(1)} %get-tuple-element.65), channel_id=1, source_target_pairs={{0,16},{1,17},{2,18},{3,19},{4,20},{5,21},{6,22},{7,23},{8,24},{9,... | collective-permute-start | bytes 491528 | tf_op jit(solution)/shard_map/ppermute | solution.py:589
  66.8 9.2 %collective-permute-start.19 = (f32[4,80,128]{2,1,0:T(8,128)S(1)}, f32[4,80,128]{2,1,0:T(8,128)S(1)}, u32[]{:S(2)}, u32[]{:S(2)}) collective-permute-start(f32[4,80,128]{2,1,0:T(8,128)S(1)} %get-tuple-element.66), channel_id=1, source_target_pairs={{0,24},{1,25},{2,26},{3,27},{4,28},{5,29},{6,30},{7,31},{8,0},{9,1... | collective-permute-start | bytes 491528 | tf_op jit(solution)/shard_map/ppermute | solution.py:589
  76.2 4.6 %collective-permute-start.20 = (f32[1,168,128]{2,1,0:T(8,128)S(1)}, f32[1,168,128]{2,1,0:T(8,128)S(1)}, u32[]{:S(2)}, u32[]{:S(2)}) collective-permute-start(f32[1,168,128]{2,1,0:T(8,128)S(1)} %get-tuple-element.70), channel_id=1, source_target_pairs={{0,2},{1,33},{2,4},{3,35},{4,6},{5,37},{6,0},{7,39},{8,10},{9,41},... | collective-permute-start | bytes 258056 | tf_op jit(solution)/shard_map/ppermute | solution.py:589
  76.2 5.0 %collective-permute-start.22 = (f32[1,168,128]{2,1,0:T(8,128)S(1)}, f32[1,168,128]{2,1,0:T(8,128)S(1)}, u32[]{:S(2)}, u32[]{:S(2)}) collective-permute-start(f32[1,168,128]{2,1,0:T(8,128)S(1)} %get-tuple-element.71), channel_id=1, source_target_pairs={{0,6},{1,97},{2,0},{3,99},{4,2},{5,101},{6,4},{7,103},{8,14},{9,10... | collective-permute-start | bytes 258056 | tf_op jit(solution)/shard_map/ppermute | solution.py:589
  78.9 4.8 %collective-permute-start.21 = (f32[1,168,128]{2,1,0:T(8,128)S(1)}, f32[1,168,128]{2,1,0:T(8,128)S(1)}, u32[]{:S(2)}, u32[]{:S(2)}) collective-permute-start(f32[1,168,128]{2,1,0:T(8,128)S(1)} %get-tuple-element.72), channel_id=1, source_target_pairs={{0,4},{1,65},{2,6},{3,67},{4,0},{5,69},{6,2},{7,71},{8,12},{9,73},... | collective-permute-start | bytes 258056 | tf_op jit(solution)/shard_map/ppermute | solution.py:589
  83.8 4.7 %collective-permute-start.23 = (f32[264,128]{1,0:T(8,128)S(1)}, f32[264,128]{1,0:T(8,128)S(1)}, u32[]{:S(2)}, u32[]{:S(2)}) collective-permute-start(f32[264,128]{1,0:T(8,128)S(1)} %bitcast.16), channel_id=1, source_target_pairs={{0,1},{1,0},{2,3},{3,2},{4,5},{5,4},{6,7},{7,6},{8,9},{9,8},{10,11... | collective-permute-start | bytes 405512 | tf_op jit(solution)/shard_map/ppermute | solution.py:606
  (10 other events, 85.2 us)
